TPU v7x, 32 devices: a whole 2x2x4 slice. The times are simulated.
32 devices in a mesh: dp: 8 (over z, y), rep: 4 (over x, core).
Axes of the slice: x: 2, y: 2, z: 4, core: 2. Of those that a mesh axis runs over, the one named last changes fastest.
Arguments:
- packet_bytes: int32 [4096, 256], P(('dp', 'rep')), may hold values from 0 to 255
- owner_index: int32 [4096], P(('dp', 'rep')), may hold values from 0 to 7, as said below
- session_id: int32 [4096], P(('dp', 'rep')), may hold values from 0 to 15
- class_label: int32 [512], P(('dp', 'rep')), may hold values from 0 to 127
- byte_table: bfloat16 [256, 64], replicated, may hold values from -6 to 6
- w_conv: bfloat16 [512, 512], replicated, may hold values from -0.25 to 0.25
- norm_gain: bfloat16 [512], replicated, may hold values from 0.099609375 to 1.8984375
- w_project: bfloat16 [512, 1536], replicated, may hold values from -7 to 7
- w_out: bfloat16 [512, 512], replicated, may hold values from -0.25 to 0.25
- w_head: bfloat16 [512, 128], replicated, may hold values from -4 to 4
Outputs:
- logits: float32 [512, 128], P(('dp', 'rep'))
- grad_table: float32 [256, 64], replicated
- grad_conv: float32 [512, 512], replicated
- grad_gain: float32 [512], replicated
- grad_project: float32 [512, 1536], replicated
- grad_out: float32 [512, 512], replicated
- grad_head: float32 [512, 128], replicated
Inputs may be any that keep to these rules, and one draw needn't show every extreme that they name: `owner_index`: of one device's packets at most 32 name any one owner; in each group along dp one owner is named by exactly 32 packets of every device of the group.
All inputs are finite; a program needn't handle non-finite values.
Results may differ from a plain program's by a relative error of at most 0.01.
Values may be sent and summed in bfloat16 or wider, within the bound.
No kernel may reach another device: no remote copies, remote signals or barrier semaphores. Data moves between devices by JAX's collectives and lax.ppermute only.
A program may use at most 128 MiB of HBM per device.

v0:
```python
import jax
import jax.numpy as jnp
from jax import lax
from jax.sharding import PartitionSpec as P

BYTES = 256
KERNEL = 8
HEADS = 8
SESS = 16


NORM_EPS = 1e-06


def silu_slope(values_in):
    sigma = jax.nn.sigmoid(values_in)
    return sigma * (1.0 + values_in * (1.0 - sigma))


def lookup_block(block_codes, byte_table):
    vocab = lax.broadcasted_iota(jnp.int32, (1, 1, 256), 2)
    onehot = (block_codes[:, :, None] == vocab).astype(jnp.bfloat16)
    return jnp.einsum("pbv,vc->pbc", onehot, byte_table, preferred_element_type=jnp.float32).astype(
        jnp.bfloat16
    )


def windows_of(byte_codes, byte_table):
    packets, length = byte_codes.shape
    blocks = byte_codes.reshape(packets // 16, 16, length)
    feats = lax.map(lambda block_codes: lookup_block(block_codes, byte_table), blocks)
    return feats.reshape(packets, length // KERNEL, KERNEL * byte_table.shape[1])


def session_layer(received, recv_session, labels_here, norm_gain, w_project, w_out, w_head):
    f32 = jnp.float32
    bf16 = jnp.bfloat16
    slot_count, model_width = received.shape
    head_dim = model_width // HEADS
    score_scale = head_dim ** (-0.5)
    as_float = received.astype(f32)
    inverse = lax.rsqrt(jnp.mean(as_float * as_float, axis=1, keepdims=True) + NORM_EPS)
    gain_f = norm_gain.astype(f32)
    norm_in = (as_float * inverse * gain_f).astype(bf16)
    projected = jnp.dot(norm_in, w_project, preferred_element_type=f32).astype(bf16)
    projected = projected.reshape(slot_count, 3, HEADS, head_dim)
    queries = projected[:, 0]
    keys_all = projected[:, 1]
    values = projected[:, 2]
    same_session = recv_session[:, None] == recv_session[None, :]
    scores = jnp.einsum("qhd,khd->hqk", queries, keys_all, preferred_element_type=f32) * score_scale
    scores = jnp.where(same_session[None], scores, -1e30)
    row_max = jnp.max(scores, axis=2, keepdims=True)
    shifted = jnp.exp(scores - row_max)
    mixing = shifted / jnp.sum(shifted, axis=2, keepdims=True)
    mixing_b = mixing.astype(bf16)
    attended = jnp.einsum("hqk,khd->qhd", mixing_b, values, preferred_element_type=f32).astype(bf16)
    attended = attended.reshape(slot_count, model_width)
    hidden = as_float + jnp.dot(attended, w_out, preferred_element_type=f32)
    member = (recv_session[None, :] == lax.broadcasted_iota(jnp.int32, (SESS, 1), 0)).astype(f32)
    counts = jnp.maximum(jnp.sum(member, axis=1, keepdims=True), 1.0)
    pooled = jnp.dot(member, hidden, precision=lax.Precision.HIGHEST) / counts
    pooled_b = pooled.astype(bf16)
    logits = jnp.dot(pooled_b, w_head, preferred_element_type=f32)
    class_probs = jax.nn.softmax(logits, axis=1)
    target = (
        labels_here[:, None] == lax.broadcasted_iota(jnp.int32, (1, w_head.shape[1]), 1)
    ).astype(f32)
    dlogits = (class_probs - target) / SESS
    grad_head = jnp.dot(pooled_b.astype(f32).T, dlogits, precision=lax.Precision.HIGHEST)
    dpooled = jnp.dot(dlogits, w_head.astype(f32).T, precision=lax.Precision.HIGHEST)
    dhidden = jnp.dot(member.T, dpooled / counts, precision=lax.Precision.HIGHEST)
    dhidden_b = dhidden.astype(bf16)
    grad_out = jnp.einsum("rk,rd->kd", attended, dhidden_b, preferred_element_type=f32)
    dattended = jnp.einsum("rd,kd->rk", dhidden_b, w_out, preferred_element_type=f32).astype(bf16)
    dattended = dattended.reshape(slot_count, HEADS, head_dim)
    dmixing = jnp.einsum("qhd,khd->hqk", dattended, values, preferred_element_type=f32)
    dvalues = jnp.einsum("hqk,qhd->khd", mixing_b, dattended, preferred_element_type=f32)
    dscores = (
        mixing * (dmixing - jnp.sum(mixing * dmixing, axis=2, keepdims=True)) * score_scale
    ).astype(bf16)
    dqueries = jnp.einsum("hqk,khd->qhd", dscores, keys_all, preferred_element_type=f32)
    dkeys = jnp.einsum("hqk,qhd->khd", dscores, queries, preferred_element_type=f32)
    dprojected = (
        jnp.stack([dqueries, dkeys, dvalues], axis=1)
        .reshape(slot_count, 3 * model_width)
        .astype(bf16)
    )
    grad_project = jnp.einsum("rk,rd->kd", norm_in, dprojected, preferred_element_type=f32)
    dnorm = jnp.einsum("rd,kd->rk", dprojected, w_project, preferred_element_type=f32)
    grad_gain = jnp.sum(dnorm * as_float * inverse, axis=0)
    scaled = dnorm * gain_f
    d_input = (
        inverse * scaled
        - as_float
        * (inverse * inverse * inverse)
        * jnp.mean(as_float * scaled, axis=1, keepdims=True)
        + dhidden
    )
    return (logits, d_input.astype(bf16), (grad_gain, grad_project, grad_out, grad_head))


def body(
    packet_bytes,
    owner_index,
    session_id,
    class_label,
    byte_table,
    w_conv,
    norm_gain,
    w_project,
    w_out,
    w_head,
):
    f32 = jnp.float32
    bf16 = jnp.bfloat16
    groups = lax.axis_size("dp")
    packet_count = packet_bytes.shape[0]
    slot_count = 2 * packet_count
    capacity = slot_count // groups
    positions = BYTES // KERNEL
    window_width = w_conv.shape[0]
    model_width = w_conv.shape[1]
    windows = windows_of(packet_bytes, byte_table).reshape(-1, window_width)
    conv = jnp.dot(windows, w_conv, preferred_element_type=f32).reshape(
        packet_count, positions, model_width
    )
    embedding = jnp.mean(jax.nn.silu(conv), axis=1).astype(bf16)
    targets = lax.broadcasted_iota(jnp.int32, (1, groups), 1)
    chosen = (owner_index[:, None] == targets).astype(jnp.int32)
    send_rank = jnp.sum((jnp.cumsum(chosen, axis=0) - 1) * chosen, axis=1)
    send_slot = owner_index * capacity + send_rank
    outgoing = jnp.zeros((slot_count, model_width), bf16).at[send_slot].set(embedding)
    out_session = jnp.full((slot_count,), -1.0, bf16).at[send_slot].set(session_id.astype(bf16))
    incoming, in_session = (
        lax.all_to_all(
            outgoing.reshape(groups, capacity, model_width),
            "dp",
            split_axis=0,
            concat_axis=0,
            tiled=True,
        ),
        lax.all_to_all(
            out_session.reshape(groups, capacity), "dp", split_axis=0, concat_axis=0, tiled=True
        ),
    )
    received = incoming.reshape(slot_count, model_width)
    recv_session = in_session.reshape(slot_count).astype(jnp.int32)
    logits, d_input, owner_grads = session_layer(
        received, recv_session, class_label, norm_gain, w_project, w_out, w_head
    )
    returned = lax.all_to_all(
        d_input.reshape(groups, capacity, model_width),
        "dp",
        split_axis=0,
        concat_axis=0,
        tiled=True,
    )
    dembedding = returned.reshape(slot_count, model_width)[send_slot]
    dconv = (
        (dembedding.astype(f32)[:, None, :] / positions * silu_slope(conv))
        .astype(bf16)
        .reshape(-1, model_width)
    )
    grad_conv = jnp.einsum("rk,rd->kd", windows, dconv, preferred_element_type=f32)
    dwindows = jnp.einsum("rd,kd->rk", dconv, w_conv, preferred_element_type=f32).astype(bf16)
    chan_count = byte_table.shape[1]
    dwindows = dwindows.reshape(packet_count // 16, 16 * BYTES, chan_count)
    code_blocks = packet_bytes.reshape(packet_count // 16, 16 * BYTES)

    def add_block(total, item):
        block_codes, block_grad = item
        onehot = (block_codes[:, None] == lax.broadcasted_iota(jnp.int32, (1, 256), 1)).astype(bf16)
        return (
            total + jnp.einsum("rv,rc->vc", onehot, block_grad, preferred_element_type=f32),
            None,
        )

    grad_table, unused = lax.scan(
        add_block, jnp.zeros((256, chan_count), f32), (code_blocks, dwindows)
    )
    grads = (grad_table, grad_conv, owner_grads[0], owner_grads[1], owner_grads[2], owner_grads[3])
    totals = lax.psum((grads[0], grads[1], grads[2], grads[3], grads[4], grads[5]), ("dp", "rep"))
    return (logits, totals[0], totals[1], totals[2], totals[3], totals[4], totals[5])


def solution(mesh):
    in_specs = (
        P(("dp", "rep"), None),
        P(("dp", "rep")),
        P(("dp", "rep")),
        P(("dp", "rep")),
        P(),
        P(),
        P(),
        P(),
        P(),
        P(),
    )
    out_specs = (P(("dp", "rep"), None), P(), P(), P(), P(), P(), P())
    return jax.shard_map(body, mesh=mesh, in_specs=in_specs, out_specs=out_specs, check_vma=False)
```

profile of v0, /device:TPU:11, one launch (start us, length us, event | category | flops | bytes accessed | tf_op | source)
XLA Modules:
  0.0 376.0 jit_solution(12326877280065003547)
XLA Ops:
  10.4 1.3 scatter_custom_fusion
  12.4 5.7 %all-to-all-start = ((bf16[8,1,32]{2,1,0:T(2,128)(2,1)}), bf16[8,1,32]{2,1,0:T(2,128)(2,1)S(1)}, u32[]{:S(2)}, u32[]{:S(2)}) async-start(bf16[8,1,32]{2,1,0:T(2,128)(2,1)} %all_to_all.16), calls=%async_computation | async-start | bytes 8192 | tf_op jit(solution)/shard_map/all_to_all | solution.py:143
  18.1 26.4 %while.21 = (s32[]{:T(128)}, bf16[8,16,256,64]{2,3,1,0:T(8,128)(2,1)}, s32[8,16,256]{2,1,0:T(8,128)}, bf16[256,64]{0,1:T(8,128)(2,1)}, s32[]{:T(128)}) while((s32[]{:T(128)}, bf16[8,16,256,64]{2,3,1,0:T(8,128)(2,1)}, s32[8,16,256]{2,1,0:T(8,128)}, bf16[256,64]{0,1:T(8,128)(2,1)}, s32[]{:T(128)}) %tuple.55), condition=%wide.region_4.5_spmd, body=%wide.region_3.4_spmd.sunk | while | flops 135528448 | bytes 606285 | solution.py:31
  18.8 2.6 fusion.106
  22.1 2.6 fusion.106
  25.4 2.6 fusion.106
  28.7 2.6 fusion.106
  32.0 2.6 fusion.106
  35.3 2.6 fusion.106
  38.6 2.6 fusion.106
  41.9 2.6 fusion.106
  44.5 8.5 %copy.48 = bf16[8,16,256,64]{3,2,1,0:T(8,128)(2,1)} copy(bf16[8,16,256,64]{2,3,1,0:T(8,128)(2,1)} %get-tuple-element.51) | data formatting | bytes 8388608 | tf_op jit(solution)/shard_map/while | solution.py:31
  53.0 11.8 %dot_general.68 = bf16[128,32,512]{2,1,0:T(8,128)(2,1)} reshape(bf16[8,16,256,64]{3,2,1,0:T(8,128)(2,1)} %copy.48) | data formatting | bytes 8388608 | tf_op jit(solution)/shard_map/dot_general | solution.py:125
  64.8 14.6 %multiply_reduce_fusion = (f32[128,512]{1,0:T(8,128)S(1)}, f32[128,32,512]{2,0,1:T(8,128)}) fusion(bf16[512,512]{1,0:T(8,128)(2,1)S(1)} %copy-done.29, bf16[128,32,512]{2,1,0:T(8,128)(2,1)} %dot_general.68), kind=kOutput, calls=%fused_computation.22 | convolution fusion | flops 2157903872 | bytes 13369344 | tf_op jit(solution)/shard_map/dot_general | solution.py:125
  80.0 11.8 %reshape_reshape.3 = bf16[4096,512]{1,0:T(8,128)(2,1)} reshape(bf16[8,16,256,64]{3,2,1,0:T(8,128)(2,1)} %copy.48) | data formatting | bytes 8388608 | tf_op jit(solution)/shard_map/reshape;reshape | solution.py:124
  91.8 1.7 scatter_custom_fusion.1
  93.6 5.4 %all-to-all-start.1 = ((bf16[8,32,512]{2,1,0:T(8,128)(2,1)}), bf16[8,32,512]{2,1,0:T(8,128)(2,1)S(1)}, u32[]{:S(2)}, u32[]{:S(2)}) async-start(bf16[8,32,512]{2,1,0:T(8,128)(2,1)} %bitcast.5), calls=%async_computation.1 | async-start | bytes 524288 | tf_op jit(solution)/shard_map/all_to_all | solution.py:136
  100.5 3.9 %all-to-all-done.1 = bf16[8,32,512]{2,1,0:T(8,128)(2,1)S(1)} async-done(((bf16[8,32,512]{2,1,0:T(8,128)(2,1)}), bf16[8,32,512]{2,1,0:T(8,128)(2,1)S(1)}, u32[]{:S(2)}, u32[]{:S(2)}) %all-to-all-start.1) | async-done | bytes 262176 | tf_op jit(solution)/shard_map/all_to_all | solution.py:136
  106.8 3.0 fusion.75
  109.8 2.0 convolution_convert_fusion.3
  114.8 1.3 fusion.56
  116.9 2.8 convolution_bitcast_fusion
  119.7 1.9 fusion.53
  121.6 5.0 %fusion.26 = bf16[256,1,8,64]{0,3,2,1:T(8,128)(2,1)} fusion(f32[8,256,256]{1,2,0:T(8,128)} %fusion.53, bf16[256,3,8,64]{0,3,2,1:T(8,128)(2,1)S(1)} %bitcast.141, f32[8,256,256]{1,2,0:T(8,128)} %get-tuple-element.94, f32[8,256]{1,0:T(8,128)} %copy-done.31), kind=kOutput, calls=%fused_computation.37 | convolution fusion | flops 70781184 | bytes 8929280 | tf_op jit(solution)/shard_map/hqk,khd->qhd/dot_general | solution.py:82
  126.6 5.0 %fusion.29 = bf16[256,1,8,64]{0,3,2,1:T(8,128)(2,1)} fusion(f32[8,256,256]{1,2,0:T(8,128)} %fusion.53, bf16[256,3,8,64]{0,3,2,1:T(8,128)(2,1)S(1)} %bitcast.142, f32[8,256,256]{1,2,0:T(8,128)} %get-tuple-element.94, f32[8,256]{1,0:T(8,128)S(1)} %copy-done.32), kind=kOutput, calls=%fused_computation.38 | convolution fusion | flops 70781184 | bytes 8929280 | tf_op jit(solution)/shard_map/hqk,qhd->khd/dot_general | solution.py:83
  132.8 1.5 fusion.49
  135.3 6.6 %all-to-all-start.2 = ((bf16[8,32,512]{2,1,0:T(8,128)(2,1)}), bf16[8,32,512]{2,1,0:T(8,128)(2,1)S(1)}, u32[]{:S(2)}, u32[]{:S(2)}) async-start(bf16[8,32,512]{2,1,0:T(8,128)(2,1)} %bitcast.21), calls=%async_computation.2 | async-start | bytes 524288 | tf_op jit(solution)/shard_map/all_to_all | solution.py:152
  143.1 2.3 fusion.78
  145.4 2.0 all-to-all-done.2
  148.4 5.0 %multiply_convert_fusion = bf16[128,32,512]{2,0,1:T(8,128)(2,1)S(1)} fusion(f32[128,32,512]{2,0,1:T(8,128)} %get-tuple-element.92, f32[128,512]{1,0:T(8,128)S(1)} %convert_multiply_fusion.2), kind=kLoop, calls=%fused_computation.21 | loop fusion | flops 18874368 | bytes 12845056 | tf_op jit(solution)/shard_map/convert_element_type | solution.py:162
  153.4 2.4 copy.56
  155.8 4.4 %convolution_convert_fusion = bf16[4096,512]{1,0:T(8,128)(2,1)} fusion(bf16[4096,512]{1,0:T(8,128)(2,1)S(1)} %bitcast.132, bf16[512,512]{1,0:T(8,128)(2,1)S(1)} %copy-done.30), kind=kOutput, calls=%fused_computation.24 | convolution fusion | flops 2149580800 | bytes 8912896 | tf_op jit(solution)/shard_map/rd,kd->rk/dot_general | solution.py:166
  160.2 3.3 fusion.77
  163.5 11.2 %reshape.174 = bf16[8,4096,64]{2,1,0:T(8,128)(2,1)} reshape(bf16[4096,512]{1,0:T(8,128)(2,1)} %convolution_convert_fusion) | data formatting | bytes 8388608 | tf_op jit(solution)/shard_map/reshape | solution.py:168
  174.7 29.5 %while.22 = (s32[]{:T(128)}, f32[256,64]{0,1:T(8,128)S(1)}, s32[8,4096]{1,0:T(8,128)S(1)}, bf16[8,4096,64]{2,1,0:T(8,128)(2,1)}, s32[]{:T(128)}, /*index=5*/s32[]{:T(128)}) while((s32[]{:T(128)}, f32[256,64]{0,1:T(8,128)S(1)}, s32[8,4096]{1,0:T(8,128)S(1)}, bf16[8,4096,64]{2,1,0:T(8,128)(2,1)}, s32[]{:T(128)}, ...), condition=%wide.region_16.17_spmd.clone, body=%wide.region_15.16_spmd.clone.sunk | while | flops 135299072 | bytes 1228895 | solution.py:179
  174.7 3.6 fusion.108
  178.4 3.6 fusion.108
  182.1 3.6 fusion.108
  185.8 3.6 fusion.108
  189.5 3.6 fusion.108
  193.2 3.6 fusion.108
  196.9 3.6 fusion.108
  200.5 3.6 fusion.108
  204.9 42.7 %psum.44 = f32[512]{0:T(512)} all-reduce(f32[512]{0:T(512)S(1)} %get-tuple-element.68), channel_id=1, replica_groups=mesh['dp'=8,'rep'=4] {'dp','rep'}, use_global_device_ids=true, to_apply=%region_20.21 | all-reduce | flops 512 | bytes 4096 | tf_op jit(solution)/shard_map/psum | solution.py:183
  247.6 112.1 %all-reduce.3.cloned.1.call-done = (f32[256,64]{0,1:T(8,128)}, f32[512,512]{1,0:T(8,128)}, f32[512,1536]{1,0:T(8,128)}, f32[512,512]{1,0:T(8,128)}, f32[512,128]{1,0:T(8,128)}) async-done(((f32[256,64]{0,1:T(8,128)}, f32[512,512]{1,0:T(8,128)}, f32[512,1536]{1,0:T(8,128)}, f32[512,512]{1,0:T(8,128)}, f32[512,128]{1,0:T(8,128)}), (f32[256,64]{0,1:T(8,128)}, f32[512,512]{1,0:T(8,128)}, f32[512,1536]{1,0:T(8,128)}, ...) | async-done | bytes 5570576 | tf_op jit(solution)/shard_map/psum | solution.py:183
  359.7 1.5 copy.84
  361.2 2.3 copy.85
  363.4 3.9 %copy.86 = f32[512,1536]{1,0:T(8,128)} copy(f32[512,1536]{1,0:T(8,128)} %get-tuple-element.187) | data formatting | bytes 6291456
  (124 shorter events, 24.7 us)
Async XLA Ops:
  7.2 98.7 %copy-start = (bf16[512,1536]{1,0:T(8,128)(2,1)S(1)}, bf16[512,1536]{1,0:T(8,128)(2,1)}, u32[]{:S(2)}) copy-start(bf16[512,1536]{1,0:T(8,128)(2,1)} %param.21) | copy-start | bytes 4718596
  12.4 81.2 %all-to-all-start = ((bf16[8,1,32]{2,1,0:T(2,128)(2,1)}), bf16[8,1,32]{2,1,0:T(2,128)(2,1)S(1)}, u32[]{:S(2)}, u32[]{:S(2)}) async-start(bf16[8,1,32]{2,1,0:T(2,128)(2,1)} %all_to_all.16), calls=%async_computation | async-start | bytes 8192 | tf_op jit(solution)/shard_map/all_to_all | solution.py:143
  53.0 11.8 %copy-start.29 = (bf16[512,512]{1,0:T(8,128)(2,1)S(1)}, bf16[512,512]{1,0:T(8,128)(2,1)}, u32[]{:S(2)}) copy-start(bf16[512,512]{1,0:T(8,128)(2,1)} %param.19) | copy-start | bytes 1572868
  64.8 15.2 %copy-start.6 = (s32[8,16,256]{2,1,0:T(8,128)S(1)}, s32[8,16,256]{2,1,0:T(8,128)}, u32[]{:S(2)}) copy-start(s32[8,16,256]{2,1,0:T(8,128)} %get-tuple-element.211) | copy-start | bytes 393220
  80.0 11.8 %copy-start.25 = (bf16[512]{0:T(512)(128)(2,1)S(1)}, bf16[512]{0:T(512)(128)(2,1)}, u32[]{:S(2)}) copy-start(bf16[512]{0:T(512)(128)(2,1)} %param.20) | copy-start | bytes 3076
  91.8 12.8 %copy-start.15 = (f32[512]{0:T(512)}, f32[512]{0:T(512)S(1)}, u32[]{:S(2)}) copy-start(f32[512]{0:T(512)S(1)} %convert_element_type.118) | copy-start | bytes 6148
  93.6 10.9 %all-to-all-start.1 = ((bf16[8,32,512]{2,1,0:T(8,128)(2,1)}), bf16[8,32,512]{2,1,0:T(8,128)(2,1)S(1)}, u32[]{:S(2)}, u32[]{:S(2)}) async-start(bf16[8,32,512]{2,1,0:T(8,128)(2,1)} %bitcast.5), calls=%async_computation.1 | async-start | bytes 524288 | tf_op jit(solution)/shard_map/all_to_all | solution.py:136
  99.1 5.3 %copy-start.17 = (s32[256]{0:T(256)}, s32[256]{0:T(256)S(1)}, u32[]{:S(2)}) copy-start(s32[256]{0:T(256)S(1)} %reshape.175) | copy-start | bytes 3076
  104.6 0.6 copy-start.13
  105.2 0.6 copy-start.19
  109.7 2.0 copy-start.31
  109.8 2.0 copy-start.3
  109.8 2.3 copy-start.18
  109.8 2.4 copy-start.28
  111.7 0.9 copy-start.8
  111.7 1.7 copy-start.26
  112.9 0.6 copy-start.9
  112.9 0.9 copy-start.21
  113.5 0.5 copy-start.23
  116.9 2.8 copy-start.4
  121.6 5.0 %copy-start.32 = (f32[8,256]{1,0:T(8,128)S(1)}, f32[8,256]{1,0:T(8,128)}, u32[]{:S(2)}) copy-start(f32[8,256]{1,0:T(8,128)} %copy-done.31) | copy-start | bytes 24580
  132.8 1.6 copy-start.20
  132.8 1.6 copy-start.16
  132.8 9.1 %copy-start.14 = (f32[8,32]{1,0:T(8,128)S(1)}, f32[8,32]{1,0:T(8,128)}, u32[]{:S(2)}) copy-start(f32[8,32]{1,0:T(8,128)} %copy-done.13) | copy-start | bytes 3076
  134.3 7.7 %copy-start.10 = (f32[16,128]{1,0:T(8,128)S(1)}, f32[16,128]{1,0:T(8,128)}, u32[]{:S(2)}) copy-start(f32[16,128]{1,0:T(8,128)} %copy-done.9) | copy-start | bytes 24580
  134.3 7.7 %copy-start.22 = (f32[16]{0:T(128)S(1)}, f32[16]{0:T(128)}, u32[]{:S(2)}) copy-start(f32[16]{0:T(128)} %copy-done.21) | copy-start | bytes 196
  134.3 7.7 %copy-start.24 = (f32[16]{0:T(128)S(1)}, f32[16]{0:T(128)}, u32[]{:S(2)}) copy-start(f32[16]{0:T(128)} %copy-done.23) | copy-start | bytes 196
  134.3 7.7 %copy-start.27 = (s32[16]{0:T(128)S(1)}, s32[16]{0:T(128)}, u32[]{:S(2)}) copy-start(s32[16]{0:T(128)} %param.17) | copy-start | bytes 196
  135.3 12.1 %all-to-all-start.2 = ((bf16[8,32,512]{2,1,0:T(8,128)(2,1)}), bf16[8,32,512]{2,1,0:T(8,128)(2,1)S(1)}, u32[]{:S(2)}, u32[]{:S(2)}) async-start(bf16[8,32,512]{2,1,0:T(8,128)(2,1)} %bitcast.21), calls=%async_computation.2 | async-start | bytes 524288 | tf_op jit(solution)/shard_map/all_to_all | solution.py:152
  141.9 217.8 %all-reduce.3.cloned.1.call-start = ((), (), s32[]{:S(2)}) async-start(), calls=%async_computation.3 | async-start | bytes 11141120 | tf_op jit(solution)/shard_map/psum | solution.py:183
  153.4 2.4 copy-start.30
  155.8 4.4 %copy-start.2 = (bf16[4096,512]{1,0:T(8,128)(2,1)S(1)}, bf16[4096,512]{1,0:T(8,128)(2,1)}, u32[]{:S(2)}) copy-start(bf16[4096,512]{1,0:T(8,128)(2,1)} %reshape_reshape.3) | copy-start | bytes 12582916
  163.5 11.2 %copy-start.11 = (f32[256,64]{0,1:T(8,128)S(1)}, f32[256,64]{0,1:T(8,128)}, u32[]{:S(2)}) copy-start(f32[256,64]{0,1:T(8,128)} %custom-call) | copy-start | bytes 196612
  204.2 0.6 copy-start.12
  363.4 3.9 %copy-start.5 = (f32[512,512]{1,0:T(8,128)S(1)}, f32[512,512]{1,0:T(8,128)}, u32[]{:S(2)}) copy-start(f32[512,512]{1,0:T(8,128)} %get-tuple-element.188) | copy-start | bytes 3145732
  363.4 5.7 %copy-start.1 = (bf16[512,1536]{1,0:T(8,128)(2,1)S(1)}, bf16[512,1536]{1,0:T(8,128)(2,1)}, u32[]{:S(2)}) copy-start(bf16[512,1536]{1,0:T(8,128)(2,1)} %param.21) | copy-start | bytes 4718596
  367.3 1.1 copy-start.7
Sparse Core Ops, SparseCore 0:
  205.0 154.6 all-reduce.2
where the time goes:
time: 382 us; the launch traced here: 376 us
  waiting for transfers between devices  118 us (31%)
  matrix products  100 us (26%)
  local copies, waits for them, and re-layouts  68 us (18%)
  blocking collectives  42.7 us (11%)
  starting transfers between devices  17.8 us (5%)
  other arithmetic  14.6 us (4%)
  between operations  14.4 us (4%)
    psum x1, waiting for transfers between devices, body(): lax.psum((grads[0], grads[1], grads[2], grads[3], grads[4], grads[5]), ('...  112 us
    psum x1, blocking collectives, body(): lax.psum((grads[0], grads[1], grads[2], grads[3], grads[4], grads[5]), ('...  42.7 us
    dot_general x8, matrix products, add_block(): jnp.einsum('rv,rc->vc', onehot, block_grad, preferred_element_type=f32)  29.1 us
    dot_general x8, matrix products, lookup_block(): jnp.einsum('pbv,vc->pbc', onehot, byte_table, preferred_element_type=jnp....  20.6 us
    dot_general x1, matrix products, body(): jnp.dot(windows, w_conv, preferred_element_type=f32)  14.6 us
    unnamed x71, local copies, waits for them, and re-layouts  12.2 us
    dot_general x1, local copies, waits for them, and re-layouts, body(): jnp.dot(windows, w_conv, preferred_element_type=f32)  11.8 us
    another operation x1, local copies, waits for them, and re-layouts, body(): windows = windows_of(packet_bytes, byte_table).reshape(-1, window_width)  11.8 us
  transfers between devices with their start and end apart: 4, of which 3 were waited for; matrix products, arithmetic and copies ran while one was open for 21% of the time, Pallas kernels for 0%

commit v1 on v0

v1 whole, which is shorter than its diff:
```python
import functools

import jax
import jax.numpy as jnp
from jax import lax
from jax.experimental import pallas as pl
from jax.experimental.pallas import tpu as pltpu
from jax.sharding import PartitionSpec as P

KERNEL = 8
HEADS = 8
NORM_EPS = 1e-06
WIN_STEP = 4
LANES = 128
VMEM_LIMIT = 56 * 2**20

f32 = jnp.float32
bf16 = jnp.bfloat16
AXES = ("dp", "rep")


def iota(shape, dim):
    return lax.broadcasted_iota(jnp.int32, shape, dim)


def dot_nn(a, b):
    return jnp.dot(a, b, preferred_element_type=f32)


def dot_nt(a, b):
    return lax.dot_general(a, b, (((1,), (1,)), ((), ())), preferred_element_type=f32)


def dot_tn(a, b):
    return lax.dot_general(a, b, (((0,), (0,)), ((), ())), preferred_element_type=f32)


def two_parts(value):
    high = value.astype(bf16)
    return high, (value - high.astype(f32)).astype(bf16)


def flag(mask):
    return jnp.where(mask, 1.0, 0.0).astype(bf16)


def embed_kernel(
    capacity, bytes_ref, own_row_ref, own_col_ref, sess_ref, table_ref, w_ref, out_ref, slope_ref, pair_ref, emb_ref
):
    step = pl.program_id(0)
    packets, length = bytes_ref.shape
    positions = length // KERNEL
    vocab, chan = table_ref.shape
    width = w_ref.shape[1]

    @pl.when(step == 0)
    def _():
        pair_ref[...] = jnp.zeros_like(pair_ref)
        pair_ref[0:vocab, 0:chan] = table_ref[...]
        pair_ref[vocab : 2 * vocab, chan : 2 * chan] = table_ref[...]
        emb_ref[...] = jnp.zeros_like(emb_ref)

    here = WIN_STEP * KERNEL
    codes = pltpu.roll(bytes_ref[...], lax.rem(length - here * step, length), 1)[:, :here]
    values = iota((packets, vocab), 1)
    pairs = []
    for k in range(KERNEL // 2):
        rows = []
        for w in range(WIN_STEP):
            j = w * KERNEL + 2 * k
            rows.append(
                jnp.concatenate([flag(codes[:, j : j + 1] == values), flag(codes[:, j + 1 : j + 2] == values)], axis=1)
            )
        pairs.append(dot_nn(jnp.concatenate(rows, axis=0), pair_ref[...]).astype(bf16))
    windows = jnp.concatenate(pairs, axis=1)
    conv = dot_nn(windows, w_ref[...])
    sigma = jax.nn.sigmoid(conv)
    act = conv * sigma
    slope_ref[...] = ((sigma + act * (1.0 - sigma)) * (1.0 / positions)).astype(bf16)
    total = emb_ref[...]
    for w in range(WIN_STEP):
        total += act[w * packets : (w + 1) * packets]
    emb_ref[...] = total

    @pl.when(step == pl.num_programs(0) - 1)
    def _():
        emb = (emb_ref[...] * (1.0 / positions)).astype(bf16)
        own_row = own_row_ref[...]
        same = (own_col_ref[...] == own_row) & (iota((packets, packets), 0) < iota((packets, packets), 1))
        rank = jnp.sum(jnp.where(same, 1.0, 0.0), axis=0, keepdims=True).astype(jnp.int32)
        place = flag(iota((out_ref.shape[0], packets), 0) == own_row * capacity + rank)
        out_ref[:, :width] = dot_nn(place, emb).astype(bf16)
        label = jnp.broadcast_to((sess_ref[...] + 1).astype(f32), (packets, LANES)).astype(bf16)
        out_ref[:, width:] = dot_nn(place, label).astype(bf16)


def embed(packet_bytes, own_row, own_col, sess_col, byte_table, w_conv, capacity, slots):
    packets, length = packet_bytes.shape
    rows = WIN_STEP * packets
    steps = length // (KERNEL * WIN_STEP)
    width = w_conv.shape[1]
    vocab, chan = byte_table.shape
    whole = lambda a: pl.BlockSpec(a.shape, lambda i: (0, 0))
    args = (packet_bytes, own_row, own_col, sess_col, byte_table, w_conv)
    return pl.pallas_call(
        functools.partial(embed_kernel, capacity),
        grid=(steps,),
        in_specs=[whole(a) for a in args],
        out_specs=[
            pl.BlockSpec((slots, width + LANES), lambda i: (0, 0)),
            pl.BlockSpec((rows, width), lambda i: (i, 0)),
        ],
        out_shape=[
            jax.ShapeDtypeStruct((slots, width + LANES), bf16),
            jax.ShapeDtypeStruct((steps * rows, width), bf16),
        ],
        scratch_shapes=[pltpu.VMEM((2 * vocab, 2 * chan), bf16), pltpu.VMEM((packets, width), f32)],
        compiler_params=pltpu.CompilerParams(vmem_limit_bytes=VMEM_LIMIT),
        name="embed",
    )(*args)


def session_kernel(
    inc_ref,
    label_ref,
    gain_ref,
    wp_ref,
    wo_ref,
    wh_ref,
    logits_ref,
    back_ref,
    early_ref,
    gain_grad_ref,
    proj_ref,
    att_ref,
    mix_ref,
    dproj_ref,
):
    slots = inc_ref.shape[0]
    width = wo_ref.shape[0]
    classes = wh_ref.shape[1]
    sessions = label_ref.shape[0]
    head = width // HEADS
    scale = head**-0.5

    embedding = inc_ref[:, :width]
    x = embedding.astype(f32)
    tags = inc_ref[:, width:].astype(f32)
    tag_col = tags[:, 0:1]
    tag_row = tags.T[0:1, :]
    gain = gain_ref[...].astype(f32)
    inverse = lax.rsqrt(jnp.mean(x * x, axis=1, keepdims=True) + NORM_EPS)
    norm_in = (x * inverse * gain).astype(bf16)
    proj_ref[...] = dot_nn(norm_in, wp_ref[...]).astype(bf16)

    def part(ref, which, h):
        at = which * width + h * head
        return ref[:, at : at + head]

    same = tag_col == tag_row
    for h in range(HEADS):
        scores = dot_nt(part(proj_ref, 0, h), part(proj_ref, 1, h)) * scale
        scores = jnp.where(same, scores, -1e30)
        shifted = jnp.exp(scores - jnp.max(scores, axis=1, keepdims=True))
        mixing = shifted / jnp.sum(shifted, axis=1, keepdims=True)
        mix_ref[h] = mixing
        att_ref[:, h * head : (h + 1) * head] = dot_nn(mixing.astype(bf16), part(proj_ref, 2, h)).astype(bf16)

    is_member = tag_row == (iota((sessions, slots), 0) + 1).astype(f32)
    member = flag(is_member)
    member_t = flag(tag_col == (iota((slots, sessions), 1) + 1).astype(f32))
    counts = jnp.maximum(jnp.sum(jnp.where(is_member, 1.0, 0.0), axis=1, keepdims=True), 1.0)
    att_high, att_low = two_parts(dot_nn(member, att_ref[...]))
    out_sum = dot_nn(att_high, wo_ref[...]) + dot_nn(att_low, wo_ref[...])
    pooled_b = ((dot_nn(member, embedding) + out_sum) / counts).astype(bf16)
    logits = dot_nn(pooled_b, wh_ref[...])
    logits_ref[...] = logits
    grown = jnp.exp(logits - jnp.max(logits, axis=1, keepdims=True))
    probs = grown / jnp.sum(grown, axis=1, keepdims=True)
    target = jnp.where(label_ref[...] == iota((sessions, classes), 1), 1.0, 0.0)
    dlogits = (probs - target) * (1.0 / sessions)
    dl_high, dl_low = two_parts(dlogits)
    grad_head = dot_tn(pooled_b, dl_high) + dot_tn(pooled_b, dl_low)
    dpooled = dot_nt(dl_high, wh_ref[...]) + dot_nt(dl_low, wh_ref[...])
    dsess = dpooled / counts
    dsess_b, dsess_low = two_parts(dsess)
    dhidden = dot_nn(member_t, dsess_b) + dot_nn(member_t, dsess_low)
    grad_out = dot_tn(att_high, dsess_b) + dot_tn(att_low, dsess_b)
    datt_s = dot_nt(dsess_b, wo_ref[...]).astype(bf16)
    datt = dot_nn(member_t, datt_s).astype(bf16)

    for h in range(HEADS):
        cols = slice(h * head, (h + 1) * head)
        mixing = mix_ref[h]
        dmix_s = dot_nt(datt_s[:, cols], part(proj_ref, 2, h))
        dmixing = jnp.sum(jnp.where(is_member, dmix_s, 0.0), axis=0, keepdims=True)
        weighted = mixing * dmixing
        dscores = ((weighted - mixing * jnp.sum(weighted, axis=1, keepdims=True)) * scale).astype(bf16)
        dq = dot_nn(dscores, part(proj_ref, 1, h))
        dk = dot_tn(dscores, part(proj_ref, 0, h))
        dv = dot_tn(mixing.astype(bf16), datt[:, cols])
        for which, d in ((0, dq), (1, dk), (2, dv)):
            at = which * width + h * head
            dproj_ref[:, at : at + head] = d.astype(bf16)

    def put(at, block):
        for s in range(block.shape[1] // LANES):
            early_ref[at + s * width : at + (s + 1) * width, :] = block[:, s * LANES : (s + 1) * LANES].astype(bf16)
        return at + block.shape[1] // LANES * width

    at = 0
    for which in range(3):
        at = put(at, dot_tn(norm_in, dproj_ref[:, which * width : (which + 1) * width]))
    at = put(at, grad_out)
    put(at, grad_head)
    dnorm = dot_nt(dproj_ref[...], wp_ref[...])
    grad_gain = jnp.sum(dnorm * x * inverse, axis=0, keepdims=True)
    gain_grad_ref[...] = jnp.zeros_like(gain_grad_ref)
    for s in range(width // LANES):
        gain_grad_ref[s : s + 1, :] = grad_gain[:, s * LANES : (s + 1) * LANES]
    scaled = dnorm * gain
    slant = jnp.mean(x * scaled, axis=1, keepdims=True) * (inverse * inverse * inverse)
    back_ref[...] = (inverse * scaled - x * slant + dhidden).astype(bf16)


def session_layer(incoming, labels, gain, w_project, w_out, w_head):
    slots = incoming.shape[0]
    width = w_out.shape[0]
    sessions, classes = labels.shape[0], w_head.shape[1]
    early_rows = width * (3 * width + width + classes) // LANES
    args = (incoming, labels, gain, w_project, w_out, w_head)
    vmem = pl.BlockSpec(memory_space=pltpu.VMEM)
    return pl.pallas_call(
        session_kernel,
        in_specs=[vmem] * len(args),
        out_specs=[vmem] * 4,
        out_shape=[
            jax.ShapeDtypeStruct((sessions, classes), f32),
            jax.ShapeDtypeStruct((slots, width), bf16),
            jax.ShapeDtypeStruct((early_rows, LANES), bf16),
            jax.ShapeDtypeStruct((16, LANES), f32),
        ],
        scratch_shapes=[
            pltpu.VMEM((slots, 3 * width), bf16),
            pltpu.VMEM((slots, width), bf16),
            pltpu.VMEM((HEADS, slots, slots), f32),
            pltpu.VMEM((slots, 3 * width), bf16),
        ],
        compiler_params=pltpu.CompilerParams(vmem_limit_bytes=VMEM_LIMIT),
        name="session_layer",
    )(*args)


def conv_back_kernel(
    capacity,
    ret_ref,
    own_row_ref,
    own_col_ref,
    codes_ref,
    slope_ref,
    table_ref,
    w_ref,
    gain_grad_ref,
    late_ref,
    dconv_ref,
    table_grad_ref,
):
    j = pl.program_id(0)
    slots, width = ret_ref.shape
    packets = own_col_ref.shape[0]
    vocab, chan = table_ref.shape
    positions = codes_ref.shape[1]

    @pl.when(j == 0)
    def _():
        same = (own_col_ref[...] == own_row_ref[...]) & (iota((packets, packets), 1) < iota((packets, packets), 0))
        rank = jnp.sum(jnp.where(same, 1.0, 0.0), axis=1, keepdims=True).astype(jnp.int32)
        place = flag(iota((packets, slots), 1) == own_col_ref[...] * capacity + rank)
        demb = dot_nn(place, ret_ref[...])
        for w in range(positions):
            at = slice(w * packets, (w + 1) * packets)
            dconv_ref[at, :] = (demb * slope_ref[at, :].astype(f32)).astype(bf16)
        table_grad_ref[...] = jnp.zeros_like(table_grad_ref)
        late_ref[...] = jnp.zeros_like(late_ref)

    values = iota((vocab, packets), 0)
    onehot = jnp.concatenate([flag(codes_ref[0, w : w + 1, :] == values) for w in range(positions)], axis=1)
    by_value = dot_nn(onehot, dconv_ref[...]).astype(bf16)
    w_rows = w_ref[pl.ds(pl.multiple_of(j * chan, chan), chan), :]
    table_grad_ref[...] += dot_nt(by_value, w_rows)
    grad_rows = dot_tn(table_ref[...], by_value).astype(bf16)
    window = KERNEL * chan
    for s in range(width // LANES):
        at = pl.multiple_of(s * window + j * chan, chan)
        late_ref[pl.ds(at, chan), :] = grad_rows[:, s * LANES : (s + 1) * LANES]

    @pl.when(j == pl.num_programs(0) - 1)
    def _():
        at = width // LANES * window
        half = vocab * chan // LANES
        late_ref[at : at + half, 0:chan] = table_grad_ref[0:half, :].astype(bf16)
        late_ref[at : at + half, chan : 2 * chan] = table_grad_ref[half : 2 * half, :].astype(bf16)
        late_ref[at + half : at + half + 16, :] = gain_grad_ref[...].astype(bf16)


def conv_back(returned, own_row, own_col, codes, slope, byte_table, w_conv, gain_grad, capacity, late_rows):
    width = w_conv.shape[1]
    whole = lambda a: pl.BlockSpec(a.shape, lambda j: (0, 0))
    args = (returned, own_row, own_col, codes, slope, byte_table, w_conv, gain_grad)
    specs = [whole(a) if a.ndim == 2 else pl.BlockSpec((1, *a.shape[1:]), lambda j: (j, 0, 0)) for a in args]
    return pl.pallas_call(
        functools.partial(conv_back_kernel, capacity),
        grid=(KERNEL,),
        in_specs=specs,
        out_specs=pl.BlockSpec((late_rows, LANES), lambda j: (0, 0)),
        out_shape=jax.ShapeDtypeStruct((late_rows, LANES), bf16),
        scratch_shapes=[pltpu.VMEM(slope.shape, bf16), pltpu.VMEM(byte_table.shape, f32)],
        compiler_params=pltpu.CompilerParams(vmem_limit_bytes=VMEM_LIMIT),
        name="conv_back",
    )(*args)


class Levels:
    def __init__(self, n_dp, n_rep):
        self.count = n_dp * n_rep
        self.index = lax.axis_index("dp") * n_rep + lax.axis_index("rep")
        self.levels = []
        stride, left = 1, self.count
        for size in (2, *[4] * 8):
            while size > 1 and left % size:
                size //= 2
            if size > 1:
                self.levels.append((stride, size))
                stride, left = stride * size, left // size
        assert left == 1

    def place(self, level):
        stride, size = level
        return lax.rem(lax.div(self.index, stride), size)

    def swap(self, value, level, d):
        stride, size = level
        return lax.ppermute(value, AXES, [(i, i + ((i // stride % size ^ d) - i // stride % size) * stride) for i in range(self.count)])

    def scatter_sum(self, value, level):
        size = level[1]
        value = value.reshape(size, value.shape[0] // size, value.shape[1])
        mine = self.place(level)
        got = [self.swap(lax.dynamic_index_in_dim(value, mine ^ d, 0, keepdims=False), level, d) for d in range(1, size)]
        total = lax.dynamic_index_in_dim(value, mine, 0, keepdims=False).astype(f32)
        for g in got:
            total = total + g.astype(f32)
        return total.astype(bf16)

    def gather(self, value, level):
        size = level[1]
        mine = self.place(level)
        got = [self.swap(value, level, d) for d in range(1, size)]
        out = jnp.zeros((size, *value.shape), value.dtype)
        for d, g in enumerate([value, *got]):
            out = lax.dynamic_update_index_in_dim(out, g, mine ^ d, 0)
        return out.reshape(size * value.shape[0], value.shape[1])

    def all_sum(self, value):
        for level in self.levels:
            value = self.scatter_sum(value, level)
        for level in self.levels[::-1]:
            value = self.gather(value, level)
        return value


def body(packet_bytes, owner_index, session_id, class_label, byte_table, w_conv, norm_gain, w_project, w_out, w_head):
    groups = lax.axis_size("dp")
    devices = Levels(groups, lax.axis_size("rep"))
    packets, length = packet_bytes.shape
    slots = 2 * packets
    capacity = slots // groups
    positions = length // KERNEL
    width = w_conv.shape[1]
    window = w_conv.shape[0]
    vocab, chan = byte_table.shape
    classes = w_head.shape[1]

    own_row = owner_index.reshape(1, packets)
    own_col = owner_index.reshape(packets, 1)
    outgoing, slope = embed(
        packet_bytes, own_row, own_col, session_id.reshape(packets, 1), byte_table, w_conv, capacity, slots
    )

    def exchange(rows):
        return lax.all_to_all(
            rows.reshape(groups, capacity, rows.shape[1]), "dp", split_axis=0, concat_axis=0, tiled=True
        ).reshape(rows.shape)

    logits, back, early, gain_grad = session_layer(
        exchange(outgoing), class_label.reshape(-1, 1), norm_gain.reshape(1, width), w_project, w_out, w_head
    )
    codes = packet_bytes.reshape(packets, positions, KERNEL).transpose(2, 1, 0)
    used = width // LANES * window + vocab * chan // LANES + 16
    unit = 8 * devices.count
    late_rows = -(-used // unit) * unit
    late = conv_back(
        exchange(back), own_row, own_col, codes, slope, byte_table, w_conv, gain_grad, capacity, late_rows
    )
    early = devices.all_sum(early).astype(f32)
    late = devices.all_sum(late).astype(f32)

    def take(rows, at, height, blocks):
        return rows[at : at + height * blocks].reshape(blocks, height, LANES).transpose(1, 0, 2).reshape(height, -1)

    wide = width // LANES
    grad_project = take(early, 0, width, 3 * wide)
    grad_out = take(early, 3 * wide * width, width, wide)
    grad_head = take(early, 4 * wide * width, width, classes // LANES)
    grad_conv = take(late, 0, window, wide)
    at = wide * window
    half = vocab * chan // LANES
    grad_table = jnp.concatenate([late[at : at + half, :chan], late[at : at + half, chan : 2 * chan]], axis=0)
    grad_gain = late[at + half : at + half + wide].reshape(width)
    return (logits, grad_table, grad_conv, grad_gain, grad_project, grad_out, grad_head)


def solution(mesh):
    split = P(AXES)
    rows = P(AXES, None)
    in_specs = (rows, split, split, split, P(), P(), P(), P(), P(), P())
    out_specs = (rows, P(), P(), P(), P(), P(), P())
    return jax.shard_map(body, mesh=mesh, in_specs=in_specs, out_specs=out_specs, check_vma=False)
```

time: 382 us -> 181 us (0.47)
  matrix products: 100 us -> 0 us
  waiting for transfers between devices: 118 us -> 44.3 us
  Pallas kernels: 0 us -> 43.3 us
  blocking collectives: 42.7 us -> 0 us
  local copies, waits for them, and re-layouts: 68 us -> 37 us
  starting transfers between devices: 17.8 us -> 47.9 us
  between operations: 14.4 us -> 1 us
  other arithmetic: 14.6 us -> 4.27 us
    psum x1 -> x0, waiting for transfers between devices: 112 us -> none  [body(): lax.psum((grads[0], grads[1], grads[2], grads[3], grads[4], grads[5]), ('...]
    dot_general x35 -> x0, matrix products: 97.1 us -> none  [the longest x8 29.1 us: add_block(): jnp.einsum('rv,rc->vc', onehot, block_grad, preferred_element_type=f32)]
    pallas_call x0 -> x3, Pallas kernels: none -> 43.3 us  [the longest x1 16.3 us: conv_back(): pl.pallas_call(functools.partial(conv_back_kernel, capacity), grid=(KERNE...]
    psum x1 -> x0, blocking collectives: 42.7 us -> none  [body(): lax.psum((grads[0], grads[1], grads[2], grads[3], grads[4], grads[5]), ('...]
    ppermute x0 -> x28, starting transfers between devices: none -> 36 us  [swap(): lax.ppermute(value, AXES, [(i, i + ((i // stride % size ^ d) - i // strid...]
    ppermute x0 -> x28, waiting for transfers between devices: none -> 33.5 us  [swap(): lax.ppermute(value, AXES, [(i, i + ((i // stride % size ^ d) - i // strid...]
    dot_general x1 -> x0, local copies, waits for them, and re-layouts: 11.8 us -> none  [body(): jnp.dot(windows, w_conv, preferred_element_type=f32)]
    another operation x1 -> x0, local copies, waits for them, and re-layouts: 11.8 us -> none  [body(): windows = windows_of(packet_bytes, byte_table).reshape(-1, window_width)]
  transfers between devices with their start and end apart: 4 -> 30, of which waited for: 3 -> 14; matrix products, arithmetic and copies ran while one was open for 21% -> 12% of each run, Pallas kernels for 0% -> 0%
where the time goes in v1:
time: 181 us; the launch traced here: 178 us
  starting transfers between devices  47.9 us (26%)
  waiting for transfers between devices  44.3 us (24%)
  Pallas kernels  43.3 us (24%)
  local copies, waits for them, and re-layouts  37 us (20%)
  other arithmetic  4.27 us (2%)
    ppermute x28, starting transfers between devices, swap(): lax.ppermute(value, AXES, [(i, i + ((i // stride % size ^ d) - i // strid...  36 us
    ppermute x28, waiting for transfers between devices, swap(): lax.ppermute(value, AXES, [(i, i + ((i // stride % size ^ d) - i // strid...  33.5 us
    pallas_call x1, Pallas kernels, conv_back(): pl.pallas_call(functools.partial(conv_back_kernel, capacity), grid=(KERNE...  16.3 us
    pallas_call x1, Pallas kernels, embed(): pl.pallas_call(functools.partial(embed_kernel, capacity), grid=(steps,),...  15 us
    pallas_call x1, Pallas kernels, session_layer(): pl.pallas_call(session_kernel, in_specs=[vmem] * len(args), out_specs=[vm...  12 us
    all_to_all x2, starting transfers between devices, exchange(): lax.all_to_all(rows.reshape(groups, capacity, rows.shape[1]), 'dp', split...  11.9 us
    all_to_all x2, waiting for transfers between devices, exchange(): lax.all_to_all(rows.reshape(groups, capacity, rows.shape[1]), 'dp', split...  10.8 us
    dynamic_update_slice x18, local copies, waits for them, and re-layouts, gather(): out = lax.dynamic_update_index_in_dim(out, g, mine ^ d, 0)  9.83 us
  transfers between devices with their start and end apart: 30, of which 14 were waited for; matrix products, arithmetic and copies ran while one was open for 12% of the time, Pallas kernels for 0%

profile of v1, /device:TPU:11, one launch (start us, length us, event | category | flops | bytes accessed | tf_op | source)
XLA Modules:
  0.0 177.8 jit_solution(5787684286025834707)
XLA Ops:
  0.7 1.4 copy.46.own_col_ref
  2.1 1.4 copy.47.sess_ref
  3.4 1.5 copy.48.table_ref
  4.9 15.0 %embed.1 = (bf16[256,640]{1,0:T(8,128)(2,1)}, bf16[4096,512]{1,0:T(8,128)(2,1)}) custom-call(s32[128,256]{1,0:T(8,128)} %bytes_ref.1, s32[1,128]{1,0:T(1,128)} %bitcast.179, s32[128,1]{1,0:T(8,128)} %copy.46.own_col_ref, s32[128,1]{1,0:T(8,128)} %copy.47.sess_ref, bf16[256,64]{1,0:T(8,128)(2,1)} %copy.48.table_ref, bf16[512,512]{1,0:T(8,128)(2,1)} %w_ref.3), custom_call_target="tpu_custom_call" | custom-call | tf_op jit(solution)/shard_map/embed/pallas_call | solution.py:105
  19.9 5.7 %all-to-all-start = ((bf16[8,32,640]{2,1,0:T(8,128)(2,1)}), bf16[8,32,640]{2,1,0:T(8,128)(2,1)S(1)}, u32[]{:S(2)}, u32[]{:S(2)}) async-start(bf16[8,32,640]{2,1,0:T(8,128)(2,1)} %bitcast.169), calls=%async_computation | async-start | bytes 655360 | tf_op jit(solution)/shard_map/all_to_all | solution.py:391
  26.9 6.1 %all-to-all-done = bf16[8,32,640]{2,1,0:T(8,128)(2,1)S(1)} async-done(((bf16[8,32,640]{2,1,0:T(8,128)(2,1)}), bf16[8,32,640]{2,1,0:T(8,128)(2,1)S(1)}, u32[]{:S(2)}, u32[]{:S(2)}) %all-to-all-start) | async-done | bytes 327712 | tf_op jit(solution)/shard_map/all_to_all | solution.py:391
  33.7 12.0 %session_layer.1 = (f32[16,128]{1,0:T(8,128)}, bf16[256,512]{1,0:T(8,128)(2,1)}, bf16[8704,128]{1,0:T(8,128)(2,1)}, f32[16,128]{1,0:T(8,128)}) custom-call(bf16[256,640]{1,0:T(8,128)(2,1)} %bitcast.153, s32[16,1]{1,0:T(8,128)} %copy.49.label_ref, bf16[1,512]{1,0:T(2,128)(2,1)} %reshape.123.gain_ref, bf16[512,1536]{1,0:T(8,128)(2,1)} %wp_ref.1, ...), custom_call_target="tpu_custom_call" | custom-call | tf_op jit(solution)/shard_map/session_layer/pallas_call | solution.py:233
  45.7 6.1 %all-to-all-start.1 = ((bf16[8,32,512]{2,1,0:T(8,128)(2,1)}), bf16[8,32,512]{2,1,0:T(8,128)(2,1)S(1)}, u32[]{:S(2)}, u32[]{:S(2)}) async-start(bf16[8,32,512]{2,1,0:T(8,128)(2,1)} %bitcast.177), calls=%async_computation.1 | async-start | bytes 524288 | tf_op jit(solution)/shard_map/all_to_all | solution.py:391
  52.6 4.7 %all-to-all-done.1 = bf16[8,32,512]{2,1,0:T(8,128)(2,1)S(1)} async-done(((bf16[8,32,512]{2,1,0:T(8,128)(2,1)}), bf16[8,32,512]{2,1,0:T(8,128)(2,1)S(1)}, u32[]{:S(2)}, u32[]{:S(2)}) %all-to-all-start.1) | async-done | bytes 262176 | tf_op jit(solution)/shard_map/all_to_all | solution.py:391
  58.1 16.3 %conv_back.1 = bf16[2304,128]{1,0:T(8,128)(2,1)} custom-call(bf16[256,512]{1,0:T(8,128)(2,1)} %bitcast.164, s32[1,128]{1,0:T(1,128)} %bitcast.180, s32[128,1]{1,0:T(8,128)} %copy.46.own_col_ref, s32[8,32,128]{2,1,0:T(8,128)} %bitcast.167, bf16[4096,512]{1,0:T(8,128)(2,1)} %get-tuple-element.16.slope_ref, bf16[256,64]{1,0:T(8,128)(2,1)} %copy.48.table_ref, ...), custom_call_target="tpu_custom_call" | custom-call | tf_op jit(solution)/shard_map/conv_back/pallas_call | solution.py:311
  75.4 3.8 %collective-permute-start = (bf16[1152,128]{1,0:T(8,128)(2,1)S(1)}, bf16[1152,128]{1,0:T(8,128)(2,1)S(1)}, u32[]{:S(2)}, u32[]{:S(2)}) collective-permute-start(bf16[1152,128]{1,0:T(8,128)(2,1)S(1)} %dynamic-slice_bitcast_fusion.1), channel_id=1, source_target_pairs={{0,1},{1,0},{2,3},{3,2},{4,5},{5,4},{6,7},{7,6},{8,9},{9,8},{10,11... | collective-permute-start | bytes 884744 | tf_op jit(solution)/shard_map/ppermute | solution.py:343
  79.2 1.2 collective-permute-done
  81.6 1.4 collective-permute-start.2
  83.0 1.2 collective-permute-start.1
  84.2 1.1 dynamic-slice_bitcast_fusion
  85.2 1.2 collective-permute-start.14
  86.8 4.3 %collective-permute-start.5 = (bf16[72,128]{1,0:T(8,128)(2,1)S(1)}, bf16[72,128]{1,0:T(8,128)(2,1)S(1)}, u32[]{:S(2)}, u32[]{:S(2)}) collective-permute-start(bf16[72,128]{1,0:T(8,128)(2,1)S(1)} %get-tuple-element.50), channel_id=1, source_target_pairs={{0,16},{1,17},{2,18},{3,19},{4,20},{5,21},{6,22},{7,23},{8,24},{9,... | collective-permute-start | bytes 55304 | tf_op jit(solution)/shard_map/ppermute | solution.py:343
  91.1 1.4 collective-permute-done.5
  92.5 1.3 collective-permute-done.4
  94.1 1.3 collective-permute-start.8
  95.4 1.2 collective-permute-start.9
  97.7 1.5 fusion
  99.3 1.2 collective-permute-start.17
  100.5 1.5 collective-permute-start.15
  102.1 1.4 collective-permute-start.11
  103.6 2.2 %collective-permute-done.17 = bf16[1088,128]{1,0:T(8,128)(2,1)S(1)} collective-permute-done((bf16[1088,128]{1,0:T(8,128)(2,1)S(1)}, bf16[1088,128]{1,0:T(8,128)(2,1)S(1)}, u32[]{:S(2)}, u32[]{:S(2)}) %collective-permute-start.17) | collective-permute-done | bytes 278560 | tf_op jit(solution)/shard_map/ppermute | solution.py:343
  105.8 1.2 collective-permute-start.12
  106.9 7.5 %collective-permute-done.16 = bf16[1088,128]{1,0:T(8,128)(2,1)S(1)} collective-permute-done((bf16[1088,128]{1,0:T(8,128)(2,1)S(1)}, bf16[1088,128]{1,0:T(8,128)(2,1)S(1)}, u32[]{:S(2)}, u32[]{:S(2)}) %collective-permute-start.16) | collective-permute-done | bytes 278560 | tf_op jit(solution)/shard_map/ppermute | solution.py:343
  115.4 2.7 %collective-permute-start.19 = (bf16[272,128]{1,0:T(8,128)(2,1)S(1)}, bf16[272,128]{1,0:T(8,128)(2,1)S(1)}, u32[]{:S(2)}, u32[]{:S(2)}) collective-permute-start(bf16[272,128]{1,0:T(8,128)(2,1)S(1)} %get-tuple-element.47), channel_id=1, source_target_pairs={{0,16},{1,17},{2,18},{3,19},{4,20},{5,21},{6,22},{7,23},{8,24},{9,... | collective-permute-start | bytes 208904 | tf_op jit(solution)/shard_map/ppermute | solution.py:343
  118.2 2.5 %collective-permute-done.19 = bf16[272,128]{1,0:T(8,128)(2,1)S(1)} collective-permute-done((bf16[272,128]{1,0:T(8,128)(2,1)S(1)}, bf16[272,128]{1,0:T(8,128)(2,1)S(1)}, u32[]{:S(2)}, u32[]{:S(2)}) %collective-permute-start.19) | collective-permute-done | bytes 69664 | tf_op jit(solution)/shard_map/ppermute | solution.py:343
  120.7 1.3 collective-permute-done.18
  122.1 1.1 collective-permute-start.21
  123.4 1.5 collective-permute-start.23
  125.7 1.7 collective-permute-done.22
  127.4 1.4 collective-permute-done.23
  128.9 5.6 %collective-permute-start.13 = (bf16[1152,128]{1,0:T(8,128)(2,1)S(1)}, bf16[1152,128]{1,0:T(8,128)(2,1)S(1)}, u32[]{:S(2)}, u32[]{:S(2)}) collective-permute-start(bf16[1152,128]{1,0:T(8,128)(2,1)S(1)} %bitcast.156), channel_id=1, source_target_pairs={{0,1},{1,0},{2,3},{3,2},{4,5},{5,4},{6,7},{7,6},{8,9},{9,8},{10,11... | collective-permute-start | bytes 884744 | tf_op jit(solution)/shard_map/ppermute | solution.py:343
  134.5 1.5 collective-permute-start.25
  136.0 1.3 collective-permute-start.26
  137.6 11.2 %collective-permute-done.25 = bf16[1088,128]{1,0:T(8,128)(2,1)S(1)} collective-permute-done((bf16[1088,128]{1,0:T(8,128)(2,1)S(1)}, bf16[1088,128]{1,0:T(8,128)(2,1)S(1)}, u32[]{:S(2)}, u32[]{:S(2)}) %collective-permute-start.25) | collective-permute-done | bytes 278560 | tf_op jit(solution)/shard_map/ppermute | solution.py:343
  150.8 4.0 %dynamic_update_slice.74 = bf16[2,1152,128]{1,0,2:T(2,128)(2,1)S(1)} dynamic-update-slice(bf16[2,1152,128]{1,0,2:T(2,128)(2,1)S(1)} %broadcast_in_dim.84, bf16[1,1152,128]{1,0,2:T(2,128)(2,1)S(1)} %copy.54, s32[]{:T(128)S(6)} %select_n.72, s32[]{:T(128)} %constant.136.clone.1, s32[]{:T(128)} %constant.136.clone.1) | dynamic-update-slice | bytes 589828 | tf_op jit(solution)/shard_map/jit(dynamic_update_index_in_dim)/dynamic_update_slice | solution.py:361
  155.6 4.0 %dynamic_update_slice.75 = bf16[2,1152,128]{1,0,2:T(2,128)(2,1)S(1)} dynamic-update-slice(bf16[2,1152,128]{1,0,2:T(2,128)(2,1)S(1)} %dynamic_update_slice.74, bf16[1,1152,128]{1,0,2:T(2,128)(2,1)S(1)} %copy.55, s32[]{:T(128)S(6)} %select_n.73, s32[]{:T(128)} %constant.136.clone.1, s32[]{:T(128)} %constant.136.clone.1) | dynamic-update-slice | bytes 589828 | tf_op jit(solution)/shard_map/jit(dynamic_update_index_in_dim)/dynamic_update_slice | solution.py:361
  160.2 1.7 reshape.132
  161.9 1.5 copy.56
  166.2 1.4 bitcast_dynamic-update-slice_fusion
  168.2 1.8 %copy-done = f32[8704,128]{1,0:T(8,128)} copy-done((f32[8704,128]{1,0:T(8,128)}, f32[8704,128]{1,0:T(8,128)S(1)}, u32[]{:S(2)}) %copy-start) | copy-done | bytes 4456472
  170.7 2.3 %copy.58 = f32[512,12,128]{0,2,1:T(8,128)} copy(f32[512,12,128]{2,0,1:T(8,128)S(1)} %bitcast.138) | data formatting | bytes 6291456 | tf_op jit(solution)/shard_map/transpose | solution.py:409
  173.1 3.6 %copy.60 = f32[512,1536]{1,0:T(8,128)} copy(f32[512,1536]{0,1:T(8,128)} %bitcast.139) | data formatting | bytes 6291456
  176.7 1.1 copy.68
  (92 shorter events, 17.4 us)
Async XLA Ops:
  0.6 25.0 %copy-start.6 = (s32[16]{0:T(128)S(1)}, s32[16]{0:T(128)}, u32[]{:S(2)}) copy-start(s32[16]{0:T(128)} %param.13) | copy-start | bytes 196
  0.6 25.7 %copy-start.5 = (bf16[512]{0:T(512)(128)(2,1)S(1)}, bf16[512]{0:T(512)(128)(2,1)}, u32[]{:S(2)}) copy-start(bf16[512]{0:T(512)(128)(2,1)} %param.16) | copy-start | bytes 3076
  19.9 13.1 %all-to-all-start = ((bf16[8,32,640]{2,1,0:T(8,128)(2,1)}), bf16[8,32,640]{2,1,0:T(8,128)(2,1)S(1)}, u32[]{:S(2)}, u32[]{:S(2)}) async-start(bf16[8,32,640]{2,1,0:T(8,128)(2,1)} %bitcast.169), calls=%async_computation | async-start | bytes 655360 | tf_op jit(solution)/shard_map/all_to_all | solution.py:391
  32.9 0.7 copy-start.2
  33.7 18.2 %copy-start.4 = (s32[128,256]{1,0:T(8,128)S(1)}, s32[128,256]{1,0:T(8,128)}, u32[]{:S(2)}) copy-start(s32[128,256]{1,0:T(8,128)} %bytes_ref.1) | copy-start | bytes 393220
  45.7 11.7 %all-to-all-start.1 = ((bf16[8,32,512]{2,1,0:T(8,128)(2,1)}), bf16[8,32,512]{2,1,0:T(8,128)(2,1)S(1)}, u32[]{:S(2)}, u32[]{:S(2)}) async-start(bf16[8,32,512]{2,1,0:T(8,128)(2,1)} %bitcast.177), calls=%async_computation.1 | async-start | bytes 524288 | tf_op jit(solution)/shard_map/all_to_all | solution.py:391
  57.4 0.7 copy-start.3
  58.1 26.1 %copy-start.1 = (bf16[8704,128]{1,0:T(8,128)(2,1)S(1)}, bf16[8704,128]{1,0:T(8,128)(2,1)}, u32[]{:S(2)}) copy-start(bf16[8704,128]{1,0:T(8,128)(2,1)} %get-tuple-element.18) | copy-start | bytes 6684676
  75.4 5.0 %collective-permute-start = (bf16[1152,128]{1,0:T(8,128)(2,1)S(1)}, bf16[1152,128]{1,0:T(8,128)(2,1)S(1)}, u32[]{:S(2)}, u32[]{:S(2)}) collective-permute-start(bf16[1152,128]{1,0:T(8,128)(2,1)S(1)} %dynamic-slice_bitcast_fusion.1), channel_id=1, source_target_pairs={{0,1},{1,0},{2,3},{3,2},{4,5},{5,4},{6,7},{7,6},{8,9},{9,8},{10,11... | collective-permute-start | bytes 884744 | tf_op jit(solution)/shard_map/ppermute | solution.py:343
  81.5 5.0 %collective-permute-start.3 = (bf16[288,128]{1,0:T(8,128)(2,1)S(1)}, bf16[288,128]{1,0:T(8,128)(2,1)S(1)}, u32[]{:S(2)}, u32[]{:S(2)}) collective-permute-start(bf16[288,128]{1,0:T(8,128)(2,1)S(1)} %get-tuple-element.43), channel_id=1, source_target_pairs={{0,6},{1,7},{2,4},{3,5},{4,2},{5,3},{6,0},{7,1},{8,14},{9,15},{10,... | collective-permute-start | bytes 221192 | tf_op jit(solution)/shard_map/ppermute | solution.py:343
  81.6 4.9 %collective-permute-start.2 = (bf16[288,128]{1,0:T(8,128)(2,1)S(1)}, bf16[288,128]{1,0:T(8,128)(2,1)S(1)}, u32[]{:S(2)}, u32[]{:S(2)}) collective-permute-start(bf16[288,128]{1,0:T(8,128)(2,1)S(1)} %get-tuple-element.44), channel_id=1, source_target_pairs={{0,4},{1,5},{2,6},{3,7},{4,0},{5,1},{6,2},{7,3},{8,12},{9,13},{10,... | collective-permute-start | bytes 221192 | tf_op jit(solution)/shard_map/ppermute | solution.py:343
  83.0 3.5 %collective-permute-start.1 = (bf16[288,128]{1,0:T(8,128)(2,1)S(1)}, bf16[288,128]{1,0:T(8,128)(2,1)S(1)}, u32[]{:S(2)}, u32[]{:S(2)}) collective-permute-start(bf16[288,128]{1,0:T(8,128)(2,1)S(1)} %get-tuple-element.42), channel_id=1, source_target_pairs={{0,2},{1,3},{2,0},{3,1},{4,6},{5,7},{6,4},{7,5},{8,10},{9,11},{10,... | collective-permute-start | bytes 221192 | tf_op jit(solution)/shard_map/ppermute | solution.py:343
  85.2 12.4 %collective-permute-start.14 = (bf16[4352,128]{1,0:T(8,128)(2,1)}, bf16[4352,128]{1,0:T(8,128)(2,1)}, u32[]{:S(2)}, u32[]{:S(2)}) collective-permute-start(bf16[4352,128]{1,0:T(8,128)(2,1)} %dynamic-slice_bitcast_fusion), channel_id=1, source_target_pairs={{0,1},{1,0},{2,3},{3,2},{4,5},{5,4},{6,7},{7,6},{8,9},{9,8},{10,11... | collective-permute-start | bytes 3342344 | tf_op jit(solution)/shard_map/ppermute | solution.py:343
  86.5 4.6 %collective-permute-start.6 = (bf16[72,128]{1,0:T(8,128)(2,1)S(1)}, bf16[72,128]{1,0:T(8,128)(2,1)S(1)}, u32[]{:S(2)}, u32[]{:S(2)}) collective-permute-start(bf16[72,128]{1,0:T(8,128)(2,1)S(1)} %get-tuple-element.49), channel_id=1, source_target_pairs={{0,24},{1,25},{2,26},{3,27},{4,28},{5,29},{6,30},{7,31},{8,16},{9,... | collective-permute-start | bytes 55304 | tf_op jit(solution)/shard_map/ppermute | solution.py:343
  86.8 5.7 %collective-permute-start.5 = (bf16[72,128]{1,0:T(8,128)(2,1)S(1)}, bf16[72,128]{1,0:T(8,128)(2,1)S(1)}, u32[]{:S(2)}, u32[]{:S(2)}) collective-permute-start(bf16[72,128]{1,0:T(8,128)(2,1)S(1)} %get-tuple-element.50), channel_id=1, source_target_pairs={{0,16},{1,17},{2,18},{3,19},{4,20},{5,21},{6,22},{7,23},{8,24},{9,... | collective-permute-start | bytes 55304 | tf_op jit(solution)/shard_map/ppermute | solution.py:343
  91.1 2.8 %collective-permute-start.4 = (bf16[72,128]{1,0:T(8,128)(2,1)S(1)}, bf16[72,128]{1,0:T(8,128)(2,1)S(1)}, u32[]{:S(2)}, u32[]{:S(2)}) collective-permute-start(bf16[72,128]{1,0:T(8,128)(2,1)S(1)} %get-tuple-element.48), channel_id=1, source_target_pairs={{0,8},{1,9},{2,10},{3,11},{4,12},{5,13},{6,14},{7,15},{8,0},{9,1},... | collective-permute-start | bytes 55304 | tf_op jit(solution)/shard_map/ppermute | solution.py:343
  93.9 2.7 %collective-permute-start.7 = (bf16[72,128]{1,0:T(8,128)(2,1)S(1)}, bf16[72,128]{1,0:T(8,128)(2,1)S(1)}, u32[]{:S(2)}, u32[]{:S(2)}) collective-permute-start(bf16[72,128]{1,0:T(8,128)(2,1)S(1)} %get-tuple-element.36), channel_id=1, source_target_pairs={{0,8},{1,9},{2,10},{3,11},{4,12},{5,13},{6,14},{7,15},{8,0},{9,1},... | collective-permute-start | bytes 55304 | tf_op jit(solution)/shard_map/ppermute | solution.py:343
  94.1 3.5 %collective-permute-start.8 = (bf16[72,128]{1,0:T(8,128)(2,1)S(1)}, bf16[72,128]{1,0:T(8,128)(2,1)S(1)}, u32[]{:S(2)}, u32[]{:S(2)}) collective-permute-start(bf16[72,128]{1,0:T(8,128)(2,1)S(1)} %get-tuple-element.36), channel_id=1, source_target_pairs={{0,16},{1,17},{2,18},{3,19},{4,20},{5,21},{6,22},{7,23},{8,24},{9,... | collective-permute-start | bytes 55304 | tf_op jit(solution)/shard_map/ppermute | solution.py:343
  95.4 6.6 %collective-permute-start.9 = (bf16[72,128]{1,0:T(8,128)(2,1)S(1)}, bf16[72,128]{1,0:T(8,128)(2,1)S(1)}, u32[]{:S(2)}, u32[]{:S(2)}) collective-permute-start(bf16[72,128]{1,0:T(8,128)(2,1)S(1)} %get-tuple-element.36), channel_id=1, source_target_pairs={{0,24},{1,25},{2,26},{3,27},{4,28},{5,29},{6,30},{7,31},{8,16},{9,... | collective-permute-start | bytes 55304 | tf_op jit(solution)/shard_map/ppermute | solution.py:343
  99.3 6.5 %collective-permute-start.17 = (bf16[1088,128]{1,0:T(8,128)(2,1)S(1)}, bf16[1088,128]{1,0:T(8,128)(2,1)S(1)}, u32[]{:S(2)}, u32[]{:S(2)}) collective-permute-start(bf16[1088,128]{1,0:T(8,128)(2,1)S(1)} %get-tuple-element.40), channel_id=1, source_target_pairs={{0,6},{1,7},{2,4},{3,5},{4,2},{5,3},{6,0},{7,1},{8,14},{9,15},{10,... | collective-permute-start | bytes 835592 | tf_op jit(solution)/shard_map/ppermute | solution.py:343
  100.5 13.9 %collective-permute-start.16 = (bf16[1088,128]{1,0:T(8,128)(2,1)S(1)}, bf16[1088,128]{1,0:T(8,128)(2,1)S(1)}, u32[]{:S(2)}, u32[]{:S(2)}) collective-permute-start(bf16[1088,128]{1,0:T(8,128)(2,1)S(1)} %get-tuple-element.41), channel_id=1, source_target_pairs={{0,4},{1,5},{2,6},{3,7},{4,0},{5,1},{6,2},{7,3},{8,12},{9,13},{10,... | collective-permute-start | bytes 835592 | tf_op jit(solution)/shard_map/ppermute | solution.py:343
  100.5 13.9 %collective-permute-start.15 = (bf16[1088,128]{1,0:T(8,128)(2,1)S(1)}, bf16[1088,128]{1,0:T(8,128)(2,1)S(1)}, u32[]{:S(2)}, u32[]{:S(2)}) collective-permute-start(bf16[1088,128]{1,0:T(8,128)(2,1)S(1)} %get-tuple-element.39), channel_id=1, source_target_pairs={{0,2},{1,3},{2,0},{3,1},{4,6},{5,7},{6,4},{7,5},{8,10},{9,11},{10,... | collective-permute-start | bytes 835592 | tf_op jit(solution)/shard_map/ppermute | solution.py:343
  102.0 16.1 %collective-permute-start.10 = (bf16[288,128]{1,0:T(8,128)(2,1)S(1)}, bf16[288,128]{1,0:T(8,128)(2,1)S(1)}, u32[]{:S(2)}, u32[]{:S(2)}) collective-permute-start(bf16[288,128]{1,0:T(8,128)(2,1)S(1)} %bitcast.171), channel_id=1, source_target_pairs={{0,2},{1,3},{2,0},{3,1},{4,6},{5,7},{6,4},{7,5},{8,10},{9,11},{10,... | collective-permute-start | bytes 221192 | tf_op jit(solution)/shard_map/ppermute | solution.py:343
  102.1 21.0 %collective-permute-start.11 = (bf16[288,128]{1,0:T(8,128)(2,1)S(1)}, bf16[288,128]{1,0:T(8,128)(2,1)S(1)}, u32[]{:S(2)}, u32[]{:S(2)}) collective-permute-start(bf16[288,128]{1,0:T(8,128)(2,1)S(1)} %bitcast.172), channel_id=1, source_target_pairs={{0,4},{1,5},{2,6},{3,7},{4,0},{5,1},{6,2},{7,3},{8,12},{9,13},{10,... | collective-permute-start | bytes 221192 | tf_op jit(solution)/shard_map/ppermute | solution.py:343
  105.8 23.1 %collective-permute-start.12 = (bf16[288,128]{1,0:T(8,128)(2,1)S(1)}, bf16[288,128]{1,0:T(8,128)(2,1)S(1)}, u32[]{:S(2)}, u32[]{:S(2)}) collective-permute-start(bf16[288,128]{1,0:T(8,128)(2,1)S(1)} %bitcast.174), channel_id=1, source_target_pairs={{0,6},{1,7},{2,4},{3,5},{4,2},{5,3},{6,0},{7,1},{8,14},{9,15},{10,... | collective-permute-start | bytes 221192 | tf_op jit(solution)/shard_map/ppermute | solution.py:343
  114.6 3.6 %collective-permute-start.20 = (bf16[272,128]{1,0:T(8,128)(2,1)S(1)}, bf16[272,128]{1,0:T(8,128)(2,1)S(1)}, u32[]{:S(2)}, u32[]{:S(2)}) collective-permute-start(bf16[272,128]{1,0:T(8,128)(2,1)S(1)} %get-tuple-element.46), channel_id=1, source_target_pairs={{0,24},{1,25},{2,26},{3,27},{4,28},{5,29},{6,30},{7,31},{8,16},{9,... | collective-permute-start | bytes 208904 | tf_op jit(solution)/shard_map/ppermute | solution.py:343
  115.4 5.3 %collective-permute-start.19 = (bf16[272,128]{1,0:T(8,128)(2,1)S(1)}, bf16[272,128]{1,0:T(8,128)(2,1)S(1)}, u32[]{:S(2)}, u32[]{:S(2)}) collective-permute-start(bf16[272,128]{1,0:T(8,128)(2,1)S(1)} %get-tuple-element.47), channel_id=1, source_target_pairs={{0,16},{1,17},{2,18},{3,19},{4,20},{5,21},{6,22},{7,23},{8,24},{9,... | collective-permute-start | bytes 208904 | tf_op jit(solution)/shard_map/ppermute | solution.py:343
  118.1 3.8 %collective-permute-start.18 = (bf16[272,128]{1,0:T(8,128)(2,1)S(1)}, bf16[272,128]{1,0:T(8,128)(2,1)S(1)}, u32[]{:S(2)}, u32[]{:S(2)}) collective-permute-start(bf16[272,128]{1,0:T(8,128)(2,1)S(1)} %get-tuple-element.45), channel_id=1, source_target_pairs={{0,8},{1,9},{2,10},{3,11},{4,12},{5,13},{6,14},{7,15},{8,0},{9,1},... | collective-permute-start | bytes 208904 | tf_op jit(solution)/shard_map/ppermute | solution.py:343
  122.1 3.6 %collective-permute-start.21 = (bf16[272,128]{1,0:T(8,128)(2,1)S(1)}, bf16[272,128]{1,0:T(8,128)(2,1)S(1)}, u32[]{:S(2)}, u32[]{:S(2)}) collective-permute-start(bf16[272,128]{1,0:T(8,128)(2,1)S(1)} %get-tuple-element.34), channel_id=1, source_target_pairs={{0,8},{1,9},{2,10},{3,11},{4,12},{5,13},{6,14},{7,15},{8,0},{9,1},... | collective-permute-start | bytes 208904 | tf_op jit(solution)/shard_map/ppermute | solution.py:343
  123.1 4.2 %collective-permute-start.22 = (bf16[272,128]{1,0:T(8,128)(2,1)S(1)}, bf16[272,128]{1,0:T(8,128)(2,1)S(1)}, u32[]{:S(2)}, u32[]{:S(2)}) collective-permute-start(bf16[272,128]{1,0:T(8,128)(2,1)S(1)} %get-tuple-element.34), channel_id=1, source_target_pairs={{0,16},{1,17},{2,18},{3,19},{4,20},{5,21},{6,22},{7,23},{8,24},{9,... | collective-permute-start | bytes 208904 | tf_op jit(solution)/shard_map/ppermute | solution.py:343
  123.4 5.4 %collective-permute-start.23 = (bf16[272,128]{1,0:T(8,128)(2,1)S(1)}, bf16[272,128]{1,0:T(8,128)(2,1)S(1)}, u32[]{:S(2)}, u32[]{:S(2)}) collective-permute-start(bf16[272,128]{1,0:T(8,128)(2,1)S(1)} %get-tuple-element.34), channel_id=1, source_target_pairs={{0,24},{1,25},{2,26},{3,27},{4,28},{5,29},{6,30},{7,31},{8,16},{9,... | collective-permute-start | bytes 208904 | tf_op jit(solution)/shard_map/ppermute | solution.py:343
  128.8 8.7 %collective-permute-start.24 = (bf16[1088,128]{1,0:T(8,128)(2,1)S(1)}, bf16[1088,128]{1,0:T(8,128)(2,1)S(1)}, u32[]{:S(2)}, u32[]{:S(2)}) collective-permute-start(bf16[1088,128]{1,0:T(8,128)(2,1)S(1)} %bitcast.160), channel_id=1, source_target_pairs={{0,2},{1,3},{2,0},{3,1},{4,6},{5,7},{6,4},{7,5},{8,10},{9,11},{10,... | collective-permute-start | bytes 835592 | tf_op jit(solution)/shard_map/ppermute | solution.py:343
  128.9 25.9 %collective-permute-start.13 = (bf16[1152,128]{1,0:T(8,128)(2,1)S(1)}, bf16[1152,128]{1,0:T(8,128)(2,1)S(1)}, u32[]{:S(2)}, u32[]{:S(2)}) collective-permute-start(bf16[1152,128]{1,0:T(8,128)(2,1)S(1)} %bitcast.156), channel_id=1, source_target_pairs={{0,1},{1,0},{2,3},{3,2},{4,5},{5,4},{6,7},{7,6},{8,9},{9,8},{10,11... | collective-permute-start | bytes 884744 | tf_op jit(solution)/shard_map/ppermute | solution.py:343
  134.5 14.3 %collective-permute-start.25 = (bf16[1088,128]{1,0:T(8,128)(2,1)S(1)}, bf16[1088,128]{1,0:T(8,128)(2,1)S(1)}, u32[]{:S(2)}, u32[]{:S(2)}) collective-permute-start(bf16[1088,128]{1,0:T(8,128)(2,1)S(1)} %bitcast.161), channel_id=1, source_target_pairs={{0,4},{1,5},{2,6},{3,7},{4,0},{5,1},{6,2},{7,3},{8,12},{9,13},{10,... | collective-permute-start | bytes 835592 | tf_op jit(solution)/shard_map/ppermute | solution.py:343
  136.0 12.8 %collective-permute-start.26 = (bf16[1088,128]{1,0:T(8,128)(2,1)S(1)}, bf16[1088,128]{1,0:T(8,128)(2,1)S(1)}, u32[]{:S(2)}, u32[]{:S(2)}) collective-permute-start(bf16[1088,128]{1,0:T(8,128)(2,1)S(1)} %bitcast.162), channel_id=1, source_target_pairs={{0,6},{1,7},{2,4},{3,5},{4,2},{5,3},{6,0},{7,1},{8,14},{9,15},{10,... | collective-permute-start | bytes 835592 | tf_op jit(solution)/shard_map/ppermute | solution.py:343
  148.9 17.3 %collective-permute-start.27 = (bf16[4352,128]{1,0:T(8,128)(2,1)S(1)}, bf16[4352,128]{1,0:T(8,128)(2,1)}, u32[]{:S(2)}, u32[]{:S(2)}) collective-permute-start(bf16[4352,128]{1,0:T(8,128)(2,1)S(1)} %bitcast.144), channel_id=1, source_target_pairs={{0,1},{1,0},{2,3},{3,2},{4,5},{5,4},{6,7},{7,6},{8,9},{9,8},{10,11... | collective-permute-start | bytes 3342344 | tf_op jit(solution)/shard_map/ppermute | solution.py:343
  167.9 2.1 %copy-start = (f32[8704,128]{1,0:T(8,128)}, f32[8704,128]{1,0:T(8,128)S(1)}, u32[]{:S(2)}) copy-start(f32[8704,128]{1,0:T(8,128)S(1)} %bitcast_convert_fusion) | copy-start | bytes 13369348
  173.1 3.6 %slice-start = ((f32[8704,128]{1,0:T(8,128)}), f32[2048,128]{1,0:T(8,128)S(1)}, s32[]{:S(2)}) async-start(f32[8704,128]{1,0:T(8,128)} %copy-done), calls=%async_computation.2 | async-start | bytes 2097152 | tf_op jit(solution)/shard_map/slice | solution.py:409

commit v2 on v1

--- a/solution.py
+++ b/solution.py
@@ -44,20 +44,33 @@
     return jnp.where(mask, 1.0, 0.0).astype(bf16)
 
 
+def spread(row, lanes):
+    return jnp.broadcast_to(row.astype(f32), (lanes, row.shape[1])).T
+
+
+def column(row):
+    return spread(row, LANES)[:, 0:1].astype(jnp.int32)
+
+
+def cost(flops, moved):
+    return pl.CostEstimate(flops=int(flops), bytes_accessed=int(moved), transcendentals=0)
+
+
 def embed_kernel(
-    capacity, bytes_ref, own_row_ref, own_col_ref, sess_ref, table_ref, w_ref, out_ref, slope_ref, pair_ref, emb_ref
+    capacity, bytes_ref, owner_ref, sess_ref, table_ref, w_ref, out_ref, slope_ref, pair_ref, emb_ref
 ):
     step = pl.program_id(0)
     packets, length = bytes_ref.shape
     positions = length // KERNEL
-    vocab, chan = table_ref.shape
+    chan, vocab = table_ref.shape
     width = w_ref.shape[1]
 
     @pl.when(step == 0)
     def _():
+        table = table_ref[...].astype(f32).T.astype(bf16)
         pair_ref[...] = jnp.zeros_like(pair_ref)
-        pair_ref[0:vocab, 0:chan] = table_ref[...]
-        pair_ref[vocab : 2 * vocab, chan : 2 * chan] = table_ref[...]
+        pair_ref[0:vocab, 0:chan] = table
+        pair_ref[vocab : 2 * vocab, chan : 2 * chan] = table
         emb_ref[...] = jnp.zeros_like(emb_ref)
 
     here = WIN_STEP * KERNEL
@@ -85,23 +98,23 @@
     @pl.when(step == pl.num_programs(0) - 1)
     def _():
         emb = (emb_ref[...] * (1.0 / positions)).astype(bf16)
-        own_row = own_row_ref[...]
-        same = (own_col_ref[...] == own_row) & (iota((packets, packets), 0) < iota((packets, packets), 1))
+        own_row = owner_ref[...]
+        same = (column(own_row) == own_row) & (iota((packets, packets), 0) < iota((packets, packets), 1))
         rank = jnp.sum(jnp.where(same, 1.0, 0.0), axis=0, keepdims=True).astype(jnp.int32)
         place = flag(iota((out_ref.shape[0], packets), 0) == own_row * capacity + rank)
         out_ref[:, :width] = dot_nn(place, emb).astype(bf16)
-        label = jnp.broadcast_to((sess_ref[...] + 1).astype(f32), (packets, LANES)).astype(bf16)
+        label = spread(sess_ref[...] + 1, LANES).astype(bf16)
         out_ref[:, width:] = dot_nn(place, label).astype(bf16)
 
 
-def embed(packet_bytes, own_row, own_col, sess_col, byte_table, w_conv, capacity, slots):
+def embed(packet_bytes, owner, session, table_t, w_conv, capacity, slots):
     packets, length = packet_bytes.shape
     rows = WIN_STEP * packets
     steps = length // (KERNEL * WIN_STEP)
     width = w_conv.shape[1]
-    vocab, chan = byte_table.shape
+    chan, vocab = table_t.shape
     whole = lambda a: pl.BlockSpec(a.shape, lambda i: (0, 0))
-    args = (packet_bytes, own_row, own_col, sess_col, byte_table, w_conv)
+    args = (packet_bytes, owner, session, table_t, w_conv)
     return pl.pallas_call(
         functools.partial(embed_kernel, capacity),
         grid=(steps,),
@@ -116,11 +129,19 @@
         ],
         scratch_shapes=[pltpu.VMEM((2 * vocab, 2 * chan), bf16), pltpu.VMEM((packets, width), f32)],
         compiler_params=pltpu.CompilerParams(vmem_limit_bytes=VMEM_LIMIT),
+        cost_estimate=cost(1e10, 5e6),
         name="embed",
     )(*args)
 
 
+def share_out(core_ref, halves_ref, keep_ref, send_ref):
+    mine = core_ref[0]
+    keep_ref[...] = halves_ref[mine]
+    send_ref[...] = halves_ref[1 - mine]
+
+
 def session_kernel(
+    core_ref,
     inc_ref,
     label_ref,
     gain_ref,
@@ -129,17 +150,19 @@
     wh_ref,
     logits_ref,
     back_ref,
-    early_ref,
+    keep_ref,
+    send_ref,
     gain_grad_ref,
     proj_ref,
     att_ref,
     mix_ref,
     dproj_ref,
+    halves_ref,
 ):
     slots = inc_ref.shape[0]
     width = wo_ref.shape[0]
     classes = wh_ref.shape[1]
-    sessions = label_ref.shape[0]
+    sessions = logits_ref.shape[0]
     head = width // HEADS
     scale = head**-0.5
 
@@ -177,7 +200,7 @@
     logits_ref[...] = logits
     grown = jnp.exp(logits - jnp.max(logits, axis=1, keepdims=True))
     probs = grown / jnp.sum(grown, axis=1, keepdims=True)
-    target = jnp.where(label_ref[...] == iota((sessions, classes), 1), 1.0, 0.0)
+    target = jnp.where(column(label_ref[...])[:sessions] == iota((sessions, classes), 1), 1.0, 0.0)
     dlogits = (probs - target) * (1.0 / sessions)
     dl_high, dl_low = two_parts(dlogits)
     grad_head = dot_tn(pooled_b, dl_high) + dot_tn(pooled_b, dl_low)
@@ -203,16 +226,20 @@
             at = which * width + h * head
             dproj_ref[:, at : at + head] = d.astype(bf16)
 
-    def put(at, block):
+    at = [0, 0]
+
+    def put(half, block):
         for s in range(block.shape[1] // LANES):
-            early_ref[at + s * width : at + (s + 1) * width, :] = block[:, s * LANES : (s + 1) * LANES].astype(bf16)
-        return at + block.shape[1] // LANES * width
-
-    at = 0
-    for which in range(3):
-        at = put(at, dot_tn(norm_in, dproj_ref[:, which * width : (which + 1) * width]))
-    at = put(at, grad_out)
-    put(at, grad_head)
+            rows = block.shape[0]
+            halves_ref[half, at[half] : at[half] + rows, :] = block[:, s * LANES : (s + 1) * LANES].astype(bf16)
+            at[half] += rows
+
+    side = 3 * width // 2
+    for half in range(2):
+        put(half, dot_tn(norm_in, dproj_ref[:, half * side : (half + 1) * side]))
+        put(half, grad_out[:, half * width // 2 : (half + 1) * width // 2])
+        put(half, grad_head[half * width // 2 : (half + 1) * width // 2, :])
+    share_out(core_ref, halves_ref, keep_ref, send_ref)
     dnorm = dot_nt(dproj_ref[...], wp_ref[...])
     grad_gain = jnp.sum(dnorm * x * inverse, axis=0, keepdims=True)
     gain_grad_ref[...] = jnp.zeros_like(gain_grad_ref)
@@ -223,21 +250,23 @@
     back_ref[...] = (inverse * scaled - x * slant + dhidden).astype(bf16)
 
 
-def session_layer(incoming, labels, gain, w_project, w_out, w_head):
+def session_layer(core, incoming, labels, gain, w_project, w_out, w_head, sessions):
     slots = incoming.shape[0]
     width = w_out.shape[0]
-    sessions, classes = labels.shape[0], w_head.shape[1]
-    early_rows = width * (3 * width + width + classes) // LANES
-    args = (incoming, labels, gain, w_project, w_out, w_head)
+    classes = w_head.shape[1]
+    half_rows = width * (3 * width + width + classes) // (2 * LANES)
+    args = (core, incoming, labels, gain, w_project, w_out, w_head)
     vmem = pl.BlockSpec(memory_space=pltpu.VMEM)
+    half = jax.ShapeDtypeStruct((half_rows, LANES), bf16)
     return pl.pallas_call(
         session_kernel,
-        in_specs=[vmem] * len(args),
-        out_specs=[vmem] * 4,
+        in_specs=[pl.BlockSpec(memory_space=pltpu.SMEM)] + [vmem] * (len(args) - 1),
+        out_specs=[vmem] * 5,
         out_shape=[
             jax.ShapeDtypeStruct((sessions, classes), f32),
             jax.ShapeDtypeStruct((slots, width), bf16),
-            jax.ShapeDtypeStruct((early_rows, LANES), bf16),
+            half,
+            half,
             jax.ShapeDtypeStruct((16, LANES), f32),
         ],
         scratch_shapes=[
@@ -245,79 +274,153 @@
             pltpu.VMEM((slots, width), bf16),
             pltpu.VMEM((HEADS, slots, slots), f32),
             pltpu.VMEM((slots, 3 * width), bf16),
+            pltpu.VMEM((2, half_rows, LANES), bf16),
         ],
         compiler_params=pltpu.CompilerParams(vmem_limit_bytes=VMEM_LIMIT),
+        cost_estimate=cost(1e10, 5e6),
         name="session_layer",
     )(*args)
 
 
 def conv_back_kernel(
     capacity,
+    core_ref,
     ret_ref,
-    own_row_ref,
-    own_col_ref,
+    owner_ref,
     codes_ref,
     slope_ref,
     table_ref,
     w_ref,
     gain_grad_ref,
-    late_ref,
+    keep_ref,
+    send_ref,
     dconv_ref,
     table_grad_ref,
+    halves_ref,
 ):
     j = pl.program_id(0)
     slots, width = ret_ref.shape
-    packets = own_col_ref.shape[0]
-    vocab, chan = table_ref.shape
+    packets = owner_ref.shape[1]
+    chan, vocab = table_ref.shape
     positions = codes_ref.shape[1]
 
     @pl.when(j == 0)
     def _():
-        same = (own_col_ref[...] == own_row_ref[...]) & (iota((packets, packets), 1) < iota((packets, packets), 0))
+        own_row = owner_ref[...]
+        own_col = column(own_row)
+        same = (own_col == own_row) & (iota((packets, packets), 1) < iota((packets, packets), 0))
         rank = jnp.sum(jnp.where(same, 1.0, 0.0), axis=1, keepdims=True).astype(jnp.int32)
-        place = flag(iota((packets, slots), 1) == own_col_ref[...] * capacity + rank)
+        place = flag(iota((packets, slots), 1) == own_col * capacity + rank)
         demb = dot_nn(place, ret_ref[...])
         for w in range(positions):
             at = slice(w * packets, (w + 1) * packets)
             dconv_ref[at, :] = (demb * slope_ref[at, :].astype(f32)).astype(bf16)
         table_grad_ref[...] = jnp.zeros_like(table_grad_ref)
-        late_ref[...] = jnp.zeros_like(late_ref)
+        halves_ref[...] = jnp.zeros_like(halves_ref)
 
     values = iota((vocab, packets), 0)
     onehot = jnp.concatenate([flag(codes_ref[0, w : w + 1, :] == values) for w in range(positions)], axis=1)
     by_value = dot_nn(onehot, dconv_ref[...]).astype(bf16)
     w_rows = w_ref[pl.ds(pl.multiple_of(j * chan, chan), chan), :]
-    table_grad_ref[...] += dot_nt(by_value, w_rows)
-    grad_rows = dot_tn(table_ref[...], by_value).astype(bf16)
+    table_grad_ref[...] += dot_nt(w_rows, by_value)
+    grad_rows = dot_nn(table_ref[...], by_value).astype(bf16)
     window = KERNEL * chan
-    for s in range(width // LANES):
-        at = pl.multiple_of(s * window + j * chan, chan)
-        late_ref[pl.ds(at, chan), :] = grad_rows[:, s * LANES : (s + 1) * LANES]
+    wide = width // (2 * LANES)
+    for half in range(2):
+        for s in range(wide):
+            at = pl.multiple_of(s * window + j * chan, chan)
+            slab = half * wide + s
+            halves_ref[half, pl.ds(at, chan), :] = grad_rows[:, slab * LANES : (slab + 1) * LANES]
 
     @pl.when(j == pl.num_programs(0) - 1)
     def _():
-        at = width // LANES * window
-        half = vocab * chan // LANES
-        late_ref[at : at + half, 0:chan] = table_grad_ref[0:half, :].astype(bf16)
-        late_ref[at : at + half, chan : 2 * chan] = table_grad_ref[half : 2 * half, :].astype(bf16)
-        late_ref[at + half : at + half + 16, :] = gain_grad_ref[...].astype(bf16)
-
-
-def conv_back(returned, own_row, own_col, codes, slope, byte_table, w_conv, gain_grad, capacity, late_rows):
-    width = w_conv.shape[1]
+        at = wide * window
+        for half in range(2):
+            table_part = table_grad_ref[:, half * vocab // 2 : (half + 1) * vocab // 2]
+            halves_ref[half, at : at + chan, :] = table_part.astype(bf16)
+        halves_ref[0, at + chan : at + chan + 16, :] = gain_grad_ref[...].astype(bf16)
+        share_out(core_ref, halves_ref, keep_ref, send_ref)
+
+
+def conv_back(core, returned, owner, codes, slope, table_t, w_conv, gain_grad, capacity, half_rows):
     whole = lambda a: pl.BlockSpec(a.shape, lambda j: (0, 0))
-    args = (returned, own_row, own_col, codes, slope, byte_table, w_conv, gain_grad)
+    args = (returned, owner, codes, slope, table_t, w_conv, gain_grad)
     specs = [whole(a) if a.ndim == 2 else pl.BlockSpec((1, *a.shape[1:]), lambda j: (j, 0, 0)) for a in args]
+    half = jax.ShapeDtypeStruct((half_rows, LANES), bf16)
     return pl.pallas_call(
         functools.partial(conv_back_kernel, capacity),
         grid=(KERNEL,),
-        in_specs=specs,
-        out_specs=pl.BlockSpec((late_rows, LANES), lambda j: (0, 0)),
-        out_shape=jax.ShapeDtypeStruct((late_rows, LANES), bf16),
-        scratch_shapes=[pltpu.VMEM(slope.shape, bf16), pltpu.VMEM(byte_table.shape, f32)],
+        in_specs=[pl.BlockSpec(memory_space=pltpu.SMEM), *specs],
+        out_specs=[whole(half), whole(half)],
+        out_shape=[half, half],
+        scratch_shapes=[
+            pltpu.VMEM(slope.shape, bf16),
+            pltpu.VMEM(table_t.shape, f32),
+            pltpu.VMEM((2, half_rows, LANES), bf16),
+        ],
         compiler_params=pltpu.CompilerParams(vmem_limit_bytes=VMEM_LIMIT),
+        cost_estimate=cost(1e10, 5e6),
         name="conv_back",
-    )(*args)
+    )(core, *args)
+
+
+def put_together(place_ref, piece_refs, halves_ref):
+    mine, k = place_ref[0], place_ref[1]
+    rows = piece_refs[0].shape[0]
+    count = len(piece_refs) // 2
+    for i, ref in enumerate(piece_refs):
+        half = mine if i < count else 1 - mine
+        at = pl.multiple_of((k ^ (i % count)) * rows, 16)
+        halves_ref[half, pl.ds(at, rows), :] = ref[...]
+
+
+def early_out_kernel(place_ref, *refs):
+    *pieces, project_ref, out_ref, head_ref, halves_ref = refs
+    put_together(place_ref, pieces, halves_ref)
+    for half in range(2):
+        at = 0
+        for ref in (project_ref, out_ref):
+            rows, side = ref.shape[0], ref.shape[1] // 2
+            for s in range(side // LANES):
+                lanes = half * side + s * LANES
+                ref[:, lanes : lanes + LANES] = halves_ref[half, at : at + rows, :].astype(f32)
+                at += rows
+        rows = head_ref.shape[0] // 2
+        head_ref[half * rows : (half + 1) * rows, :] = halves_ref[half, at : at + rows, :].astype(f32)
+
+
+def late_out_kernel(place_ref, *refs):
+    *pieces, conv_ref, table_ref, gain_ref, halves_ref = refs
+    put_together(place_ref, pieces, halves_ref)
+    for half in range(2):
+        at = 0
+        rows, side = conv_ref.shape[0], conv_ref.shape[1] // 2
+        for s in range(side // LANES):
+            lanes = half * side + s * LANES
+            conv_ref[:, lanes : lanes + LANES] = halves_ref[half, at : at + rows, :].astype(f32)
+            at += rows
+        chan, vocab = table_ref.shape
+        table_ref[:, half * vocab // 2 : (half + 1) * vocab // 2] = halves_ref[half, at : at + chan, :].astype(f32)
+        at += chan
+        if half == 0:
+            gain = halves_ref[0, at : at + 16, :].astype(f32)
+            for s in range(gain_ref.shape[1] // LANES):
+                gain_ref[:, s * LANES : (s + 1) * LANES] = gain[s : s + 1, :]
+
+
+def assemble(kernel, place, pieces, shapes, name):
+    vmem = pl.BlockSpec(memory_space=pltpu.VMEM)
+    rows = len(pieces) // 2 * pieces[0].shape[0]
+    return pl.pallas_call(
+        kernel,
+        in_specs=[pl.BlockSpec(memory_space=pltpu.SMEM)] + [vmem] * len(pieces),
+        out_specs=[vmem] * len(shapes),
+        out_shape=[jax.ShapeDtypeStruct(s, f32) for s in shapes],
+        scratch_shapes=[pltpu.VMEM((2, rows, LANES), bf16)],
+        compiler_params=pltpu.CompilerParams(vmem_limit_bytes=VMEM_LIMIT),
+        cost_estimate=cost(1e9, 5e6),
+        name=name,
+    )(place, *pieces)
 
 
 class Levels:
@@ -361,12 +464,20 @@
             out = lax.dynamic_update_index_in_dim(out, g, mine ^ d, 0)
         return out.reshape(size * value.shape[0], value.shape[1])
 
-    def all_sum(self, value):
-        for level in self.levels:
-            value = self.scatter_sum(value, level)
-        for level in self.levels[::-1]:
-            value = self.gather(value, level)
-        return value
+    def exchange_sum(self, value, level):
+        terms = [value] + [self.swap(value, level, d) for d in range(1, level[1])]
+        terms = [t.astype(f32) for t in terms]
+        while len(terms) > 1:
+            terms = [a + b for a, b in zip(terms[::2], terms[1::2], strict=True)]
+        return terms[0].astype(bf16)
+
+    def pair_sum(self, keep, send):
+        return (keep.astype(f32) + self.swap(send, self.levels[0], 1).astype(f32)).astype(bf16)
+
+    def pieces(self, value):
+        quad = self.levels[1]
+        own = [value] + [self.swap(value, quad, d) for d in range(1, quad[1])]
+        return own + [self.swap(p, self.levels[0], 1) for p in own]
 
 
 def body(packet_bytes, owner_index, session_id, class_label, byte_table, w_conv, norm_gain, w_project, w_out, w_head):
@@ -380,44 +491,54 @@
     window = w_conv.shape[0]
     vocab, chan = byte_table.shape
     classes = w_head.shape[1]
-
-    own_row = owner_index.reshape(1, packets)
-    own_col = owner_index.reshape(packets, 1)
-    outgoing, slope = embed(
-        packet_bytes, own_row, own_col, session_id.reshape(packets, 1), byte_table, w_conv, capacity, slots
-    )
+    sessions = class_label.shape[0]
+    core = devices.place(devices.levels[0]).reshape(1)
+    place = jnp.stack([devices.place(level) for level in devices.levels[:2]])
+
+    owner = owner_index.reshape(1, packets)
+    table_t = byte_table.T
+    outgoing, slope = embed(packet_bytes, owner, session_id.reshape(1, packets), table_t, w_conv, capacity, slots)
 
     def exchange(rows):
         return lax.all_to_all(
             rows.reshape(groups, capacity, rows.shape[1]), "dp", split_axis=0, concat_axis=0, tiled=True
         ).reshape(rows.shape)
 
-    logits, back, early, gain_grad = session_layer(
-        exchange(outgoing), class_label.reshape(-1, 1), norm_gain.reshape(1, width), w_project, w_out, w_head
+    logits, back, keep, send, gain_grad = session_layer(
+        core,
+        exchange(outgoing),
+        class_label.reshape(1, sessions),
+        norm_gain.reshape(1, width),
+        w_project,
+        w_out,
+        w_head,
+        sessions,
     )
+    early = devices.pair_sum(keep, send)
     codes = packet_bytes.reshape(packets, positions, KERNEL).transpose(2, 1, 0)
-    used = width // LANES * window + vocab * chan // LANES + 16
-    unit = 8 * devices.count
-    late_rows = -(-used // unit) * unit
-    late = conv_back(
-        exchange(back), own_row, own_col, codes, slope, byte_table, w_conv, gain_grad, capacity, late_rows
+    used = window * width // (2 * LANES) + chan * vocab // (2 * LANES) + 16
+    unit = 64
+    half_rows = -(-used // unit) * unit
+    returned, early = lax.optimization_barrier((exchange(back), early))
+    keep, send = conv_back(
+        core, returned, owner, codes, slope, table_t, w_conv, gain_grad, capacity, half_rows
     )
-    early = devices.all_sum(early).astype(f32)
-    late = devices.all_sum(late).astype(f32)
-
-    def take(rows, at, height, blocks):
-        return rows[at : at + height * blocks].reshape(blocks, height, LANES).transpose(1, 0, 2).reshape(height, -1)
-
-    wide = width // LANES
-    grad_project = take(early, 0, width, 3 * wide)
-    grad_out = take(early, 3 * wide * width, width, wide)
-    grad_head = take(early, 4 * wide * width, width, classes // LANES)
-    grad_conv = take(late, 0, window, wide)
-    at = wide * window
-    half = vocab * chan // LANES
-    grad_table = jnp.concatenate([late[at : at + half, :chan], late[at : at + half, chan : 2 * chan]], axis=0)
-    grad_gain = late[at + half : at + half + wide].reshape(width)
-    return (logits, grad_table, grad_conv, grad_gain, grad_project, grad_out, grad_head)
+    _, quad, *upper = devices.levels
+    early = devices.scatter_sum(early, quad)
+    for level in upper:
+        early = devices.scatter_sum(early, level)
+    for level in upper[::-1]:
+        early = devices.gather(early, level)
+    late = devices.scatter_sum(devices.pair_sum(keep, send), quad)
+    for level in upper:
+        late = devices.exchange_sum(late, level)
+    grad_project, grad_out, grad_head = assemble(
+        early_out_kernel, place, devices.pieces(early), [w_project.shape, w_out.shape, w_head.shape], "early_out"
+    )
+    grad_conv, table_grad, gain_grad = assemble(
+        late_out_kernel, place, devices.pieces(late), [w_conv.shape, table_t.shape, (1, width)], "late_out"
+    )
+    return (logits, table_grad.T, grad_conv, gain_grad.reshape(width), grad_project, grad_out, grad_head)
 
 
 def solution(mesh):

time: 181 us -> 136 us (0.75); the launches traced: 178 us -> 135 us
  local copies, waits for them, and re-layouts: 37 us -> 4.51 us
  waiting for transfers between devices: 44.3 us -> 29.7 us
  Pallas kernels: 43.3 us -> 50.1 us
  other arithmetic: 4.27 us -> 1.28 us
    ppermute x28 -> x31, waiting for transfers between devices: 33.5 us -> 15.8 us  [swap(): lax.ppermute(value, AXES, [(i, i + ((i // stride % size ^ d) - i // strid...]
    dynamic_update_slice x18 -> x3, local copies, waits for them, and re-layouts: 9.83 us -> 0.05 us  [gather(): out = lax.dynamic_update_index_in_dim(out, g, mine ^ d, 0)]
    reshape x6 -> x0, local copies, waits for them, and re-layouts: 7.79 us -> none  [the longest x3 4.32 us: take(): rows[at:at + height * blocks].reshape(blocks, height, LANES)]
    unnamed x19 -> x43, local copies, waits for them, and re-layouts: 9.6 us -> 3.04 us
    pallas_call x1 -> x3, Pallas kernels: 12 us -> 18.3 us  [the longest x1 12 us: session_layer(): pl.pallas_call(session_kernel, in_specs=[pl.BlockSpec(memory_space=pltpu....]
    all_to_all x2, waiting for transfers between devices: 10.8 us -> 13.9 us  [exchange(): lax.all_to_all(rows.reshape(groups, capacity, rows.shape[1]), 'dp', split...]
    convert_element_type x4 -> x2, other arithmetic: 2.8 us -> 0.2 us  [scatter_sum(): return total.astype(bf16)]
    transpose x1 -> x0, local copies, waits for them, and re-layouts: 2.34 us -> none  [take(): rows[at:at + height * blocks].reshape(blocks, height, LANES)]
  transfers between devices with their start and end apart: 30 -> 33, of which waited for: 14 -> 9; matrix products, arithmetic and copies ran while one was open for 12% -> 2% of each run, Pallas kernels for 0% -> 14%
where the time goes in v2:
time: 136 us; the launch traced here: 135 us
  Pallas kernels  50.1 us (37%)
  starting transfers between devices  48.7 us (36%)
  waiting for transfers between devices  29.7 us (22%)
  local copies, waits for them, and re-layouts  4.51 us (3%)
    ppermute x31, starting transfers between devices, swap(): lax.ppermute(value, AXES, [(i, i + ((i // stride % size ^ d) - i // strid...  38.2 us
    pallas_call x1, Pallas kernels, conv_back(): pl.pallas_call(functools.partial(conv_back_kernel, capacity), grid=(KERNE...  16.6 us
    ppermute x31, waiting for transfers between devices, swap(): lax.ppermute(value, AXES, [(i, i + ((i // stride % size ^ d) - i // strid...  15.8 us
    pallas_call x1, Pallas kernels, embed(): pl.pallas_call(functools.partial(embed_kernel, capacity), grid=(steps,),...  15.1 us
    all_to_all x2, waiting for transfers between devices, exchange(): lax.all_to_all(rows.reshape(groups, capacity, rows.shape[1]), 'dp', split...  13.9 us
    pallas_call x1, Pallas kernels, session_layer(): pl.pallas_call(session_kernel, in_specs=[pl.BlockSpec(memory_space=pltpu....  12 us
    all_to_all x2, starting transfers between devices, exchange(): lax.all_to_all(rows.reshape(groups, capacity, rows.shape[1]), 'dp', split...  10.4 us
    pallas_call x2, Pallas kernels, assemble(): pl.pallas_call(kernel, in_specs=[pl.BlockSpec(memory_space=pltpu.SMEM)] +...  6.29 us
  transfers between devices with their start and end apart: 33, of which 9 were waited for; matrix products, arithmetic and copies ran while one was open for 2% of the time, Pallas kernels for 14%

profile of v2, /device:TPU:11, one launch (start us, length us, event | category | flops | bytes accessed | tf_op | source)
XLA Modules:
  0.0 135.2 jit_solution(3855519949696402906)
XLA Ops:
  0.6 15.1 %embed.1 = (bf16[256,640]{1,0:T(8,128)(2,1)}, bf16[4096,512]{1,0:T(8,128)(2,1)}) custom-call(s32[128,256]{1,0:T(8,128)} %bytes_ref.1, s32[1,128]{1,0:T(1,128)} %bitcast.76, s32[1,128]{1,0:T(1,128)} %bitcast.74, bf16[64,256]{1,0:T(8,128)(2,1)} %bitcast.72, bf16[512,512]{1,0:T(8,128)(2,1)} %w_ref.3), custom_call_target="tpu_custom_call" | custom-call | flops 10000000000 | bytes 5000000 | tf_op jit(solution)/shard_map/embed/pallas_call | solution.py:118
  15.8 5.7 %all-to-all-start = ((bf16[8,32,640]{2,1,0:T(8,128)(2,1)}), bf16[8,32,640]{2,1,0:T(8,128)(2,1)S(1)}, u32[]{:S(2)}, u32[]{:S(2)}) async-start(bf16[8,32,640]{2,1,0:T(8,128)(2,1)} %bitcast.64), calls=%async_computation | async-start | bytes 655360 | tf_op jit(solution)/shard_map/all_to_all | solution.py:503
  21.5 0.6 reshape.71.gain_ref
  22.1 6.7 %all-to-all-done = bf16[8,32,640]{2,1,0:T(8,128)(2,1)S(1)} async-done(((bf16[8,32,640]{2,1,0:T(8,128)(2,1)}), bf16[8,32,640]{2,1,0:T(8,128)(2,1)S(1)}, u32[]{:S(2)}, u32[]{:S(2)}) %all-to-all-start) | async-done | bytes 327712 | tf_op jit(solution)/shard_map/all_to_all | solution.py:503
  28.8 0.7 copy-done.1
  29.5 12.0 %session_layer.1 = (f32[16,128]{1,0:T(8,128)}, bf16[256,512]{1,0:T(8,128)(2,1)}, bf16[4352,128]{1,0:T(8,128)(2,1)}, bf16[4352,128]{1,0:T(8,128)(2,1)}, f32[16,128]{1,0:T(8,128)}) custom-call(s32[1]{0:T(128)} %bitcast.core_ref, bf16[256,640]{1,0:T(8,128)(2,1)} %bitcast.63, s32[1,16]{1,0:T(1,128)} %bitcast.75, bf16[1,512]{1,0:T(2,128)(2,1)} %reshape.71.gain_ref, ...), custom_call_target="tpu_custom_call" | custom-call | flops 10000000000 | bytes 5000000 | tf_op jit(solution)/shard_map/session_layer/pallas_call | solution.py:261
  41.6 3.2 %collective-permute-start = (bf16[4352,128]{1,0:T(8,128)(2,1)}, bf16[4352,128]{1,0:T(8,128)(2,1)S(1)}, u32[]{:S(2)}, u32[]{:S(2)}) collective-permute-start(bf16[4352,128]{1,0:T(8,128)(2,1)} %get-tuple-element.28), channel_id=1, source_target_pairs={{0,1},{1,0},{2,3},{3,2},{4,5},{5,4},{6,7},{7,6},{8,9},{9,8},{10,11... | collective-permute-start | bytes 3342344 | tf_op jit(solution)/shard_map/ppermute | solution.py:446
  44.9 0.7 copy.20
  45.6 4.7 %all-to-all-start.1 = ((bf16[8,32,512]{2,1,0:T(8,128)(2,1)}), bf16[8,32,512]{2,1,0:T(8,128)(2,1)}, u32[]{:S(2)}, u32[]{:S(2)}) async-start(bf16[8,32,512]{2,1,0:T(8,128)(2,1)} %bitcast.70), calls=%async_computation.1 | async-start | bytes 524288 | tf_op jit(solution)/shard_map/all_to_all | solution.py:503
  50.3 0.3 add_convert_fusion
  50.6 7.2 %all-to-all-done.1 = bf16[8,32,512]{2,1,0:T(8,128)(2,1)} async-done(((bf16[8,32,512]{2,1,0:T(8,128)(2,1)}), bf16[8,32,512]{2,1,0:T(8,128)(2,1)}, u32[]{:S(2)}, u32[]{:S(2)}) %all-to-all-start.1) | async-done | bytes 262176 | tf_op jit(solution)/shard_map/all_to_all | solution.py:503
  57.8 1.2 collective-permute-start.17
  59.0 0.3 collective-permute-start.16
  59.3 1.2 collective-permute-start.15
  60.5 16.6 %conv_back.1 = (bf16[1152,128]{1,0:T(8,128)(2,1)}, bf16[1152,128]{1,0:T(8,128)(2,1)}) custom-call(s32[1]{0:T(128)} %bitcast.core_ref, bf16[256,512]{1,0:T(8,128)(2,1)} %bitcast.9.ret_ref, s32[1,128]{1,0:T(1,128)} %bitcast.77, s32[8,32,128]{2,1,0:T(8,128)} %bitcast.71, bf16[4096,512]{1,0:T(8,128)(2,1)} %get-tuple-element.30.slope_ref, ...), custom_call_target="tpu_custom_call" | custom-call | flops 10000000000 | bytes 5000000 | tf_op jit(solution)/shard_map/conv_back/pallas_call | solution.py:350
  77.2 2.7 %collective-permute-start.1 = (bf16[1152,128]{1,0:T(8,128)(2,1)}, bf16[1152,128]{1,0:T(8,128)(2,1)S(1)}, u32[]{:S(2)}, u32[]{:S(2)}) collective-permute-start(bf16[1152,128]{1,0:T(8,128)(2,1)} %get-tuple-element.33), channel_id=1, source_target_pairs={{0,1},{1,0},{2,3},{3,2},{4,5},{5,4},{6,7},{7,6},{8,9},{9,8},{10,11... | collective-permute-start | bytes 884744 | tf_op jit(solution)/shard_map/ppermute | solution.py:446
  80.1 2.8 %collective-permute-start.19 = (bf16[272,128]{1,0:T(8,128)(2,1)S(1)}, bf16[272,128]{1,0:T(8,128)(2,1)S(1)}, u32[]{:S(2)}, u32[]{:S(2)}) collective-permute-start(bf16[272,128]{1,0:T(8,128)(2,1)S(1)} %get-tuple-element.51), channel_id=1, source_target_pairs={{0,16},{1,17},{2,18},{3,19},{4,20},{5,21},{6,22},{7,23},{8,24},{9,... | collective-permute-start | bytes 208904 | tf_op jit(solution)/shard_map/ppermute | solution.py:446
  83.0 1.2 collective-permute-start.4
  84.2 0.3 collective-permute-start.3
  84.5 1.2 collective-permute-start.2
  85.8 1.0 collective-permute-done.19
  86.8 0.2 collective-permute-done.18
  87.1 3.0 %collective-permute-start.21 = (bf16[272,128]{1,0:T(8,128)(2,1)S(1)}, bf16[272,128]{1,0:T(8,128)(2,1)S(1)}, u32[]{:S(2)}, u32[]{:S(2)}) collective-permute-start(bf16[272,128]{1,0:T(8,128)(2,1)S(1)} %get-tuple-element.42), channel_id=1, source_target_pairs={{0,8},{1,9},{2,10},{3,11},{4,12},{5,13},{6,14},{7,15},{8,0},{9,1},... | collective-permute-start | bytes 208904 | tf_op jit(solution)/shard_map/ppermute | solution.py:446
  90.1 1.3 collective-permute-start.23
  91.4 0.3 collective-permute-start.7
  91.7 4.2 %collective-permute-start.6 = (bf16[288,128]{1,0:T(8,128)(2,1)S(1)}, bf16[288,128]{1,0:T(8,128)(2,1)S(1)}, u32[]{:S(2)}, u32[]{:S(2)}) collective-permute-start(bf16[288,128]{1,0:T(8,128)(2,1)S(1)} %fusion.5), channel_id=1, source_target_pairs={{0,16},{1,17},{2,18},{3,19},{4,20},{5,21},{6,22},{7,23},{8,24},{9,... | collective-permute-start | bytes 221192 | tf_op jit(solution)/shard_map/ppermute | solution.py:446
  95.9 3.3 %collective-permute-done.23 = bf16[272,128]{1,0:T(8,128)(2,1)S(1)} collective-permute-done((bf16[272,128]{1,0:T(8,128)(2,1)S(1)}, bf16[272,128]{1,0:T(8,128)(2,1)S(1)}, u32[]{:S(2)}, u32[]{:S(2)}) %collective-permute-start.23) | collective-permute-done | bytes 69664 | tf_op jit(solution)/shard_map/ppermute | solution.py:446
  99.3 1.3 collective-permute-start.25
  100.5 1.8 %collective-permute-done.7 = bf16[288,128]{1,0:T(8,128)(2,1)S(1)} collective-permute-done((bf16[288,128]{1,0:T(8,128)(2,1)S(1)}, bf16[288,128]{1,0:T(8,128)(2,1)S(1)}, u32[]{:S(2)}, u32[]{:S(2)}) %collective-permute-start.7) | collective-permute-done | bytes 73760 | tf_op jit(solution)/shard_map/ppermute | solution.py:446
  102.3 1.0 collective-permute-start.26
  103.4 1.3 collective-permute-start.8
  104.6 0.5 collective-permute-start.9
  105.1 7.7 %collective-permute-done.8.refs_1_ = bf16[288,128]{1,0:T(8,128)(2,1)S(1)} collective-permute-done((bf16[288,128]{1,0:T(8,128)(2,1)S(1)}, bf16[288,128]{1,0:T(8,128)(2,1)S(1)}, u32[]{:S(2)}, u32[]{:S(2)}) %collective-permute-start.8) | collective-permute-done | bytes 73760 | tf_op jit(solution)/shard_map/ppermute | solution.py:446
  112.8 4.8 %collective-permute-start.11 = (bf16[288,128]{1,0:T(8,128)(2,1)S(1)}, bf16[288,128]{1,0:T(8,128)(2,1)S(1)}, u32[]{:S(2)}, u32[]{:S(2)}) collective-permute-start(bf16[288,128]{1,0:T(8,128)(2,1)S(1)} %add_convert_fusion.2.refs_0_), channel_id=1, source_target_pairs={{0,1},{1,0},{2,3},{3,2},{4,5},{5,4},{6,7},{7,6},{8,9},{9,8},{10,11... | collective-permute-start | bytes 221192 | tf_op jit(solution)/shard_map/ppermute | solution.py:446
  117.6 5.2 %collective-permute-start.12 = (bf16[288,128]{1,0:T(8,128)(2,1)S(1)}, bf16[288,128]{1,0:T(8,128)(2,1)S(1)}, u32[]{:S(2)}, u32[]{:S(2)}) collective-permute-start(bf16[288,128]{1,0:T(8,128)(2,1)S(1)} %collective-permute-done.8.refs_1_), channel_id=1, source_target_pairs={{0,1},{1,0},{2,3},{3,2},{4,5},{5,4},{6,7},{7,6},{8,9},{9,8},{10,11... | collective-permute-start | bytes 221192 | tf_op jit(solution)/shard_map/ppermute | solution.py:446
  122.9 0.8 collective-permute-done.12.refs_5_
  123.7 0.4 collective-permute-start.27
  124.0 0.2 collective-permute-start.28
  124.2 0.4 collective-permute-start.29
  124.6 0.2 collective-permute-start.30
  124.7 0.4 collective-permute-start.14
  125.1 0.6 pad_add_fusion.place_ref
  125.7 0.9 collective-permute-done.14.refs_7_
  126.6 0.6 copy-done.20
  127.2 2.3 %late_out.1 = (f32[512,512]{1,0:T(8,128)}, f32[64,256]{1,0:T(8,128)}, f32[1,512]{1,0:T(1,128)}) custom-call(s32[2]{0:T(128)} %pad_add_fusion.place_ref, bf16[288,128]{1,0:T(8,128)(2,1)} %copy-done.5, bf16[288,128]{1,0:T(8,128)(2,1)} %copy-done.14, bf16[288,128]{1,0:T(8,128)(2,1)} %copy-done.15, bf16[288,128]{1,0:T(8,128)(2,1)} %copy-done.16, ...), custom_call_target="tpu_custom_call" | custom-call | flops 1000000000 | bytes 5000000 | tf_op jit(solution)/shard_map/late_out/pallas_call | solution.py:414
  129.6 0.6 copy-done.10
  130.5 0.7 copy-done.13
  131.2 4.0 %early_out.1 = (f32[512,1536]{1,0:T(8,128)}, f32[512,512]{1,0:T(8,128)}, f32[512,128]{1,0:T(8,128)}) custom-call(s32[2]{0:T(128)} %pad_add_fusion.place_ref, bf16[1088,128]{1,0:T(8,128)(2,1)} %bitcast.69, bf16[1088,128]{1,0:T(8,128)(2,1)} %copy-done.7, bf16[1088,128]{1,0:T(8,128)(2,1)} %copy-done.8, bf16[1088,128]{1,0:T(8,128)(2,1)} %copy-done.9, ...), custom_call_target="tpu_custom_call" | custom-call | flops 1000000000 | bytes 5000000 | tf_op jit(solution)/shard_map/early_out/pallas_call | solution.py:414
  (82 shorter events, 1.2 us)
Async XLA Ops:
  0.6 20.8 %copy-start.6 = (bf16[512]{0:T(512)(128)(2,1)S(1)}, bf16[512]{0:T(512)(128)(2,1)}, u32[]{:S(2)}) copy-start(bf16[512]{0:T(512)(128)(2,1)} %param.16) | copy-start | bytes 3076
  15.8 13.1 %all-to-all-start = ((bf16[8,32,640]{2,1,0:T(8,128)(2,1)}), bf16[8,32,640]{2,1,0:T(8,128)(2,1)S(1)}, u32[]{:S(2)}, u32[]{:S(2)}) async-start(bf16[8,32,640]{2,1,0:T(8,128)(2,1)} %bitcast.64), calls=%async_computation | async-start | bytes 655360 | tf_op jit(solution)/shard_map/all_to_all | solution.py:503
  29.5 15.2 %copy-start.4 = (s32[128,256]{1,0:T(8,128)S(1)}, s32[128,256]{1,0:T(8,128)}, u32[]{:S(2)}) copy-start(s32[128,256]{1,0:T(8,128)} %bytes_ref.1) | copy-start | bytes 393220
  41.6 8.7 %copy-start = (bf16[4352,128]{1,0:T(8,128)(2,1)S(1)}, bf16[4352,128]{1,0:T(8,128)(2,1)}, u32[]{:S(2)}) copy-start(bf16[4352,128]{1,0:T(8,128)(2,1)} %get-tuple-element.27) | copy-start | bytes 3342340
  41.6 8.7 %collective-permute-start = (bf16[4352,128]{1,0:T(8,128)(2,1)}, bf16[4352,128]{1,0:T(8,128)(2,1)S(1)}, u32[]{:S(2)}, u32[]{:S(2)}) collective-permute-start(bf16[4352,128]{1,0:T(8,128)(2,1)} %get-tuple-element.28), channel_id=1, source_target_pairs={{0,1},{1,0},{2,3},{3,2},{4,5},{5,4},{6,7},{7,6},{8,9},{9,8},{10,11... | collective-permute-start | bytes 3342344 | tf_op jit(solution)/shard_map/ppermute | solution.py:446
  45.6 12.2 %all-to-all-start.1 = ((bf16[8,32,512]{2,1,0:T(8,128)(2,1)}), bf16[8,32,512]{2,1,0:T(8,128)(2,1)}, u32[]{:S(2)}, u32[]{:S(2)}) async-start(bf16[8,32,512]{2,1,0:T(8,128)(2,1)} %bitcast.70), calls=%async_computation.1 | async-start | bytes 524288 | tf_op jit(solution)/shard_map/all_to_all | solution.py:503
  57.8 22.0 %collective-permute-start.17 = (bf16[1088,128]{1,0:T(8,128)(2,1)S(1)}, bf16[1088,128]{1,0:T(8,128)(2,1)S(1)}, u32[]{:S(2)}, u32[]{:S(2)}) collective-permute-start(bf16[1088,128]{1,0:T(8,128)(2,1)S(1)} %get-tuple-element.44), channel_id=1, source_target_pairs={{0,6},{1,7},{2,4},{3,5},{4,2},{5,3},{6,0},{7,1},{8,14},{9,15},{10,... | collective-permute-start | bytes 835592 | tf_op jit(solution)/shard_map/ppermute | solution.py:446
  59.0 20.8 %collective-permute-start.16 = (bf16[1088,128]{1,0:T(8,128)(2,1)S(1)}, bf16[1088,128]{1,0:T(8,128)(2,1)S(1)}, u32[]{:S(2)}, u32[]{:S(2)}) collective-permute-start(bf16[1088,128]{1,0:T(8,128)(2,1)S(1)} %get-tuple-element.45), channel_id=1, source_target_pairs={{0,4},{1,5},{2,6},{3,7},{4,0},{5,1},{6,2},{7,3},{8,12},{9,13},{10,... | collective-permute-start | bytes 835592 | tf_op jit(solution)/shard_map/ppermute | solution.py:446
  59.3 20.5 %collective-permute-start.15 = (bf16[1088,128]{1,0:T(8,128)(2,1)S(1)}, bf16[1088,128]{1,0:T(8,128)(2,1)S(1)}, u32[]{:S(2)}, u32[]{:S(2)}) collective-permute-start(bf16[1088,128]{1,0:T(8,128)(2,1)S(1)} %get-tuple-element.43), channel_id=1, source_target_pairs={{0,2},{1,3},{2,0},{3,1},{4,6},{5,7},{6,4},{7,5},{8,10},{9,11},{10,... | collective-permute-start | bytes 835592 | tf_op jit(solution)/shard_map/ppermute | solution.py:446
  77.2 5.8 %copy-start.2 = (bf16[1152,128]{1,0:T(8,128)(2,1)S(1)}, bf16[1152,128]{1,0:T(8,128)(2,1)}, u32[]{:S(2)}) copy-start(bf16[1152,128]{1,0:T(8,128)(2,1)} %get-tuple-element.32) | copy-start | bytes 884740
  77.2 5.8 %collective-permute-start.1 = (bf16[1152,128]{1,0:T(8,128)(2,1)}, bf16[1152,128]{1,0:T(8,128)(2,1)S(1)}, u32[]{:S(2)}, u32[]{:S(2)}) collective-permute-start(bf16[1152,128]{1,0:T(8,128)(2,1)} %get-tuple-element.33), channel_id=1, source_target_pairs={{0,1},{1,0},{2,3},{3,2},{4,5},{5,4},{6,7},{7,6},{8,9},{9,8},{10,11... | collective-permute-start | bytes 884744 | tf_op jit(solution)/shard_map/ppermute | solution.py:446
  80.1 4.5 %collective-permute-start.20 = (bf16[272,128]{1,0:T(8,128)(2,1)S(1)}, bf16[272,128]{1,0:T(8,128)(2,1)S(1)}, u32[]{:S(2)}, u32[]{:S(2)}) collective-permute-start(bf16[272,128]{1,0:T(8,128)(2,1)S(1)} %get-tuple-element.50), channel_id=1, source_target_pairs={{0,24},{1,25},{2,26},{3,27},{4,28},{5,29},{6,30},{7,31},{8,16},{9,... | collective-permute-start | bytes 208904 | tf_op jit(solution)/shard_map/ppermute | solution.py:446
  80.1 6.6 %collective-permute-start.19 = (bf16[272,128]{1,0:T(8,128)(2,1)S(1)}, bf16[272,128]{1,0:T(8,128)(2,1)S(1)}, u32[]{:S(2)}, u32[]{:S(2)}) collective-permute-start(bf16[272,128]{1,0:T(8,128)(2,1)S(1)} %get-tuple-element.51), channel_id=1, source_target_pairs={{0,16},{1,17},{2,18},{3,19},{4,20},{5,21},{6,22},{7,23},{8,24},{9,... | collective-permute-start | bytes 208904 | tf_op jit(solution)/shard_map/ppermute | solution.py:446
  82.9 4.1 %collective-permute-start.18 = (bf16[272,128]{1,0:T(8,128)(2,1)S(1)}, bf16[272,128]{1,0:T(8,128)(2,1)S(1)}, u32[]{:S(2)}, u32[]{:S(2)}) collective-permute-start(bf16[272,128]{1,0:T(8,128)(2,1)S(1)} %get-tuple-element.49), channel_id=1, source_target_pairs={{0,8},{1,9},{2,10},{3,11},{4,12},{5,13},{6,14},{7,15},{8,0},{9,1},... | collective-permute-start | bytes 208904 | tf_op jit(solution)/shard_map/ppermute | solution.py:446
  83.0 7.0 %collective-permute-start.4 = (bf16[288,128]{1,0:T(8,128)(2,1)S(1)}, bf16[288,128]{1,0:T(8,128)(2,1)S(1)}, u32[]{:S(2)}, u32[]{:S(2)}) collective-permute-start(bf16[288,128]{1,0:T(8,128)(2,1)S(1)} %get-tuple-element.47), channel_id=1, source_target_pairs={{0,6},{1,7},{2,4},{3,5},{4,2},{5,3},{6,0},{7,1},{8,14},{9,15},{10,... | collective-permute-start | bytes 221192 | tf_op jit(solution)/shard_map/ppermute | solution.py:446
  84.2 7.1 %collective-permute-start.3 = (bf16[288,128]{1,0:T(8,128)(2,1)S(1)}, bf16[288,128]{1,0:T(8,128)(2,1)S(1)}, u32[]{:S(2)}, u32[]{:S(2)}) collective-permute-start(bf16[288,128]{1,0:T(8,128)(2,1)S(1)} %get-tuple-element.48), channel_id=1, source_target_pairs={{0,4},{1,5},{2,6},{3,7},{4,0},{5,1},{6,2},{7,3},{8,12},{9,13},{10,... | collective-permute-start | bytes 221192 | tf_op jit(solution)/shard_map/ppermute | solution.py:446
  84.5 6.8 %collective-permute-start.2 = (bf16[288,128]{1,0:T(8,128)(2,1)S(1)}, bf16[288,128]{1,0:T(8,128)(2,1)S(1)}, u32[]{:S(2)}, u32[]{:S(2)}) collective-permute-start(bf16[288,128]{1,0:T(8,128)(2,1)S(1)} %get-tuple-element.46), channel_id=1, source_target_pairs={{0,2},{1,3},{2,0},{3,1},{4,6},{5,7},{6,4},{7,5},{8,10},{9,11},{10,... | collective-permute-start | bytes 221192 | tf_op jit(solution)/shard_map/ppermute | solution.py:446
  87.1 8.7 %collective-permute-start.21 = (bf16[272,128]{1,0:T(8,128)(2,1)S(1)}, bf16[272,128]{1,0:T(8,128)(2,1)S(1)}, u32[]{:S(2)}, u32[]{:S(2)}) collective-permute-start(bf16[272,128]{1,0:T(8,128)(2,1)S(1)} %get-tuple-element.42), channel_id=1, source_target_pairs={{0,8},{1,9},{2,10},{3,11},{4,12},{5,13},{6,14},{7,15},{8,0},{9,1},... | collective-permute-start | bytes 208904 | tf_op jit(solution)/shard_map/ppermute | solution.py:446
  90.1 5.8 %collective-permute-start.22 = (bf16[272,128]{1,0:T(8,128)(2,1)S(1)}, bf16[272,128]{1,0:T(8,128)(2,1)S(1)}, u32[]{:S(2)}, u32[]{:S(2)}) collective-permute-start(bf16[272,128]{1,0:T(8,128)(2,1)S(1)} %get-tuple-element.42), channel_id=1, source_target_pairs={{0,16},{1,17},{2,18},{3,19},{4,20},{5,21},{6,22},{7,23},{8,24},{9,... | collective-permute-start | bytes 208904 | tf_op jit(solution)/shard_map/ppermute | solution.py:446
  90.1 9.1 %collective-permute-start.23 = (bf16[272,128]{1,0:T(8,128)(2,1)S(1)}, bf16[272,128]{1,0:T(8,128)(2,1)S(1)}, u32[]{:S(2)}, u32[]{:S(2)}) collective-permute-start(bf16[272,128]{1,0:T(8,128)(2,1)S(1)} %get-tuple-element.42), channel_id=1, source_target_pairs={{0,24},{1,25},{2,26},{3,27},{4,28},{5,29},{6,30},{7,31},{8,16},{9,... | collective-permute-start | bytes 208904 | tf_op jit(solution)/shard_map/ppermute | solution.py:446
  91.4 11.0 %collective-permute-start.7 = (bf16[288,128]{1,0:T(8,128)(2,1)S(1)}, bf16[288,128]{1,0:T(8,128)(2,1)S(1)}, u32[]{:S(2)}, u32[]{:S(2)}) collective-permute-start(bf16[288,128]{1,0:T(8,128)(2,1)S(1)} %fusion.5), channel_id=1, source_target_pairs={{0,24},{1,25},{2,26},{3,27},{4,28},{5,29},{6,30},{7,31},{8,16},{9,... | collective-permute-start | bytes 221192 | tf_op jit(solution)/shard_map/ppermute | solution.py:446
  91.7 11.6 %collective-permute-start.6 = (bf16[288,128]{1,0:T(8,128)(2,1)S(1)}, bf16[288,128]{1,0:T(8,128)(2,1)S(1)}, u32[]{:S(2)}, u32[]{:S(2)}) collective-permute-start(bf16[288,128]{1,0:T(8,128)(2,1)S(1)} %fusion.5), channel_id=1, source_target_pairs={{0,16},{1,17},{2,18},{3,19},{4,20},{5,21},{6,22},{7,23},{8,24},{9,... | collective-permute-start | bytes 221192 | tf_op jit(solution)/shard_map/ppermute | solution.py:446
  95.8 7.5 %collective-permute-start.5 = (bf16[288,128]{1,0:T(8,128)(2,1)S(1)}, bf16[288,128]{1,0:T(8,128)(2,1)S(1)}, u32[]{:S(2)}, u32[]{:S(2)}) collective-permute-start(bf16[288,128]{1,0:T(8,128)(2,1)S(1)} %fusion.5), channel_id=1, source_target_pairs={{0,8},{1,9},{2,10},{3,11},{4,12},{5,13},{6,14},{7,15},{8,0},{9,1},... | collective-permute-start | bytes 221192 | tf_op jit(solution)/shard_map/ppermute | solution.py:446
  99.2 30.4 %copy-start.3 = (bf16[4,272,128]{2,1,0:T(8,128)(2,1)}, bf16[4,272,128]{2,1,0:T(8,128)(2,1)S(1)}, u32[]{:S(2)}) copy-start(bf16[4,272,128]{2,1,0:T(8,128)(2,1)S(1)} %bitcast_dynamic-update-slice_fusion) | copy-start | bytes 835588
  99.2 24.9 %collective-permute-start.24 = (bf16[1088,128]{1,0:T(8,128)(2,1)S(1)}, bf16[1088,128]{1,0:T(8,128)(2,1)S(1)}, u32[]{:S(2)}, u32[]{:S(2)}) collective-permute-start(bf16[1088,128]{1,0:T(8,128)(2,1)S(1)} %bitcast.65), channel_id=1, source_target_pairs={{0,2},{1,3},{2,0},{3,1},{4,6},{5,7},{6,4},{7,5},{8,10},{9,11},{10,... | collective-permute-start | bytes 835592 | tf_op jit(solution)/shard_map/ppermute | solution.py:446
  99.3 25.0 %collective-permute-start.25 = (bf16[1088,128]{1,0:T(8,128)(2,1)S(1)}, bf16[1088,128]{1,0:T(8,128)(2,1)S(1)}, u32[]{:S(2)}, u32[]{:S(2)}) collective-permute-start(bf16[1088,128]{1,0:T(8,128)(2,1)S(1)} %bitcast.66), channel_id=1, source_target_pairs={{0,4},{1,5},{2,6},{3,7},{4,0},{5,1},{6,2},{7,3},{8,12},{9,13},{10,... | collective-permute-start | bytes 835592 | tf_op jit(solution)/shard_map/ppermute | solution.py:446
  102.3 22.2 %collective-permute-start.26 = (bf16[1088,128]{1,0:T(8,128)(2,1)S(1)}, bf16[1088,128]{1,0:T(8,128)(2,1)S(1)}, u32[]{:S(2)}, u32[]{:S(2)}) collective-permute-start(bf16[1088,128]{1,0:T(8,128)(2,1)S(1)} %bitcast.67), channel_id=1, source_target_pairs={{0,6},{1,7},{2,4},{3,5},{4,2},{5,3},{6,0},{7,1},{8,14},{9,15},{10,... | collective-permute-start | bytes 835592 | tf_op jit(solution)/shard_map/ppermute | solution.py:446
  103.3 23.2 %copy-start.5 = (bf16[288,128]{1,0:T(8,128)(2,1)}, bf16[288,128]{1,0:T(8,128)(2,1)S(1)}, u32[]{:S(2)}) copy-start(bf16[288,128]{1,0:T(8,128)(2,1)S(1)} %add_convert_fusion.2.refs_0_) | copy-start | bytes 221188
  103.4 9.5 %collective-permute-start.8 = (bf16[288,128]{1,0:T(8,128)(2,1)S(1)}, bf16[288,128]{1,0:T(8,128)(2,1)S(1)}, u32[]{:S(2)}, u32[]{:S(2)}) collective-permute-start(bf16[288,128]{1,0:T(8,128)(2,1)S(1)} %add_convert_fusion.2.refs_0_), channel_id=1, source_target_pairs={{0,2},{1,3},{2,0},{3,1},{4,6},{5,7},{6,4},{7,5},{8,10},{9,11},{10,... | collective-permute-start | bytes 221192 | tf_op jit(solution)/shard_map/ppermute | solution.py:446
  104.6 8.2 %collective-permute-start.9 = (bf16[288,128]{1,0:T(8,128)(2,1)S(1)}, bf16[288,128]{1,0:T(8,128)(2,1)S(1)}, u32[]{:S(2)}, u32[]{:S(2)}) collective-permute-start(bf16[288,128]{1,0:T(8,128)(2,1)S(1)} %add_convert_fusion.2.refs_0_), channel_id=1, source_target_pairs={{0,4},{1,5},{2,6},{3,7},{4,0},{5,1},{6,2},{7,3},{8,12},{9,13},{10,... | collective-permute-start | bytes 221192 | tf_op jit(solution)/shard_map/ppermute | solution.py:446
  112.8 13.7 %copy-start.14 = (bf16[288,128]{1,0:T(8,128)(2,1)}, bf16[288,128]{1,0:T(8,128)(2,1)S(1)}, u32[]{:S(2)}) copy-start(bf16[288,128]{1,0:T(8,128)(2,1)S(1)} %collective-permute-done.8.refs_1_) | copy-start | bytes 221188
  112.8 4.8 %collective-permute-start.10 = (bf16[288,128]{1,0:T(8,128)(2,1)S(1)}, bf16[288,128]{1,0:T(8,128)(2,1)S(1)}, u32[]{:S(2)}, u32[]{:S(2)}) collective-permute-start(bf16[288,128]{1,0:T(8,128)(2,1)S(1)} %add_convert_fusion.2.refs_0_), channel_id=1, source_target_pairs={{0,6},{1,7},{2,4},{3,5},{4,2},{5,3},{6,0},{7,1},{8,14},{9,15},{10,... | collective-permute-start | bytes 221192 | tf_op jit(solution)/shard_map/ppermute | solution.py:446
  112.8 13.7 %copy-start.15 = (bf16[288,128]{1,0:T(8,128)(2,1)}, bf16[288,128]{1,0:T(8,128)(2,1)S(1)}, u32[]{:S(2)}) copy-start(bf16[288,128]{1,0:T(8,128)(2,1)S(1)} %collective-permute-done.9.refs_2_) | copy-start | bytes 221188
  112.8 9.9 %collective-permute-start.11 = (bf16[288,128]{1,0:T(8,128)(2,1)S(1)}, bf16[288,128]{1,0:T(8,128)(2,1)S(1)}, u32[]{:S(2)}, u32[]{:S(2)}) collective-permute-start(bf16[288,128]{1,0:T(8,128)(2,1)S(1)} %add_convert_fusion.2.refs_0_), channel_id=1, source_target_pairs={{0,1},{1,0},{2,3},{3,2},{4,5},{5,4},{6,7},{7,6},{8,9},{9,8},{10,11... | collective-permute-start | bytes 221192 | tf_op jit(solution)/shard_map/ppermute | solution.py:446
  117.6 9.0 %copy-start.16 = (bf16[288,128]{1,0:T(8,128)(2,1)}, bf16[288,128]{1,0:T(8,128)(2,1)S(1)}, u32[]{:S(2)}) copy-start(bf16[288,128]{1,0:T(8,128)(2,1)S(1)} %collective-permute-done.10.refs_3_) | copy-start | bytes 221188
  117.6 6.1 %collective-permute-start.12 = (bf16[288,128]{1,0:T(8,128)(2,1)S(1)}, bf16[288,128]{1,0:T(8,128)(2,1)S(1)}, u32[]{:S(2)}, u32[]{:S(2)}) collective-permute-start(bf16[288,128]{1,0:T(8,128)(2,1)S(1)} %collective-permute-done.8.refs_1_), channel_id=1, source_target_pairs={{0,1},{1,0},{2,3},{3,2},{4,5},{5,4},{6,7},{7,6},{8,9},{9,8},{10,11... | collective-permute-start | bytes 221192 | tf_op jit(solution)/shard_map/ppermute | solution.py:446
  122.8 3.8 %copy-start.17 = (bf16[288,128]{1,0:T(8,128)(2,1)}, bf16[288,128]{1,0:T(8,128)(2,1)S(1)}, u32[]{:S(2)}) copy-start(bf16[288,128]{1,0:T(8,128)(2,1)S(1)} %collective-permute-done.11.refs_4_) | copy-start | bytes 221188
  122.8 2.0 %collective-permute-start.13 = (bf16[288,128]{1,0:T(8,128)(2,1)S(1)}, bf16[288,128]{1,0:T(8,128)(2,1)S(1)}, u32[]{:S(2)}, u32[]{:S(2)}) collective-permute-start(bf16[288,128]{1,0:T(8,128)(2,1)S(1)} %collective-permute-done.9.refs_2_), channel_id=1, source_target_pairs={{0,1},{1,0},{2,3},{3,2},{4,5},{5,4},{6,7},{7,6},{8,9},{9,8},{10,11... | collective-permute-start | bytes 221192 | tf_op jit(solution)/shard_map/ppermute | solution.py:446
  123.7 2.9 %copy-start.18 = (bf16[288,128]{1,0:T(8,128)(2,1)}, bf16[288,128]{1,0:T(8,128)(2,1)S(1)}, u32[]{:S(2)}) copy-start(bf16[288,128]{1,0:T(8,128)(2,1)S(1)} %collective-permute-done.12.refs_5_) | copy-start | bytes 221188
  123.7 5.9 %collective-permute-start.27 = (bf16[1088,128]{1,0:T(8,128)(2,1)S(1)}, bf16[1088,128]{1,0:T(8,128)(2,1)S(1)}, u32[]{:S(2)}, u32[]{:S(2)}) collective-permute-start(bf16[1088,128]{1,0:T(8,128)(2,1)S(1)} %bitcast.68), channel_id=1, source_target_pairs={{0,1},{1,0},{2,3},{3,2},{4,5},{5,4},{6,7},{7,6},{8,9},{9,8},{10,11... | collective-permute-start | bytes 835592 | tf_op jit(solution)/shard_map/ppermute | solution.py:446
  124.0 5.5 %copy-start.7 = (bf16[1088,128]{1,0:T(8,128)(2,1)}, bf16[1088,128]{1,0:T(8,128)(2,1)S(1)}, u32[]{:S(2)}) copy-start(bf16[1088,128]{1,0:T(8,128)(2,1)S(1)} %collective-permute-done.24.refs_1_) | copy-start | bytes 835588
  124.0 5.5 %collective-permute-start.28 = (bf16[1088,128]{1,0:T(8,128)(2,1)S(1)}, bf16[1088,128]{1,0:T(8,128)(2,1)S(1)}, u32[]{:S(2)}, u32[]{:S(2)}) collective-permute-start(bf16[1088,128]{1,0:T(8,128)(2,1)S(1)} %collective-permute-done.24.refs_1_), channel_id=1, source_target_pairs={{0,1},{1,0},{2,3},{3,2},{4,5},{5,4},{6,7},{7,6},{8,9},{9,8},{10,11... | collective-permute-start | bytes 835592 | tf_op jit(solution)/shard_map/ppermute | solution.py:446
  124.2 5.3 %copy-start.8 = (bf16[1088,128]{1,0:T(8,128)(2,1)}, bf16[1088,128]{1,0:T(8,128)(2,1)S(1)}, u32[]{:S(2)}) copy-start(bf16[1088,128]{1,0:T(8,128)(2,1)S(1)} %collective-permute-done.25.refs_2_) | copy-start | bytes 835588
  124.2 5.4 %collective-permute-start.29 = (bf16[1088,128]{1,0:T(8,128)(2,1)S(1)}, bf16[1088,128]{1,0:T(8,128)(2,1)S(1)}, u32[]{:S(2)}, u32[]{:S(2)}) collective-permute-start(bf16[1088,128]{1,0:T(8,128)(2,1)S(1)} %collective-permute-done.25.refs_2_), channel_id=1, source_target_pairs={{0,1},{1,0},{2,3},{3,2},{4,5},{5,4},{6,7},{7,6},{8,9},{9,8},{10,11... | collective-permute-start | bytes 835592 | tf_op jit(solution)/shard_map/ppermute | solution.py:446
  124.6 5.0 %copy-start.9 = (bf16[1088,128]{1,0:T(8,128)(2,1)}, bf16[1088,128]{1,0:T(8,128)(2,1)S(1)}, u32[]{:S(2)}) copy-start(bf16[1088,128]{1,0:T(8,128)(2,1)S(1)} %collective-permute-done.26.refs_3_) | copy-start | bytes 835588
  124.6 5.0 %collective-permute-start.30 = (bf16[1088,128]{1,0:T(8,128)(2,1)S(1)}, bf16[1088,128]{1,0:T(8,128)(2,1)S(1)}, u32[]{:S(2)}, u32[]{:S(2)}) collective-permute-start(bf16[1088,128]{1,0:T(8,128)(2,1)S(1)} %collective-permute-done.26.refs_3_), channel_id=1, source_target_pairs={{0,1},{1,0},{2,3},{3,2},{4,5},{5,4},{6,7},{7,6},{8,9},{9,8},{10,11... | collective-permute-start | bytes 835592 | tf_op jit(solution)/shard_map/ppermute | solution.py:446
  124.7 1.9 %copy-start.19 = (bf16[288,128]{1,0:T(8,128)(2,1)}, bf16[288,128]{1,0:T(8,128)(2,1)S(1)}, u32[]{:S(2)}) copy-start(bf16[288,128]{1,0:T(8,128)(2,1)S(1)} %collective-permute-done.13.refs_6_) | copy-start | bytes 221188
  124.7 1.8 %collective-permute-start.14 = (bf16[288,128]{1,0:T(8,128)(2,1)S(1)}, bf16[288,128]{1,0:T(8,128)(2,1)S(1)}, u32[]{:S(2)}, u32[]{:S(2)}) collective-permute-start(bf16[288,128]{1,0:T(8,128)(2,1)S(1)} %collective-permute-done.10.refs_3_), channel_id=1, source_target_pairs={{0,1},{1,0},{2,3},{3,2},{4,5},{5,4},{6,7},{7,6},{8,9},{9,8},{10,11... | collective-permute-start | bytes 221192 | tf_op jit(solution)/shard_map/ppermute | solution.py:446
  (6 other events, 4.4 us)

commit v3 on v2

--- a/solution.py
+++ b/solution.py
@@ -10,9 +10,9 @@
 KERNEL = 8
 HEADS = 8
 NORM_EPS = 1e-06
-WIN_STEP = 4
+WIN_STEP = 8
 LANES = 128
-VMEM_LIMIT = 56 * 2**20
+VMEM_LIMIT = 28 * 2**20
 
 f32 = jnp.float32
 bf16 = jnp.bfloat16
@@ -42,6 +42,14 @@
 
 def flag(mask):
     return jnp.where(mask, 1.0, 0.0).astype(bf16)
+
+
+def onehot(codes, values):
+    return jnp.where(codes == values, jnp.ones((), bf16), jnp.zeros((), bf16))
+
+
+def small_iota(shape, dim):
+    return iota(shape, dim).astype(f32).astype(bf16)
 
 
 def spread(row, lanes):
@@ -75,14 +83,15 @@
 
     here = WIN_STEP * KERNEL
     codes = pltpu.roll(bytes_ref[...], lax.rem(length - here * step, length), 1)[:, :here]
-    values = iota((packets, vocab), 1)
+    codes = codes.astype(f32).astype(bf16)
+    values = small_iota((packets, vocab), 1)
     pairs = []
     for k in range(KERNEL // 2):
         rows = []
         for w in range(WIN_STEP):
             j = w * KERNEL + 2 * k
             rows.append(
-                jnp.concatenate([flag(codes[:, j : j + 1] == values), flag(codes[:, j + 1 : j + 2] == values)], axis=1)
+                jnp.concatenate([onehot(codes[:, j : j + 1], values), onehot(codes[:, j + 1 : j + 2], values)], axis=1)
             )
         pairs.append(dot_nn(jnp.concatenate(rows, axis=0), pair_ref[...]).astype(bf16))
     windows = jnp.concatenate(pairs, axis=1)
@@ -128,7 +137,7 @@
             jax.ShapeDtypeStruct((steps * rows, width), bf16),
         ],
         scratch_shapes=[pltpu.VMEM((2 * vocab, 2 * chan), bf16), pltpu.VMEM((packets, width), f32)],
-        compiler_params=pltpu.CompilerParams(vmem_limit_bytes=VMEM_LIMIT),
+        compiler_params=pltpu.CompilerParams(vmem_limit_bytes=2 * VMEM_LIMIT),
         cost_estimate=cost(1e10, 5e6),
         name="embed",
     )(*args)
@@ -282,27 +291,33 @@
     )(*args)
 
 
+def add_by_value(codes_ref, dconv_ref, table_ref, w_rows, table_grad_ref):
+    packets = codes_ref.shape[2]
+    vocab = table_ref.shape[1]
+    values = small_iota((vocab, packets), 0)
+    codes = codes_ref[0].astype(f32).astype(bf16)
+    chosen = [onehot(codes[w : w + 1, :], values) for w in range(codes_ref.shape[1])]
+    by_value = dot_nn(jnp.concatenate(chosen, axis=1), dconv_ref[...]).astype(bf16)
+    table_grad_ref[...] += dot_nt(w_rows, by_value)
+    return dot_nn(table_ref[...], by_value).astype(bf16)
+
+
 def conv_back_kernel(
     capacity,
-    core_ref,
     ret_ref,
     owner_ref,
     codes_ref,
     slope_ref,
     table_ref,
     w_ref,
-    gain_grad_ref,
-    keep_ref,
-    send_ref,
     dconv_ref,
+    rows_ref,
     table_grad_ref,
-    halves_ref,
 ):
     j = pl.program_id(0)
     slots, width = ret_ref.shape
     packets = owner_ref.shape[1]
-    chan, vocab = table_ref.shape
-    positions = codes_ref.shape[1]
+    chan = table_ref.shape[0]
 
     @pl.when(j == 0)
     def _():
@@ -312,55 +327,102 @@
         rank = jnp.sum(jnp.where(same, 1.0, 0.0), axis=1, keepdims=True).astype(jnp.int32)
         place = flag(iota((packets, slots), 1) == own_col * capacity + rank)
         demb = dot_nn(place, ret_ref[...])
-        for w in range(positions):
+        for w in range(codes_ref.shape[1]):
             at = slice(w * packets, (w + 1) * packets)
             dconv_ref[at, :] = (demb * slope_ref[at, :].astype(f32)).astype(bf16)
         table_grad_ref[...] = jnp.zeros_like(table_grad_ref)
+
+    at = pl.ds(pl.multiple_of(j * chan, chan), chan)
+    rows_ref[at, :] = add_by_value(codes_ref, dconv_ref, table_ref, w_ref[at, :], table_grad_ref)
+
+
+def conv_back_rest_kernel(
+    core_ref,
+    codes_ref,
+    dconv_ref,
+    table_ref,
+    w_ref,
+    first_rows_ref,
+    first_table_ref,
+    gain_grad_ref,
+    keep_ref,
+    send_ref,
+    rows_ref,
+    table_grad_ref,
+    halves_ref,
+):
+    j = pl.program_id(0)
+    width = dconv_ref.shape[1]
+    chan, vocab = table_ref.shape
+    window = w_ref.shape[0]
+    done = first_rows_ref.shape[0]
+
+    @pl.when(j == 0)
+    def _():
+        rows_ref[0:done, :] = first_rows_ref[...]
+        table_grad_ref[...] = first_table_ref[...]
         halves_ref[...] = jnp.zeros_like(halves_ref)
 
-    values = iota((vocab, packets), 0)
-    onehot = jnp.concatenate([flag(codes_ref[0, w : w + 1, :] == values) for w in range(positions)], axis=1)
-    by_value = dot_nn(onehot, dconv_ref[...]).astype(bf16)
-    w_rows = w_ref[pl.ds(pl.multiple_of(j * chan, chan), chan), :]
-    table_grad_ref[...] += dot_nt(w_rows, by_value)
-    grad_rows = dot_nn(table_ref[...], by_value).astype(bf16)
-    window = KERNEL * chan
-    wide = width // (2 * LANES)
-    for half in range(2):
-        for s in range(wide):
-            at = pl.multiple_of(s * window + j * chan, chan)
-            slab = half * wide + s
-            halves_ref[half, pl.ds(at, chan), :] = grad_rows[:, slab * LANES : (slab + 1) * LANES]
+    at = pl.ds(pl.multiple_of(done + j * chan, chan), chan)
+    rows_ref[at, :] = add_by_value(codes_ref, dconv_ref, table_ref, w_ref[at, :], table_grad_ref)
 
     @pl.when(j == pl.num_programs(0) - 1)
     def _():
-        at = wide * window
+        wide = width // (2 * LANES)
         for half in range(2):
+            for s in range(wide):
+                slab = half * wide + s
+                halves_ref[half, s * window : (s + 1) * window, :] = rows_ref[:, slab * LANES : (slab + 1) * LANES]
+            end = wide * window
             table_part = table_grad_ref[:, half * vocab // 2 : (half + 1) * vocab // 2]
-            halves_ref[half, at : at + chan, :] = table_part.astype(bf16)
-        halves_ref[0, at + chan : at + chan + 16, :] = gain_grad_ref[...].astype(bf16)
+            halves_ref[half, end : end + chan, :] = table_part.astype(bf16)
+        halves_ref[0, end + chan : end + chan + 16, :] = gain_grad_ref[...].astype(bf16)
         share_out(core_ref, halves_ref, keep_ref, send_ref)
 
 
-def conv_back(core, returned, owner, codes, slope, table_t, w_conv, gain_grad, capacity, half_rows):
-    whole = lambda a: pl.BlockSpec(a.shape, lambda j: (0, 0))
-    args = (returned, owner, codes, slope, table_t, w_conv, gain_grad)
+def whole(a):
+    return pl.BlockSpec(a.shape, lambda j: (0,) * len(a.shape))
+
+
+def conv_back(returned, owner, codes, slope, table_t, w_conv, capacity, steps):
+    args = (returned, owner, codes, slope, table_t, w_conv)
+    chan = table_t.shape[0]
     specs = [whole(a) if a.ndim == 2 else pl.BlockSpec((1, *a.shape[1:]), lambda j: (j, 0, 0)) for a in args]
+    outs = [
+        jax.ShapeDtypeStruct(slope.shape, bf16),
+        jax.ShapeDtypeStruct((steps * chan, w_conv.shape[1]), bf16),
+        jax.ShapeDtypeStruct(table_t.shape, f32),
+    ]
+    return pl.pallas_call(
+        functools.partial(conv_back_kernel, capacity),
+        grid=(steps,),
+        in_specs=specs,
+        out_specs=[whole(o) for o in outs],
+        out_shape=outs,
+        compiler_params=pltpu.CompilerParams(vmem_limit_bytes=VMEM_LIMIT),
+        cost_estimate=cost(8e9, 1e7),
+        name="conv_back",
+    )(*args)
+
+
+def conv_back_rest(core, codes, dconv, table_t, w_conv, rows, table_grad, gain_grad, half_rows, first):
+    args = (codes, dconv, table_t, w_conv, rows, table_grad, gain_grad)
+    specs = [whole(a) if a.ndim == 2 else pl.BlockSpec((1, *a.shape[1:]), lambda j: (j + first, 0, 0)) for a in args]
     half = jax.ShapeDtypeStruct((half_rows, LANES), bf16)
     return pl.pallas_call(
-        functools.partial(conv_back_kernel, capacity),
-        grid=(KERNEL,),
+        conv_back_rest_kernel,
+        grid=(KERNEL - first,),
         in_specs=[pl.BlockSpec(memory_space=pltpu.SMEM), *specs],
         out_specs=[whole(half), whole(half)],
         out_shape=[half, half],
         scratch_shapes=[
-            pltpu.VMEM(slope.shape, bf16),
+            pltpu.VMEM(w_conv.shape, bf16),
             pltpu.VMEM(table_t.shape, f32),
             pltpu.VMEM((2, half_rows, LANES), bf16),
         ],
         compiler_params=pltpu.CompilerParams(vmem_limit_bytes=VMEM_LIMIT),
-        cost_estimate=cost(1e10, 5e6),
-        name="conv_back",
+        cost_estimate=cost(6e9, 6e6),
+        name="conv_back_rest",
     )(core, *args)
 
 
@@ -445,11 +507,13 @@
         stride, size = level
         return lax.ppermute(value, AXES, [(i, i + ((i // stride % size ^ d) - i // stride % size) * stride) for i in range(self.count)])
 
-    def scatter_sum(self, value, level):
+    def scatter_sum(self, value, level, other=None):
         size = level[1]
         value = value.reshape(size, value.shape[0] // size, value.shape[1])
         mine = self.place(level)
         got = [self.swap(lax.dynamic_index_in_dim(value, mine ^ d, 0, keepdims=False), level, d) for d in range(1, size)]
+        if other is not None:
+            got = after(got, other)
         total = lax.dynamic_index_in_dim(value, mine, 0, keepdims=False).astype(f32)
         for g in got:
             total = total + g.astype(f32)
@@ -478,6 +542,10 @@
         quad = self.levels[1]
         own = [value] + [self.swap(value, quad, d) for d in range(1, quad[1])]
         return own + [self.swap(p, self.levels[0], 1) for p in own]
+
+
+def after(value, other):
+    return lax.optimization_barrier((value, other))[0]
 
 
 def body(packet_bytes, owner_index, session_id, class_label, byte_table, w_conv, norm_gain, w_project, w_out, w_head):
@@ -519,14 +587,17 @@
     used = window * width // (2 * LANES) + chan * vocab // (2 * LANES) + 16
     unit = 64
     half_rows = -(-used // unit) * unit
-    returned, early = lax.optimization_barrier((exchange(back), early))
-    keep, send = conv_back(
-        core, returned, owner, codes, slope, table_t, w_conv, gain_grad, capacity, half_rows
+    first = KERNEL // 2
+    _, quad, *upper = devices.levels
+    dconv, rows, table_rows = conv_back(
+        after(exchange(back), early), owner, codes, slope, table_t, w_conv, capacity, first
     )
-    _, quad, *upper = devices.levels
-    early = devices.scatter_sum(early, quad)
+    early = devices.scatter_sum(early, quad, rows)
+    keep, send = conv_back_rest(
+        core, codes, dconv, table_t, w_conv, rows, after(table_rows, early), gain_grad, half_rows, first
+    )
     for level in upper:
-        early = devices.scatter_sum(early, level)
+        early = devices.scatter_sum(early, level, keep)
     for level in upper[::-1]:
         early = devices.gather(early, level)
     late = devices.scatter_sum(devices.pair_sum(keep, send), quad)

time: 136 us -> 122 us (0.90)
  Pallas kernels: 50.1 us -> 40.5 us
  waiting for transfers between devices: 29.7 us -> 20.5 us
  starting transfers between devices: 48.7 us -> 50.6 us
    ppermute x31, waiting for transfers between devices: 15.8 us -> 8.9 us  [swap(): lax.ppermute(value, AXES, [(i, i + ((i // stride % size ^ d) - i // strid...]
    pallas_call x1 -> x2, Pallas kernels: 16.6 us -> 13.4 us  [the longest x1 7.29 us: conv_back(): pl.pallas_call(functools.partial(conv_back_kernel, capacity), grid=(steps...]
    pallas_call x1, Pallas kernels: 15.1 us -> 12.4 us  [embed(): pl.pallas_call(functools.partial(embed_kernel, capacity), grid=(steps,),...]
    ppermute x31, starting transfers between devices: 38.2 us -> 40.8 us  [swap(): lax.ppermute(value, AXES, [(i, i + ((i // stride % size ^ d) - i // strid...]
    all_to_all x2, waiting for transfers between devices: 13.9 us -> 11.6 us  [exchange(): lax.all_to_all(rows.reshape(groups, capacity, rows.shape[1]), 'dp', split...]
    unnamed x43 -> x21, local copies, waits for them, and re-layouts: 3.04 us -> 5.1 us
    pallas_call x1, Pallas kernels: 12 us -> 10 us  [session_layer(): pl.pallas_call(session_kernel, in_specs=[pl.BlockSpec(memory_space=pltpu....]
    pallas_call x2, Pallas kernels: 6.29 us -> 4.68 us  [assemble(): pl.pallas_call(kernel, in_specs=[pl.BlockSpec(memory_space=pltpu.SMEM)] +...]
  transfers between devices with their start and end apart: 33 -> 33, of which waited for: 9 -> 10; matrix products, arithmetic and copies ran while one was open for 2% -> 2% of each run, Pallas kernels for 14% -> 13%
where the time goes in v3:
time: 122 us; the launch traced here: 120 us
  starting transfers between devices  50.6 us (41%)
  Pallas kernels  40.5 us (33%)
  waiting for transfers between devices  20.5 us (17%)
  local copies, waits for them, and re-layouts  5.32 us (4%)
  other arithmetic  1.99 us (2%)
    ppermute x31, starting transfers between devices, swap(): lax.ppermute(value, AXES, [(i, i + ((i // stride % size ^ d) - i // strid...  40.8 us
    pallas_call x1, Pallas kernels, embed(): pl.pallas_call(functools.partial(embed_kernel, capacity), grid=(steps,),...  12.4 us
    all_to_all x2, waiting for transfers between devices, exchange(): lax.all_to_all(rows.reshape(groups, capacity, rows.shape[1]), 'dp', split...  11.6 us
    pallas_call x1, Pallas kernels, session_layer(): pl.pallas_call(session_kernel, in_specs=[pl.BlockSpec(memory_space=pltpu....  10 us
    all_to_all x2, starting transfers between devices, exchange(): lax.all_to_all(rows.reshape(groups, capacity, rows.shape[1]), 'dp', split...  9.82 us
    ppermute x31, waiting for transfers between devices, swap(): lax.ppermute(value, AXES, [(i, i + ((i // stride % size ^ d) - i // strid...  8.9 us
    pallas_call x1, Pallas kernels, conv_back(): pl.pallas_call(functools.partial(conv_back_kernel, capacity), grid=(steps...  7.29 us
    pallas_call x1, Pallas kernels, conv_back_rest(): pl.pallas_call(conv_back_rest_kernel, grid=(KERNEL - first,), in_specs=[p...  6.07 us
  transfers between devices with their start and end apart: 33, of which 10 were waited for; matrix products, arithmetic and copies ran while one was open for 2% of the time, Pallas kernels for 13%

profile of v3, /device:TPU:11, one launch (start us, length us, event | category | flops | bytes accessed | tf_op | source)
XLA Modules:
  0.0 119.9 jit_solution(13295386725873594270)
XLA Ops:
  0.7 12.4 %embed.1 = (bf16[256,640]{1,0:T(8,128)(2,1)}, bf16[4096,512]{1,0:T(8,128)(2,1)}) custom-call(s32[128,256]{1,0:T(8,128)} %bytes_ref.1, s32[1,128]{1,0:T(1,128)} %bitcast.69, s32[1,128]{1,0:T(1,128)} %bitcast.79, bf16[64,256]{1,0:T(8,128)(2,1)} %bitcast.65, bf16[512,512]{1,0:T(8,128)(2,1)} %w_ref.5), custom_call_target="tpu_custom_call" | custom-call | flops 10000000000 | bytes 5000000 | tf_op jit(solution)/shard_map/embed/pallas_call | solution.py:127
  13.1 5.7 %all-to-all-start = ((bf16[8,32,640]{2,1,0:T(8,128)(2,1)}), bf16[8,32,640]{2,1,0:T(8,128)(2,1)S(1)}, u32[]{:S(2)}, u32[]{:S(2)}) async-start(bf16[8,32,640]{2,1,0:T(8,128)(2,1)} %bitcast.78), calls=%async_computation | async-start | bytes 655360 | tf_op jit(solution)/shard_map/all_to_all | solution.py:571
  18.8 7.3 %all-to-all-done = bf16[8,32,640]{2,1,0:T(8,128)(2,1)S(1)} async-done(((bf16[8,32,640]{2,1,0:T(8,128)(2,1)}), bf16[8,32,640]{2,1,0:T(8,128)(2,1)S(1)}, u32[]{:S(2)}, u32[]{:S(2)}) %all-to-all-start) | async-done | bytes 327712 | tf_op jit(solution)/shard_map/all_to_all | solution.py:571
  26.2 0.9 copy-done.3
  27.1 10.0 %session_layer.1 = (f32[16,128]{1,0:T(8,128)}, bf16[256,512]{1,0:T(8,128)(2,1)}, bf16[4352,128]{1,0:T(8,128)(2,1)S(1)}, bf16[4352,128]{1,0:T(8,128)(2,1)}, f32[16,128]{1,0:T(8,128)S(1)}) custom-call(s32[1]{0:T(128)} %bitcast.core_ref, bf16[256,640]{1,0:T(8,128)(2,1)S(1)} %bitcast.56, s32[1,16]{1,0:T(1,128)S(1)} %bitcast.68, ...), custom_call_target="tpu_custom_call" | custom-call | flops 10000000000 | bytes 5000000 | tf_op jit(solution)/shard_map/session_layer/pallas_call | solution.py:270
  37.1 3.2 %collective-permute-start = (bf16[4352,128]{1,0:T(8,128)(2,1)}, bf16[4352,128]{1,0:T(8,128)(2,1)S(1)}, u32[]{:S(2)}, u32[]{:S(2)}) collective-permute-start(bf16[4352,128]{1,0:T(8,128)(2,1)} %get-tuple-element.37), channel_id=1, source_target_pairs={{0,1},{1,0},{2,3},{3,2},{4,5},{5,4},{6,7},{7,6},{8,9},{9,8},{10,11... | collective-permute-start | bytes 3342344 | tf_op jit(solution)/shard_map/ppermute | solution.py:508
  40.3 1.0 copy.17
  41.4 4.1 %all-to-all-start.1 = ((bf16[8,32,512]{2,1,0:T(8,128)(2,1)}), bf16[8,32,512]{2,1,0:T(8,128)(2,1)S(1)}, u32[]{:S(2)}, u32[]{:S(2)}) async-start(bf16[8,32,512]{2,1,0:T(8,128)(2,1)} %bitcast.10), calls=%async_computation.1 | async-start | bytes 524288 | tf_op jit(solution)/shard_map/all_to_all | solution.py:571
  45.5 1.0 copy-done.8
  46.5 1.5 %add_convert_fusion = bf16[4352,128]{1,0:T(8,128)(2,1)S(1)} fusion(bf16[4352,128]{1,0:T(8,128)(2,1)} %copy-done.8, bf16[4352,128]{1,0:T(8,128)(2,1)S(1)} %get-tuple-element.36), kind=kLoop, calls=%fused_computation | loop fusion | flops 2228224 | bytes 3342336 | tf_op jit(solution)/shard_map/convert_element_type | solution.py:539
  48.1 4.2 %all-to-all-done.1 = bf16[8,32,512]{2,1,0:T(8,128)(2,1)S(1)} async-done(((bf16[8,32,512]{2,1,0:T(8,128)(2,1)}), bf16[8,32,512]{2,1,0:T(8,128)(2,1)S(1)}, u32[]{:S(2)}, u32[]{:S(2)}) %all-to-all-start.1) | async-done | bytes 262176 | tf_op jit(solution)/shard_map/all_to_all | solution.py:571
  52.4 0.3 collective-permute-start.1
  52.7 1.5 %collective-permute-start.2 = (bf16[1088,128]{1,0:T(8,128)(2,1)S(1)}, bf16[1088,128]{1,0:T(8,128)(2,1)S(1)}, u32[]{:S(2)}, u32[]{:S(2)}) collective-permute-start(bf16[1088,128]{1,0:T(8,128)(2,1)S(1)} %get-tuple-element.62), channel_id=1, source_target_pairs={{0,4},{1,5},{2,6},{3,7},{4,0},{5,1},{6,2},{7,3},{8,12},{9,13},{10,... | collective-permute-start | bytes 835592 | tf_op jit(solution)/shard_map/ppermute | solution.py:508
  54.2 0.9 collective-permute-start.3
  55.2 2.2 %copy-done.7 = bf16[4096,512]{1,0:T(8,128)(2,1)S(1)} copy-done((bf16[4096,512]{1,0:T(8,128)(2,1)S(1)}, bf16[4096,512]{1,0:T(8,128)(2,1)}, u32[]{:S(2)}) %copy-start.7) | copy-done | bytes 4194328
  57.4 7.3 %conv_back.1 = (bf16[4096,512]{1,0:T(8,128)(2,1)S(1)}, bf16[256,512]{1,0:T(8,128)(2,1)S(1)}, f32[64,256]{1,0:T(8,128)S(1)}) custom-call(bf16[256,512]{1,0:T(8,128)(2,1)S(1)} %bitcast.62, s32[1,128]{1,0:T(1,128)S(1)} %bitcast.70, s32[8,32,128]{2,1,0:T(8,128)S(1)} %bitcast.63, bf16[4096,512]{1,0:T(8,128)(2,1)S(1)} %copy-done.7, bf16[64,256]{1,0:T(8,128)(2,1)S(1)} %bitcast.66, ...), custom_call_target="tpu_custom_call" | custom-call | flops 8000000000 | bytes 10000000 | tf_op jit(solution)/shard_map/conv_back/pallas_call | solution.py:396
  64.7 2.1 %collective-permute-done.3 = bf16[1088,128]{1,0:T(8,128)(2,1)S(1)} collective-permute-done((bf16[1088,128]{1,0:T(8,128)(2,1)S(1)}, bf16[1088,128]{1,0:T(8,128)(2,1)S(1)}, u32[]{:S(2)}, u32[]{:S(2)}) %collective-permute-start.3) | collective-permute-done | bytes 278560 | tf_op jit(solution)/shard_map/ppermute | solution.py:508
  67.0 3.0 %collective-permute-start.19 = (bf16[272,128]{1,0:T(8,128)(2,1)S(1)}, bf16[272,128]{1,0:T(8,128)(2,1)S(1)}, u32[]{:S(2)}, u32[]{:S(2)}) collective-permute-start(bf16[272,128]{1,0:T(8,128)(2,1)S(1)} %get-tuple-element.68), channel_id=1, source_target_pairs={{0,16},{1,17},{2,18},{3,19},{4,20},{5,21},{6,22},{7,23},{8,24},{9,... | collective-permute-start | bytes 208904 | tf_op jit(solution)/shard_map/ppermute | solution.py:508
  70.0 0.2 collective-permute-start.20
  70.2 6.1 %conv_back_rest.1 = (bf16[1152,128]{1,0:T(8,128)(2,1)S(1)}, bf16[1152,128]{1,0:T(8,128)(2,1)S(1)}) custom-call(s32[1]{0:T(128)} %bitcast.core_ref, s32[8,32,128]{2,1,0:T(8,128)S(1)} %bitcast.64, bf16[4096,512]{1,0:T(8,128)(2,1)S(1)} %get-tuple-element.40.dconv_ref, bf16[64,256]{1,0:T(8,128)(2,1)S(1)} %bitcast.67, bf16[512,512]{1,0:T(8,128)(2,1)S(1)} %copy-done.2, ...), custom_call_target="tpu_custom_call" | custom-call | flops 6000000000 | bytes 6000000 | tf_op jit(solution)/shard_map/conv_back_rest/pallas_call | solution.py:412
  76.4 1.2 %collective-permute-start.21 = (bf16[272,128]{1,0:T(8,128)(2,1)S(1)}, bf16[272,128]{1,0:T(8,128)(2,1)S(1)}, u32[]{:S(2)}, u32[]{:S(2)}) collective-permute-start(bf16[272,128]{1,0:T(8,128)(2,1)S(1)} %get-tuple-element.60), channel_id=1, source_target_pairs={{0,8},{1,9},{2,10},{3,11},{4,12},{5,13},{6,14},{7,15},{8,0},{9,1},... | collective-permute-start | bytes 208904 | tf_op jit(solution)/shard_map/ppermute | solution.py:508
  77.7 3.0 %collective-permute-start.4 = (bf16[1152,128]{1,0:T(8,128)(2,1)S(1)}, bf16[1152,128]{1,0:T(8,128)(2,1)S(1)}, u32[]{:S(2)}, u32[]{:S(2)}) collective-permute-start(bf16[1152,128]{1,0:T(8,128)(2,1)S(1)} %get-tuple-element.49), channel_id=1, source_target_pairs={{0,1},{1,0},{2,3},{3,2},{4,5},{5,4},{6,7},{7,6},{8,9},{9,8},{10,11... | collective-permute-start | bytes 884744 | tf_op jit(solution)/shard_map/ppermute | solution.py:508
  80.7 1.3 %collective-permute-start.22 = (bf16[272,128]{1,0:T(8,128)(2,1)S(1)}, bf16[272,128]{1,0:T(8,128)(2,1)S(1)}, u32[]{:S(2)}, u32[]{:S(2)}) collective-permute-start(bf16[272,128]{1,0:T(8,128)(2,1)S(1)} %get-tuple-element.60), channel_id=1, source_target_pairs={{0,16},{1,17},{2,18},{3,19},{4,20},{5,21},{6,22},{7,23},{8,24},{9,... | collective-permute-start | bytes 208904 | tf_op jit(solution)/shard_map/ppermute | solution.py:508
  82.0 0.5 collective-permute-start.23
  82.6 1.5 %collective-permute-start.7 = (bf16[288,128]{1,0:T(8,128)(2,1)S(1)}, bf16[288,128]{1,0:T(8,128)(2,1)S(1)}, u32[]{:S(2)}, u32[]{:S(2)}) collective-permute-start(bf16[288,128]{1,0:T(8,128)(2,1)S(1)} %get-tuple-element.65), channel_id=1, source_target_pairs={{0,6},{1,7},{2,4},{3,5},{4,2},{5,3},{6,0},{7,1},{8,14},{9,15},{10,... | collective-permute-start | bytes 221192 | tf_op jit(solution)/shard_map/ppermute | solution.py:508
  84.1 0.2 collective-permute-start.6
  84.3 1.0 collective-permute-start.5
  85.4 1.4 %collective-permute-done.7 = bf16[288,128]{1,0:T(8,128)(2,1)S(1)} collective-permute-done((bf16[288,128]{1,0:T(8,128)(2,1)S(1)}, bf16[288,128]{1,0:T(8,128)(2,1)S(1)}, u32[]{:S(2)}, u32[]{:S(2)}) %collective-permute-start.7) | collective-permute-done | bytes 73760 | tf_op jit(solution)/shard_map/ppermute | solution.py:508
  86.8 2.2 %collective-permute-done.6 = bf16[288,128]{1,0:T(8,128)(2,1)S(1)} collective-permute-done((bf16[288,128]{1,0:T(8,128)(2,1)S(1)}, bf16[288,128]{1,0:T(8,128)(2,1)S(1)}, u32[]{:S(2)}, u32[]{:S(2)}) %collective-permute-start.6) | collective-permute-done | bytes 73760 | tf_op jit(solution)/shard_map/ppermute | solution.py:508
  89.1 0.6 collective-permute-start.10
  89.6 3.4 %collective-permute-start.9 = (bf16[288,128]{1,0:T(8,128)(2,1)S(1)}, bf16[288,128]{1,0:T(8,128)(2,1)S(1)}, u32[]{:S(2)}, u32[]{:S(2)}) collective-permute-start(bf16[288,128]{1,0:T(8,128)(2,1)S(1)} %fusion.5), channel_id=1, source_target_pairs={{0,16},{1,17},{2,18},{3,19},{4,20},{5,21},{6,22},{7,23},{8,24},{9,... | collective-permute-start | bytes 221192 | tf_op jit(solution)/shard_map/ppermute | solution.py:508
  93.1 1.1 collective-permute-start.24
  94.2 0.8 collective-permute-start.25
  94.9 0.9 collective-permute-start.26
  95.8 0.5 collective-permute-done.8
  96.3 1.1 collective-permute-start.11
  97.4 0.8 collective-permute-start.12
  98.2 0.7 collective-permute-done.24.refs_1_
  98.9 1.5 %collective-permute-start.13 = (bf16[288,128]{1,0:T(8,128)(2,1)S(1)}, bf16[288,128]{1,0:T(8,128)(2,1)S(1)}, u32[]{:S(2)}, u32[]{:S(2)}) collective-permute-start(bf16[288,128]{1,0:T(8,128)(2,1)S(1)} %add_convert_fusion.2.refs_0_), channel_id=1, source_target_pairs={{0,6},{1,7},{2,4},{3,5},{4,2},{5,3},{6,0},{7,1},{8,14},{9,15},{10,... | collective-permute-start | bytes 221192 | tf_op jit(solution)/shard_map/ppermute | solution.py:508
  100.3 0.4 collective-permute-done.25.refs_2_
  100.8 10.0 %collective-permute-start.14 = (bf16[288,128]{1,0:T(8,128)(2,1)S(1)}, bf16[288,128]{1,0:T(8,128)(2,1)S(1)}, u32[]{:S(2)}, u32[]{:S(2)}) collective-permute-start(bf16[288,128]{1,0:T(8,128)(2,1)S(1)} %add_convert_fusion.2.refs_0_), channel_id=1, source_target_pairs={{0,1},{1,0},{2,3},{3,2},{4,5},{5,4},{6,7},{7,6},{8,9},{9,8},{10,11... | collective-permute-start | bytes 221192 | tf_op jit(solution)/shard_map/ppermute | solution.py:508
  110.8 1.6 %collective-permute-start.16 = (bf16[288,128]{1,0:T(8,128)(2,1)S(1)}, bf16[288,128]{1,0:T(8,128)(2,1)S(1)}, u32[]{:S(2)}, u32[]{:S(2)}) collective-permute-start(bf16[288,128]{1,0:T(8,128)(2,1)S(1)} %collective-permute-done.12.refs_2_), channel_id=1, source_target_pairs={{0,1},{1,0},{2,3},{3,2},{4,5},{5,4},{6,7},{7,6},{8,9},{9,8},{10,11... | collective-permute-start | bytes 221192 | tf_op jit(solution)/shard_map/ppermute | solution.py:508
  112.4 0.5 collective-permute-start.28
  112.9 0.4 collective-permute-start.30
  113.4 0.2 collective-permute-start.17
  113.7 1.5 %collective-permute-done.17.refs_7_ = bf16[288,128]{1,0:T(8,128)(2,1)S(1)} collective-permute-done((bf16[288,128]{1,0:T(8,128)(2,1)S(1)}, bf16[288,128]{1,0:T(8,128)(2,1)S(1)}, u32[]{:S(2)}, u32[]{:S(2)}) %collective-permute-start.17) | collective-permute-done | bytes 73760 | tf_op jit(solution)/shard_map/ppermute | solution.py:508
  115.2 1.7 %late_out.1 = (f32[512,512]{1,0:T(8,128)}, f32[64,256]{1,0:T(8,128)}, f32[1,512]{1,0:T(1,128)}) custom-call(s32[2]{0:T(128)S(1)} %pad_add_fusion.place_ref, bf16[288,128]{1,0:T(8,128)(2,1)S(1)} %add_convert_fusion.2.refs_0_, bf16[288,128]{1,0:T(8,128)(2,1)S(1)} %collective-permute-done.11.refs_1_, bf16[288,128]{1,0:T(8,128)(2,1)S(1)} %collective-permute-done.12.refs_2_, ...), custom_call_target="tpu_custom_call" | custom-call | flops 1000000000 | bytes 5000000 | tf_op jit(solution)/shard_map/late_out/pallas_call | solution.py:476
  116.9 3.0 %early_out.1 = (f32[512,1536]{1,0:T(8,128)}, f32[512,512]{1,0:T(8,128)}, f32[512,128]{1,0:T(8,128)}) custom-call(s32[2]{0:T(128)S(1)} %pad_add_fusion.place_ref, bf16[1088,128]{1,0:T(8,128)(2,1)S(1)} %bitcast.61, bf16[1088,128]{1,0:T(8,128)(2,1)S(1)} %collective-permute-done.24.refs_1_, bf16[1088,128]{1,0:T(8,128)(2,1)S(1)} %collective-permute-done.25.refs_2_, ...), custom_call_target="tpu_custom_call" | custom-call | flops 1000000000 | bytes 5000000 | tf_op jit(solution)/shard_map/early_out/pallas_call | solution.py:476
  (61 shorter events, 1.0 us)
Async XLA Ops:
  0.6 18.2 %copy-start.9 = (bf16[512]{0:T(512)(128)(2,1)S(1)}, bf16[512]{0:T(512)(128)(2,1)}, u32[]{:S(2)}) copy-start(bf16[512]{0:T(512)(128)(2,1)} %param.16) | copy-start | bytes 3076
  0.6 25.5 %copy-start = (bf16[512,1536]{1,0:T(8,128)(2,1)S(1)}, bf16[512,1536]{1,0:T(8,128)(2,1)}, u32[]{:S(2)}) copy-start(bf16[512,1536]{1,0:T(8,128)(2,1)} %wp_ref.1) | copy-start | bytes 4718596
  0.7 25.5 %copy-start.1 = (bf16[512,512]{1,0:T(8,128)(2,1)S(1)}, bf16[512,512]{1,0:T(8,128)(2,1)}, u32[]{:S(2)}) copy-start(bf16[512,512]{1,0:T(8,128)(2,1)} %wo_ref.1) | copy-start | bytes 1572868
  0.7 25.5 %copy-start.5 = (s32[16]{0:T(128)S(1)}, s32[16]{0:T(128)}, u32[]{:S(2)}) copy-start(s32[16]{0:T(128)} %param.13) | copy-start | bytes 196
  13.1 13.0 %all-to-all-start = ((bf16[8,32,640]{2,1,0:T(8,128)(2,1)}), bf16[8,32,640]{2,1,0:T(8,128)(2,1)S(1)}, u32[]{:S(2)}, u32[]{:S(2)}) async-start(bf16[8,32,640]{2,1,0:T(8,128)(2,1)} %bitcast.78), calls=%async_computation | async-start | bytes 655360 | tf_op jit(solution)/shard_map/all_to_all | solution.py:571
  26.2 0.9 copy-start.3
  37.1 8.4 %collective-permute-start = (bf16[4352,128]{1,0:T(8,128)(2,1)}, bf16[4352,128]{1,0:T(8,128)(2,1)S(1)}, u32[]{:S(2)}, u32[]{:S(2)}) collective-permute-start(bf16[4352,128]{1,0:T(8,128)(2,1)} %get-tuple-element.37), channel_id=1, source_target_pairs={{0,1},{1,0},{2,3},{3,2},{4,5},{5,4},{6,7},{7,6},{8,9},{9,8},{10,11... | collective-permute-start | bytes 3342344 | tf_op jit(solution)/shard_map/ppermute | solution.py:508
  41.4 10.9 %all-to-all-start.1 = ((bf16[8,32,512]{2,1,0:T(8,128)(2,1)}), bf16[8,32,512]{2,1,0:T(8,128)(2,1)S(1)}, u32[]{:S(2)}, u32[]{:S(2)}) async-start(bf16[8,32,512]{2,1,0:T(8,128)(2,1)} %bitcast.10), calls=%async_computation.1 | async-start | bytes 524288 | tf_op jit(solution)/shard_map/all_to_all | solution.py:571
  45.5 1.0 copy-start.8
  48.1 7.1 %copy-start.2 = (bf16[512,512]{1,0:T(8,128)(2,1)S(1)}, bf16[512,512]{1,0:T(8,128)(2,1)}, u32[]{:S(2)}) copy-start(bf16[512,512]{1,0:T(8,128)(2,1)} %w_ref.5) | copy-start | bytes 1572868
  48.1 7.1 %copy-start.4 = (bf16[256,64]{0,1:T(8,128)(2,1)S(1)}, bf16[256,64]{0,1:T(8,128)(2,1)}, u32[]{:S(2)}) copy-start(bf16[256,64]{0,1:T(8,128)(2,1)} %param.14) | copy-start | bytes 98308
  48.1 7.1 %copy-start.6 = (s32[128]{0:T(128)S(1)}, s32[128]{0:T(128)}, u32[]{:S(2)}) copy-start(s32[128]{0:T(128)} %param.11) | copy-start | bytes 1540
  52.4 12.2 %collective-permute-start.1 = (bf16[1088,128]{1,0:T(8,128)(2,1)S(1)}, bf16[1088,128]{1,0:T(8,128)(2,1)S(1)}, u32[]{:S(2)}, u32[]{:S(2)}) collective-permute-start(bf16[1088,128]{1,0:T(8,128)(2,1)S(1)} %get-tuple-element.63), channel_id=1, source_target_pairs={{0,2},{1,3},{2,0},{3,1},{4,6},{5,7},{6,4},{7,5},{8,10},{9,11},{10,... | collective-permute-start | bytes 835592 | tf_op jit(solution)/shard_map/ppermute | solution.py:508
  52.7 11.9 %collective-permute-start.2 = (bf16[1088,128]{1,0:T(8,128)(2,1)S(1)}, bf16[1088,128]{1,0:T(8,128)(2,1)S(1)}, u32[]{:S(2)}, u32[]{:S(2)}) collective-permute-start(bf16[1088,128]{1,0:T(8,128)(2,1)S(1)} %get-tuple-element.62), channel_id=1, source_target_pairs={{0,4},{1,5},{2,6},{3,7},{4,0},{5,1},{6,2},{7,3},{8,12},{9,13},{10,... | collective-permute-start | bytes 835592 | tf_op jit(solution)/shard_map/ppermute | solution.py:508
  54.2 12.5 %collective-permute-start.3 = (bf16[1088,128]{1,0:T(8,128)(2,1)S(1)}, bf16[1088,128]{1,0:T(8,128)(2,1)S(1)}, u32[]{:S(2)}, u32[]{:S(2)}) collective-permute-start(bf16[1088,128]{1,0:T(8,128)(2,1)S(1)} %get-tuple-element.61), channel_id=1, source_target_pairs={{0,6},{1,7},{2,4},{3,5},{4,2},{5,3},{6,0},{7,1},{8,14},{9,15},{10,... | collective-permute-start | bytes 835592 | tf_op jit(solution)/shard_map/ppermute | solution.py:508
  55.2 2.2 %copy-start.7 = (bf16[4096,512]{1,0:T(8,128)(2,1)S(1)}, bf16[4096,512]{1,0:T(8,128)(2,1)}, u32[]{:S(2)}) copy-start(bf16[4096,512]{1,0:T(8,128)(2,1)} %get-tuple-element.39.slope_ref) | copy-start | bytes 12582916
  66.9 9.3 %collective-permute-start.18 = (bf16[272,128]{1,0:T(8,128)(2,1)S(1)}, bf16[272,128]{1,0:T(8,128)(2,1)S(1)}, u32[]{:S(2)}, u32[]{:S(2)}) collective-permute-start(bf16[272,128]{1,0:T(8,128)(2,1)S(1)} %get-tuple-element.69), channel_id=1, source_target_pairs={{0,8},{1,9},{2,10},{3,11},{4,12},{5,13},{6,14},{7,15},{8,0},{9,1},... | collective-permute-start | bytes 208904 | tf_op jit(solution)/shard_map/ppermute | solution.py:508
  67.0 9.3 %collective-permute-start.19 = (bf16[272,128]{1,0:T(8,128)(2,1)S(1)}, bf16[272,128]{1,0:T(8,128)(2,1)S(1)}, u32[]{:S(2)}, u32[]{:S(2)}) collective-permute-start(bf16[272,128]{1,0:T(8,128)(2,1)S(1)} %get-tuple-element.68), channel_id=1, source_target_pairs={{0,16},{1,17},{2,18},{3,19},{4,20},{5,21},{6,22},{7,23},{8,24},{9,... | collective-permute-start | bytes 208904 | tf_op jit(solution)/shard_map/ppermute | solution.py:508
  70.0 6.3 %collective-permute-start.20 = (bf16[272,128]{1,0:T(8,128)(2,1)S(1)}, bf16[272,128]{1,0:T(8,128)(2,1)S(1)}, u32[]{:S(2)}, u32[]{:S(2)}) collective-permute-start(bf16[272,128]{1,0:T(8,128)(2,1)S(1)} %get-tuple-element.67), channel_id=1, source_target_pairs={{0,24},{1,25},{2,26},{3,27},{4,28},{5,29},{6,30},{7,31},{8,16},{9,... | collective-permute-start | bytes 208904 | tf_op jit(solution)/shard_map/ppermute | solution.py:508
  76.4 6.1 %collective-permute-start.21 = (bf16[272,128]{1,0:T(8,128)(2,1)S(1)}, bf16[272,128]{1,0:T(8,128)(2,1)S(1)}, u32[]{:S(2)}, u32[]{:S(2)}) collective-permute-start(bf16[272,128]{1,0:T(8,128)(2,1)S(1)} %get-tuple-element.60), channel_id=1, source_target_pairs={{0,8},{1,9},{2,10},{3,11},{4,12},{5,13},{6,14},{7,15},{8,0},{9,1},... | collective-permute-start | bytes 208904 | tf_op jit(solution)/shard_map/ppermute | solution.py:508
  77.7 4.8 %collective-permute-start.4 = (bf16[1152,128]{1,0:T(8,128)(2,1)S(1)}, bf16[1152,128]{1,0:T(8,128)(2,1)S(1)}, u32[]{:S(2)}, u32[]{:S(2)}) collective-permute-start(bf16[1152,128]{1,0:T(8,128)(2,1)S(1)} %get-tuple-element.49), channel_id=1, source_target_pairs={{0,1},{1,0},{2,3},{3,2},{4,5},{5,4},{6,7},{7,6},{8,9},{9,8},{10,11... | collective-permute-start | bytes 884744 | tf_op jit(solution)/shard_map/ppermute | solution.py:508
  80.7 4.8 %collective-permute-start.22 = (bf16[272,128]{1,0:T(8,128)(2,1)S(1)}, bf16[272,128]{1,0:T(8,128)(2,1)S(1)}, u32[]{:S(2)}, u32[]{:S(2)}) collective-permute-start(bf16[272,128]{1,0:T(8,128)(2,1)S(1)} %get-tuple-element.60), channel_id=1, source_target_pairs={{0,16},{1,17},{2,18},{3,19},{4,20},{5,21},{6,22},{7,23},{8,24},{9,... | collective-permute-start | bytes 208904 | tf_op jit(solution)/shard_map/ppermute | solution.py:508
  82.0 11.1 %collective-permute-start.23 = (bf16[272,128]{1,0:T(8,128)(2,1)S(1)}, bf16[272,128]{1,0:T(8,128)(2,1)S(1)}, u32[]{:S(2)}, u32[]{:S(2)}) collective-permute-start(bf16[272,128]{1,0:T(8,128)(2,1)S(1)} %get-tuple-element.60), channel_id=1, source_target_pairs={{0,24},{1,25},{2,26},{3,27},{4,28},{5,29},{6,30},{7,31},{8,16},{9,... | collective-permute-start | bytes 208904 | tf_op jit(solution)/shard_map/ppermute | solution.py:508
  82.6 4.2 %collective-permute-start.7 = (bf16[288,128]{1,0:T(8,128)(2,1)S(1)}, bf16[288,128]{1,0:T(8,128)(2,1)S(1)}, u32[]{:S(2)}, u32[]{:S(2)}) collective-permute-start(bf16[288,128]{1,0:T(8,128)(2,1)S(1)} %get-tuple-element.65), channel_id=1, source_target_pairs={{0,6},{1,7},{2,4},{3,5},{4,2},{5,3},{6,0},{7,1},{8,14},{9,15},{10,... | collective-permute-start | bytes 221192 | tf_op jit(solution)/shard_map/ppermute | solution.py:508
  84.1 4.9 %collective-permute-start.6 = (bf16[288,128]{1,0:T(8,128)(2,1)S(1)}, bf16[288,128]{1,0:T(8,128)(2,1)S(1)}, u32[]{:S(2)}, u32[]{:S(2)}) collective-permute-start(bf16[288,128]{1,0:T(8,128)(2,1)S(1)} %get-tuple-element.66), channel_id=1, source_target_pairs={{0,4},{1,5},{2,6},{3,7},{4,0},{5,1},{6,2},{7,3},{8,12},{9,13},{10,... | collective-permute-start | bytes 221192 | tf_op jit(solution)/shard_map/ppermute | solution.py:508
  84.3 4.7 %collective-permute-start.5 = (bf16[288,128]{1,0:T(8,128)(2,1)S(1)}, bf16[288,128]{1,0:T(8,128)(2,1)S(1)}, u32[]{:S(2)}, u32[]{:S(2)}) collective-permute-start(bf16[288,128]{1,0:T(8,128)(2,1)S(1)} %get-tuple-element.64), channel_id=1, source_target_pairs={{0,2},{1,3},{2,0},{3,1},{4,6},{5,7},{6,4},{7,5},{8,10},{9,11},{10,... | collective-permute-start | bytes 221192 | tf_op jit(solution)/shard_map/ppermute | solution.py:508
  89.1 5.9 %collective-permute-start.10 = (bf16[288,128]{1,0:T(8,128)(2,1)S(1)}, bf16[288,128]{1,0:T(8,128)(2,1)S(1)}, u32[]{:S(2)}, u32[]{:S(2)}) collective-permute-start(bf16[288,128]{1,0:T(8,128)(2,1)S(1)} %fusion.5), channel_id=1, source_target_pairs={{0,24},{1,25},{2,26},{3,27},{4,28},{5,29},{6,30},{7,31},{8,16},{9,... | collective-permute-start | bytes 221192 | tf_op jit(solution)/shard_map/ppermute | solution.py:508
  89.6 6.2 %collective-permute-start.9 = (bf16[288,128]{1,0:T(8,128)(2,1)S(1)}, bf16[288,128]{1,0:T(8,128)(2,1)S(1)}, u32[]{:S(2)}, u32[]{:S(2)}) collective-permute-start(bf16[288,128]{1,0:T(8,128)(2,1)S(1)} %fusion.5), channel_id=1, source_target_pairs={{0,16},{1,17},{2,18},{3,19},{4,20},{5,21},{6,22},{7,23},{8,24},{9,... | collective-permute-start | bytes 221192 | tf_op jit(solution)/shard_map/ppermute | solution.py:508
  93.1 3.2 %collective-permute-start.8 = (bf16[288,128]{1,0:T(8,128)(2,1)S(1)}, bf16[288,128]{1,0:T(8,128)(2,1)S(1)}, u32[]{:S(2)}, u32[]{:S(2)}) collective-permute-start(bf16[288,128]{1,0:T(8,128)(2,1)S(1)} %fusion.5), channel_id=1, source_target_pairs={{0,8},{1,9},{2,10},{3,11},{4,12},{5,13},{6,14},{7,15},{8,0},{9,1},... | collective-permute-start | bytes 221192 | tf_op jit(solution)/shard_map/ppermute | solution.py:508
  93.1 5.8 %collective-permute-start.24 = (bf16[1088,128]{1,0:T(8,128)(2,1)S(1)}, bf16[1088,128]{1,0:T(8,128)(2,1)S(1)}, u32[]{:S(2)}, u32[]{:S(2)}) collective-permute-start(bf16[1088,128]{1,0:T(8,128)(2,1)S(1)} %bitcast.57), channel_id=1, source_target_pairs={{0,2},{1,3},{2,0},{3,1},{4,6},{5,7},{6,4},{7,5},{8,10},{9,11},{10,... | collective-permute-start | bytes 835592 | tf_op jit(solution)/shard_map/ppermute | solution.py:508
  94.2 6.6 %collective-permute-start.25 = (bf16[1088,128]{1,0:T(8,128)(2,1)S(1)}, bf16[1088,128]{1,0:T(8,128)(2,1)S(1)}, u32[]{:S(2)}, u32[]{:S(2)}) collective-permute-start(bf16[1088,128]{1,0:T(8,128)(2,1)S(1)} %bitcast.58), channel_id=1, source_target_pairs={{0,4},{1,5},{2,6},{3,7},{4,0},{5,1},{6,2},{7,3},{8,12},{9,13},{10,... | collective-permute-start | bytes 835592 | tf_op jit(solution)/shard_map/ppermute | solution.py:508
  94.9 17.4 %collective-permute-start.26 = (bf16[1088,128]{1,0:T(8,128)(2,1)S(1)}, bf16[1088,128]{1,0:T(8,128)(2,1)S(1)}, u32[]{:S(2)}, u32[]{:S(2)}) collective-permute-start(bf16[1088,128]{1,0:T(8,128)(2,1)S(1)} %bitcast.59), channel_id=1, source_target_pairs={{0,6},{1,7},{2,4},{3,5},{4,2},{5,3},{6,0},{7,1},{8,14},{9,15},{10,... | collective-permute-start | bytes 835592 | tf_op jit(solution)/shard_map/ppermute | solution.py:508
  96.3 14.5 %collective-permute-start.11 = (bf16[288,128]{1,0:T(8,128)(2,1)S(1)}, bf16[288,128]{1,0:T(8,128)(2,1)S(1)}, u32[]{:S(2)}, u32[]{:S(2)}) collective-permute-start(bf16[288,128]{1,0:T(8,128)(2,1)S(1)} %add_convert_fusion.2.refs_0_), channel_id=1, source_target_pairs={{0,2},{1,3},{2,0},{3,1},{4,6},{5,7},{6,4},{7,5},{8,10},{9,11},{10,... | collective-permute-start | bytes 221192 | tf_op jit(solution)/shard_map/ppermute | solution.py:508
  97.4 13.4 %collective-permute-start.12 = (bf16[288,128]{1,0:T(8,128)(2,1)S(1)}, bf16[288,128]{1,0:T(8,128)(2,1)S(1)}, u32[]{:S(2)}, u32[]{:S(2)}) collective-permute-start(bf16[288,128]{1,0:T(8,128)(2,1)S(1)} %add_convert_fusion.2.refs_0_), channel_id=1, source_target_pairs={{0,4},{1,5},{2,6},{3,7},{4,0},{5,1},{6,2},{7,3},{8,12},{9,13},{10,... | collective-permute-start | bytes 221192 | tf_op jit(solution)/shard_map/ppermute | solution.py:508
  98.9 13.5 %collective-permute-start.13 = (bf16[288,128]{1,0:T(8,128)(2,1)S(1)}, bf16[288,128]{1,0:T(8,128)(2,1)S(1)}, u32[]{:S(2)}, u32[]{:S(2)}) collective-permute-start(bf16[288,128]{1,0:T(8,128)(2,1)S(1)} %add_convert_fusion.2.refs_0_), channel_id=1, source_target_pairs={{0,6},{1,7},{2,4},{3,5},{4,2},{5,3},{6,0},{7,1},{8,14},{9,15},{10,... | collective-permute-start | bytes 221192 | tf_op jit(solution)/shard_map/ppermute | solution.py:508
  100.8 12.1 %collective-permute-start.14 = (bf16[288,128]{1,0:T(8,128)(2,1)S(1)}, bf16[288,128]{1,0:T(8,128)(2,1)S(1)}, u32[]{:S(2)}, u32[]{:S(2)}) collective-permute-start(bf16[288,128]{1,0:T(8,128)(2,1)S(1)} %add_convert_fusion.2.refs_0_), channel_id=1, source_target_pairs={{0,1},{1,0},{2,3},{3,2},{4,5},{5,4},{6,7},{7,6},{8,9},{9,8},{10,11... | collective-permute-start | bytes 221192 | tf_op jit(solution)/shard_map/ppermute | solution.py:508
  110.8 2.2 %collective-permute-start.15 = (bf16[288,128]{1,0:T(8,128)(2,1)S(1)}, bf16[288,128]{1,0:T(8,128)(2,1)S(1)}, u32[]{:S(2)}, u32[]{:S(2)}) collective-permute-start(bf16[288,128]{1,0:T(8,128)(2,1)S(1)} %collective-permute-done.11.refs_1_), channel_id=1, source_target_pairs={{0,1},{1,0},{2,3},{3,2},{4,5},{5,4},{6,7},{7,6},{8,9},{9,8},{10,11... | collective-permute-start | bytes 221192 | tf_op jit(solution)/shard_map/ppermute | solution.py:508
  110.8 2.6 %collective-permute-start.16 = (bf16[288,128]{1,0:T(8,128)(2,1)S(1)}, bf16[288,128]{1,0:T(8,128)(2,1)S(1)}, u32[]{:S(2)}, u32[]{:S(2)}) collective-permute-start(bf16[288,128]{1,0:T(8,128)(2,1)S(1)} %collective-permute-done.12.refs_2_), channel_id=1, source_target_pairs={{0,1},{1,0},{2,3},{3,2},{4,5},{5,4},{6,7},{7,6},{8,9},{9,8},{10,11... | collective-permute-start | bytes 221192 | tf_op jit(solution)/shard_map/ppermute | solution.py:508
  112.4 4.6 %collective-permute-start.27 = (bf16[1088,128]{1,0:T(8,128)(2,1)S(1)}, bf16[1088,128]{1,0:T(8,128)(2,1)S(1)}, u32[]{:S(2)}, u32[]{:S(2)}) collective-permute-start(bf16[1088,128]{1,0:T(8,128)(2,1)S(1)} %bitcast.60), channel_id=1, source_target_pairs={{0,1},{1,0},{2,3},{3,2},{4,5},{5,4},{6,7},{7,6},{8,9},{9,8},{10,11... | collective-permute-start | bytes 835592 | tf_op jit(solution)/shard_map/ppermute | solution.py:508
  112.4 4.6 %collective-permute-start.28 = (bf16[1088,128]{1,0:T(8,128)(2,1)S(1)}, bf16[1088,128]{1,0:T(8,128)(2,1)S(1)}, u32[]{:S(2)}, u32[]{:S(2)}) collective-permute-start(bf16[1088,128]{1,0:T(8,128)(2,1)S(1)} %collective-permute-done.24.refs_1_), channel_id=1, source_target_pairs={{0,1},{1,0},{2,3},{3,2},{4,5},{5,4},{6,7},{7,6},{8,9},{9,8},{10,11... | collective-permute-start | bytes 835592 | tf_op jit(solution)/shard_map/ppermute | solution.py:508
  112.9 4.0 %collective-permute-start.29 = (bf16[1088,128]{1,0:T(8,128)(2,1)S(1)}, bf16[1088,128]{1,0:T(8,128)(2,1)S(1)}, u32[]{:S(2)}, u32[]{:S(2)}) collective-permute-start(bf16[1088,128]{1,0:T(8,128)(2,1)S(1)} %collective-permute-done.25.refs_2_), channel_id=1, source_target_pairs={{0,1},{1,0},{2,3},{3,2},{4,5},{5,4},{6,7},{7,6},{8,9},{9,8},{10,11... | collective-permute-start | bytes 835592 | tf_op jit(solution)/shard_map/ppermute | solution.py:508
  112.9 4.0 %collective-permute-start.30 = (bf16[1088,128]{1,0:T(8,128)(2,1)S(1)}, bf16[1088,128]{1,0:T(8,128)(2,1)S(1)}, u32[]{:S(2)}, u32[]{:S(2)}) collective-permute-start(bf16[1088,128]{1,0:T(8,128)(2,1)S(1)} %collective-permute-done.26.refs_3_), channel_id=1, source_target_pairs={{0,1},{1,0},{2,3},{3,2},{4,5},{5,4},{6,7},{7,6},{8,9},{9,8},{10,11... | collective-permute-start | bytes 835592 | tf_op jit(solution)/shard_map/ppermute | solution.py:508
  113.4 1.8 %collective-permute-start.17 = (bf16[288,128]{1,0:T(8,128)(2,1)S(1)}, bf16[288,128]{1,0:T(8,128)(2,1)S(1)}, u32[]{:S(2)}, u32[]{:S(2)}) collective-permute-start(bf16[288,128]{1,0:T(8,128)(2,1)S(1)} %collective-permute-done.13.refs_3_), channel_id=1, source_target_pairs={{0,1},{1,0},{2,3},{3,2},{4,5},{5,4},{6,7},{7,6},{8,9},{9,8},{10,11... | collective-permute-start | bytes 221192 | tf_op jit(solution)/shard_map/ppermute | solution.py:508

commit v4 on v2

--- a/solution.py
+++ b/solution.py
@@ -10,9 +10,10 @@
 KERNEL = 8
 HEADS = 8
 NORM_EPS = 1e-06
-WIN_STEP = 4
+WIN_STEP = 8
+SLOPE_PIECES = 4
 LANES = 128
-VMEM_LIMIT = 56 * 2**20
+VMEM_LIMIT = 28 * 2**20
 
 f32 = jnp.float32
 bf16 = jnp.bfloat16
@@ -44,6 +45,14 @@
     return jnp.where(mask, 1.0, 0.0).astype(bf16)
 
 
+def onehot(codes, values):
+    return jnp.where(codes == values, jnp.ones((), bf16), jnp.zeros((), bf16))
+
+
+def small_iota(shape, dim):
+    return iota(shape, dim).astype(f32).astype(bf16)
+
+
 def spread(row, lanes):
     return jnp.broadcast_to(row.astype(f32), (lanes, row.shape[1])).T
 
@@ -57,7 +66,7 @@
 
 
 def embed_kernel(
-    capacity, bytes_ref, owner_ref, sess_ref, table_ref, w_ref, out_ref, slope_ref, pair_ref, emb_ref
+    capacity, bytes_ref, owner_ref, sess_ref, table_ref, w_ref, out_ref, slope_ref, codes_ref, pair_ref, emb_ref, turned_ref
 ):
     step = pl.program_id(0)
     packets, length = bytes_ref.shape
@@ -72,17 +81,21 @@
         pair_ref[0:vocab, 0:chan] = table
         pair_ref[vocab : 2 * vocab, chan : 2 * chan] = table
         emb_ref[...] = jnp.zeros_like(emb_ref)
+        turned_ref[...] = bytes_ref[...].astype(f32).T
+        for j in range(KERNEL):
+            codes_ref[j] = turned_ref[pl.ds(j, positions, stride=KERNEL), :].astype(bf16)
 
     here = WIN_STEP * KERNEL
     codes = pltpu.roll(bytes_ref[...], lax.rem(length - here * step, length), 1)[:, :here]
-    values = iota((packets, vocab), 1)
+    codes = codes.astype(f32).astype(bf16)
+    values = small_iota((packets, vocab), 1)
     pairs = []
     for k in range(KERNEL // 2):
         rows = []
         for w in range(WIN_STEP):
             j = w * KERNEL + 2 * k
             rows.append(
-                jnp.concatenate([flag(codes[:, j : j + 1] == values), flag(codes[:, j + 1 : j + 2] == values)], axis=1)
+                jnp.concatenate([onehot(codes[:, j : j + 1], values), onehot(codes[:, j + 1 : j + 2], values)], axis=1)
             )
         pairs.append(dot_nn(jnp.concatenate(rows, axis=0), pair_ref[...]).astype(bf16))
     windows = jnp.concatenate(pairs, axis=1)
@@ -122,13 +135,19 @@
         out_specs=[
             pl.BlockSpec((slots, width + LANES), lambda i: (0, 0)),
             pl.BlockSpec((rows, width), lambda i: (i, 0)),
+            pl.BlockSpec((KERNEL, length // KERNEL, packets), lambda i: (0, 0, 0)),
         ],
         out_shape=[
             jax.ShapeDtypeStruct((slots, width + LANES), bf16),
             jax.ShapeDtypeStruct((steps * rows, width), bf16),
+            jax.ShapeDtypeStruct((KERNEL, length // KERNEL, packets), bf16),
         ],
-        scratch_shapes=[pltpu.VMEM((2 * vocab, 2 * chan), bf16), pltpu.VMEM((packets, width), f32)],
-        compiler_params=pltpu.CompilerParams(vmem_limit_bytes=VMEM_LIMIT),
+        scratch_shapes=[
+            pltpu.VMEM((2 * vocab, 2 * chan), bf16),
+            pltpu.VMEM((packets, width), f32),
+            pltpu.VMEM((length, packets), f32),
+        ],
+        compiler_params=pltpu.CompilerParams(vmem_limit_bytes=2 * VMEM_LIMIT),
         cost_estimate=cost(1e10, 5e6),
         name="embed",
     )(*args)
@@ -282,6 +301,17 @@
     )(*args)
 
 
+def add_by_value(codes_ref, dconv_ref, table_ref, w_rows, table_grad_ref):
+    packets = codes_ref.shape[2]
+    vocab = table_ref.shape[1]
+    values = small_iota((vocab, packets), 0)
+    codes = codes_ref[0]
+    chosen = [onehot(codes[w : w + 1, :], values) for w in range(codes_ref.shape[1])]
+    by_value = dot_nn(jnp.concatenate(chosen, axis=1), dconv_ref[...]).astype(bf16)
+    table_grad_ref[...] += dot_nt(w_rows, by_value)
+    return dot_nn(table_ref[...], by_value).astype(bf16)
+
+
 def conv_back_kernel(
     capacity,
     core_ref,
@@ -295,57 +325,65 @@
     keep_ref,
     send_ref,
     dconv_ref,
+    held_ref,
+    rows_ref,
     table_grad_ref,
     halves_ref,
+    sem_ref,
 ):
     j = pl.program_id(0)
     slots, width = ret_ref.shape
     packets = owner_ref.shape[1]
     chan, vocab = table_ref.shape
-    positions = codes_ref.shape[1]
+    window = w_ref.shape[0]
+    piece = slope_ref.shape[0] // SLOPE_PIECES
 
     @pl.when(j == 0)
     def _():
+        copies = []
+        for i in range(SLOPE_PIECES):
+            at = pl.ds(i * piece, piece)
+            copies.append(pltpu.make_async_copy(slope_ref.at[at, :], held_ref.at[at, :], sem_ref.at[i]))
+            copies[i].start()
         own_row = owner_ref[...]
         own_col = column(own_row)
         same = (own_col == own_row) & (iota((packets, packets), 1) < iota((packets, packets), 0))
         rank = jnp.sum(jnp.where(same, 1.0, 0.0), axis=1, keepdims=True).astype(jnp.int32)
         place = flag(iota((packets, slots), 1) == own_col * capacity + rank)
         demb = dot_nn(place, ret_ref[...])
-        for w in range(positions):
-            at = slice(w * packets, (w + 1) * packets)
-            dconv_ref[at, :] = (demb * slope_ref[at, :].astype(f32)).astype(bf16)
+        halves_ref[...] = jnp.zeros_like(halves_ref)
         table_grad_ref[...] = jnp.zeros_like(table_grad_ref)
-        halves_ref[...] = jnp.zeros_like(halves_ref)
-
-    values = iota((vocab, packets), 0)
-    onehot = jnp.concatenate([flag(codes_ref[0, w : w + 1, :] == values) for w in range(positions)], axis=1)
-    by_value = dot_nn(onehot, dconv_ref[...]).astype(bf16)
-    w_rows = w_ref[pl.ds(pl.multiple_of(j * chan, chan), chan), :]
-    table_grad_ref[...] += dot_nt(w_rows, by_value)
-    grad_rows = dot_nn(table_ref[...], by_value).astype(bf16)
-    window = KERNEL * chan
-    wide = width // (2 * LANES)
-    for half in range(2):
-        for s in range(wide):
-            at = pl.multiple_of(s * window + j * chan, chan)
-            slab = half * wide + s
-            halves_ref[half, pl.ds(at, chan), :] = grad_rows[:, slab * LANES : (slab + 1) * LANES]
+        for i in range(SLOPE_PIECES):
+            copies[i].wait()
+            for first in range(i * piece, (i + 1) * piece, packets):
+                at = slice(first, first + packets)
+                dconv_ref[at, :] = (demb * held_ref[at, :].astype(f32)).astype(bf16)
+
+    at = pl.ds(pl.multiple_of(j * chan, chan), chan)
+    rows_ref[at, :] = add_by_value(codes_ref, dconv_ref, table_ref, w_ref[at, :], table_grad_ref)
 
     @pl.when(j == pl.num_programs(0) - 1)
     def _():
-        at = wide * window
+        wide = width // (2 * LANES)
         for half in range(2):
+            for s in range(wide):
+                slab = half * wide + s
+                halves_ref[half, s * window : (s + 1) * window, :] = rows_ref[:, slab * LANES : (slab + 1) * LANES]
+            end = wide * window
             table_part = table_grad_ref[:, half * vocab // 2 : (half + 1) * vocab // 2]
-            halves_ref[half, at : at + chan, :] = table_part.astype(bf16)
-        halves_ref[0, at + chan : at + chan + 16, :] = gain_grad_ref[...].astype(bf16)
+            halves_ref[half, end : end + chan, :] = table_part.astype(bf16)
+        halves_ref[0, end + chan : end + chan + 16, :] = gain_grad_ref[...].astype(bf16)
         share_out(core_ref, halves_ref, keep_ref, send_ref)
 
 
+def whole(a):
+    return pl.BlockSpec(a.shape, lambda j: (0,) * len(a.shape))
+
+
 def conv_back(core, returned, owner, codes, slope, table_t, w_conv, gain_grad, capacity, half_rows):
-    whole = lambda a: pl.BlockSpec(a.shape, lambda j: (0, 0))
     args = (returned, owner, codes, slope, table_t, w_conv, gain_grad)
     specs = [whole(a) if a.ndim == 2 else pl.BlockSpec((1, *a.shape[1:]), lambda j: (j, 0, 0)) for a in args]
+    specs[3] = pl.BlockSpec(memory_space=pl.ANY)
     half = jax.ShapeDtypeStruct((half_rows, LANES), bf16)
     return pl.pallas_call(
         functools.partial(conv_back_kernel, capacity),
@@ -355,23 +393,30 @@
         out_shape=[half, half],
         scratch_shapes=[
             pltpu.VMEM(slope.shape, bf16),
+            pltpu.VMEM(slope.shape, bf16),
+            pltpu.VMEM(w_conv.shape, bf16),
             pltpu.VMEM(table_t.shape, f32),
             pltpu.VMEM((2, half_rows, LANES), bf16),
+            pltpu.SemaphoreType.DMA((SLOPE_PIECES,)),
         ],
-        compiler_params=pltpu.CompilerParams(vmem_limit_bytes=VMEM_LIMIT),
-        cost_estimate=cost(1e10, 5e6),
+        compiler_params=pltpu.CompilerParams(vmem_limit_bytes=28 * 2**20),
+        cost_estimate=cost(1e9, 1e6),
         name="conv_back",
     )(core, *args)
 
 
 def put_together(place_ref, piece_refs, halves_ref):
     mine, k = place_ref[0], place_ref[1]
-    rows = piece_refs[0].shape[0]
-    count = len(piece_refs) // 2
-    for i, ref in enumerate(piece_refs):
-        half = mine if i < count else 1 - mine
-        at = pl.multiple_of((k ^ (i % count)) * rows, 16)
-        halves_ref[half, pl.ds(at, rows), :] = ref[...]
+    count = 4
+    rows = halves_ref.shape[1] // count
+    for d in range(count):
+        at = pl.multiple_of((k ^ d) * rows, 16)
+        if len(piece_refs) == count:
+            own, other = piece_refs[d][0:rows, :], piece_refs[d][rows : 2 * rows, :]
+        else:
+            own, other = piece_refs[d][...], piece_refs[count + d][...]
+        halves_ref[mine, pl.ds(at, rows), :] = own
+        halves_ref[1 - mine, pl.ds(at, rows), :] = other
 
 
 def early_out_kernel(place_ref, *refs):
@@ -410,7 +455,7 @@
 
 def assemble(kernel, place, pieces, shapes, name):
     vmem = pl.BlockSpec(memory_space=pltpu.VMEM)
-    rows = len(pieces) // 2 * pieces[0].shape[0]
+    rows = sum(p.shape[0] for p in pieces) // 2
     return pl.pallas_call(
         kernel,
         in_specs=[pl.BlockSpec(memory_space=pltpu.SMEM)] + [vmem] * len(pieces),
@@ -445,27 +490,31 @@
         stride, size = level
         return lax.ppermute(value, AXES, [(i, i + ((i // stride % size ^ d) - i // stride % size) * stride) for i in range(self.count)])
 
-    def scatter_sum(self, value, level):
+    def scatter_sum(self, value, level, other=None):
         size = level[1]
         value = value.reshape(size, value.shape[0] // size, value.shape[1])
         mine = self.place(level)
         got = [self.swap(lax.dynamic_index_in_dim(value, mine ^ d, 0, keepdims=False), level, d) for d in range(1, size)]
+        if other is not None:
+            got = after(got, other)
         total = lax.dynamic_index_in_dim(value, mine, 0, keepdims=False).astype(f32)
         for g in got:
             total = total + g.astype(f32)
         return total.astype(bf16)
 
-    def gather(self, value, level):
+    def gather(self, value, level, other=None):
         size = level[1]
         mine = self.place(level)
         got = [self.swap(value, level, d) for d in range(1, size)]
+        if other is not None:
+            got = after(got, other)
         out = jnp.zeros((size, *value.shape), value.dtype)
         for d, g in enumerate([value, *got]):
             out = lax.dynamic_update_index_in_dim(out, g, mine ^ d, 0)
         return out.reshape(size * value.shape[0], value.shape[1])
 
-    def exchange_sum(self, value, level):
-        terms = [value] + [self.swap(value, level, d) for d in range(1, level[1])]
+    def exchange_sum(self, value, level, other):
+        terms = [value] + after([self.swap(value, level, d) for d in range(1, level[1])], other)
         terms = [t.astype(f32) for t in terms]
         while len(terms) > 1:
             terms = [a + b for a, b in zip(terms[::2], terms[1::2], strict=True)]
@@ -474,10 +523,21 @@
     def pair_sum(self, keep, send):
         return (keep.astype(f32) + self.swap(send, self.levels[0], 1).astype(f32)).astype(bf16)
 
-    def pieces(self, value):
+    def join(self, value):
+        return jnp.concatenate([value, self.swap(value, self.levels[0], 1)], axis=0)
+
+    def joint_pieces(self, both):
         quad = self.levels[1]
-        own = [value] + [self.swap(value, quad, d) for d in range(1, quad[1])]
+        return [both] + [self.swap(both, quad, d) for d in range(1, quad[1])]
+
+    def pieces(self, value, other):
+        quad = self.levels[1]
+        own = [value] + after([self.swap(value, quad, d) for d in range(1, quad[1])], other)
         return own + [self.swap(p, self.levels[0], 1) for p in own]
+
+
+def after(value, other):
+    return lax.optimization_barrier((value, other))[0]
 
 
 def body(packet_bytes, owner_index, session_id, class_label, byte_table, w_conv, norm_gain, w_project, w_out, w_head):
@@ -486,18 +546,16 @@
     packets, length = packet_bytes.shape
     slots = 2 * packets
     capacity = slots // groups
-    positions = length // KERNEL
     width = w_conv.shape[1]
     window = w_conv.shape[0]
     vocab, chan = byte_table.shape
-    classes = w_head.shape[1]
     sessions = class_label.shape[0]
     core = devices.place(devices.levels[0]).reshape(1)
     place = jnp.stack([devices.place(level) for level in devices.levels[:2]])
 
     owner = owner_index.reshape(1, packets)
     table_t = byte_table.T
-    outgoing, slope = embed(packet_bytes, owner, session_id.reshape(1, packets), table_t, w_conv, capacity, slots)
+    outgoing, slope, codes = embed(packet_bytes, owner, session_id.reshape(1, packets), table_t, w_conv, capacity, slots)
 
     def exchange(rows):
         return lax.all_to_all(
@@ -515,28 +573,28 @@
         sessions,
     )
     early = devices.pair_sum(keep, send)
-    codes = packet_bytes.reshape(packets, positions, KERNEL).transpose(2, 1, 0)
     used = window * width // (2 * LANES) + chan * vocab // (2 * LANES) + 16
     unit = 64
     half_rows = -(-used // unit) * unit
-    returned, early = lax.optimization_barrier((exchange(back), early))
+    _, quad, *upper = devices.levels
     keep, send = conv_back(
-        core, returned, owner, codes, slope, table_t, w_conv, gain_grad, capacity, half_rows
+        core, after(exchange(back), early), owner, codes, slope, table_t, w_conv, gain_grad, capacity, half_rows
     )
-    _, quad, *upper = devices.levels
-    early = devices.scatter_sum(early, quad)
+    early = devices.scatter_sum(early, quad, keep)
+    late = devices.pair_sum(keep, send)
     for level in upper:
-        early = devices.scatter_sum(early, level)
+        early = devices.scatter_sum(early, level, late)
+    late = devices.scatter_sum(late, quad, early)
     for level in upper[::-1]:
         early = devices.gather(early, level)
-    late = devices.scatter_sum(devices.pair_sum(keep, send), quad)
     for level in upper:
-        late = devices.exchange_sum(late, level)
+        late = devices.exchange_sum(late, level, early)
+    late = devices.join(late)
     grad_project, grad_out, grad_head = assemble(
-        early_out_kernel, place, devices.pieces(early), [w_project.shape, w_out.shape, w_head.shape], "early_out"
+        early_out_kernel, place, devices.pieces(early, late), [w_project.shape, w_out.shape, w_head.shape], "early_out"
     )
     grad_conv, table_grad, gain_grad = assemble(
-        late_out_kernel, place, devices.pieces(late), [w_conv.shape, table_t.shape, (1, width)], "late_out"
+        late_out_kernel, after(place, grad_head), devices.joint_pieces(late), [w_conv.shape, table_t.shape, (1, width)], "late_out"
     )
     return (logits, table_grad.T, grad_conv, gain_grad.reshape(width), grad_project, grad_out, grad_head)
 

time: 136 us -> 117 us (0.86)
  Pallas kernels: 50.1 us -> 40.6 us
  starting transfers between devices: 48.7 us -> 43.1 us
  waiting for transfers between devices: 29.7 us -> 25.4 us
    all_to_all x2, waiting for transfers between devices: 13.9 us -> 8.96 us  [exchange(): lax.all_to_all(rows.reshape(groups, capacity, rows.shape[1]), 'dp', split...]
    ppermute x31 -> x28, starting transfers between devices: 38.2 us -> 33.3 us  [swap(): lax.ppermute(value, AXES, [(i, i + ((i // stride % size ^ d) - i // strid...]
    pallas_call x1, Pallas kernels: 16.6 us -> 13.3 us  [conv_back(): pl.pallas_call(functools.partial(conv_back_kernel, capacity), grid=(KERNE...]
    pallas_call x1, Pallas kernels: 15.1 us -> 12.6 us  [embed(): pl.pallas_call(functools.partial(embed_kernel, capacity), grid=(steps,),...]
    pallas_call x1, Pallas kernels: 12 us -> 10.1 us  [session_layer(): pl.pallas_call(session_kernel, in_specs=[pl.BlockSpec(memory_space=pltpu....]
    pallas_call x2, Pallas kernels: 6.29 us -> 4.68 us  [assemble(): pl.pallas_call(kernel, in_specs=[pl.BlockSpec(memory_space=pltpu.SMEM)] +...]
    ppermute x31 -> x28, waiting for transfers between devices: 15.8 us -> 16.4 us  [swap(): lax.ppermute(value, AXES, [(i, i + ((i // stride % size ^ d) - i // strid...]
    unnamed x43 -> x20, local copies, waits for them, and re-layouts: 3.04 us -> 3.12 us
  transfers between devices with their start and end apart: 33 -> 30, of which waited for: 9 -> 10; matrix products, arithmetic and copies ran while one was open for 2% -> 3% of each run, Pallas kernels for 14% -> 14%
where the time goes in v4:
time: 117 us; the launch traced here: 116 us
  starting transfers between devices  43.1 us (37%)
  Pallas kernels  40.6 us (35%)
  waiting for transfers between devices  25.4 us (22%)
  local copies, waits for them, and re-layouts  4.19 us (4%)
  other arithmetic  2.01 us (2%)
    ppermute x28, starting transfers between devices, swap(): lax.ppermute(value, AXES, [(i, i + ((i // stride % size ^ d) - i // strid...  33.3 us
    ppermute x28, waiting for transfers between devices, swap(): lax.ppermute(value, AXES, [(i, i + ((i // stride % size ^ d) - i // strid...  16.4 us
    pallas_call x1, Pallas kernels, conv_back(): pl.pallas_call(functools.partial(conv_back_kernel, capacity), grid=(KERNE...  13.3 us
    pallas_call x1, Pallas kernels, embed(): pl.pallas_call(functools.partial(embed_kernel, capacity), grid=(steps,),...  12.6 us
    pallas_call x1, Pallas kernels, session_layer(): pl.pallas_call(session_kernel, in_specs=[pl.BlockSpec(memory_space=pltpu....  10.1 us
    all_to_all x2, starting transfers between devices, exchange(): lax.all_to_all(rows.reshape(groups, capacity, rows.shape[1]), 'dp', split...  9.81 us
    all_to_all x2, waiting for transfers between devices, exchange(): lax.all_to_all(rows.reshape(groups, capacity, rows.shape[1]), 'dp', split...  8.96 us
    pallas_call x2, Pallas kernels, assemble(): pl.pallas_call(kernel, in_specs=[pl.BlockSpec(memory_space=pltpu.SMEM)] +...  4.68 us
  transfers between devices with their start and end apart: 30, of which 10 were waited for; matrix products, arithmetic and copies ran while one was open for 3% of the time, Pallas kernels for 14%

profile of v4, /device:TPU:11, one launch (start us, length us, event | category | flops | bytes accessed | tf_op | source)
XLA Modules:
  0.0 116.1 jit_solution(2984176745869831157)
XLA Ops:
  0.7 12.6 %embed.1 = (bf16[256,640]{1,0:T(8,128)(2,1)}, bf16[4096,512]{1,0:T(8,128)(2,1)}, bf16[8,32,128]{2,1,0:T(8,128)(2,1)}) custom-call(s32[128,256]{1,0:T(8,128)} %bytes_ref.1, s32[1,128]{1,0:T(1,128)} %bitcast.61, s32[1,128]{1,0:T(1,128)} %bitcast.71, bf16[64,256]{1,0:T(8,128)(2,1)} %bitcast.59, bf16[512,512]{1,0:T(8,128)(2,1)} %w_ref.3), custom_call_target="tpu_custom_call" | custom-call | flops 10000000000 | bytes 5000000 | tf_op jit(solution)/shard_map/embed/pallas_call | solution.py:131
  13.2 5.7 %all-to-all-start = ((bf16[8,32,640]{2,1,0:T(8,128)(2,1)}), bf16[8,32,640]{2,1,0:T(8,128)(2,1)S(1)}, u32[]{:S(2)}, u32[]{:S(2)}) async-start(bf16[8,32,640]{2,1,0:T(8,128)(2,1)} %bitcast.70), calls=%async_computation | async-start | bytes 655360 | tf_op jit(solution)/shard_map/all_to_all | solution.py:561
  19.0 7.3 %all-to-all-done = bf16[8,32,640]{2,1,0:T(8,128)(2,1)S(1)} async-done(((bf16[8,32,640]{2,1,0:T(8,128)(2,1)}), bf16[8,32,640]{2,1,0:T(8,128)(2,1)S(1)}, u32[]{:S(2)}, u32[]{:S(2)}) %all-to-all-start) | async-done | bytes 327712 | tf_op jit(solution)/shard_map/all_to_all | solution.py:561
  26.3 0.9 copy-done.7
  27.2 10.1 %session_layer.1 = (f32[16,128]{1,0:T(8,128)}, bf16[256,512]{1,0:T(8,128)(2,1)}, bf16[4352,128]{1,0:T(8,128)(2,1)S(1)}, bf16[4352,128]{1,0:T(8,128)(2,1)}, f32[16,128]{1,0:T(8,128)S(1)}) custom-call(s32[1]{0:T(128)} %bitcast.core_ref, bf16[256,640]{1,0:T(8,128)(2,1)S(1)} %bitcast.53, s32[1,16]{1,0:T(1,128)S(1)} %bitcast.63, ...), custom_call_target="tpu_custom_call" | custom-call | flops 10000000000 | bytes 5000000 | tf_op jit(solution)/shard_map/session_layer/pallas_call | solution.py:280
  37.3 3.2 %collective-permute-start = (bf16[4352,128]{1,0:T(8,128)(2,1)}, bf16[4352,128]{1,0:T(8,128)(2,1)}, u32[]{:S(2)}, u32[]{:S(2)}) collective-permute-start(bf16[4352,128]{1,0:T(8,128)(2,1)} %get-tuple-element.43), channel_id=1, source_target_pairs={{0,1},{1,0},{2,3},{3,2},{4,5},{5,4},{6,7},{7,6},{8,9},{9,8},{10,11... | collective-permute-start | bytes 3342344 | tf_op jit(solution)/shard_map/ppermute | solution.py:491
  40.5 4.1 %all-to-all-start.1 = ((bf16[8,32,512]{2,1,0:T(8,128)(2,1)}), bf16[8,32,512]{2,1,0:T(8,128)(2,1)S(1)}, u32[]{:S(2)}, u32[]{:S(2)}) async-start(bf16[8,32,512]{2,1,0:T(8,128)(2,1)} %bitcast.13), calls=%async_computation.1 | async-start | bytes 524288 | tf_op jit(solution)/shard_map/all_to_all | solution.py:561
  44.6 1.5 %add_convert_fusion = bf16[4352,128]{1,0:T(8,128)(2,1)S(1)} fusion(bf16[4352,128]{1,0:T(8,128)(2,1)} %collective-permute-done, bf16[4352,128]{1,0:T(8,128)(2,1)S(1)} %get-tuple-element.42), kind=kLoop, calls=%fused_computation | loop fusion | flops 2228224 | bytes 3342336 | tf_op jit(solution)/shard_map/convert_element_type | solution.py:524
  46.1 0.9 dynamic-slice_bitcast_fusion
  47.1 0.3 collective-permute-start.1
  47.3 1.2 %collective-permute-start.2 = (bf16[1088,128]{1,0:T(8,128)(2,1)}, bf16[1088,128]{1,0:T(8,128)(2,1)S(1)}, u32[]{:S(2)}, u32[]{:S(2)}) collective-permute-start(bf16[1088,128]{1,0:T(8,128)(2,1)} %get-tuple-element.76), channel_id=1, source_target_pairs={{0,4},{1,5},{2,6},{3,7},{4,0},{5,1},{6,2},{7,3},{8,12},{9,13},{10,... | collective-permute-start | bytes 835592 | tf_op jit(solution)/shard_map/ppermute | solution.py:491
  48.5 1.2 %collective-permute-start.3 = (bf16[1088,128]{1,0:T(8,128)(2,1)}, bf16[1088,128]{1,0:T(8,128)(2,1)S(1)}, u32[]{:S(2)}, u32[]{:S(2)}) collective-permute-start(bf16[1088,128]{1,0:T(8,128)(2,1)} %get-tuple-element.75), channel_id=1, source_target_pairs={{0,6},{1,7},{2,4},{3,5},{4,2},{5,3},{6,0},{7,1},{8,14},{9,15},{10,... | collective-permute-start | bytes 835592 | tf_op jit(solution)/shard_map/ppermute | solution.py:491
  49.7 1.6 %all-to-all-done.1 = bf16[8,32,512]{2,1,0:T(8,128)(2,1)S(1)} async-done(((bf16[8,32,512]{2,1,0:T(8,128)(2,1)}), bf16[8,32,512]{2,1,0:T(8,128)(2,1)S(1)}, u32[]{:S(2)}, u32[]{:S(2)}) %all-to-all-start.1) | async-done | bytes 262176 | tf_op jit(solution)/shard_map/all_to_all | solution.py:561
  51.4 2.2 %copy-done = bf16[4096,512]{1,0:T(8,128)(2,1)S(1)} copy-done((bf16[4096,512]{1,0:T(8,128)(2,1)S(1)}, bf16[4096,512]{1,0:T(8,128)(2,1)}, u32[]{:S(2)}) %copy-start) | copy-done | bytes 4194328
  53.6 13.3 %conv_back.1 = (bf16[1152,128]{1,0:T(8,128)(2,1)S(1)}, bf16[1152,128]{1,0:T(8,128)(2,1)S(1)}) custom-call(s32[1]{0:T(128)} %bitcast.core_ref, bf16[256,512]{1,0:T(8,128)(2,1)S(1)} %bitcast.52, s32[1,128]{1,0:T(1,128)S(1)} %bitcast.62, bf16[8,32,128]{2,1,0:T(8,128)(2,1)S(1)} %copy-done.2, bf16[4096,512]{1,0:T(8,128)(2,1)S(1)} %copy-done, ...), custom_call_target="tpu_custom_call" | custom-call | flops 1000000000 | bytes 1000000 | tf_op jit(solution)/shard_map/conv_back/pallas_call | solution.py:388
  66.9 2.6 %collective-permute-start.7 = (bf16[1152,128]{1,0:T(8,128)(2,1)S(1)}, bf16[1152,128]{1,0:T(8,128)(2,1)S(1)}, u32[]{:S(2)}, u32[]{:S(2)}) collective-permute-start(bf16[1152,128]{1,0:T(8,128)(2,1)S(1)} %get-tuple-element.53), channel_id=1, source_target_pairs={{0,1},{1,0},{2,3},{3,2},{4,5},{5,4},{6,7},{7,6},{8,9},{9,8},{10,11... | collective-permute-start | bytes 884744 | tf_op jit(solution)/shard_map/ppermute | solution.py:491
  69.5 0.2 fusion.2
  69.7 0.8 collective-permute-start.4
  70.4 0.4 collective-permute-start.5
  70.8 1.6 %collective-permute-start.6 = (bf16[272,128]{1,0:T(8,128)(2,1)S(1)}, bf16[272,128]{1,0:T(8,128)(2,1)S(1)}, u32[]{:S(2)}, u32[]{:S(2)}) collective-permute-start(bf16[272,128]{1,0:T(8,128)(2,1)S(1)} %get-tuple-element.81), channel_id=1, source_target_pairs={{0,24},{1,25},{2,26},{3,27},{4,28},{5,29},{6,30},{7,31},{8,16},{9,... | collective-permute-start | bytes 208904 | tf_op jit(solution)/shard_map/ppermute | solution.py:491
  72.4 0.1 add_convert_fusion.1
  72.5 0.3 collective-permute-start.14
  72.8 0.3 collective-permute-start.15
  73.1 0.4 collective-permute-done.4
  73.5 1.7 %collective-permute-start.16 = (bf16[288,128]{1,0:T(8,128)(2,1)S(1)}, bf16[288,128]{1,0:T(8,128)(2,1)S(1)}, u32[]{:S(2)}, u32[]{:S(2)}) collective-permute-start(bf16[288,128]{1,0:T(8,128)(2,1)S(1)} %get-tuple-element.78), channel_id=1, source_target_pairs={{0,6},{1,7},{2,4},{3,5},{4,2},{5,3},{6,0},{7,1},{8,14},{9,15},{10,... | collective-permute-start | bytes 221192 | tf_op jit(solution)/shard_map/ppermute | solution.py:491
  75.2 3.9 %collective-permute-done.6 = bf16[272,128]{1,0:T(8,128)(2,1)S(1)} collective-permute-done((bf16[272,128]{1,0:T(8,128)(2,1)S(1)}, bf16[272,128]{1,0:T(8,128)(2,1)S(1)}, u32[]{:S(2)}, u32[]{:S(2)}) %collective-permute-start.6) | collective-permute-done | bytes 69664 | tf_op jit(solution)/shard_map/ppermute | solution.py:491
  79.3 1.4 %collective-permute-start.9 = (bf16[272,128]{1,0:T(8,128)(2,1)S(1)}, bf16[272,128]{1,0:T(8,128)(2,1)S(1)}, u32[]{:S(2)}, u32[]{:S(2)}) collective-permute-start(bf16[272,128]{1,0:T(8,128)(2,1)S(1)} %get-tuple-element.74), channel_id=1, source_target_pairs={{0,16},{1,17},{2,18},{3,19},{4,20},{5,21},{6,22},{7,23},{8,24},{9,... | collective-permute-start | bytes 208904 | tf_op jit(solution)/shard_map/ppermute | solution.py:491
  80.7 1.3 %collective-permute-start.10 = (bf16[272,128]{1,0:T(8,128)(2,1)S(1)}, bf16[272,128]{1,0:T(8,128)(2,1)S(1)}, u32[]{:S(2)}, u32[]{:S(2)}) collective-permute-start(bf16[272,128]{1,0:T(8,128)(2,1)S(1)} %get-tuple-element.74), channel_id=1, source_target_pairs={{0,24},{1,25},{2,26},{3,27},{4,28},{5,29},{6,30},{7,31},{8,16},{9,... | collective-permute-start | bytes 208904 | tf_op jit(solution)/shard_map/ppermute | solution.py:491
  82.0 1.0 collective-permute-start.17
  83.0 0.4 collective-permute-start.18
  83.4 1.3 %collective-permute-start.19 = (bf16[288,128]{1,0:T(8,128)(2,1)S(1)}, bf16[288,128]{1,0:T(8,128)(2,1)S(1)}, u32[]{:S(2)}, u32[]{:S(2)}) collective-permute-start(bf16[288,128]{1,0:T(8,128)(2,1)S(1)} %fusion.5), channel_id=1, source_target_pairs={{0,24},{1,25},{2,26},{3,27},{4,28},{5,29},{6,30},{7,31},{8,16},{9,... | collective-permute-start | bytes 221192 | tf_op jit(solution)/shard_map/ppermute | solution.py:491
  84.7 4.5 %collective-permute-done.10 = bf16[272,128]{1,0:T(8,128)(2,1)S(1)} collective-permute-done((bf16[272,128]{1,0:T(8,128)(2,1)S(1)}, bf16[272,128]{1,0:T(8,128)(2,1)S(1)}, u32[]{:S(2)}, u32[]{:S(2)}) %collective-permute-start.10) | collective-permute-done | bytes 69664 | tf_op jit(solution)/shard_map/ppermute | solution.py:491
  89.2 0.1 collective-permute-start.11
  89.3 0.4 collective-permute-start.12
  89.7 2.2 %collective-permute-start.13 = (bf16[1088,128]{1,0:T(8,128)(2,1)S(1)}, bf16[1088,128]{1,0:T(8,128)(2,1)S(1)}, u32[]{:S(2)}, u32[]{:S(2)}) collective-permute-start(bf16[1088,128]{1,0:T(8,128)(2,1)S(1)} %bitcast.56), channel_id=1, source_target_pairs={{0,6},{1,7},{2,4},{3,5},{4,2},{5,3},{6,0},{7,1},{8,14},{9,15},{10,... | collective-permute-start | bytes 835592 | tf_op jit(solution)/shard_map/ppermute | solution.py:491
  92.0 2.3 %collective-permute-done.19 = bf16[288,128]{1,0:T(8,128)(2,1)S(1)} collective-permute-done((bf16[288,128]{1,0:T(8,128)(2,1)S(1)}, bf16[288,128]{1,0:T(8,128)(2,1)S(1)}, u32[]{:S(2)}, u32[]{:S(2)}) %collective-permute-start.19) | collective-permute-done | bytes 73760 | tf_op jit(solution)/shard_map/ppermute | solution.py:491
  94.3 2.8 %collective-permute-start.20 = (bf16[288,128]{1,0:T(8,128)(2,1)S(1)}, bf16[288,128]{1,0:T(8,128)(2,1)S(1)}, u32[]{:S(2)}, u32[]{:S(2)}) collective-permute-start(bf16[288,128]{1,0:T(8,128)(2,1)S(1)} %add_convert_fusion.2), channel_id=1, source_target_pairs={{0,1},{1,0},{2,3},{3,2},{4,5},{5,4},{6,7},{7,6},{8,9},{9,8},{10,11... | collective-permute-start | bytes 221192 | tf_op jit(solution)/shard_map/ppermute | solution.py:491
  97.1 0.8 collective-permute-done.20
  98.0 0.8 collective-permute-done.13.refs_3_
  98.8 5.7 %collective-permute-start.22 = (bf16[1088,128]{1,0:T(8,128)(2,1)S(1)}, bf16[1088,128]{1,0:T(8,128)(2,1)S(1)}, u32[]{:S(2)}, u32[]{:S(2)}) collective-permute-start(bf16[1088,128]{1,0:T(8,128)(2,1)S(1)} %collective-permute-done.11.refs_1_), channel_id=1, source_target_pairs={{0,1},{1,0},{2,3},{3,2},{4,5},{5,4},{6,7},{7,6},{8,9},{9,8},{10,11... | collective-permute-start | bytes 835592 | tf_op jit(solution)/shard_map/ppermute | solution.py:491
  104.5 0.5 collective-permute-start.24
  105.0 1.3 %collective-permute-start.25 = (bf16[576,128]{1,0:T(8,128)(2,1)S(1)}, bf16[576,128]{1,0:T(8,128)(2,1)S(1)}, u32[]{:S(2)}, u32[]{:S(2)}) collective-permute-start(bf16[576,128]{1,0:T(8,128)(2,1)S(1)} %pad_maximum_fusion.refs_0_), channel_id=1, source_target_pairs={{0,2},{1,3},{2,0},{3,1},{4,6},{5,7},{6,4},{7,5},{8,10},{9,11},{10,... | collective-permute-start | bytes 442376 | tf_op jit(solution)/shard_map/ppermute | solution.py:491
  106.3 0.2 collective-permute-start.26
  106.5 1.2 collective-permute-start.27
  107.7 3.0 %early_out.1 = (f32[512,1536]{1,0:T(8,128)}, f32[512,512]{1,0:T(8,128)}, f32[512,128]{1,0:T(8,128)}) custom-call(s32[2]{0:T(128)S(1)} %pad_add_fusion.place_ref, bf16[1088,128]{1,0:T(8,128)(2,1)S(1)} %bitcast.58, bf16[1088,128]{1,0:T(8,128)(2,1)S(1)} %collective-permute-done.11.refs_1_, bf16[1088,128]{1,0:T(8,128)(2,1)S(1)} %collective-permute-done.12.refs_2_, ...), custom_call_target="tpu_custom_call" | custom-call | flops 1000000000 | bytes 5000000 | tf_op jit(solution)/shard_map/early_out/pallas_call | solution.py:459
  110.7 1.0 collective-permute-done.26.refs_2_
  111.7 2.7 %collective-permute-done.27.refs_3_ = bf16[576,128]{1,0:T(8,128)(2,1)S(1)} collective-permute-done((bf16[576,128]{1,0:T(8,128)(2,1)S(1)}, bf16[576,128]{1,0:T(8,128)(2,1)S(1)}, u32[]{:S(2)}, u32[]{:S(2)}) %collective-permute-start.27) | collective-permute-done | bytes 147488 | tf_op jit(solution)/shard_map/ppermute | solution.py:491
  114.4 1.7 %late_out.1 = (f32[512,512]{1,0:T(8,128)}, f32[64,256]{1,0:T(8,128)}, f32[1,512]{1,0:T(1,128)}) custom-call(s32[2]{0:T(128)S(1)} %pad_add_fusion.place_ref, bf16[576,128]{1,0:T(8,128)(2,1)S(1)} %pad_maximum_fusion.refs_0_, bf16[576,128]{1,0:T(8,128)(2,1)S(1)} %collective-permute-done.25.refs_1_, bf16[576,128]{1,0:T(8,128)(2,1)S(1)} %collective-permute-done.26.refs_2_, ...), custom_call_target="tpu_custom_call" | custom-call | flops 1000000000 | bytes 5000000 | tf_op jit(solution)/shard_map/late_out/pallas_call | solution.py:459
  (53 shorter events, 0.6 us)
Async XLA Ops:
  0.6 18.3 %copy-start.9 = (bf16[512]{0:T(512)(128)(2,1)S(1)}, bf16[512]{0:T(512)(128)(2,1)}, u32[]{:S(2)}) copy-start(bf16[512]{0:T(512)(128)(2,1)} %param.16) | copy-start | bytes 3076
  0.6 25.6 %copy-start.5 = (bf16[512,1536]{1,0:T(8,128)(2,1)S(1)}, bf16[512,1536]{1,0:T(8,128)(2,1)}, u32[]{:S(2)}) copy-start(bf16[512,1536]{1,0:T(8,128)(2,1)} %wp_ref.1) | copy-start | bytes 4718596
  0.7 25.6 %copy-start.6 = (bf16[512,512]{1,0:T(8,128)(2,1)S(1)}, bf16[512,512]{1,0:T(8,128)(2,1)}, u32[]{:S(2)}) copy-start(bf16[512,512]{1,0:T(8,128)(2,1)} %wo_ref.1) | copy-start | bytes 1572868
  0.7 25.6 %copy-start.8 = (s32[16]{0:T(128)S(1)}, s32[16]{0:T(128)}, u32[]{:S(2)}) copy-start(s32[16]{0:T(128)} %param.13) | copy-start | bytes 196
  13.2 13.1 %all-to-all-start = ((bf16[8,32,640]{2,1,0:T(8,128)(2,1)}), bf16[8,32,640]{2,1,0:T(8,128)(2,1)S(1)}, u32[]{:S(2)}, u32[]{:S(2)}) async-start(bf16[8,32,640]{2,1,0:T(8,128)(2,1)} %bitcast.70), calls=%async_computation | async-start | bytes 655360 | tf_op jit(solution)/shard_map/all_to_all | solution.py:561
  26.3 0.9 copy-start.7
  37.3 7.3 %collective-permute-start = (bf16[4352,128]{1,0:T(8,128)(2,1)}, bf16[4352,128]{1,0:T(8,128)(2,1)}, u32[]{:S(2)}, u32[]{:S(2)}) collective-permute-start(bf16[4352,128]{1,0:T(8,128)(2,1)} %get-tuple-element.43), channel_id=1, source_target_pairs={{0,1},{1,0},{2,3},{3,2},{4,5},{5,4},{6,7},{7,6},{8,9},{9,8},{10,11... | collective-permute-start | bytes 3342344 | tf_op jit(solution)/shard_map/ppermute | solution.py:491
  40.5 10.9 %all-to-all-start.1 = ((bf16[8,32,512]{2,1,0:T(8,128)(2,1)}), bf16[8,32,512]{2,1,0:T(8,128)(2,1)S(1)}, u32[]{:S(2)}, u32[]{:S(2)}) async-start(bf16[8,32,512]{2,1,0:T(8,128)(2,1)} %bitcast.13), calls=%async_computation.1 | async-start | bytes 524288 | tf_op jit(solution)/shard_map/all_to_all | solution.py:561
  46.1 5.3 %copy-start.1 = (bf16[512,512]{1,0:T(8,128)(2,1)S(1)}, bf16[512,512]{1,0:T(8,128)(2,1)}, u32[]{:S(2)}) copy-start(bf16[512,512]{1,0:T(8,128)(2,1)} %w_ref.3) | copy-start | bytes 1572868
  46.1 5.3 %copy-start.2 = (bf16[8,32,128]{2,1,0:T(8,128)(2,1)S(1)}, bf16[8,32,128]{2,1,0:T(8,128)(2,1)}, u32[]{:S(2)}) copy-start(bf16[8,32,128]{2,1,0:T(8,128)(2,1)} %get-tuple-element.46.codes_ref) | copy-start | bytes 196612
  46.1 5.2 %copy-start.3 = (bf16[256,64]{0,1:T(8,128)(2,1)S(1)}, bf16[256,64]{0,1:T(8,128)(2,1)}, u32[]{:S(2)}) copy-start(bf16[256,64]{0,1:T(8,128)(2,1)} %param.14) | copy-start | bytes 98308
  46.1 5.2 %copy-start.4 = (s32[128]{0:T(128)S(1)}, s32[128]{0:T(128)}, u32[]{:S(2)}) copy-start(s32[128]{0:T(128)} %param.11) | copy-start | bytes 1540
  47.1 22.4 %collective-permute-start.1 = (bf16[1088,128]{1,0:T(8,128)(2,1)}, bf16[1088,128]{1,0:T(8,128)(2,1)S(1)}, u32[]{:S(2)}, u32[]{:S(2)}) collective-permute-start(bf16[1088,128]{1,0:T(8,128)(2,1)} %get-tuple-element.77), channel_id=1, source_target_pairs={{0,2},{1,3},{2,0},{3,1},{4,6},{5,7},{6,4},{7,5},{8,10},{9,11},{10,... | collective-permute-start | bytes 835592 | tf_op jit(solution)/shard_map/ppermute | solution.py:491
  47.3 22.1 %collective-permute-start.2 = (bf16[1088,128]{1,0:T(8,128)(2,1)}, bf16[1088,128]{1,0:T(8,128)(2,1)S(1)}, u32[]{:S(2)}, u32[]{:S(2)}) collective-permute-start(bf16[1088,128]{1,0:T(8,128)(2,1)} %get-tuple-element.76), channel_id=1, source_target_pairs={{0,4},{1,5},{2,6},{3,7},{4,0},{5,1},{6,2},{7,3},{8,12},{9,13},{10,... | collective-permute-start | bytes 835592 | tf_op jit(solution)/shard_map/ppermute | solution.py:491
  48.5 20.9 %collective-permute-start.3 = (bf16[1088,128]{1,0:T(8,128)(2,1)}, bf16[1088,128]{1,0:T(8,128)(2,1)S(1)}, u32[]{:S(2)}, u32[]{:S(2)}) collective-permute-start(bf16[1088,128]{1,0:T(8,128)(2,1)} %get-tuple-element.75), channel_id=1, source_target_pairs={{0,6},{1,7},{2,4},{3,5},{4,2},{5,3},{6,0},{7,1},{8,14},{9,15},{10,... | collective-permute-start | bytes 835592 | tf_op jit(solution)/shard_map/ppermute | solution.py:491
  51.4 2.2 %copy-start = (bf16[4096,512]{1,0:T(8,128)(2,1)S(1)}, bf16[4096,512]{1,0:T(8,128)(2,1)}, u32[]{:S(2)}) copy-start(bf16[4096,512]{1,0:T(8,128)(2,1)} %get-tuple-element.47.slope_ref) | copy-start | bytes 12582916
  66.9 5.5 %collective-permute-start.7 = (bf16[1152,128]{1,0:T(8,128)(2,1)S(1)}, bf16[1152,128]{1,0:T(8,128)(2,1)S(1)}, u32[]{:S(2)}, u32[]{:S(2)}) collective-permute-start(bf16[1152,128]{1,0:T(8,128)(2,1)S(1)} %get-tuple-element.53), channel_id=1, source_target_pairs={{0,1},{1,0},{2,3},{3,2},{4,5},{5,4},{6,7},{7,6},{8,9},{9,8},{10,11... | collective-permute-start | bytes 884744 | tf_op jit(solution)/shard_map/ppermute | solution.py:491
  69.7 3.8 %collective-permute-start.4 = (bf16[272,128]{1,0:T(8,128)(2,1)S(1)}, bf16[272,128]{1,0:T(8,128)(2,1)S(1)}, u32[]{:S(2)}, u32[]{:S(2)}) collective-permute-start(bf16[272,128]{1,0:T(8,128)(2,1)S(1)} %get-tuple-element.83), channel_id=1, source_target_pairs={{0,8},{1,9},{2,10},{3,11},{4,12},{5,13},{6,14},{7,15},{8,0},{9,1},... | collective-permute-start | bytes 208904 | tf_op jit(solution)/shard_map/ppermute | solution.py:491
  70.4 4.8 %collective-permute-start.5 = (bf16[272,128]{1,0:T(8,128)(2,1)S(1)}, bf16[272,128]{1,0:T(8,128)(2,1)S(1)}, u32[]{:S(2)}, u32[]{:S(2)}) collective-permute-start(bf16[272,128]{1,0:T(8,128)(2,1)S(1)} %get-tuple-element.82), channel_id=1, source_target_pairs={{0,16},{1,17},{2,18},{3,19},{4,20},{5,21},{6,22},{7,23},{8,24},{9,... | collective-permute-start | bytes 208904 | tf_op jit(solution)/shard_map/ppermute | solution.py:491
  70.8 8.3 %collective-permute-start.6 = (bf16[272,128]{1,0:T(8,128)(2,1)S(1)}, bf16[272,128]{1,0:T(8,128)(2,1)S(1)}, u32[]{:S(2)}, u32[]{:S(2)}) collective-permute-start(bf16[272,128]{1,0:T(8,128)(2,1)S(1)} %get-tuple-element.81), channel_id=1, source_target_pairs={{0,24},{1,25},{2,26},{3,27},{4,28},{5,29},{6,30},{7,31},{8,16},{9,... | collective-permute-start | bytes 208904 | tf_op jit(solution)/shard_map/ppermute | solution.py:491
  72.5 8.2 %collective-permute-start.14 = (bf16[288,128]{1,0:T(8,128)(2,1)S(1)}, bf16[288,128]{1,0:T(8,128)(2,1)S(1)}, u32[]{:S(2)}, u32[]{:S(2)}) collective-permute-start(bf16[288,128]{1,0:T(8,128)(2,1)S(1)} %get-tuple-element.80), channel_id=1, source_target_pairs={{0,2},{1,3},{2,0},{3,1},{4,6},{5,7},{6,4},{7,5},{8,10},{9,11},{10,... | collective-permute-start | bytes 221192 | tf_op jit(solution)/shard_map/ppermute | solution.py:491
  72.8 9.1 %collective-permute-start.15 = (bf16[288,128]{1,0:T(8,128)(2,1)S(1)}, bf16[288,128]{1,0:T(8,128)(2,1)S(1)}, u32[]{:S(2)}, u32[]{:S(2)}) collective-permute-start(bf16[288,128]{1,0:T(8,128)(2,1)S(1)} %get-tuple-element.79), channel_id=1, source_target_pairs={{0,4},{1,5},{2,6},{3,7},{4,0},{5,1},{6,2},{7,3},{8,12},{9,13},{10,... | collective-permute-start | bytes 221192 | tf_op jit(solution)/shard_map/ppermute | solution.py:491
  73.5 8.4 %collective-permute-start.16 = (bf16[288,128]{1,0:T(8,128)(2,1)S(1)}, bf16[288,128]{1,0:T(8,128)(2,1)S(1)}, u32[]{:S(2)}, u32[]{:S(2)}) collective-permute-start(bf16[288,128]{1,0:T(8,128)(2,1)S(1)} %get-tuple-element.78), channel_id=1, source_target_pairs={{0,6},{1,7},{2,4},{3,5},{4,2},{5,3},{6,0},{7,1},{8,14},{9,15},{10,... | collective-permute-start | bytes 221192 | tf_op jit(solution)/shard_map/ppermute | solution.py:491
  79.2 4.2 %collective-permute-start.8 = (bf16[272,128]{1,0:T(8,128)(2,1)S(1)}, bf16[272,128]{1,0:T(8,128)(2,1)S(1)}, u32[]{:S(2)}, u32[]{:S(2)}) collective-permute-start(bf16[272,128]{1,0:T(8,128)(2,1)S(1)} %get-tuple-element.74), channel_id=1, source_target_pairs={{0,8},{1,9},{2,10},{3,11},{4,12},{5,13},{6,14},{7,15},{8,0},{9,1},... | collective-permute-start | bytes 208904 | tf_op jit(solution)/shard_map/ppermute | solution.py:491
  79.3 5.4 %collective-permute-start.9 = (bf16[272,128]{1,0:T(8,128)(2,1)S(1)}, bf16[272,128]{1,0:T(8,128)(2,1)S(1)}, u32[]{:S(2)}, u32[]{:S(2)}) collective-permute-start(bf16[272,128]{1,0:T(8,128)(2,1)S(1)} %get-tuple-element.74), channel_id=1, source_target_pairs={{0,16},{1,17},{2,18},{3,19},{4,20},{5,21},{6,22},{7,23},{8,24},{9,... | collective-permute-start | bytes 208904 | tf_op jit(solution)/shard_map/ppermute | solution.py:491
  80.7 8.6 %collective-permute-start.10 = (bf16[272,128]{1,0:T(8,128)(2,1)S(1)}, bf16[272,128]{1,0:T(8,128)(2,1)S(1)}, u32[]{:S(2)}, u32[]{:S(2)}) collective-permute-start(bf16[272,128]{1,0:T(8,128)(2,1)S(1)} %get-tuple-element.74), channel_id=1, source_target_pairs={{0,24},{1,25},{2,26},{3,27},{4,28},{5,29},{6,30},{7,31},{8,16},{9,... | collective-permute-start | bytes 208904 | tf_op jit(solution)/shard_map/ppermute | solution.py:491
  82.0 7.8 %collective-permute-start.17 = (bf16[288,128]{1,0:T(8,128)(2,1)S(1)}, bf16[288,128]{1,0:T(8,128)(2,1)S(1)}, u32[]{:S(2)}, u32[]{:S(2)}) collective-permute-start(bf16[288,128]{1,0:T(8,128)(2,1)S(1)} %fusion.5), channel_id=1, source_target_pairs={{0,8},{1,9},{2,10},{3,11},{4,12},{5,13},{6,14},{7,15},{8,0},{9,1},... | collective-permute-start | bytes 221192 | tf_op jit(solution)/shard_map/ppermute | solution.py:491
  83.0 8.9 %collective-permute-start.18 = (bf16[288,128]{1,0:T(8,128)(2,1)S(1)}, bf16[288,128]{1,0:T(8,128)(2,1)S(1)}, u32[]{:S(2)}, u32[]{:S(2)}) collective-permute-start(bf16[288,128]{1,0:T(8,128)(2,1)S(1)} %fusion.5), channel_id=1, source_target_pairs={{0,16},{1,17},{2,18},{3,19},{4,20},{5,21},{6,22},{7,23},{8,24},{9,... | collective-permute-start | bytes 221192 | tf_op jit(solution)/shard_map/ppermute | solution.py:491
  83.4 10.8 %collective-permute-start.19 = (bf16[288,128]{1,0:T(8,128)(2,1)S(1)}, bf16[288,128]{1,0:T(8,128)(2,1)S(1)}, u32[]{:S(2)}, u32[]{:S(2)}) collective-permute-start(bf16[288,128]{1,0:T(8,128)(2,1)S(1)} %fusion.5), channel_id=1, source_target_pairs={{0,24},{1,25},{2,26},{3,27},{4,28},{5,29},{6,30},{7,31},{8,16},{9,... | collective-permute-start | bytes 221192 | tf_op jit(solution)/shard_map/ppermute | solution.py:491
  89.2 8.8 %collective-permute-start.11 = (bf16[1088,128]{1,0:T(8,128)(2,1)S(1)}, bf16[1088,128]{1,0:T(8,128)(2,1)S(1)}, u32[]{:S(2)}, u32[]{:S(2)}) collective-permute-start(bf16[1088,128]{1,0:T(8,128)(2,1)S(1)} %bitcast.54), channel_id=1, source_target_pairs={{0,2},{1,3},{2,0},{3,1},{4,6},{5,7},{6,4},{7,5},{8,10},{9,11},{10,... | collective-permute-start | bytes 835592 | tf_op jit(solution)/shard_map/ppermute | solution.py:491
  89.3 8.7 %collective-permute-start.12 = (bf16[1088,128]{1,0:T(8,128)(2,1)S(1)}, bf16[1088,128]{1,0:T(8,128)(2,1)S(1)}, u32[]{:S(2)}, u32[]{:S(2)}) collective-permute-start(bf16[1088,128]{1,0:T(8,128)(2,1)S(1)} %bitcast.55), channel_id=1, source_target_pairs={{0,4},{1,5},{2,6},{3,7},{4,0},{5,1},{6,2},{7,3},{8,12},{9,13},{10,... | collective-permute-start | bytes 835592 | tf_op jit(solution)/shard_map/ppermute | solution.py:491
  89.7 9.1 %collective-permute-start.13 = (bf16[1088,128]{1,0:T(8,128)(2,1)S(1)}, bf16[1088,128]{1,0:T(8,128)(2,1)S(1)}, u32[]{:S(2)}, u32[]{:S(2)}) collective-permute-start(bf16[1088,128]{1,0:T(8,128)(2,1)S(1)} %bitcast.56), channel_id=1, source_target_pairs={{0,6},{1,7},{2,4},{3,5},{4,2},{5,3},{6,0},{7,1},{8,14},{9,15},{10,... | collective-permute-start | bytes 835592 | tf_op jit(solution)/shard_map/ppermute | solution.py:491
  94.3 3.7 %collective-permute-start.20 = (bf16[288,128]{1,0:T(8,128)(2,1)S(1)}, bf16[288,128]{1,0:T(8,128)(2,1)S(1)}, u32[]{:S(2)}, u32[]{:S(2)}) collective-permute-start(bf16[288,128]{1,0:T(8,128)(2,1)S(1)} %add_convert_fusion.2), channel_id=1, source_target_pairs={{0,1},{1,0},{2,3},{3,2},{4,5},{5,4},{6,7},{7,6},{8,9},{9,8},{10,11... | collective-permute-start | bytes 221192 | tf_op jit(solution)/shard_map/ppermute | solution.py:491
  97.1 9.3 %collective-permute-start.21 = (bf16[1088,128]{1,0:T(8,128)(2,1)S(1)}, bf16[1088,128]{1,0:T(8,128)(2,1)S(1)}, u32[]{:S(2)}, u32[]{:S(2)}) collective-permute-start(bf16[1088,128]{1,0:T(8,128)(2,1)S(1)} %bitcast.57), channel_id=1, source_target_pairs={{0,1},{1,0},{2,3},{3,2},{4,5},{5,4},{6,7},{7,6},{8,9},{9,8},{10,11... | collective-permute-start | bytes 835592 | tf_op jit(solution)/shard_map/ppermute | solution.py:491
  98.8 7.7 %collective-permute-start.22 = (bf16[1088,128]{1,0:T(8,128)(2,1)S(1)}, bf16[1088,128]{1,0:T(8,128)(2,1)S(1)}, u32[]{:S(2)}, u32[]{:S(2)}) collective-permute-start(bf16[1088,128]{1,0:T(8,128)(2,1)S(1)} %collective-permute-done.11.refs_1_), channel_id=1, source_target_pairs={{0,1},{1,0},{2,3},{3,2},{4,5},{5,4},{6,7},{7,6},{8,9},{9,8},{10,11... | collective-permute-start | bytes 835592 | tf_op jit(solution)/shard_map/ppermute | solution.py:491
  104.5 3.2 %collective-permute-start.23 = (bf16[1088,128]{1,0:T(8,128)(2,1)S(1)}, bf16[1088,128]{1,0:T(8,128)(2,1)S(1)}, u32[]{:S(2)}, u32[]{:S(2)}) collective-permute-start(bf16[1088,128]{1,0:T(8,128)(2,1)S(1)} %collective-permute-done.12.refs_2_), channel_id=1, source_target_pairs={{0,1},{1,0},{2,3},{3,2},{4,5},{5,4},{6,7},{7,6},{8,9},{9,8},{10,11... | collective-permute-start | bytes 835592 | tf_op jit(solution)/shard_map/ppermute | solution.py:491
  104.5 3.2 %collective-permute-start.24 = (bf16[1088,128]{1,0:T(8,128)(2,1)S(1)}, bf16[1088,128]{1,0:T(8,128)(2,1)S(1)}, u32[]{:S(2)}, u32[]{:S(2)}) collective-permute-start(bf16[1088,128]{1,0:T(8,128)(2,1)S(1)} %collective-permute-done.13.refs_3_), channel_id=1, source_target_pairs={{0,1},{1,0},{2,3},{3,2},{4,5},{5,4},{6,7},{7,6},{8,9},{9,8},{10,11... | collective-permute-start | bytes 835592 | tf_op jit(solution)/shard_map/ppermute | solution.py:491
  105.0 5.7 %collective-permute-start.25 = (bf16[576,128]{1,0:T(8,128)(2,1)S(1)}, bf16[576,128]{1,0:T(8,128)(2,1)S(1)}, u32[]{:S(2)}, u32[]{:S(2)}) collective-permute-start(bf16[576,128]{1,0:T(8,128)(2,1)S(1)} %pad_maximum_fusion.refs_0_), channel_id=1, source_target_pairs={{0,2},{1,3},{2,0},{3,1},{4,6},{5,7},{6,4},{7,5},{8,10},{9,11},{10,... | collective-permute-start | bytes 442376 | tf_op jit(solution)/shard_map/ppermute | solution.py:491
  106.3 5.4 %collective-permute-start.26 = (bf16[576,128]{1,0:T(8,128)(2,1)S(1)}, bf16[576,128]{1,0:T(8,128)(2,1)S(1)}, u32[]{:S(2)}, u32[]{:S(2)}) collective-permute-start(bf16[576,128]{1,0:T(8,128)(2,1)S(1)} %pad_maximum_fusion.refs_0_), channel_id=1, source_target_pairs={{0,4},{1,5},{2,6},{3,7},{4,0},{5,1},{6,2},{7,3},{8,12},{9,13},{10,... | collective-permute-start | bytes 442376 | tf_op jit(solution)/shard_map/ppermute | solution.py:491
  106.5 7.9 %collective-permute-start.27 = (bf16[576,128]{1,0:T(8,128)(2,1)S(1)}, bf16[576,128]{1,0:T(8,128)(2,1)S(1)}, u32[]{:S(2)}, u32[]{:S(2)}) collective-permute-start(bf16[576,128]{1,0:T(8,128)(2,1)S(1)} %pad_maximum_fusion.refs_0_), channel_id=1, source_target_pairs={{0,6},{1,7},{2,4},{3,5},{4,2},{5,3},{6,0},{7,1},{8,14},{9,15},{10,... | collective-permute-start | bytes 442376 | tf_op jit(solution)/shard_map/ppermute | solution.py:491

commit v5 on v4

--- a/solution.py
+++ b/solution.py
@@ -11,7 +11,6 @@
 HEADS = 8
 NORM_EPS = 1e-06
 WIN_STEP = 8
-SLOPE_PIECES = 4
 LANES = 128
 VMEM_LIMIT = 28 * 2**20
 
@@ -65,8 +64,27 @@
     return pl.CostEstimate(flops=int(flops), bytes_accessed=int(moved), transcendentals=0)
 
 
+def slot_places(owner_ref, slots, capacity):
+    own_row = owner_ref[...]
+    packets = own_row.shape[1]
+    ahead = (column(own_row) == own_row) & (iota((packets, packets), 0) < iota((packets, packets), 1))
+    rank = jnp.sum(jnp.where(ahead, 1.0, 0.0), axis=0, keepdims=True).astype(jnp.int32)
+    return flag(iota((slots, packets), 0) == own_row * capacity + rank)
+
+
 def embed_kernel(
-    capacity, bytes_ref, owner_ref, sess_ref, table_ref, w_ref, out_ref, slope_ref, codes_ref, pair_ref, emb_ref, turned_ref
+    capacity,
+    bytes_ref,
+    owner_ref,
+    sess_ref,
+    table_ref,
+    w_ref,
+    out_ref,
+    slope_ref,
+    codes_ref,
+    emb_ref,
+    turned_ref,
+    w_turned_ref,
 ):
     step = pl.program_id(0)
     packets, length = bytes_ref.shape
@@ -76,46 +94,38 @@
 
     @pl.when(step == 0)
     def _():
-        table = table_ref[...].astype(f32).T.astype(bf16)
-        pair_ref[...] = jnp.zeros_like(pair_ref)
-        pair_ref[0:vocab, 0:chan] = table
-        pair_ref[vocab : 2 * vocab, chan : 2 * chan] = table
         emb_ref[...] = jnp.zeros_like(emb_ref)
+        w_turned_ref[...] = w_ref[...].astype(f32).T.astype(bf16)
         turned_ref[...] = bytes_ref[...].astype(f32).T
         for j in range(KERNEL):
             codes_ref[j] = turned_ref[pl.ds(j, positions, stride=KERNEL), :].astype(bf16)
 
     here = WIN_STEP * KERNEL
-    codes = pltpu.roll(bytes_ref[...], lax.rem(length - here * step, length), 1)[:, :here]
-    codes = codes.astype(f32).astype(bf16)
-    values = small_iota((packets, vocab), 1)
-    pairs = []
-    for k in range(KERNEL // 2):
+    codes = turned_ref[pl.ds(pl.multiple_of(step * here, here), here), :].astype(jnp.int32)
+    parts = [table_ref[:, at : at + LANES].astype(f32) for at in range(0, vocab, LANES)]
+    windows = []
+    for w in range(WIN_STEP):
         rows = []
-        for w in range(WIN_STEP):
-            j = w * KERNEL + 2 * k
-            rows.append(
-                jnp.concatenate([onehot(codes[:, j : j + 1], values), onehot(codes[:, j + 1 : j + 2], values)], axis=1)
-            )
-        pairs.append(dot_nn(jnp.concatenate(rows, axis=0), pair_ref[...]).astype(bf16))
-    windows = jnp.concatenate(pairs, axis=1)
-    conv = dot_nn(windows, w_ref[...])
+        for j in range(w * KERNEL, (w + 1) * KERNEL):
+            code = jnp.broadcast_to(codes[j : j + 1, :], (chan, packets))
+            lane = code & (LANES - 1)
+            found = [jnp.take_along_axis(p, lane, axis=1, mode="promise_in_bounds") for p in parts]
+            rows.append(jnp.where(code < LANES, found[0], found[1]).astype(bf16))
+        windows.append(jnp.concatenate(rows, axis=0))
+    conv = dot_nn(w_turned_ref[...], jnp.concatenate(windows, axis=1))
     sigma = jax.nn.sigmoid(conv)
     act = conv * sigma
     slope_ref[...] = ((sigma + act * (1.0 - sigma)) * (1.0 / positions)).astype(bf16)
     total = emb_ref[...]
     for w in range(WIN_STEP):
-        total += act[w * packets : (w + 1) * packets]
+        total += act[:, w * packets : (w + 1) * packets]
     emb_ref[...] = total
 
     @pl.when(step == pl.num_programs(0) - 1)
     def _():
         emb = (emb_ref[...] * (1.0 / positions)).astype(bf16)
-        own_row = owner_ref[...]
-        same = (column(own_row) == own_row) & (iota((packets, packets), 0) < iota((packets, packets), 1))
-        rank = jnp.sum(jnp.where(same, 1.0, 0.0), axis=0, keepdims=True).astype(jnp.int32)
-        place = flag(iota((out_ref.shape[0], packets), 0) == own_row * capacity + rank)
-        out_ref[:, :width] = dot_nn(place, emb).astype(bf16)
+        place = slot_places(owner_ref, out_ref.shape[0], capacity)
+        out_ref[:, :width] = dot_nt(place, emb).astype(bf16)
         label = spread(sess_ref[...] + 1, LANES).astype(bf16)
         out_ref[:, width:] = dot_nn(place, label).astype(bf16)
 
@@ -125,7 +135,6 @@
     rows = WIN_STEP * packets
     steps = length // (KERNEL * WIN_STEP)
     width = w_conv.shape[1]
-    chan, vocab = table_t.shape
     whole = lambda a: pl.BlockSpec(a.shape, lambda i: (0, 0))
     args = (packet_bytes, owner, session, table_t, w_conv)
     return pl.pallas_call(
@@ -134,18 +143,18 @@
         in_specs=[whole(a) for a in args],
         out_specs=[
             pl.BlockSpec((slots, width + LANES), lambda i: (0, 0)),
-            pl.BlockSpec((rows, width), lambda i: (i, 0)),
+            pl.BlockSpec((width, rows), lambda i: (0, i)),
             pl.BlockSpec((KERNEL, length // KERNEL, packets), lambda i: (0, 0, 0)),
         ],
         out_shape=[
             jax.ShapeDtypeStruct((slots, width + LANES), bf16),
-            jax.ShapeDtypeStruct((steps * rows, width), bf16),
+            jax.ShapeDtypeStruct((width, steps * rows), bf16),
             jax.ShapeDtypeStruct((KERNEL, length // KERNEL, packets), bf16),
         ],
         scratch_shapes=[
-            pltpu.VMEM((2 * vocab, 2 * chan), bf16),
-            pltpu.VMEM((packets, width), f32),
+            pltpu.VMEM((width, packets), f32),
             pltpu.VMEM((length, packets), f32),
+            pltpu.VMEM((width, w_conv.shape[0]), bf16),
         ],
         compiler_params=pltpu.CompilerParams(vmem_limit_bytes=2 * VMEM_LIMIT),
         cost_estimate=cost(1e10, 5e6),
@@ -325,39 +334,24 @@
     keep_ref,
     send_ref,
     dconv_ref,
-    held_ref,
     rows_ref,
     table_grad_ref,
     halves_ref,
-    sem_ref,
 ):
     j = pl.program_id(0)
     slots, width = ret_ref.shape
     packets = owner_ref.shape[1]
     chan, vocab = table_ref.shape
     window = w_ref.shape[0]
-    piece = slope_ref.shape[0] // SLOPE_PIECES
 
     @pl.when(j == 0)
     def _():
-        copies = []
-        for i in range(SLOPE_PIECES):
-            at = pl.ds(i * piece, piece)
-            copies.append(pltpu.make_async_copy(slope_ref.at[at, :], held_ref.at[at, :], sem_ref.at[i]))
-            copies[i].start()
-        own_row = owner_ref[...]
-        own_col = column(own_row)
-        same = (own_col == own_row) & (iota((packets, packets), 1) < iota((packets, packets), 0))
-        rank = jnp.sum(jnp.where(same, 1.0, 0.0), axis=1, keepdims=True).astype(jnp.int32)
-        place = flag(iota((packets, slots), 1) == own_col * capacity + rank)
-        demb = dot_nn(place, ret_ref[...])
+        demb = dot_tn(slot_places(owner_ref, slots, capacity), ret_ref[...])
         halves_ref[...] = jnp.zeros_like(halves_ref)
         table_grad_ref[...] = jnp.zeros_like(table_grad_ref)
-        for i in range(SLOPE_PIECES):
-            copies[i].wait()
-            for first in range(i * piece, (i + 1) * piece, packets):
-                at = slice(first, first + packets)
-                dconv_ref[at, :] = (demb * held_ref[at, :].astype(f32)).astype(bf16)
+        for first in range(0, slope_ref.shape[1], packets):
+            at = slice(first, first + packets)
+            dconv_ref[at, :] = (demb * slope_ref[:, at].astype(f32).T).astype(bf16)
 
     at = pl.ds(pl.multiple_of(j * chan, chan), chan)
     rows_ref[at, :] = add_by_value(codes_ref, dconv_ref, table_ref, w_ref[at, :], table_grad_ref)
@@ -383,7 +377,6 @@
 def conv_back(core, returned, owner, codes, slope, table_t, w_conv, gain_grad, capacity, half_rows):
     args = (returned, owner, codes, slope, table_t, w_conv, gain_grad)
     specs = [whole(a) if a.ndim == 2 else pl.BlockSpec((1, *a.shape[1:]), lambda j: (j, 0, 0)) for a in args]
-    specs[3] = pl.BlockSpec(memory_space=pl.ANY)
     half = jax.ShapeDtypeStruct((half_rows, LANES), bf16)
     return pl.pallas_call(
         functools.partial(conv_back_kernel, capacity),
@@ -392,12 +385,10 @@
         out_specs=[whole(half), whole(half)],
         out_shape=[half, half],
         scratch_shapes=[
-            pltpu.VMEM(slope.shape, bf16),
-            pltpu.VMEM(slope.shape, bf16),
+            pltpu.VMEM(slope.shape[::-1], bf16),
             pltpu.VMEM(w_conv.shape, bf16),
             pltpu.VMEM(table_t.shape, f32),
             pltpu.VMEM((2, half_rows, LANES), bf16),
-            pltpu.SemaphoreType.DMA((SLOPE_PIECES,)),
         ],
         compiler_params=pltpu.CompilerParams(vmem_limit_bytes=28 * 2**20),
         cost_estimate=cost(1e9, 1e6),

time: 117 us -> 113 us (0.966)
  Pallas kernels: 40.6 us -> 36.6 us
    pallas_call x1, Pallas kernels: 12.6 us -> 8.52 us  [embed(): pl.pallas_call(functools.partial(embed_kernel, capacity), grid=(steps,),...]
  transfers between devices with their start and end apart: 30 -> 30, of which waited for: 10 -> 10; matrix products, arithmetic and copies ran while one was open for 3% -> 3% of each run, Pallas kernels for 14% -> 15%
where the time goes in v5:
time: 113 us; the launch traced here: 112 us
  starting transfers between devices  43.2 us (38%)
  Pallas kernels  36.6 us (32%)
  waiting for transfers between devices  25.3 us (22%)
  local copies, waits for them, and re-layouts  4.19 us (4%)
  other arithmetic  2.01 us (2%)
    ppermute x28, starting transfers between devices, swap(): lax.ppermute(value, AXES, [(i, i + ((i // stride % size ^ d) - i // strid...  33.4 us
    ppermute x28, waiting for transfers between devices, swap(): lax.ppermute(value, AXES, [(i, i + ((i // stride % size ^ d) - i // strid...  16.3 us
    pallas_call x1, Pallas kernels, conv_back(): pl.pallas_call(functools.partial(conv_back_kernel, capacity), grid=(KERNE...  13.3 us
    pallas_call x1, Pallas kernels, session_layer(): pl.pallas_call(session_kernel, in_specs=[pl.BlockSpec(memory_space=pltpu....  10.1 us
    all_to_all x2, starting transfers between devices, exchange(): lax.all_to_all(rows.reshape(groups, capacity, rows.shape[1]), 'dp', split...  9.8 us
    all_to_all x2, waiting for transfers between devices, exchange(): lax.all_to_all(rows.reshape(groups, capacity, rows.shape[1]), 'dp', split...  8.97 us
    pallas_call x1, Pallas kernels, embed(): pl.pallas_call(functools.partial(embed_kernel, capacity), grid=(steps,),...  8.52 us
    pallas_call x2, Pallas kernels, assemble(): pl.pallas_call(kernel, in_specs=[pl.BlockSpec(memory_space=pltpu.SMEM)] +...  4.68 us
  transfers between devices with their start and end apart: 30, of which 10 were waited for; matrix products, arithmetic and copies ran while one was open for 3% of the time, Pallas kernels for 15%

profile of v5, /device:TPU:11, one launch (start us, length us, event | category | flops | bytes accessed | tf_op | source)
XLA Modules:
  0.0 112.1 jit_solution(16698742690466409566)
XLA Ops:
  0.7 8.5 %embed.1 = (bf16[256,640]{1,0:T(8,128)(2,1)}, bf16[512,4096]{1,0:T(8,128)(2,1)}, bf16[8,32,128]{2,1,0:T(8,128)(2,1)}) custom-call(s32[128,256]{1,0:T(8,128)} %bytes_ref.1, s32[1,128]{1,0:T(1,128)} %bitcast.61, s32[1,128]{1,0:T(1,128)} %bitcast.71, bf16[64,256]{1,0:T(8,128)(2,1)} %bitcast.59, bf16[512,512]{1,0:T(8,128)(2,1)} %w_ref.3), custom_call_target="tpu_custom_call" | custom-call | flops 10000000000 | bytes 5000000 | tf_op jit(solution)/shard_map/embed/pallas_call | solution.py:140
  9.2 5.7 %all-to-all-start = ((bf16[8,32,640]{2,1,0:T(8,128)(2,1)}), bf16[8,32,640]{2,1,0:T(8,128)(2,1)S(1)}, u32[]{:S(2)}, u32[]{:S(2)}) async-start(bf16[8,32,640]{2,1,0:T(8,128)(2,1)} %bitcast.70), calls=%async_computation | async-start | bytes 655360 | tf_op jit(solution)/shard_map/all_to_all | solution.py:552
  14.9 7.3 %all-to-all-done = bf16[8,32,640]{2,1,0:T(8,128)(2,1)S(1)} async-done(((bf16[8,32,640]{2,1,0:T(8,128)(2,1)}), bf16[8,32,640]{2,1,0:T(8,128)(2,1)S(1)}, u32[]{:S(2)}, u32[]{:S(2)}) %all-to-all-start) | async-done | bytes 327712 | tf_op jit(solution)/shard_map/all_to_all | solution.py:552
  22.3 0.9 copy-done.7
  23.2 10.1 %session_layer.1 = (f32[16,128]{1,0:T(8,128)}, bf16[256,512]{1,0:T(8,128)(2,1)}, bf16[4352,128]{1,0:T(8,128)(2,1)S(1)}, bf16[4352,128]{1,0:T(8,128)(2,1)}, f32[16,128]{1,0:T(8,128)S(1)}) custom-call(s32[1]{0:T(128)} %bitcast.core_ref, bf16[256,640]{1,0:T(8,128)(2,1)S(1)} %bitcast.53, s32[1,16]{1,0:T(1,128)S(1)} %bitcast.63, ...), custom_call_target="tpu_custom_call" | custom-call | flops 10000000000 | bytes 5000000 | tf_op jit(solution)/shard_map/session_layer/pallas_call | solution.py:289
  33.2 3.2 %collective-permute-start = (bf16[4352,128]{1,0:T(8,128)(2,1)}, bf16[4352,128]{1,0:T(8,128)(2,1)}, u32[]{:S(2)}, u32[]{:S(2)}) collective-permute-start(bf16[4352,128]{1,0:T(8,128)(2,1)} %get-tuple-element.43), channel_id=1, source_target_pairs={{0,1},{1,0},{2,3},{3,2},{4,5},{5,4},{6,7},{7,6},{8,9},{9,8},{10,11... | collective-permute-start | bytes 3342344 | tf_op jit(solution)/shard_map/ppermute | solution.py:482
  36.4 4.1 %all-to-all-start.1 = ((bf16[8,32,512]{2,1,0:T(8,128)(2,1)}), bf16[8,32,512]{2,1,0:T(8,128)(2,1)S(1)}, u32[]{:S(2)}, u32[]{:S(2)}) async-start(bf16[8,32,512]{2,1,0:T(8,128)(2,1)} %bitcast.13), calls=%async_computation.1 | async-start | bytes 524288 | tf_op jit(solution)/shard_map/all_to_all | solution.py:552
  40.5 1.5 %add_convert_fusion = bf16[4352,128]{1,0:T(8,128)(2,1)S(1)} fusion(bf16[4352,128]{1,0:T(8,128)(2,1)} %collective-permute-done, bf16[4352,128]{1,0:T(8,128)(2,1)S(1)} %get-tuple-element.42), kind=kLoop, calls=%fused_computation | loop fusion | flops 2228224 | bytes 3342336 | tf_op jit(solution)/shard_map/convert_element_type | solution.py:515
  42.1 0.9 dynamic-slice_bitcast_fusion
  43.0 0.3 collective-permute-start.1
  43.3 1.2 %collective-permute-start.2 = (bf16[1088,128]{1,0:T(8,128)(2,1)}, bf16[1088,128]{1,0:T(8,128)(2,1)S(1)}, u32[]{:S(2)}, u32[]{:S(2)}) collective-permute-start(bf16[1088,128]{1,0:T(8,128)(2,1)} %get-tuple-element.76), channel_id=1, source_target_pairs={{0,4},{1,5},{2,6},{3,7},{4,0},{5,1},{6,2},{7,3},{8,12},{9,13},{10,... | collective-permute-start | bytes 835592 | tf_op jit(solution)/shard_map/ppermute | solution.py:482
  44.5 1.2 %collective-permute-start.3 = (bf16[1088,128]{1,0:T(8,128)(2,1)}, bf16[1088,128]{1,0:T(8,128)(2,1)S(1)}, u32[]{:S(2)}, u32[]{:S(2)}) collective-permute-start(bf16[1088,128]{1,0:T(8,128)(2,1)} %get-tuple-element.75), channel_id=1, source_target_pairs={{0,6},{1,7},{2,4},{3,5},{4,2},{5,3},{6,0},{7,1},{8,14},{9,15},{10,... | collective-permute-start | bytes 835592 | tf_op jit(solution)/shard_map/ppermute | solution.py:482
  45.7 1.7 %all-to-all-done.1 = bf16[8,32,512]{2,1,0:T(8,128)(2,1)S(1)} async-done(((bf16[8,32,512]{2,1,0:T(8,128)(2,1)}), bf16[8,32,512]{2,1,0:T(8,128)(2,1)S(1)}, u32[]{:S(2)}, u32[]{:S(2)}) %all-to-all-start.1) | async-done | bytes 262176 | tf_op jit(solution)/shard_map/all_to_all | solution.py:552
  47.4 2.2 %copy-done = bf16[512,4096]{1,0:T(8,128)(2,1)S(1)} copy-done((bf16[512,4096]{1,0:T(8,128)(2,1)S(1)}, bf16[512,4096]{1,0:T(8,128)(2,1)}, u32[]{:S(2)}) %copy-start) | copy-done | bytes 4194328
  49.5 13.3 %conv_back.1 = (bf16[1152,128]{1,0:T(8,128)(2,1)S(1)}, bf16[1152,128]{1,0:T(8,128)(2,1)S(1)}) custom-call(s32[1]{0:T(128)} %bitcast.core_ref, bf16[256,512]{1,0:T(8,128)(2,1)S(1)} %bitcast.52, s32[1,128]{1,0:T(1,128)S(1)} %bitcast.62, bf16[8,32,128]{2,1,0:T(8,128)(2,1)S(1)} %copy-done.2, bf16[512,4096]{1,0:T(8,128)(2,1)S(1)} %copy-done, ...), custom_call_target="tpu_custom_call" | custom-call | flops 1000000000 | bytes 1000000 | tf_op jit(solution)/shard_map/conv_back/pallas_call | solution.py:381
  62.9 2.6 %collective-permute-start.7 = (bf16[1152,128]{1,0:T(8,128)(2,1)S(1)}, bf16[1152,128]{1,0:T(8,128)(2,1)S(1)}, u32[]{:S(2)}, u32[]{:S(2)}) collective-permute-start(bf16[1152,128]{1,0:T(8,128)(2,1)S(1)} %get-tuple-element.53), channel_id=1, source_target_pairs={{0,1},{1,0},{2,3},{3,2},{4,5},{5,4},{6,7},{7,6},{8,9},{9,8},{10,11... | collective-permute-start | bytes 884744 | tf_op jit(solution)/shard_map/ppermute | solution.py:482
  65.4 0.2 fusion.2
  65.6 0.8 collective-permute-start.4
  66.4 0.4 collective-permute-start.5
  66.8 1.6 %collective-permute-start.6 = (bf16[272,128]{1,0:T(8,128)(2,1)S(1)}, bf16[272,128]{1,0:T(8,128)(2,1)S(1)}, u32[]{:S(2)}, u32[]{:S(2)}) collective-permute-start(bf16[272,128]{1,0:T(8,128)(2,1)S(1)} %get-tuple-element.81), channel_id=1, source_target_pairs={{0,24},{1,25},{2,26},{3,27},{4,28},{5,29},{6,30},{7,31},{8,16},{9,... | collective-permute-start | bytes 208904 | tf_op jit(solution)/shard_map/ppermute | solution.py:482
  68.4 0.1 add_convert_fusion.1
  68.5 0.3 collective-permute-start.14
  68.8 0.3 collective-permute-start.15
  69.1 0.3 collective-permute-done.4
  69.5 1.7 %collective-permute-start.16 = (bf16[288,128]{1,0:T(8,128)(2,1)S(1)}, bf16[288,128]{1,0:T(8,128)(2,1)S(1)}, u32[]{:S(2)}, u32[]{:S(2)}) collective-permute-start(bf16[288,128]{1,0:T(8,128)(2,1)S(1)} %get-tuple-element.78), channel_id=1, source_target_pairs={{0,6},{1,7},{2,4},{3,5},{4,2},{5,3},{6,0},{7,1},{8,14},{9,15},{10,... | collective-permute-start | bytes 221192 | tf_op jit(solution)/shard_map/ppermute | solution.py:482
  71.2 3.9 %collective-permute-done.6 = bf16[272,128]{1,0:T(8,128)(2,1)S(1)} collective-permute-done((bf16[272,128]{1,0:T(8,128)(2,1)S(1)}, bf16[272,128]{1,0:T(8,128)(2,1)S(1)}, u32[]{:S(2)}, u32[]{:S(2)}) %collective-permute-start.6) | collective-permute-done | bytes 69664 | tf_op jit(solution)/shard_map/ppermute | solution.py:482
  75.3 1.4 %collective-permute-start.9 = (bf16[272,128]{1,0:T(8,128)(2,1)S(1)}, bf16[272,128]{1,0:T(8,128)(2,1)S(1)}, u32[]{:S(2)}, u32[]{:S(2)}) collective-permute-start(bf16[272,128]{1,0:T(8,128)(2,1)S(1)} %get-tuple-element.74), channel_id=1, source_target_pairs={{0,16},{1,17},{2,18},{3,19},{4,20},{5,21},{6,22},{7,23},{8,24},{9,... | collective-permute-start | bytes 208904 | tf_op jit(solution)/shard_map/ppermute | solution.py:482
  76.6 1.3 %collective-permute-start.10 = (bf16[272,128]{1,0:T(8,128)(2,1)S(1)}, bf16[272,128]{1,0:T(8,128)(2,1)S(1)}, u32[]{:S(2)}, u32[]{:S(2)}) collective-permute-start(bf16[272,128]{1,0:T(8,128)(2,1)S(1)} %get-tuple-element.74), channel_id=1, source_target_pairs={{0,24},{1,25},{2,26},{3,27},{4,28},{5,29},{6,30},{7,31},{8,16},{9,... | collective-permute-start | bytes 208904 | tf_op jit(solution)/shard_map/ppermute | solution.py:482
  78.0 1.0 collective-permute-start.17
  79.0 0.4 collective-permute-start.18
  79.4 1.3 %collective-permute-start.19 = (bf16[288,128]{1,0:T(8,128)(2,1)S(1)}, bf16[288,128]{1,0:T(8,128)(2,1)S(1)}, u32[]{:S(2)}, u32[]{:S(2)}) collective-permute-start(bf16[288,128]{1,0:T(8,128)(2,1)S(1)} %fusion.5), channel_id=1, source_target_pairs={{0,24},{1,25},{2,26},{3,27},{4,28},{5,29},{6,30},{7,31},{8,16},{9,... | collective-permute-start | bytes 221192 | tf_op jit(solution)/shard_map/ppermute | solution.py:482
  80.7 4.5 %collective-permute-done.10 = bf16[272,128]{1,0:T(8,128)(2,1)S(1)} collective-permute-done((bf16[272,128]{1,0:T(8,128)(2,1)S(1)}, bf16[272,128]{1,0:T(8,128)(2,1)S(1)}, u32[]{:S(2)}, u32[]{:S(2)}) %collective-permute-start.10) | collective-permute-done | bytes 69664 | tf_op jit(solution)/shard_map/ppermute | solution.py:482
  85.2 0.2 collective-permute-start.11
  85.4 0.3 collective-permute-start.12
  85.7 2.2 %collective-permute-start.13 = (bf16[1088,128]{1,0:T(8,128)(2,1)S(1)}, bf16[1088,128]{1,0:T(8,128)(2,1)S(1)}, u32[]{:S(2)}, u32[]{:S(2)}) collective-permute-start(bf16[1088,128]{1,0:T(8,128)(2,1)S(1)} %bitcast.56), channel_id=1, source_target_pairs={{0,6},{1,7},{2,4},{3,5},{4,2},{5,3},{6,0},{7,1},{8,14},{9,15},{10,... | collective-permute-start | bytes 835592 | tf_op jit(solution)/shard_map/ppermute | solution.py:482
  87.9 2.3 %collective-permute-done.19 = bf16[288,128]{1,0:T(8,128)(2,1)S(1)} collective-permute-done((bf16[288,128]{1,0:T(8,128)(2,1)S(1)}, bf16[288,128]{1,0:T(8,128)(2,1)S(1)}, u32[]{:S(2)}, u32[]{:S(2)}) %collective-permute-start.19) | collective-permute-done | bytes 73760 | tf_op jit(solution)/shard_map/ppermute | solution.py:482
  90.3 2.8 %collective-permute-start.20 = (bf16[288,128]{1,0:T(8,128)(2,1)S(1)}, bf16[288,128]{1,0:T(8,128)(2,1)S(1)}, u32[]{:S(2)}, u32[]{:S(2)}) collective-permute-start(bf16[288,128]{1,0:T(8,128)(2,1)S(1)} %add_convert_fusion.2), channel_id=1, source_target_pairs={{0,1},{1,0},{2,3},{3,2},{4,5},{5,4},{6,7},{7,6},{8,9},{9,8},{10,11... | collective-permute-start | bytes 221192 | tf_op jit(solution)/shard_map/ppermute | solution.py:482
  93.1 0.8 collective-permute-done.20
  94.0 0.8 collective-permute-done.13.refs_3_
  94.8 5.7 %collective-permute-start.22 = (bf16[1088,128]{1,0:T(8,128)(2,1)S(1)}, bf16[1088,128]{1,0:T(8,128)(2,1)S(1)}, u32[]{:S(2)}, u32[]{:S(2)}) collective-permute-start(bf16[1088,128]{1,0:T(8,128)(2,1)S(1)} %collective-permute-done.11.refs_1_), channel_id=1, source_target_pairs={{0,1},{1,0},{2,3},{3,2},{4,5},{5,4},{6,7},{7,6},{8,9},{9,8},{10,11... | collective-permute-start | bytes 835592 | tf_op jit(solution)/shard_map/ppermute | solution.py:482
  100.5 0.5 collective-permute-start.24
  101.0 1.2 %collective-permute-start.25 = (bf16[576,128]{1,0:T(8,128)(2,1)S(1)}, bf16[576,128]{1,0:T(8,128)(2,1)S(1)}, u32[]{:S(2)}, u32[]{:S(2)}) collective-permute-start(bf16[576,128]{1,0:T(8,128)(2,1)S(1)} %pad_maximum_fusion.refs_0_), channel_id=1, source_target_pairs={{0,2},{1,3},{2,0},{3,1},{4,6},{5,7},{6,4},{7,5},{8,10},{9,11},{10,... | collective-permute-start | bytes 442376 | tf_op jit(solution)/shard_map/ppermute | solution.py:482
  102.3 0.2 collective-permute-start.26
  102.5 1.2 %collective-permute-start.27 = (bf16[576,128]{1,0:T(8,128)(2,1)S(1)}, bf16[576,128]{1,0:T(8,128)(2,1)S(1)}, u32[]{:S(2)}, u32[]{:S(2)}) collective-permute-start(bf16[576,128]{1,0:T(8,128)(2,1)S(1)} %pad_maximum_fusion.refs_0_), channel_id=1, source_target_pairs={{0,6},{1,7},{2,4},{3,5},{4,2},{5,3},{6,0},{7,1},{8,14},{9,15},{10,... | collective-permute-start | bytes 442376 | tf_op jit(solution)/shard_map/ppermute | solution.py:482
  103.8 3.0 %early_out.1 = (f32[512,1536]{1,0:T(8,128)}, f32[512,512]{1,0:T(8,128)}, f32[512,128]{1,0:T(8,128)}) custom-call(s32[2]{0:T(128)S(1)} %pad_add_fusion.place_ref, bf16[1088,128]{1,0:T(8,128)(2,1)S(1)} %bitcast.58, bf16[1088,128]{1,0:T(8,128)(2,1)S(1)} %collective-permute-done.11.refs_1_, bf16[1088,128]{1,0:T(8,128)(2,1)S(1)} %collective-permute-done.12.refs_2_, ...), custom_call_target="tpu_custom_call" | custom-call | flops 1000000000 | bytes 5000000 | tf_op jit(solution)/shard_map/early_out/pallas_call | solution.py:450
  106.8 0.9 collective-permute-done.26.refs_2_
  107.7 2.7 %collective-permute-done.27.refs_3_ = bf16[576,128]{1,0:T(8,128)(2,1)S(1)} collective-permute-done((bf16[576,128]{1,0:T(8,128)(2,1)S(1)}, bf16[576,128]{1,0:T(8,128)(2,1)S(1)}, u32[]{:S(2)}, u32[]{:S(2)}) %collective-permute-start.27) | collective-permute-done | bytes 147488 | tf_op jit(solution)/shard_map/ppermute | solution.py:482
  110.4 1.7 %late_out.1 = (f32[512,512]{1,0:T(8,128)}, f32[64,256]{1,0:T(8,128)}, f32[1,512]{1,0:T(1,128)}) custom-call(s32[2]{0:T(128)S(1)} %pad_add_fusion.place_ref, bf16[576,128]{1,0:T(8,128)(2,1)S(1)} %pad_maximum_fusion.refs_0_, bf16[576,128]{1,0:T(8,128)(2,1)S(1)} %collective-permute-done.25.refs_1_, bf16[576,128]{1,0:T(8,128)(2,1)S(1)} %collective-permute-done.26.refs_2_, ...), custom_call_target="tpu_custom_call" | custom-call | flops 1000000000 | bytes 5000000 | tf_op jit(solution)/shard_map/late_out/pallas_call | solution.py:450
  (53 shorter events, 0.6 us)
Async XLA Ops:
  0.6 14.3 %copy-start.9 = (bf16[512]{0:T(512)(128)(2,1)S(1)}, bf16[512]{0:T(512)(128)(2,1)}, u32[]{:S(2)}) copy-start(bf16[512]{0:T(512)(128)(2,1)} %param.16) | copy-start | bytes 3076
  0.6 21.6 %copy-start.5 = (bf16[512,1536]{1,0:T(8,128)(2,1)S(1)}, bf16[512,1536]{1,0:T(8,128)(2,1)}, u32[]{:S(2)}) copy-start(bf16[512,1536]{1,0:T(8,128)(2,1)} %wp_ref.1) | copy-start | bytes 4718596
  0.7 21.6 %copy-start.6 = (bf16[512,512]{1,0:T(8,128)(2,1)S(1)}, bf16[512,512]{1,0:T(8,128)(2,1)}, u32[]{:S(2)}) copy-start(bf16[512,512]{1,0:T(8,128)(2,1)} %wo_ref.1) | copy-start | bytes 1572868
  0.7 21.6 %copy-start.8 = (s32[16]{0:T(128)S(1)}, s32[16]{0:T(128)}, u32[]{:S(2)}) copy-start(s32[16]{0:T(128)} %param.13) | copy-start | bytes 196
  9.2 13.0 %all-to-all-start = ((bf16[8,32,640]{2,1,0:T(8,128)(2,1)}), bf16[8,32,640]{2,1,0:T(8,128)(2,1)S(1)}, u32[]{:S(2)}, u32[]{:S(2)}) async-start(bf16[8,32,640]{2,1,0:T(8,128)(2,1)} %bitcast.70), calls=%async_computation | async-start | bytes 655360 | tf_op jit(solution)/shard_map/all_to_all | solution.py:552
  22.3 0.9 copy-start.7
  33.2 7.3 %collective-permute-start = (bf16[4352,128]{1,0:T(8,128)(2,1)}, bf16[4352,128]{1,0:T(8,128)(2,1)}, u32[]{:S(2)}, u32[]{:S(2)}) collective-permute-start(bf16[4352,128]{1,0:T(8,128)(2,1)} %get-tuple-element.43), channel_id=1, source_target_pairs={{0,1},{1,0},{2,3},{3,2},{4,5},{5,4},{6,7},{7,6},{8,9},{9,8},{10,11... | collective-permute-start | bytes 3342344 | tf_op jit(solution)/shard_map/ppermute | solution.py:482
  36.4 10.9 %all-to-all-start.1 = ((bf16[8,32,512]{2,1,0:T(8,128)(2,1)}), bf16[8,32,512]{2,1,0:T(8,128)(2,1)S(1)}, u32[]{:S(2)}, u32[]{:S(2)}) async-start(bf16[8,32,512]{2,1,0:T(8,128)(2,1)} %bitcast.13), calls=%async_computation.1 | async-start | bytes 524288 | tf_op jit(solution)/shard_map/all_to_all | solution.py:552
  42.1 5.3 %copy-start.1 = (bf16[512,512]{1,0:T(8,128)(2,1)S(1)}, bf16[512,512]{1,0:T(8,128)(2,1)}, u32[]{:S(2)}) copy-start(bf16[512,512]{1,0:T(8,128)(2,1)} %w_ref.3) | copy-start | bytes 1572868
  42.1 5.3 %copy-start.2 = (bf16[8,32,128]{2,1,0:T(8,128)(2,1)S(1)}, bf16[8,32,128]{2,1,0:T(8,128)(2,1)}, u32[]{:S(2)}) copy-start(bf16[8,32,128]{2,1,0:T(8,128)(2,1)} %get-tuple-element.46.codes_ref) | copy-start | bytes 196612
  42.1 5.3 %copy-start.3 = (bf16[256,64]{0,1:T(8,128)(2,1)S(1)}, bf16[256,64]{0,1:T(8,128)(2,1)}, u32[]{:S(2)}) copy-start(bf16[256,64]{0,1:T(8,128)(2,1)} %param.14) | copy-start | bytes 98308
  42.1 5.2 %copy-start.4 = (s32[128]{0:T(128)S(1)}, s32[128]{0:T(128)}, u32[]{:S(2)}) copy-start(s32[128]{0:T(128)} %param.11) | copy-start | bytes 1540
  43.0 22.4 %collective-permute-start.1 = (bf16[1088,128]{1,0:T(8,128)(2,1)}, bf16[1088,128]{1,0:T(8,128)(2,1)S(1)}, u32[]{:S(2)}, u32[]{:S(2)}) collective-permute-start(bf16[1088,128]{1,0:T(8,128)(2,1)} %get-tuple-element.77), channel_id=1, source_target_pairs={{0,2},{1,3},{2,0},{3,1},{4,6},{5,7},{6,4},{7,5},{8,10},{9,11},{10,... | collective-permute-start | bytes 835592 | tf_op jit(solution)/shard_map/ppermute | solution.py:482
  43.3 22.1 %collective-permute-start.2 = (bf16[1088,128]{1,0:T(8,128)(2,1)}, bf16[1088,128]{1,0:T(8,128)(2,1)S(1)}, u32[]{:S(2)}, u32[]{:S(2)}) collective-permute-start(bf16[1088,128]{1,0:T(8,128)(2,1)} %get-tuple-element.76), channel_id=1, source_target_pairs={{0,4},{1,5},{2,6},{3,7},{4,0},{5,1},{6,2},{7,3},{8,12},{9,13},{10,... | collective-permute-start | bytes 835592 | tf_op jit(solution)/shard_map/ppermute | solution.py:482
  44.5 21.0 %collective-permute-start.3 = (bf16[1088,128]{1,0:T(8,128)(2,1)}, bf16[1088,128]{1,0:T(8,128)(2,1)S(1)}, u32[]{:S(2)}, u32[]{:S(2)}) collective-permute-start(bf16[1088,128]{1,0:T(8,128)(2,1)} %get-tuple-element.75), channel_id=1, source_target_pairs={{0,6},{1,7},{2,4},{3,5},{4,2},{5,3},{6,0},{7,1},{8,14},{9,15},{10,... | collective-permute-start | bytes 835592 | tf_op jit(solution)/shard_map/ppermute | solution.py:482
  47.4 2.2 %copy-start = (bf16[512,4096]{1,0:T(8,128)(2,1)S(1)}, bf16[512,4096]{1,0:T(8,128)(2,1)}, u32[]{:S(2)}) copy-start(bf16[512,4096]{1,0:T(8,128)(2,1)} %get-tuple-element.47.slope_ref) | copy-start | bytes 12582916
  62.9 5.5 %collective-permute-start.7 = (bf16[1152,128]{1,0:T(8,128)(2,1)S(1)}, bf16[1152,128]{1,0:T(8,128)(2,1)S(1)}, u32[]{:S(2)}, u32[]{:S(2)}) collective-permute-start(bf16[1152,128]{1,0:T(8,128)(2,1)S(1)} %get-tuple-element.53), channel_id=1, source_target_pairs={{0,1},{1,0},{2,3},{3,2},{4,5},{5,4},{6,7},{7,6},{8,9},{9,8},{10,11... | collective-permute-start | bytes 884744 | tf_op jit(solution)/shard_map/ppermute | solution.py:482
  65.6 3.8 %collective-permute-start.4 = (bf16[272,128]{1,0:T(8,128)(2,1)S(1)}, bf16[272,128]{1,0:T(8,128)(2,1)S(1)}, u32[]{:S(2)}, u32[]{:S(2)}) collective-permute-start(bf16[272,128]{1,0:T(8,128)(2,1)S(1)} %get-tuple-element.83), channel_id=1, source_target_pairs={{0,8},{1,9},{2,10},{3,11},{4,12},{5,13},{6,14},{7,15},{8,0},{9,1},... | collective-permute-start | bytes 208904 | tf_op jit(solution)/shard_map/ppermute | solution.py:482
  66.4 4.8 %collective-permute-start.5 = (bf16[272,128]{1,0:T(8,128)(2,1)S(1)}, bf16[272,128]{1,0:T(8,128)(2,1)S(1)}, u32[]{:S(2)}, u32[]{:S(2)}) collective-permute-start(bf16[272,128]{1,0:T(8,128)(2,1)S(1)} %get-tuple-element.82), channel_id=1, source_target_pairs={{0,16},{1,17},{2,18},{3,19},{4,20},{5,21},{6,22},{7,23},{8,24},{9,... | collective-permute-start | bytes 208904 | tf_op jit(solution)/shard_map/ppermute | solution.py:482
  66.8 8.3 %collective-permute-start.6 = (bf16[272,128]{1,0:T(8,128)(2,1)S(1)}, bf16[272,128]{1,0:T(8,128)(2,1)S(1)}, u32[]{:S(2)}, u32[]{:S(2)}) collective-permute-start(bf16[272,128]{1,0:T(8,128)(2,1)S(1)} %get-tuple-element.81), channel_id=1, source_target_pairs={{0,24},{1,25},{2,26},{3,27},{4,28},{5,29},{6,30},{7,31},{8,16},{9,... | collective-permute-start | bytes 208904 | tf_op jit(solution)/shard_map/ppermute | solution.py:482
  68.5 8.2 %collective-permute-start.14 = (bf16[288,128]{1,0:T(8,128)(2,1)S(1)}, bf16[288,128]{1,0:T(8,128)(2,1)S(1)}, u32[]{:S(2)}, u32[]{:S(2)}) collective-permute-start(bf16[288,128]{1,0:T(8,128)(2,1)S(1)} %get-tuple-element.80), channel_id=1, source_target_pairs={{0,2},{1,3},{2,0},{3,1},{4,6},{5,7},{6,4},{7,5},{8,10},{9,11},{10,... | collective-permute-start | bytes 221192 | tf_op jit(solution)/shard_map/ppermute | solution.py:482
  68.8 9.1 %collective-permute-start.15 = (bf16[288,128]{1,0:T(8,128)(2,1)S(1)}, bf16[288,128]{1,0:T(8,128)(2,1)S(1)}, u32[]{:S(2)}, u32[]{:S(2)}) collective-permute-start(bf16[288,128]{1,0:T(8,128)(2,1)S(1)} %get-tuple-element.79), channel_id=1, source_target_pairs={{0,4},{1,5},{2,6},{3,7},{4,0},{5,1},{6,2},{7,3},{8,12},{9,13},{10,... | collective-permute-start | bytes 221192 | tf_op jit(solution)/shard_map/ppermute | solution.py:482
  69.5 8.4 %collective-permute-start.16 = (bf16[288,128]{1,0:T(8,128)(2,1)S(1)}, bf16[288,128]{1,0:T(8,128)(2,1)S(1)}, u32[]{:S(2)}, u32[]{:S(2)}) collective-permute-start(bf16[288,128]{1,0:T(8,128)(2,1)S(1)} %get-tuple-element.78), channel_id=1, source_target_pairs={{0,6},{1,7},{2,4},{3,5},{4,2},{5,3},{6,0},{7,1},{8,14},{9,15},{10,... | collective-permute-start | bytes 221192 | tf_op jit(solution)/shard_map/ppermute | solution.py:482
  75.2 4.2 %collective-permute-start.8 = (bf16[272,128]{1,0:T(8,128)(2,1)S(1)}, bf16[272,128]{1,0:T(8,128)(2,1)S(1)}, u32[]{:S(2)}, u32[]{:S(2)}) collective-permute-start(bf16[272,128]{1,0:T(8,128)(2,1)S(1)} %get-tuple-element.74), channel_id=1, source_target_pairs={{0,8},{1,9},{2,10},{3,11},{4,12},{5,13},{6,14},{7,15},{8,0},{9,1},... | collective-permute-start | bytes 208904 | tf_op jit(solution)/shard_map/ppermute | solution.py:482
  75.3 5.4 %collective-permute-start.9 = (bf16[272,128]{1,0:T(8,128)(2,1)S(1)}, bf16[272,128]{1,0:T(8,128)(2,1)S(1)}, u32[]{:S(2)}, u32[]{:S(2)}) collective-permute-start(bf16[272,128]{1,0:T(8,128)(2,1)S(1)} %get-tuple-element.74), channel_id=1, source_target_pairs={{0,16},{1,17},{2,18},{3,19},{4,20},{5,21},{6,22},{7,23},{8,24},{9,... | collective-permute-start | bytes 208904 | tf_op jit(solution)/shard_map/ppermute | solution.py:482
  76.6 8.6 %collective-permute-start.10 = (bf16[272,128]{1,0:T(8,128)(2,1)S(1)}, bf16[272,128]{1,0:T(8,128)(2,1)S(1)}, u32[]{:S(2)}, u32[]{:S(2)}) collective-permute-start(bf16[272,128]{1,0:T(8,128)(2,1)S(1)} %get-tuple-element.74), channel_id=1, source_target_pairs={{0,24},{1,25},{2,26},{3,27},{4,28},{5,29},{6,30},{7,31},{8,16},{9,... | collective-permute-start | bytes 208904 | tf_op jit(solution)/shard_map/ppermute | solution.py:482
  78.0 7.8 %collective-permute-start.17 = (bf16[288,128]{1,0:T(8,128)(2,1)S(1)}, bf16[288,128]{1,0:T(8,128)(2,1)S(1)}, u32[]{:S(2)}, u32[]{:S(2)}) collective-permute-start(bf16[288,128]{1,0:T(8,128)(2,1)S(1)} %fusion.5), channel_id=1, source_target_pairs={{0,8},{1,9},{2,10},{3,11},{4,12},{5,13},{6,14},{7,15},{8,0},{9,1},... | collective-permute-start | bytes 221192 | tf_op jit(solution)/shard_map/ppermute | solution.py:482
  79.0 8.9 %collective-permute-start.18 = (bf16[288,128]{1,0:T(8,128)(2,1)S(1)}, bf16[288,128]{1,0:T(8,128)(2,1)S(1)}, u32[]{:S(2)}, u32[]{:S(2)}) collective-permute-start(bf16[288,128]{1,0:T(8,128)(2,1)S(1)} %fusion.5), channel_id=1, source_target_pairs={{0,16},{1,17},{2,18},{3,19},{4,20},{5,21},{6,22},{7,23},{8,24},{9,... | collective-permute-start | bytes 221192 | tf_op jit(solution)/shard_map/ppermute | solution.py:482
  79.4 10.8 %collective-permute-start.19 = (bf16[288,128]{1,0:T(8,128)(2,1)S(1)}, bf16[288,128]{1,0:T(8,128)(2,1)S(1)}, u32[]{:S(2)}, u32[]{:S(2)}) collective-permute-start(bf16[288,128]{1,0:T(8,128)(2,1)S(1)} %fusion.5), channel_id=1, source_target_pairs={{0,24},{1,25},{2,26},{3,27},{4,28},{5,29},{6,30},{7,31},{8,16},{9,... | collective-permute-start | bytes 221192 | tf_op jit(solution)/shard_map/ppermute | solution.py:482
  85.2 8.8 %collective-permute-start.11 = (bf16[1088,128]{1,0:T(8,128)(2,1)S(1)}, bf16[1088,128]{1,0:T(8,128)(2,1)S(1)}, u32[]{:S(2)}, u32[]{:S(2)}) collective-permute-start(bf16[1088,128]{1,0:T(8,128)(2,1)S(1)} %bitcast.54), channel_id=1, source_target_pairs={{0,2},{1,3},{2,0},{3,1},{4,6},{5,7},{6,4},{7,5},{8,10},{9,11},{10,... | collective-permute-start | bytes 835592 | tf_op jit(solution)/shard_map/ppermute | solution.py:482
  85.4 8.5 %collective-permute-start.12 = (bf16[1088,128]{1,0:T(8,128)(2,1)S(1)}, bf16[1088,128]{1,0:T(8,128)(2,1)S(1)}, u32[]{:S(2)}, u32[]{:S(2)}) collective-permute-start(bf16[1088,128]{1,0:T(8,128)(2,1)S(1)} %bitcast.55), channel_id=1, source_target_pairs={{0,4},{1,5},{2,6},{3,7},{4,0},{5,1},{6,2},{7,3},{8,12},{9,13},{10,... | collective-permute-start | bytes 835592 | tf_op jit(solution)/shard_map/ppermute | solution.py:482
  85.7 9.1 %collective-permute-start.13 = (bf16[1088,128]{1,0:T(8,128)(2,1)S(1)}, bf16[1088,128]{1,0:T(8,128)(2,1)S(1)}, u32[]{:S(2)}, u32[]{:S(2)}) collective-permute-start(bf16[1088,128]{1,0:T(8,128)(2,1)S(1)} %bitcast.56), channel_id=1, source_target_pairs={{0,6},{1,7},{2,4},{3,5},{4,2},{5,3},{6,0},{7,1},{8,14},{9,15},{10,... | collective-permute-start | bytes 835592 | tf_op jit(solution)/shard_map/ppermute | solution.py:482
  90.3 3.7 %collective-permute-start.20 = (bf16[288,128]{1,0:T(8,128)(2,1)S(1)}, bf16[288,128]{1,0:T(8,128)(2,1)S(1)}, u32[]{:S(2)}, u32[]{:S(2)}) collective-permute-start(bf16[288,128]{1,0:T(8,128)(2,1)S(1)} %add_convert_fusion.2), channel_id=1, source_target_pairs={{0,1},{1,0},{2,3},{3,2},{4,5},{5,4},{6,7},{7,6},{8,9},{9,8},{10,11... | collective-permute-start | bytes 221192 | tf_op jit(solution)/shard_map/ppermute | solution.py:482
  93.1 9.3 %collective-permute-start.21 = (bf16[1088,128]{1,0:T(8,128)(2,1)S(1)}, bf16[1088,128]{1,0:T(8,128)(2,1)S(1)}, u32[]{:S(2)}, u32[]{:S(2)}) collective-permute-start(bf16[1088,128]{1,0:T(8,128)(2,1)S(1)} %bitcast.57), channel_id=1, source_target_pairs={{0,1},{1,0},{2,3},{3,2},{4,5},{5,4},{6,7},{7,6},{8,9},{9,8},{10,11... | collective-permute-start | bytes 835592 | tf_op jit(solution)/shard_map/ppermute | solution.py:482
  94.8 7.7 %collective-permute-start.22 = (bf16[1088,128]{1,0:T(8,128)(2,1)S(1)}, bf16[1088,128]{1,0:T(8,128)(2,1)S(1)}, u32[]{:S(2)}, u32[]{:S(2)}) collective-permute-start(bf16[1088,128]{1,0:T(8,128)(2,1)S(1)} %collective-permute-done.11.refs_1_), channel_id=1, source_target_pairs={{0,1},{1,0},{2,3},{3,2},{4,5},{5,4},{6,7},{7,6},{8,9},{9,8},{10,11... | collective-permute-start | bytes 835592 | tf_op jit(solution)/shard_map/ppermute | solution.py:482
  100.5 3.2 %collective-permute-start.23 = (bf16[1088,128]{1,0:T(8,128)(2,1)S(1)}, bf16[1088,128]{1,0:T(8,128)(2,1)S(1)}, u32[]{:S(2)}, u32[]{:S(2)}) collective-permute-start(bf16[1088,128]{1,0:T(8,128)(2,1)S(1)} %collective-permute-done.12.refs_2_), channel_id=1, source_target_pairs={{0,1},{1,0},{2,3},{3,2},{4,5},{5,4},{6,7},{7,6},{8,9},{9,8},{10,11... | collective-permute-start | bytes 835592 | tf_op jit(solution)/shard_map/ppermute | solution.py:482
  100.5 3.2 %collective-permute-start.24 = (bf16[1088,128]{1,0:T(8,128)(2,1)S(1)}, bf16[1088,128]{1,0:T(8,128)(2,1)S(1)}, u32[]{:S(2)}, u32[]{:S(2)}) collective-permute-start(bf16[1088,128]{1,0:T(8,128)(2,1)S(1)} %collective-permute-done.13.refs_3_), channel_id=1, source_target_pairs={{0,1},{1,0},{2,3},{3,2},{4,5},{5,4},{6,7},{7,6},{8,9},{9,8},{10,11... | collective-permute-start | bytes 835592 | tf_op jit(solution)/shard_map/ppermute | solution.py:482
  101.0 5.7 %collective-permute-start.25 = (bf16[576,128]{1,0:T(8,128)(2,1)S(1)}, bf16[576,128]{1,0:T(8,128)(2,1)S(1)}, u32[]{:S(2)}, u32[]{:S(2)}) collective-permute-start(bf16[576,128]{1,0:T(8,128)(2,1)S(1)} %pad_maximum_fusion.refs_0_), channel_id=1, source_target_pairs={{0,2},{1,3},{2,0},{3,1},{4,6},{5,7},{6,4},{7,5},{8,10},{9,11},{10,... | collective-permute-start | bytes 442376 | tf_op jit(solution)/shard_map/ppermute | solution.py:482
  102.3 5.4 %collective-permute-start.26 = (bf16[576,128]{1,0:T(8,128)(2,1)S(1)}, bf16[576,128]{1,0:T(8,128)(2,1)S(1)}, u32[]{:S(2)}, u32[]{:S(2)}) collective-permute-start(bf16[576,128]{1,0:T(8,128)(2,1)S(1)} %pad_maximum_fusion.refs_0_), channel_id=1, source_target_pairs={{0,4},{1,5},{2,6},{3,7},{4,0},{5,1},{6,2},{7,3},{8,12},{9,13},{10,... | collective-permute-start | bytes 442376 | tf_op jit(solution)/shard_map/ppermute | solution.py:482
  102.5 7.9 %collective-permute-start.27 = (bf16[576,128]{1,0:T(8,128)(2,1)S(1)}, bf16[576,128]{1,0:T(8,128)(2,1)S(1)}, u32[]{:S(2)}, u32[]{:S(2)}) collective-permute-start(bf16[576,128]{1,0:T(8,128)(2,1)S(1)} %pad_maximum_fusion.refs_0_), channel_id=1, source_target_pairs={{0,6},{1,7},{2,4},{3,5},{4,2},{5,3},{6,0},{7,1},{8,14},{9,15},{10,... | collective-permute-start | bytes 442376 | tf_op jit(solution)/shard_map/ppermute | solution.py:482

commit v6 on v5

--- a/solution.py
+++ b/solution.py
@@ -11,6 +11,7 @@
 HEADS = 8
 NORM_EPS = 1e-06
 WIN_STEP = 8
+BYTE_STEP = 4
 LANES = 128
 VMEM_LIMIT = 28 * 2**20
 
@@ -162,10 +163,13 @@
     )(*args)
 
 
-def share_out(core_ref, halves_ref, keep_ref, send_ref):
-    mine = core_ref[0]
-    keep_ref[...] = halves_ref[mine]
-    send_ref[...] = halves_ref[1 - mine]
+def share_out(place_ref, halves_ref, keep_ref, send_ref):
+    mine, k = place_ref[0] & 1, place_ref[0] >> 1
+    rows = keep_ref.shape[0] // 4
+    for d in range(4):
+        at = pl.ds(pl.multiple_of((k ^ d) * rows, 16), rows)
+        keep_ref[d * rows : (d + 1) * rows, :] = halves_ref[mine, at, :]
+        send_ref[d * rows : (d + 1) * rows, :] = halves_ref[1 - mine, at, :]
 
 
 def session_kernel(
@@ -310,15 +314,20 @@
     )(*args)
 
 
-def add_by_value(codes_ref, dconv_ref, table_ref, w_rows, table_grad_ref):
-    packets = codes_ref.shape[2]
-    vocab = table_ref.shape[1]
+def add_by_value(codes_ref, dconv_ref, table_ref, w_ref, rows_ref, table_grad_ref, step):
+    places, positions, packets = codes_ref.shape
+    chan, vocab = table_ref.shape
     values = small_iota((vocab, packets), 0)
-    codes = codes_ref[0]
-    chosen = [onehot(codes[w : w + 1, :], values) for w in range(codes_ref.shape[1])]
-    by_value = dot_nn(jnp.concatenate(chosen, axis=1), dconv_ref[...]).astype(bf16)
-    table_grad_ref[...] += dot_nt(w_rows, by_value)
-    return dot_nn(table_ref[...], by_value).astype(bf16)
+    blocks = []
+    for i in range(places):
+        codes = codes_ref[i]
+        blocks.append(jnp.concatenate([onehot(codes[w : w + 1, :], values) for w in range(positions)], axis=1))
+    sums = dot_nn(jnp.concatenate(blocks, axis=0), dconv_ref[...]).astype(bf16)
+    for i in range(places):
+        by_value = sums[i * vocab : (i + 1) * vocab]
+        at = pl.ds(pl.multiple_of((step * places + i) * chan, chan), chan)
+        table_grad_ref[...] += dot_nt(w_ref[at, :], by_value)
+        rows_ref[at, :] = dot_nn(table_ref[...], by_value).astype(bf16)
 
 
 def conv_back_kernel(
@@ -353,8 +362,7 @@
             at = slice(first, first + packets)
             dconv_ref[at, :] = (demb * slope_ref[:, at].astype(f32).T).astype(bf16)
 
-    at = pl.ds(pl.multiple_of(j * chan, chan), chan)
-    rows_ref[at, :] = add_by_value(codes_ref, dconv_ref, table_ref, w_ref[at, :], table_grad_ref)
+    add_by_value(codes_ref, dconv_ref, table_ref, w_ref, rows_ref, table_grad_ref, j)
 
     @pl.when(j == pl.num_programs(0) - 1)
     def _():
@@ -376,11 +384,11 @@
 
 def conv_back(core, returned, owner, codes, slope, table_t, w_conv, gain_grad, capacity, half_rows):
     args = (returned, owner, codes, slope, table_t, w_conv, gain_grad)
-    specs = [whole(a) if a.ndim == 2 else pl.BlockSpec((1, *a.shape[1:]), lambda j: (j, 0, 0)) for a in args]
+    specs = [whole(a) if a.ndim == 2 else pl.BlockSpec((BYTE_STEP, *a.shape[1:]), lambda j: (j, 0, 0)) for a in args]
     half = jax.ShapeDtypeStruct((half_rows, LANES), bf16)
     return pl.pallas_call(
         functools.partial(conv_back_kernel, capacity),
-        grid=(KERNEL,),
+        grid=(KERNEL // BYTE_STEP,),
         in_specs=[pl.BlockSpec(memory_space=pltpu.SMEM), *specs],
         out_specs=[whole(half), whole(half)],
         out_shape=[half, half],
@@ -397,7 +405,7 @@
 
 
 def put_together(place_ref, piece_refs, halves_ref):
-    mine, k = place_ref[0], place_ref[1]
+    mine, k = place_ref[0] & 1, place_ref[0] >> 1
     count = 4
     rows = halves_ref.shape[1] // count
     for d in range(count):
@@ -512,7 +520,17 @@
         return terms[0].astype(bf16)
 
     def pair_sum(self, keep, send):
-        return (keep.astype(f32) + self.swap(send, self.levels[0], 1).astype(f32)).astype(bf16)
+        got = self.swap(send, self.levels[0], 1)
+        rows = keep.shape[0] // 4
+        cut = [slice(d * rows, (d + 1) * rows) for d in range(4)]
+        return [(keep[c].astype(f32) + got[c].astype(f32)).astype(bf16) for c in cut]
+
+    def quarter_sum(self, quarters, other):
+        got = after([self.swap(quarters[d], self.levels[1], d) for d in range(1, 4)], other)
+        total = quarters[0].astype(f32)
+        for g in got:
+            total = total + g.astype(f32)
+        return total.astype(bf16)
 
     def join(self, value):
         return jnp.concatenate([value, self.swap(value, self.levels[0], 1)], axis=0)
@@ -541,8 +559,7 @@
     window = w_conv.shape[0]
     vocab, chan = byte_table.shape
     sessions = class_label.shape[0]
-    core = devices.place(devices.levels[0]).reshape(1)
-    place = jnp.stack([devices.place(level) for level in devices.levels[:2]])
+    place = lax.rem(devices.index, 8).reshape(1)
 
     owner = owner_index.reshape(1, packets)
     table_t = byte_table.T
@@ -554,7 +571,7 @@
         ).reshape(rows.shape)
 
     logits, back, keep, send, gain_grad = session_layer(
-        core,
+        place,
         exchange(outgoing),
         class_label.reshape(1, sessions),
         norm_gain.reshape(1, width),
@@ -567,15 +584,15 @@
     used = window * width // (2 * LANES) + chan * vocab // (2 * LANES) + 16
     unit = 64
     half_rows = -(-used // unit) * unit
-    _, quad, *upper = devices.levels
+    _, _, *upper = devices.levels
     keep, send = conv_back(
-        core, after(exchange(back), early), owner, codes, slope, table_t, w_conv, gain_grad, capacity, half_rows
+        place, after(exchange(back), early), owner, codes, slope, table_t, w_conv, gain_grad, capacity, half_rows
     )
-    early = devices.scatter_sum(early, quad, keep)
+    early = devices.quarter_sum(early, keep)
     late = devices.pair_sum(keep, send)
     for level in upper:
         early = devices.scatter_sum(early, level, late)
-    late = devices.scatter_sum(late, quad, early)
+    late = devices.quarter_sum(late, early)
     for level in upper[::-1]:
         early = devices.gather(early, level)
     for level in upper:

time: 113 us -> 113 us (level)
  waiting for transfers between devices: 25.3 us -> 34.1 us
  starting transfers between devices: 43.2 us -> 38.3 us
  Pallas kernels: 36.6 us -> 33.3 us
    ppermute x28, waiting for transfers between devices: 16.3 us -> 24 us  [swap(): lax.ppermute(value, AXES, [(i, i + ((i // stride % size ^ d) - i // strid...]
    ppermute x28, starting transfers between devices: 33.4 us -> 28.5 us  [swap(): lax.ppermute(value, AXES, [(i, i + ((i // stride % size ^ d) - i // strid...]
    pallas_call x1, Pallas kernels: 13.3 us -> 11.5 us  [conv_back(): pl.pallas_call(functools.partial(conv_back_kernel, capacity), grid=(KERNE...]
    all_to_all x2, waiting for transfers between devices: 8.97 us -> 10.1 us  [exchange(): lax.all_to_all(rows.reshape(groups, capacity, rows.shape[1]), 'dp', split...]
  transfers between devices with their start and end apart: 30 -> 30, of which waited for: 10 -> 12; matrix products, arithmetic and copies ran while one was open for 3% -> 2% of each run, Pallas kernels for 15% -> 12%
where the time goes in v6:
time: 113 us; the launch traced here: 112 us
  starting transfers between devices  38.3 us (34%)
  waiting for transfers between devices  34.1 us (30%)
  Pallas kernels  33.3 us (29%)
  local copies, waits for them, and re-layouts  3.74 us (3%)
  other arithmetic  1.97 us (2%)
    ppermute x28, starting transfers between devices, swap(): lax.ppermute(value, AXES, [(i, i + ((i // stride % size ^ d) - i // strid...  28.5 us
    ppermute x28, waiting for transfers between devices, swap(): lax.ppermute(value, AXES, [(i, i + ((i // stride % size ^ d) - i // strid...  24 us
    pallas_call x1, Pallas kernels, conv_back(): pl.pallas_call(functools.partial(conv_back_kernel, capacity), grid=(KERNE...  11.5 us
    all_to_all x2, waiting for transfers between devices, exchange(): lax.all_to_all(rows.reshape(groups, capacity, rows.shape[1]), 'dp', split...  10.1 us
    all_to_all x2, starting transfers between devices, exchange(): lax.all_to_all(rows.reshape(groups, capacity, rows.shape[1]), 'dp', split...  9.8 us
    pallas_call x1, Pallas kernels, session_layer(): pl.pallas_call(session_kernel, in_specs=[pl.BlockSpec(memory_space=pltpu....  9.75 us
    pallas_call x1, Pallas kernels, embed(): pl.pallas_call(functools.partial(embed_kernel, capacity), grid=(steps,),...  8.45 us
    unnamed x20, local copies, waits for them, and re-layouts  3.62 us
  transfers between devices with their start and end apart: 30, of which 12 were waited for; matrix products, arithmetic and copies ran while one was open for 2% of the time, Pallas kernels for 12%

profile of v6, /device:TPU:11, one launch (start us, length us, event | category | flops | bytes accessed | tf_op | source)
XLA Modules:
  0.0 112.3 jit_solution(306418503593038581)
XLA Ops:
  0.7 8.4 %embed.1 = (bf16[256,640]{1,0:T(8,128)(2,1)}, bf16[512,4096]{1,0:T(8,128)(2,1)}, bf16[8,32,128]{2,1,0:T(8,128)(2,1)}) custom-call(s32[128,256]{1,0:T(8,128)} %bytes_ref.1, s32[1,128]{1,0:T(1,128)} %bitcast.40, s32[1,128]{1,0:T(1,128)} %bitcast.46, bf16[64,256]{1,0:T(8,128)(2,1)} %bitcast.38, bf16[512,512]{1,0:T(8,128)(2,1)} %w_ref.3), custom_call_target="tpu_custom_call" | custom-call | flops 10000000000 | bytes 5000000 | tf_op jit(solution)/shard_map/embed/pallas_call | solution.py:141
  9.1 5.7 %all-to-all-start = ((bf16[8,32,640]{2,1,0:T(8,128)(2,1)}), bf16[8,32,640]{2,1,0:T(8,128)(2,1)S(1)}, u32[]{:S(2)}, u32[]{:S(2)}) async-start(bf16[8,32,640]{2,1,0:T(8,128)(2,1)} %bitcast.45), calls=%async_computation | async-start | bytes 655360 | tf_op jit(solution)/shard_map/all_to_all | solution.py:569
  14.8 7.3 %all-to-all-done = bf16[8,32,640]{2,1,0:T(8,128)(2,1)S(1)} async-done(((bf16[8,32,640]{2,1,0:T(8,128)(2,1)}), bf16[8,32,640]{2,1,0:T(8,128)(2,1)S(1)}, u32[]{:S(2)}, u32[]{:S(2)}) %all-to-all-start) | async-done | bytes 327712 | tf_op jit(solution)/shard_map/all_to_all | solution.py:569
  22.2 1.4 %copy-done.5 = bf16[512,1536]{1,0:T(8,128)(2,1)S(1)} copy-done((bf16[512,1536]{1,0:T(8,128)(2,1)S(1)}, bf16[512,1536]{1,0:T(8,128)(2,1)}, u32[]{:S(2)}) %copy-start.5) | copy-done | bytes 1572888
  23.6 9.8 %session_layer.1 = (f32[16,128]{1,0:T(8,128)}, bf16[256,512]{1,0:T(8,128)(2,1)}, bf16[4352,128]{1,0:T(8,128)(2,1)S(1)}, bf16[4352,128]{1,0:T(8,128)(2,1)S(1)}, f32[16,128]{1,0:T(8,128)S(1)}) custom-call(s32[1]{0:T(128)} %bitcast.core_ref.place_ref, bf16[256,640]{1,0:T(8,128)(2,1)S(1)} %bitcast.32, s32[1,16]{1,0:T(1,128)S(1)} %bitcast.42, ...), custom_call_target="tpu_custom_call" | custom-call | flops 10000000000 | bytes 5000000 | tf_op jit(solution)/shard_map/session_layer/pallas_call | solution.py:293
  33.3 3.2 %collective-permute-start = (bf16[4352,128]{1,0:T(8,128)(2,1)S(1)}, bf16[4352,128]{1,0:T(8,128)(2,1)}, u32[]{:S(2)}, u32[]{:S(2)}) collective-permute-start(bf16[4352,128]{1,0:T(8,128)(2,1)S(1)} %get-tuple-element.43), channel_id=1, source_target_pairs={{0,1},{1,0},{2,3},{3,2},{4,5},{5,4},{6,7},{7,6},{8,9},{9,8},{10,11... | collective-permute-start | bytes 3342344 | tf_op jit(solution)/shard_map/ppermute | solution.py:490
  36.5 4.1 %all-to-all-start.1 = ((bf16[8,32,512]{2,1,0:T(8,128)(2,1)}), bf16[8,32,512]{2,1,0:T(8,128)(2,1)S(1)}, u32[]{:S(2)}, u32[]{:S(2)}) async-start(bf16[8,32,512]{2,1,0:T(8,128)(2,1)} %bitcast.7), calls=%async_computation.1 | async-start | bytes 524288 | tf_op jit(solution)/shard_map/all_to_all | solution.py:569
  40.7 1.6 %add_convert_fusion.4 = (bf16[1088,128]{1,0:T(8,128)(2,1)S(1)}, bf16[1088,128]{1,0:T(8,128)(2,1)S(1)}, bf16[1088,128]{1,0:T(8,128)(2,1)S(1)}, bf16[1088,128]{1,0:T(8,128)(2,1)S(1)}) fusion(bf16[4352,128]{1,0:T(8,128)(2,1)} %collective-permute-done, bf16[4352,128]{1,0:T(8,128)(2,1)S(1)} %get-tuple-element.42), kind=kLoop, calls=%fused_computation.4 | loop fusion | flops 2228224 | bytes 3342336 | tf_op jit(solution)/shard_map/convert_element_type | solution.py:526
  42.2 0.3 collective-permute-start.1
  42.5 1.2 %collective-permute-start.2 = (bf16[1088,128]{1,0:T(8,128)(2,1)S(1)}, bf16[1088,128]{1,0:T(8,128)(2,1)S(1)}, u32[]{:S(2)}, u32[]{:S(2)}) collective-permute-start(bf16[1088,128]{1,0:T(8,128)(2,1)S(1)} %get-tuple-element.77), channel_id=1, source_target_pairs={{0,4},{1,5},{2,6},{3,7},{4,0},{5,1},{6,2},{7,3},{8,12},{9,13},{10,... | collective-permute-start | bytes 835592 | tf_op jit(solution)/shard_map/ppermute | solution.py:490
  43.7 1.2 %collective-permute-start.3 = (bf16[1088,128]{1,0:T(8,128)(2,1)S(1)}, bf16[1088,128]{1,0:T(8,128)(2,1)S(1)}, u32[]{:S(2)}, u32[]{:S(2)}) collective-permute-start(bf16[1088,128]{1,0:T(8,128)(2,1)S(1)} %get-tuple-element.76), channel_id=1, source_target_pairs={{0,6},{1,7},{2,4},{3,5},{4,2},{5,3},{6,0},{7,1},{8,14},{9,15},{10,... | collective-permute-start | bytes 835592 | tf_op jit(solution)/shard_map/ppermute | solution.py:490
  44.9 2.8 %all-to-all-done.1 = bf16[8,32,512]{2,1,0:T(8,128)(2,1)S(1)} async-done(((bf16[8,32,512]{2,1,0:T(8,128)(2,1)}), bf16[8,32,512]{2,1,0:T(8,128)(2,1)S(1)}, u32[]{:S(2)}, u32[]{:S(2)}) %all-to-all-start.1) | async-done | bytes 262176 | tf_op jit(solution)/shard_map/all_to_all | solution.py:569
  47.8 2.2 %copy-done = bf16[512,4096]{1,0:T(8,128)(2,1)S(1)} copy-done((bf16[512,4096]{1,0:T(8,128)(2,1)S(1)}, bf16[512,4096]{1,0:T(8,128)(2,1)}, u32[]{:S(2)}) %copy-start) | copy-done | bytes 4194328
  49.9 11.5 %conv_back.1 = (bf16[1152,128]{1,0:T(8,128)(2,1)S(1)}, bf16[1152,128]{1,0:T(8,128)(2,1)S(1)}) custom-call(s32[1]{0:T(128)} %bitcast.core_ref.place_ref, bf16[256,512]{1,0:T(8,128)(2,1)S(1)} %bitcast.31, s32[1,128]{1,0:T(1,128)S(1)} %bitcast.41, bf16[8,32,128]{2,1,0:T(8,128)(2,1)S(1)} %copy-done.2, bf16[512,4096]{1,0:T(8,128)(2,1)S(1)} %copy-done, ...), custom_call_target="tpu_custom_call" | custom-call | flops 1000000000 | bytes 1000000 | tf_op jit(solution)/shard_map/conv_back/pallas_call | solution.py:389
  61.5 2.3 %collective-permute-start.7 = (bf16[1152,128]{1,0:T(8,128)(2,1)S(1)}, bf16[1152,128]{1,0:T(8,128)(2,1)S(1)}, u32[]{:S(2)}, u32[]{:S(2)}) collective-permute-start(bf16[1152,128]{1,0:T(8,128)(2,1)S(1)} %get-tuple-element.53), channel_id=1, source_target_pairs={{0,1},{1,0},{2,3},{3,2},{4,5},{5,4},{6,7},{7,6},{8,9},{9,8},{10,11... | collective-permute-start | bytes 884744 | tf_op jit(solution)/shard_map/ppermute | solution.py:490
  63.8 0.2 add_convert_fusion
  64.0 0.7 collective-permute-start.4
  64.6 0.4 collective-permute-start.5
  65.1 1.6 %collective-permute-start.6 = (bf16[272,128]{1,0:T(8,128)(2,1)S(1)}, bf16[272,128]{1,0:T(8,128)(2,1)S(1)}, u32[]{:S(2)}, u32[]{:S(2)}) collective-permute-start(bf16[272,128]{1,0:T(8,128)(2,1)S(1)} %get-tuple-element.83), channel_id=1, source_target_pairs={{0,24},{1,25},{2,26},{3,27},{4,28},{5,29},{6,30},{7,31},{8,16},{9,... | collective-permute-start | bytes 208904 | tf_op jit(solution)/shard_map/ppermute | solution.py:490
  66.7 0.1 add_convert_fusion.7
  66.8 0.3 collective-permute-start.14
  67.1 0.3 collective-permute-start.15
  67.4 0.4 collective-permute-done.4
  67.8 1.7 %collective-permute-start.16 = (bf16[288,128]{1,0:T(8,128)(2,1)S(1)}, bf16[288,128]{1,0:T(8,128)(2,1)S(1)}, u32[]{:S(2)}, u32[]{:S(2)}) collective-permute-start(bf16[288,128]{1,0:T(8,128)(2,1)S(1)} %get-tuple-element.79), channel_id=1, source_target_pairs={{0,6},{1,7},{2,4},{3,5},{4,2},{5,3},{6,0},{7,1},{8,14},{9,15},{10,... | collective-permute-start | bytes 221192 | tf_op jit(solution)/shard_map/ppermute | solution.py:490
  69.5 4.0 %collective-permute-done.6 = bf16[272,128]{1,0:T(8,128)(2,1)S(1)} collective-permute-done((bf16[272,128]{1,0:T(8,128)(2,1)S(1)}, bf16[272,128]{1,0:T(8,128)(2,1)S(1)}, u32[]{:S(2)}, u32[]{:S(2)}) %collective-permute-start.6) | collective-permute-done | bytes 69664 | tf_op jit(solution)/shard_map/ppermute | solution.py:490
  73.6 0.1 collective-permute-start.8
  73.7 1.2 %collective-permute-start.9 = (bf16[272,128]{1,0:T(8,128)(2,1)S(1)}, bf16[272,128]{1,0:T(8,128)(2,1)S(1)}, u32[]{:S(2)}, u32[]{:S(2)}) collective-permute-start(bf16[272,128]{1,0:T(8,128)(2,1)S(1)} %get-tuple-element.74), channel_id=1, source_target_pairs={{0,16},{1,17},{2,18},{3,19},{4,20},{5,21},{6,22},{7,23},{8,24},{9,... | collective-permute-start | bytes 208904 | tf_op jit(solution)/shard_map/ppermute | solution.py:490
  74.9 1.4 %collective-permute-start.10 = (bf16[272,128]{1,0:T(8,128)(2,1)S(1)}, bf16[272,128]{1,0:T(8,128)(2,1)S(1)}, u32[]{:S(2)}, u32[]{:S(2)}) collective-permute-start(bf16[272,128]{1,0:T(8,128)(2,1)S(1)} %get-tuple-element.74), channel_id=1, source_target_pairs={{0,24},{1,25},{2,26},{3,27},{4,28},{5,29},{6,30},{7,31},{8,16},{9,... | collective-permute-start | bytes 208904 | tf_op jit(solution)/shard_map/ppermute | solution.py:490
  76.4 1.0 collective-permute-start.17
  77.4 0.3 collective-permute-start.18
  77.7 1.4 %collective-permute-start.19 = (bf16[288,128]{1,0:T(8,128)(2,1)S(1)}, bf16[288,128]{1,0:T(8,128)(2,1)S(1)}, u32[]{:S(2)}, u32[]{:S(2)}) collective-permute-start(bf16[288,128]{1,0:T(8,128)(2,1)S(1)} %add_convert_fusion.6), channel_id=1, source_target_pairs={{0,24},{1,25},{2,26},{3,27},{4,28},{5,29},{6,30},{7,31},{8,16},{9,... | collective-permute-start | bytes 221192 | tf_op jit(solution)/shard_map/ppermute | solution.py:490
  79.1 6.8 %collective-permute-done.10 = bf16[272,128]{1,0:T(8,128)(2,1)S(1)} collective-permute-done((bf16[272,128]{1,0:T(8,128)(2,1)S(1)}, bf16[272,128]{1,0:T(8,128)(2,1)S(1)}, u32[]{:S(2)}, u32[]{:S(2)}) %collective-permute-start.10) | collective-permute-done | bytes 69664 | tf_op jit(solution)/shard_map/ppermute | solution.py:490
  85.9 0.3 collective-permute-start.11
  86.2 2.4 %collective-permute-start.13 = (bf16[1088,128]{1,0:T(8,128)(2,1)S(1)}, bf16[1088,128]{1,0:T(8,128)(2,1)S(1)}, u32[]{:S(2)}, u32[]{:S(2)}) collective-permute-start(bf16[1088,128]{1,0:T(8,128)(2,1)S(1)} %bitcast.35), channel_id=1, source_target_pairs={{0,6},{1,7},{2,4},{3,5},{4,2},{5,3},{6,0},{7,1},{8,14},{9,15},{10,... | collective-permute-start | bytes 835592 | tf_op jit(solution)/shard_map/ppermute | solution.py:490
  88.6 0.4 collective-permute-done.19
  89.1 2.3 %collective-permute-start.20 = (bf16[288,128]{1,0:T(8,128)(2,1)S(1)}, bf16[288,128]{1,0:T(8,128)(2,1)S(1)}, u32[]{:S(2)}, u32[]{:S(2)}) collective-permute-start(bf16[288,128]{1,0:T(8,128)(2,1)S(1)} %add_convert_fusion.5), channel_id=1, source_target_pairs={{0,1},{1,0},{2,3},{3,2},{4,5},{5,4},{6,7},{7,6},{8,9},{9,8},{10,11... | collective-permute-start | bytes 221192 | tf_op jit(solution)/shard_map/ppermute | solution.py:490
  91.3 0.1 collective-permute-start.21
  91.4 0.8 collective-permute-done.20
  92.3 7.3 %collective-permute-done.12.refs_2_ = bf16[1088,128]{1,0:T(8,128)(2,1)S(1)} collective-permute-done((bf16[1088,128]{1,0:T(8,128)(2,1)S(1)}, bf16[1088,128]{1,0:T(8,128)(2,1)S(1)}, u32[]{:S(2)}, u32[]{:S(2)}) %collective-permute-start.12) | collective-permute-done | bytes 278560 | tf_op jit(solution)/shard_map/ppermute | solution.py:490
  99.6 1.7 %collective-permute-start.22 = (bf16[1088,128]{1,0:T(8,128)(2,1)S(1)}, bf16[1088,128]{1,0:T(8,128)(2,1)S(1)}, u32[]{:S(2)}, u32[]{:S(2)}) collective-permute-start(bf16[1088,128]{1,0:T(8,128)(2,1)S(1)} %collective-permute-done.11.refs_1_), channel_id=1, source_target_pairs={{0,1},{1,0},{2,3},{3,2},{4,5},{5,4},{6,7},{7,6},{8,9},{9,8},{10,11... | collective-permute-start | bytes 835592 | tf_op jit(solution)/shard_map/ppermute | solution.py:490
  101.3 0.5 collective-permute-start.24
  101.8 1.2 %collective-permute-start.25 = (bf16[576,128]{1,0:T(8,128)(2,1)S(1)}, bf16[576,128]{1,0:T(8,128)(2,1)S(1)}, u32[]{:S(2)}, u32[]{:S(2)}) collective-permute-start(bf16[576,128]{1,0:T(8,128)(2,1)S(1)} %pad_maximum_fusion.refs_0_), channel_id=1, source_target_pairs={{0,2},{1,3},{2,0},{3,1},{4,6},{5,7},{6,4},{7,5},{8,10},{9,11},{10,... | collective-permute-start | bytes 442376 | tf_op jit(solution)/shard_map/ppermute | solution.py:490
  103.0 1.4 %collective-permute-start.27 = (bf16[576,128]{1,0:T(8,128)(2,1)S(1)}, bf16[576,128]{1,0:T(8,128)(2,1)S(1)}, u32[]{:S(2)}, u32[]{:S(2)}) collective-permute-start(bf16[576,128]{1,0:T(8,128)(2,1)S(1)} %pad_maximum_fusion.refs_0_), channel_id=1, source_target_pairs={{0,6},{1,7},{2,4},{3,5},{4,2},{5,3},{6,0},{7,1},{8,14},{9,15},{10,... | collective-permute-start | bytes 442376 | tf_op jit(solution)/shard_map/ppermute | solution.py:490
  104.4 2.4 %early_out.1 = (f32[512,1536]{1,0:T(8,128)}, f32[512,512]{1,0:T(8,128)}, f32[512,128]{1,0:T(8,128)}) custom-call(s32[1]{0:T(128)} %bitcast.core_ref.place_ref, bf16[1088,128]{1,0:T(8,128)(2,1)S(1)} %bitcast.37, bf16[1088,128]{1,0:T(8,128)(2,1)S(1)} %collective-permute-done.11.refs_1_, bf16[1088,128]{1,0:T(8,128)(2,1)S(1)} %collective-permute-done.12.refs_2_, ...), custom_call_target="tpu_custom_call" | custom-call | flops 1000000000 | bytes 5000000 | tf_op jit(solution)/shard_map/early_out/pallas_call | solution.py:458
  106.9 0.4 collective-permute-done.25.refs_1_
  107.3 1.1 %collective-permute-done.26.refs_2_ = bf16[576,128]{1,0:T(8,128)(2,1)S(1)} collective-permute-done((bf16[576,128]{1,0:T(8,128)(2,1)S(1)}, bf16[576,128]{1,0:T(8,128)(2,1)S(1)}, u32[]{:S(2)}, u32[]{:S(2)}) %collective-permute-start.26) | collective-permute-done | bytes 147488 | tf_op jit(solution)/shard_map/ppermute | solution.py:490
  108.4 2.7 %collective-permute-done.27.refs_3_ = bf16[576,128]{1,0:T(8,128)(2,1)S(1)} collective-permute-done((bf16[576,128]{1,0:T(8,128)(2,1)S(1)}, bf16[576,128]{1,0:T(8,128)(2,1)S(1)}, u32[]{:S(2)}, u32[]{:S(2)}) %collective-permute-start.27) | collective-permute-done | bytes 147488 | tf_op jit(solution)/shard_map/ppermute | solution.py:490
  111.1 1.2 %late_out.1 = (f32[512,512]{1,0:T(8,128)}, f32[64,256]{1,0:T(8,128)}, f32[1,512]{1,0:T(1,128)}) custom-call(s32[1]{0:T(128)} %bitcast.core_ref.place_ref, bf16[576,128]{1,0:T(8,128)(2,1)S(1)} %pad_maximum_fusion.refs_0_, bf16[576,128]{1,0:T(8,128)(2,1)S(1)} %collective-permute-done.25.refs_1_, bf16[576,128]{1,0:T(8,128)(2,1)S(1)} %collective-permute-done.26.refs_2_, ...), custom_call_target="tpu_custom_call" | custom-call | flops 1000000000 | bytes 5000000 | tf_op jit(solution)/shard_map/late_out/pallas_call | solution.py:458
  (50 shorter events, 0.4 us)
Async XLA Ops:
  0.6 14.2 %copy-start.9 = (bf16[512]{0:T(512)(128)(2,1)S(1)}, bf16[512]{0:T(512)(128)(2,1)}, u32[]{:S(2)}) copy-start(bf16[512]{0:T(512)(128)(2,1)} %param.16) | copy-start | bytes 3076
  0.6 21.5 %copy-start.6 = (bf16[512,512]{1,0:T(8,128)(2,1)S(1)}, bf16[512,512]{1,0:T(8,128)(2,1)}, u32[]{:S(2)}) copy-start(bf16[512,512]{1,0:T(8,128)(2,1)} %wo_ref.1) | copy-start | bytes 1572868
  0.7 21.5 %copy-start.7 = (bf16[512,128]{1,0:T(8,128)(2,1)S(1)}, bf16[512,128]{1,0:T(8,128)(2,1)}, u32[]{:S(2)}) copy-start(bf16[512,128]{1,0:T(8,128)(2,1)} %wh_ref.1) | copy-start | bytes 393220
  0.7 21.5 %copy-start.8 = (s32[16]{0:T(128)S(1)}, s32[16]{0:T(128)}, u32[]{:S(2)}) copy-start(s32[16]{0:T(128)} %param.13) | copy-start | bytes 196
  9.1 13.0 %all-to-all-start = ((bf16[8,32,640]{2,1,0:T(8,128)(2,1)}), bf16[8,32,640]{2,1,0:T(8,128)(2,1)S(1)}, u32[]{:S(2)}, u32[]{:S(2)}) async-start(bf16[8,32,640]{2,1,0:T(8,128)(2,1)} %bitcast.45), calls=%async_computation | async-start | bytes 655360 | tf_op jit(solution)/shard_map/all_to_all | solution.py:569
  22.2 1.4 %copy-start.5 = (bf16[512,1536]{1,0:T(8,128)(2,1)S(1)}, bf16[512,1536]{1,0:T(8,128)(2,1)}, u32[]{:S(2)}) copy-start(bf16[512,1536]{1,0:T(8,128)(2,1)} %wp_ref.1) | copy-start | bytes 4718596
  33.3 7.3 %collective-permute-start = (bf16[4352,128]{1,0:T(8,128)(2,1)S(1)}, bf16[4352,128]{1,0:T(8,128)(2,1)}, u32[]{:S(2)}, u32[]{:S(2)}) collective-permute-start(bf16[4352,128]{1,0:T(8,128)(2,1)S(1)} %get-tuple-element.43), channel_id=1, source_target_pairs={{0,1},{1,0},{2,3},{3,2},{4,5},{5,4},{6,7},{7,6},{8,9},{9,8},{10,11... | collective-permute-start | bytes 3342344 | tf_op jit(solution)/shard_map/ppermute | solution.py:490
  36.5 11.2 %all-to-all-start.1 = ((bf16[8,32,512]{2,1,0:T(8,128)(2,1)}), bf16[8,32,512]{2,1,0:T(8,128)(2,1)S(1)}, u32[]{:S(2)}, u32[]{:S(2)}) async-start(bf16[8,32,512]{2,1,0:T(8,128)(2,1)} %bitcast.7), calls=%async_computation.1 | async-start | bytes 524288 | tf_op jit(solution)/shard_map/all_to_all | solution.py:569
  40.6 7.1 %copy-start.1 = (bf16[512,512]{1,0:T(8,128)(2,1)S(1)}, bf16[512,512]{1,0:T(8,128)(2,1)}, u32[]{:S(2)}) copy-start(bf16[512,512]{1,0:T(8,128)(2,1)} %w_ref.3) | copy-start | bytes 1572868
  40.6 7.1 %copy-start.2 = (bf16[8,32,128]{2,1,0:T(8,128)(2,1)S(1)}, bf16[8,32,128]{2,1,0:T(8,128)(2,1)}, u32[]{:S(2)}) copy-start(bf16[8,32,128]{2,1,0:T(8,128)(2,1)} %get-tuple-element.46.codes_ref) | copy-start | bytes 196612
  40.6 7.1 %copy-start.3 = (bf16[256,64]{0,1:T(8,128)(2,1)S(1)}, bf16[256,64]{0,1:T(8,128)(2,1)}, u32[]{:S(2)}) copy-start(bf16[256,64]{0,1:T(8,128)(2,1)} %param.14) | copy-start | bytes 98308
  40.6 7.1 %copy-start.4 = (s32[128]{0:T(128)S(1)}, s32[128]{0:T(128)}, u32[]{:S(2)}) copy-start(s32[128]{0:T(128)} %param.11) | copy-start | bytes 1540
  42.2 21.5 %collective-permute-start.1 = (bf16[1088,128]{1,0:T(8,128)(2,1)S(1)}, bf16[1088,128]{1,0:T(8,128)(2,1)S(1)}, u32[]{:S(2)}, u32[]{:S(2)}) collective-permute-start(bf16[1088,128]{1,0:T(8,128)(2,1)S(1)} %get-tuple-element.78), channel_id=1, source_target_pairs={{0,2},{1,3},{2,0},{3,1},{4,6},{5,7},{6,4},{7,5},{8,10},{9,11},{10,... | collective-permute-start | bytes 835592 | tf_op jit(solution)/shard_map/ppermute | solution.py:490
  42.5 21.2 %collective-permute-start.2 = (bf16[1088,128]{1,0:T(8,128)(2,1)S(1)}, bf16[1088,128]{1,0:T(8,128)(2,1)S(1)}, u32[]{:S(2)}, u32[]{:S(2)}) collective-permute-start(bf16[1088,128]{1,0:T(8,128)(2,1)S(1)} %get-tuple-element.77), channel_id=1, source_target_pairs={{0,4},{1,5},{2,6},{3,7},{4,0},{5,1},{6,2},{7,3},{8,12},{9,13},{10,... | collective-permute-start | bytes 835592 | tf_op jit(solution)/shard_map/ppermute | solution.py:490
  43.7 20.0 %collective-permute-start.3 = (bf16[1088,128]{1,0:T(8,128)(2,1)S(1)}, bf16[1088,128]{1,0:T(8,128)(2,1)S(1)}, u32[]{:S(2)}, u32[]{:S(2)}) collective-permute-start(bf16[1088,128]{1,0:T(8,128)(2,1)S(1)} %get-tuple-element.76), channel_id=1, source_target_pairs={{0,6},{1,7},{2,4},{3,5},{4,2},{5,3},{6,0},{7,1},{8,14},{9,15},{10,... | collective-permute-start | bytes 835592 | tf_op jit(solution)/shard_map/ppermute | solution.py:490
  47.8 2.2 %copy-start = (bf16[512,4096]{1,0:T(8,128)(2,1)S(1)}, bf16[512,4096]{1,0:T(8,128)(2,1)}, u32[]{:S(2)}) copy-start(bf16[512,4096]{1,0:T(8,128)(2,1)} %get-tuple-element.47.slope_ref) | copy-start | bytes 12582916
  61.5 5.2 %collective-permute-start.7 = (bf16[1152,128]{1,0:T(8,128)(2,1)S(1)}, bf16[1152,128]{1,0:T(8,128)(2,1)S(1)}, u32[]{:S(2)}, u32[]{:S(2)}) collective-permute-start(bf16[1152,128]{1,0:T(8,128)(2,1)S(1)} %get-tuple-element.53), channel_id=1, source_target_pairs={{0,1},{1,0},{2,3},{3,2},{4,5},{5,4},{6,7},{7,6},{8,9},{9,8},{10,11... | collective-permute-start | bytes 884744 | tf_op jit(solution)/shard_map/ppermute | solution.py:490
  64.0 3.8 %collective-permute-start.4 = (bf16[272,128]{1,0:T(8,128)(2,1)S(1)}, bf16[272,128]{1,0:T(8,128)(2,1)S(1)}, u32[]{:S(2)}, u32[]{:S(2)}) collective-permute-start(bf16[272,128]{1,0:T(8,128)(2,1)S(1)} %get-tuple-element.85), channel_id=1, source_target_pairs={{0,8},{1,9},{2,10},{3,11},{4,12},{5,13},{6,14},{7,15},{8,0},{9,1},... | collective-permute-start | bytes 208904 | tf_op jit(solution)/shard_map/ppermute | solution.py:490
  64.6 4.9 %collective-permute-start.5 = (bf16[272,128]{1,0:T(8,128)(2,1)S(1)}, bf16[272,128]{1,0:T(8,128)(2,1)S(1)}, u32[]{:S(2)}, u32[]{:S(2)}) collective-permute-start(bf16[272,128]{1,0:T(8,128)(2,1)S(1)} %get-tuple-element.84), channel_id=1, source_target_pairs={{0,16},{1,17},{2,18},{3,19},{4,20},{5,21},{6,22},{7,23},{8,24},{9,... | collective-permute-start | bytes 208904 | tf_op jit(solution)/shard_map/ppermute | solution.py:490
  65.1 8.4 %collective-permute-start.6 = (bf16[272,128]{1,0:T(8,128)(2,1)S(1)}, bf16[272,128]{1,0:T(8,128)(2,1)S(1)}, u32[]{:S(2)}, u32[]{:S(2)}) collective-permute-start(bf16[272,128]{1,0:T(8,128)(2,1)S(1)} %get-tuple-element.83), channel_id=1, source_target_pairs={{0,24},{1,25},{2,26},{3,27},{4,28},{5,29},{6,30},{7,31},{8,16},{9,... | collective-permute-start | bytes 208904 | tf_op jit(solution)/shard_map/ppermute | solution.py:490
  66.8 8.2 %collective-permute-start.14 = (bf16[288,128]{1,0:T(8,128)(2,1)S(1)}, bf16[288,128]{1,0:T(8,128)(2,1)S(1)}, u32[]{:S(2)}, u32[]{:S(2)}) collective-permute-start(bf16[288,128]{1,0:T(8,128)(2,1)S(1)} %get-tuple-element.81), channel_id=1, source_target_pairs={{0,2},{1,3},{2,0},{3,1},{4,6},{5,7},{6,4},{7,5},{8,10},{9,11},{10,... | collective-permute-start | bytes 221192 | tf_op jit(solution)/shard_map/ppermute | solution.py:490
  67.1 9.2 %collective-permute-start.15 = (bf16[288,128]{1,0:T(8,128)(2,1)S(1)}, bf16[288,128]{1,0:T(8,128)(2,1)S(1)}, u32[]{:S(2)}, u32[]{:S(2)}) collective-permute-start(bf16[288,128]{1,0:T(8,128)(2,1)S(1)} %get-tuple-element.80), channel_id=1, source_target_pairs={{0,4},{1,5},{2,6},{3,7},{4,0},{5,1},{6,2},{7,3},{8,12},{9,13},{10,... | collective-permute-start | bytes 221192 | tf_op jit(solution)/shard_map/ppermute | solution.py:490
  67.8 8.5 %collective-permute-start.16 = (bf16[288,128]{1,0:T(8,128)(2,1)S(1)}, bf16[288,128]{1,0:T(8,128)(2,1)S(1)}, u32[]{:S(2)}, u32[]{:S(2)}) collective-permute-start(bf16[288,128]{1,0:T(8,128)(2,1)S(1)} %get-tuple-element.79), channel_id=1, source_target_pairs={{0,6},{1,7},{2,4},{3,5},{4,2},{5,3},{6,0},{7,1},{8,14},{9,15},{10,... | collective-permute-start | bytes 221192 | tf_op jit(solution)/shard_map/ppermute | solution.py:490
  73.6 4.1 %collective-permute-start.8 = (bf16[272,128]{1,0:T(8,128)(2,1)S(1)}, bf16[272,128]{1,0:T(8,128)(2,1)S(1)}, u32[]{:S(2)}, u32[]{:S(2)}) collective-permute-start(bf16[272,128]{1,0:T(8,128)(2,1)S(1)} %get-tuple-element.74), channel_id=1, source_target_pairs={{0,8},{1,9},{2,10},{3,11},{4,12},{5,13},{6,14},{7,15},{8,0},{9,1},... | collective-permute-start | bytes 208904 | tf_op jit(solution)/shard_map/ppermute | solution.py:490
  73.7 5.4 %collective-permute-start.9 = (bf16[272,128]{1,0:T(8,128)(2,1)S(1)}, bf16[272,128]{1,0:T(8,128)(2,1)S(1)}, u32[]{:S(2)}, u32[]{:S(2)}) collective-permute-start(bf16[272,128]{1,0:T(8,128)(2,1)S(1)} %get-tuple-element.74), channel_id=1, source_target_pairs={{0,16},{1,17},{2,18},{3,19},{4,20},{5,21},{6,22},{7,23},{8,24},{9,... | collective-permute-start | bytes 208904 | tf_op jit(solution)/shard_map/ppermute | solution.py:490
  74.9 11.0 %collective-permute-start.10 = (bf16[272,128]{1,0:T(8,128)(2,1)S(1)}, bf16[272,128]{1,0:T(8,128)(2,1)S(1)}, u32[]{:S(2)}, u32[]{:S(2)}) collective-permute-start(bf16[272,128]{1,0:T(8,128)(2,1)S(1)} %get-tuple-element.74), channel_id=1, source_target_pairs={{0,24},{1,25},{2,26},{3,27},{4,28},{5,29},{6,30},{7,31},{8,16},{9,... | collective-permute-start | bytes 208904 | tf_op jit(solution)/shard_map/ppermute | solution.py:490
  76.4 9.9 %collective-permute-start.17 = (bf16[288,128]{1,0:T(8,128)(2,1)S(1)}, bf16[288,128]{1,0:T(8,128)(2,1)S(1)}, u32[]{:S(2)}, u32[]{:S(2)}) collective-permute-start(bf16[288,128]{1,0:T(8,128)(2,1)S(1)} %add_convert_fusion.6), channel_id=1, source_target_pairs={{0,8},{1,9},{2,10},{3,11},{4,12},{5,13},{6,14},{7,15},{8,0},{9,1},... | collective-permute-start | bytes 221192 | tf_op jit(solution)/shard_map/ppermute | solution.py:490
  77.4 11.2 %collective-permute-start.18 = (bf16[288,128]{1,0:T(8,128)(2,1)S(1)}, bf16[288,128]{1,0:T(8,128)(2,1)S(1)}, u32[]{:S(2)}, u32[]{:S(2)}) collective-permute-start(bf16[288,128]{1,0:T(8,128)(2,1)S(1)} %add_convert_fusion.6), channel_id=1, source_target_pairs={{0,16},{1,17},{2,18},{3,19},{4,20},{5,21},{6,22},{7,23},{8,24},{9,... | collective-permute-start | bytes 221192 | tf_op jit(solution)/shard_map/ppermute | solution.py:490
  77.7 11.3 %collective-permute-start.19 = (bf16[288,128]{1,0:T(8,128)(2,1)S(1)}, bf16[288,128]{1,0:T(8,128)(2,1)S(1)}, u32[]{:S(2)}, u32[]{:S(2)}) collective-permute-start(bf16[288,128]{1,0:T(8,128)(2,1)S(1)} %add_convert_fusion.6), channel_id=1, source_target_pairs={{0,24},{1,25},{2,26},{3,27},{4,28},{5,29},{6,30},{7,31},{8,16},{9,... | collective-permute-start | bytes 221192 | tf_op jit(solution)/shard_map/ppermute | solution.py:490
  85.9 6.4 %collective-permute-start.11 = (bf16[1088,128]{1,0:T(8,128)(2,1)S(1)}, bf16[1088,128]{1,0:T(8,128)(2,1)S(1)}, u32[]{:S(2)}, u32[]{:S(2)}) collective-permute-start(bf16[1088,128]{1,0:T(8,128)(2,1)S(1)} %bitcast.33), channel_id=1, source_target_pairs={{0,2},{1,3},{2,0},{3,1},{4,6},{5,7},{6,4},{7,5},{8,10},{9,11},{10,... | collective-permute-start | bytes 835592 | tf_op jit(solution)/shard_map/ppermute | solution.py:490
  86.2 13.4 %collective-permute-start.12 = (bf16[1088,128]{1,0:T(8,128)(2,1)S(1)}, bf16[1088,128]{1,0:T(8,128)(2,1)S(1)}, u32[]{:S(2)}, u32[]{:S(2)}) collective-permute-start(bf16[1088,128]{1,0:T(8,128)(2,1)S(1)} %bitcast.34), channel_id=1, source_target_pairs={{0,4},{1,5},{2,6},{3,7},{4,0},{5,1},{6,2},{7,3},{8,12},{9,13},{10,... | collective-permute-start | bytes 835592 | tf_op jit(solution)/shard_map/ppermute | solution.py:490
  86.2 13.4 %collective-permute-start.13 = (bf16[1088,128]{1,0:T(8,128)(2,1)S(1)}, bf16[1088,128]{1,0:T(8,128)(2,1)S(1)}, u32[]{:S(2)}, u32[]{:S(2)}) collective-permute-start(bf16[1088,128]{1,0:T(8,128)(2,1)S(1)} %bitcast.35), channel_id=1, source_target_pairs={{0,6},{1,7},{2,4},{3,5},{4,2},{5,3},{6,0},{7,1},{8,14},{9,15},{10,... | collective-permute-start | bytes 835592 | tf_op jit(solution)/shard_map/ppermute | solution.py:490
  89.1 3.2 %collective-permute-start.20 = (bf16[288,128]{1,0:T(8,128)(2,1)S(1)}, bf16[288,128]{1,0:T(8,128)(2,1)S(1)}, u32[]{:S(2)}, u32[]{:S(2)}) collective-permute-start(bf16[288,128]{1,0:T(8,128)(2,1)S(1)} %add_convert_fusion.5), channel_id=1, source_target_pairs={{0,1},{1,0},{2,3},{3,2},{4,5},{5,4},{6,7},{7,6},{8,9},{9,8},{10,11... | collective-permute-start | bytes 221192 | tf_op jit(solution)/shard_map/ppermute | solution.py:490
  91.3 11.6 %collective-permute-start.21 = (bf16[1088,128]{1,0:T(8,128)(2,1)S(1)}, bf16[1088,128]{1,0:T(8,128)(2,1)S(1)}, u32[]{:S(2)}, u32[]{:S(2)}) collective-permute-start(bf16[1088,128]{1,0:T(8,128)(2,1)S(1)} %bitcast.36), channel_id=1, source_target_pairs={{0,1},{1,0},{2,3},{3,2},{4,5},{5,4},{6,7},{7,6},{8,9},{9,8},{10,11... | collective-permute-start | bytes 835592 | tf_op jit(solution)/shard_map/ppermute | solution.py:490
  99.6 3.4 %collective-permute-start.22 = (bf16[1088,128]{1,0:T(8,128)(2,1)S(1)}, bf16[1088,128]{1,0:T(8,128)(2,1)S(1)}, u32[]{:S(2)}, u32[]{:S(2)}) collective-permute-start(bf16[1088,128]{1,0:T(8,128)(2,1)S(1)} %collective-permute-done.11.refs_1_), channel_id=1, source_target_pairs={{0,1},{1,0},{2,3},{3,2},{4,5},{5,4},{6,7},{7,6},{8,9},{9,8},{10,11... | collective-permute-start | bytes 835592 | tf_op jit(solution)/shard_map/ppermute | solution.py:490
  101.3 3.2 %collective-permute-start.23 = (bf16[1088,128]{1,0:T(8,128)(2,1)S(1)}, bf16[1088,128]{1,0:T(8,128)(2,1)S(1)}, u32[]{:S(2)}, u32[]{:S(2)}) collective-permute-start(bf16[1088,128]{1,0:T(8,128)(2,1)S(1)} %collective-permute-done.12.refs_2_), channel_id=1, source_target_pairs={{0,1},{1,0},{2,3},{3,2},{4,5},{5,4},{6,7},{7,6},{8,9},{9,8},{10,11... | collective-permute-start | bytes 835592 | tf_op jit(solution)/shard_map/ppermute | solution.py:490
  101.3 3.2 %collective-permute-start.24 = (bf16[1088,128]{1,0:T(8,128)(2,1)S(1)}, bf16[1088,128]{1,0:T(8,128)(2,1)S(1)}, u32[]{:S(2)}, u32[]{:S(2)}) collective-permute-start(bf16[1088,128]{1,0:T(8,128)(2,1)S(1)} %collective-permute-done.13.refs_3_), channel_id=1, source_target_pairs={{0,1},{1,0},{2,3},{3,2},{4,5},{5,4},{6,7},{7,6},{8,9},{9,8},{10,11... | collective-permute-start | bytes 835592 | tf_op jit(solution)/shard_map/ppermute | solution.py:490
  101.8 5.5 %collective-permute-start.25 = (bf16[576,128]{1,0:T(8,128)(2,1)S(1)}, bf16[576,128]{1,0:T(8,128)(2,1)S(1)}, u32[]{:S(2)}, u32[]{:S(2)}) collective-permute-start(bf16[576,128]{1,0:T(8,128)(2,1)S(1)} %pad_maximum_fusion.refs_0_), channel_id=1, source_target_pairs={{0,2},{1,3},{2,0},{3,1},{4,6},{5,7},{6,4},{7,5},{8,10},{9,11},{10,... | collective-permute-start | bytes 442376 | tf_op jit(solution)/shard_map/ppermute | solution.py:490
  103.0 5.4 %collective-permute-start.26 = (bf16[576,128]{1,0:T(8,128)(2,1)S(1)}, bf16[576,128]{1,0:T(8,128)(2,1)S(1)}, u32[]{:S(2)}, u32[]{:S(2)}) collective-permute-start(bf16[576,128]{1,0:T(8,128)(2,1)S(1)} %pad_maximum_fusion.refs_0_), channel_id=1, source_target_pairs={{0,4},{1,5},{2,6},{3,7},{4,0},{5,1},{6,2},{7,3},{8,12},{9,13},{10,... | collective-permute-start | bytes 442376 | tf_op jit(solution)/shard_map/ppermute | solution.py:490
  103.0 8.1 %collective-permute-start.27 = (bf16[576,128]{1,0:T(8,128)(2,1)S(1)}, bf16[576,128]{1,0:T(8,128)(2,1)S(1)}, u32[]{:S(2)}, u32[]{:S(2)}) collective-permute-start(bf16[576,128]{1,0:T(8,128)(2,1)S(1)} %pad_maximum_fusion.refs_0_), channel_id=1, source_target_pairs={{0,6},{1,7},{2,4},{3,5},{4,2},{5,3},{6,0},{7,1},{8,14},{9,15},{10,... | collective-permute-start | bytes 442376 | tf_op jit(solution)/shard_map/ppermute | solution.py:490

commit v7 on v6

--- a/solution.py
+++ b/solution.py
@@ -164,7 +164,7 @@
 
 
 def share_out(place_ref, halves_ref, keep_ref, send_ref):
-    mine, k = place_ref[0] & 1, place_ref[0] >> 1
+    mine, k = place_ref[0], place_ref[1]
     rows = keep_ref.shape[0] // 4
     for d in range(4):
         at = pl.ds(pl.multiple_of((k ^ d) * rows, 16), rows)
@@ -405,7 +405,7 @@
 
 
 def put_together(place_ref, piece_refs, halves_ref):
-    mine, k = place_ref[0] & 1, place_ref[0] >> 1
+    mine, k = place_ref[0], place_ref[1]
     count = 4
     rows = halves_ref.shape[1] // count
     for d in range(count):
@@ -559,7 +559,7 @@
     window = w_conv.shape[0]
     vocab, chan = byte_table.shape
     sessions = class_label.shape[0]
-    place = lax.rem(devices.index, 8).reshape(1)
+    place = jnp.stack([devices.place(level) for level in devices.levels[:2]])
 
     owner = owner_index.reshape(1, packets)
     table_t = byte_table.T

time: 113 us -> 113 us (level)
  waiting for transfers between devices: 34.1 us -> 26.5 us
  starting transfers between devices: 38.3 us -> 43 us
  Pallas kernels: 33.3 us -> 35.6 us
    ppermute x28, waiting for transfers between devices: 24 us -> 16.8 us  [swap(): lax.ppermute(value, AXES, [(i, i + ((i // stride % size ^ d) - i // strid...]
    ppermute x28, starting transfers between devices: 28.5 us -> 33.2 us  [swap(): lax.ppermute(value, AXES, [(i, i + ((i // stride % size ^ d) - i // strid...]
  transfers between devices with their start and end apart: 30 -> 30, of which waited for: 12 -> 10; matrix products, arithmetic and copies ran while one was open for 2% -> 2% of each run, Pallas kernels for 12% -> 14%
where the time goes in v7:
time: 113 us; the launch traced here: 112 us
  starting transfers between devices  43 us (38%)
  Pallas kernels  35.6 us (32%)
  waiting for transfers between devices  26.5 us (23%)
  local copies, waits for them, and re-layouts  3.74 us (3%)
  other arithmetic  2.04 us (2%)
    ppermute x28, starting transfers between devices, swap(): lax.ppermute(value, AXES, [(i, i + ((i // stride % size ^ d) - i // strid...  33.2 us
    ppermute x28, waiting for transfers between devices, swap(): lax.ppermute(value, AXES, [(i, i + ((i // stride % size ^ d) - i // strid...  16.8 us
    pallas_call x1, Pallas kernels, conv_back(): pl.pallas_call(functools.partial(conv_back_kernel, capacity), grid=(KERNE...  12.1 us
    pallas_call x1, Pallas kernels, session_layer(): pl.pallas_call(session_kernel, in_specs=[pl.BlockSpec(memory_space=pltpu....  10.3 us
    all_to_all x2, starting transfers between devices, exchange(): lax.all_to_all(rows.reshape(groups, capacity, rows.shape[1]), 'dp', split...  9.8 us
    all_to_all x2, waiting for transfers between devices, exchange(): lax.all_to_all(rows.reshape(groups, capacity, rows.shape[1]), 'dp', split...  9.72 us
    pallas_call x1, Pallas kernels, embed(): pl.pallas_call(functools.partial(embed_kernel, capacity), grid=(steps,),...  8.45 us
    pallas_call x2, Pallas kernels, assemble(): pl.pallas_call(kernel, in_specs=[pl.BlockSpec(memory_space=pltpu.SMEM)] +...  4.68 us
  transfers between devices with their start and end apart: 30, of which 10 were waited for; matrix products, arithmetic and copies ran while one was open for 2% of the time, Pallas kernels for 14%

profile of v7, /device:TPU:11, one launch (start us, length us, event | category | flops | bytes accessed | tf_op | source)
XLA Modules:
  0.0 111.6 jit_solution(3245356929581531195)
XLA Ops:
  0.7 8.4 %embed.1 = (bf16[256,640]{1,0:T(8,128)(2,1)}, bf16[512,4096]{1,0:T(8,128)(2,1)}, bf16[8,32,128]{2,1,0:T(8,128)(2,1)}) custom-call(s32[128,256]{1,0:T(8,128)} %bytes_ref.1, s32[1,128]{1,0:T(1,128)} %bitcast.41, s32[1,128]{1,0:T(1,128)} %bitcast.47, bf16[64,256]{1,0:T(8,128)(2,1)} %bitcast.39, bf16[512,512]{1,0:T(8,128)(2,1)} %w_ref.3), custom_call_target="tpu_custom_call" | custom-call | flops 10000000000 | bytes 5000000 | tf_op jit(solution)/shard_map/embed/pallas_call | solution.py:141
  9.1 5.7 %all-to-all-start = ((bf16[8,32,640]{2,1,0:T(8,128)(2,1)}), bf16[8,32,640]{2,1,0:T(8,128)(2,1)S(1)}, u32[]{:S(2)}, u32[]{:S(2)}) async-start(bf16[8,32,640]{2,1,0:T(8,128)(2,1)} %bitcast.46), calls=%async_computation | async-start | bytes 655360 | tf_op jit(solution)/shard_map/all_to_all | solution.py:569
  14.8 0.1 pad_add_fusion.core_ref.place_ref
  14.9 7.2 %all-to-all-done = bf16[8,32,640]{2,1,0:T(8,128)(2,1)S(1)} async-done(((bf16[8,32,640]{2,1,0:T(8,128)(2,1)}), bf16[8,32,640]{2,1,0:T(8,128)(2,1)S(1)}, u32[]{:S(2)}, u32[]{:S(2)}) %all-to-all-start) | async-done | bytes 327712 | tf_op jit(solution)/shard_map/all_to_all | solution.py:569
  22.2 1.4 %copy-done.5 = bf16[512,1536]{1,0:T(8,128)(2,1)S(1)} copy-done((bf16[512,1536]{1,0:T(8,128)(2,1)S(1)}, bf16[512,1536]{1,0:T(8,128)(2,1)}, u32[]{:S(2)}) %copy-start.5) | copy-done | bytes 1572888
  23.6 10.3 %session_layer.1 = (f32[16,128]{1,0:T(8,128)}, bf16[256,512]{1,0:T(8,128)(2,1)}, bf16[4352,128]{1,0:T(8,128)(2,1)S(1)}, bf16[4352,128]{1,0:T(8,128)(2,1)S(1)}, f32[16,128]{1,0:T(8,128)S(1)}) custom-call(s32[2]{0:T(128)S(1)} %pad_add_fusion.core_ref.place_ref, bf16[256,640]{1,0:T(8,128)(2,1)S(1)} %bitcast.33, s32[1,16]{1,0:T(1,128)S(1)} %bitcast.43, ...), custom_call_target="tpu_custom_call" | custom-call | flops 10000000000 | bytes 5000000 | tf_op jit(solution)/shard_map/session_layer/pallas_call | solution.py:293
  33.9 3.2 %collective-permute-start = (bf16[4352,128]{1,0:T(8,128)(2,1)S(1)}, bf16[4352,128]{1,0:T(8,128)(2,1)}, u32[]{:S(2)}, u32[]{:S(2)}) collective-permute-start(bf16[4352,128]{1,0:T(8,128)(2,1)S(1)} %get-tuple-element.43), channel_id=1, source_target_pairs={{0,1},{1,0},{2,3},{3,2},{4,5},{5,4},{6,7},{7,6},{8,9},{9,8},{10,11... | collective-permute-start | bytes 3342344 | tf_op jit(solution)/shard_map/ppermute | solution.py:490
  37.1 4.1 %all-to-all-start.1 = ((bf16[8,32,512]{2,1,0:T(8,128)(2,1)}), bf16[8,32,512]{2,1,0:T(8,128)(2,1)S(1)}, u32[]{:S(2)}, u32[]{:S(2)}) async-start(bf16[8,32,512]{2,1,0:T(8,128)(2,1)} %bitcast.8), calls=%async_computation.1 | async-start | bytes 524288 | tf_op jit(solution)/shard_map/all_to_all | solution.py:569
  41.2 1.6 %add_convert_fusion.4 = (bf16[1088,128]{1,0:T(8,128)(2,1)S(1)}, bf16[1088,128]{1,0:T(8,128)(2,1)S(1)}, bf16[1088,128]{1,0:T(8,128)(2,1)S(1)}, bf16[1088,128]{1,0:T(8,128)(2,1)S(1)}) fusion(bf16[4352,128]{1,0:T(8,128)(2,1)} %collective-permute-done, bf16[4352,128]{1,0:T(8,128)(2,1)S(1)} %get-tuple-element.42), kind=kLoop, calls=%fused_computation.4 | loop fusion | flops 2228224 | bytes 3342336 | tf_op jit(solution)/shard_map/convert_element_type | solution.py:526
  42.8 0.3 collective-permute-start.1
  43.1 1.2 %collective-permute-start.2 = (bf16[1088,128]{1,0:T(8,128)(2,1)S(1)}, bf16[1088,128]{1,0:T(8,128)(2,1)S(1)}, u32[]{:S(2)}, u32[]{:S(2)}) collective-permute-start(bf16[1088,128]{1,0:T(8,128)(2,1)S(1)} %get-tuple-element.77), channel_id=1, source_target_pairs={{0,4},{1,5},{2,6},{3,7},{4,0},{5,1},{6,2},{7,3},{8,12},{9,13},{10,... | collective-permute-start | bytes 835592 | tf_op jit(solution)/shard_map/ppermute | solution.py:490
  44.3 1.2 %collective-permute-start.3 = (bf16[1088,128]{1,0:T(8,128)(2,1)S(1)}, bf16[1088,128]{1,0:T(8,128)(2,1)S(1)}, u32[]{:S(2)}, u32[]{:S(2)}) collective-permute-start(bf16[1088,128]{1,0:T(8,128)(2,1)S(1)} %get-tuple-element.76), channel_id=1, source_target_pairs={{0,6},{1,7},{2,4},{3,5},{4,2},{5,3},{6,0},{7,1},{8,14},{9,15},{10,... | collective-permute-start | bytes 835592 | tf_op jit(solution)/shard_map/ppermute | solution.py:490
  45.5 2.5 %all-to-all-done.1 = bf16[8,32,512]{2,1,0:T(8,128)(2,1)S(1)} async-done(((bf16[8,32,512]{2,1,0:T(8,128)(2,1)}), bf16[8,32,512]{2,1,0:T(8,128)(2,1)S(1)}, u32[]{:S(2)}, u32[]{:S(2)}) %all-to-all-start.1) | async-done | bytes 262176 | tf_op jit(solution)/shard_map/all_to_all | solution.py:569
  48.0 2.2 %copy-done = bf16[512,4096]{1,0:T(8,128)(2,1)S(1)} copy-done((bf16[512,4096]{1,0:T(8,128)(2,1)S(1)}, bf16[512,4096]{1,0:T(8,128)(2,1)}, u32[]{:S(2)}) %copy-start) | copy-done | bytes 4194328
  50.2 12.1 %conv_back.1 = (bf16[1152,128]{1,0:T(8,128)(2,1)S(1)}, bf16[1152,128]{1,0:T(8,128)(2,1)S(1)}) custom-call(s32[2]{0:T(128)S(1)} %pad_add_fusion.core_ref.place_ref, bf16[256,512]{1,0:T(8,128)(2,1)S(1)} %bitcast.32, s32[1,128]{1,0:T(1,128)S(1)} %bitcast.42, bf16[8,32,128]{2,1,0:T(8,128)(2,1)S(1)} %copy-done.2, bf16[512,4096]{1,0:T(8,128)(2,1)S(1)} %copy-done, ...), custom_call_target="tpu_custom_call" | custom-call | flops 1000000000 | bytes 1000000 | tf_op jit(solution)/shard_map/conv_back/pallas_call | solution.py:389
  62.3 2.6 %collective-permute-start.7 = (bf16[1152,128]{1,0:T(8,128)(2,1)S(1)}, bf16[1152,128]{1,0:T(8,128)(2,1)S(1)}, u32[]{:S(2)}, u32[]{:S(2)}) collective-permute-start(bf16[1152,128]{1,0:T(8,128)(2,1)S(1)} %get-tuple-element.53), channel_id=1, source_target_pairs={{0,1},{1,0},{2,3},{3,2},{4,5},{5,4},{6,7},{7,6},{8,9},{9,8},{10,11... | collective-permute-start | bytes 884744 | tf_op jit(solution)/shard_map/ppermute | solution.py:490
  64.9 0.2 add_convert_fusion
  65.1 0.7 collective-permute-start.4
  65.9 0.4 collective-permute-start.5
  66.2 1.6 %collective-permute-start.6 = (bf16[272,128]{1,0:T(8,128)(2,1)S(1)}, bf16[272,128]{1,0:T(8,128)(2,1)S(1)}, u32[]{:S(2)}, u32[]{:S(2)}) collective-permute-start(bf16[272,128]{1,0:T(8,128)(2,1)S(1)} %get-tuple-element.83), channel_id=1, source_target_pairs={{0,24},{1,25},{2,26},{3,27},{4,28},{5,29},{6,30},{7,31},{8,16},{9,... | collective-permute-start | bytes 208904 | tf_op jit(solution)/shard_map/ppermute | solution.py:490
  67.8 0.1 add_convert_fusion.7
  67.9 0.3 collective-permute-start.14
  68.2 0.3 collective-permute-start.15
  68.6 0.4 collective-permute-done.4
  69.0 1.7 %collective-permute-start.16 = (bf16[288,128]{1,0:T(8,128)(2,1)S(1)}, bf16[288,128]{1,0:T(8,128)(2,1)S(1)}, u32[]{:S(2)}, u32[]{:S(2)}) collective-permute-start(bf16[288,128]{1,0:T(8,128)(2,1)S(1)} %get-tuple-element.79), channel_id=1, source_target_pairs={{0,6},{1,7},{2,4},{3,5},{4,2},{5,3},{6,0},{7,1},{8,14},{9,15},{10,... | collective-permute-start | bytes 221192 | tf_op jit(solution)/shard_map/ppermute | solution.py:490
  70.6 3.9 %collective-permute-done.6 = bf16[272,128]{1,0:T(8,128)(2,1)S(1)} collective-permute-done((bf16[272,128]{1,0:T(8,128)(2,1)S(1)}, bf16[272,128]{1,0:T(8,128)(2,1)S(1)}, u32[]{:S(2)}, u32[]{:S(2)}) %collective-permute-start.6) | collective-permute-done | bytes 69664 | tf_op jit(solution)/shard_map/ppermute | solution.py:490
  74.8 1.3 %collective-permute-start.9 = (bf16[272,128]{1,0:T(8,128)(2,1)S(1)}, bf16[272,128]{1,0:T(8,128)(2,1)S(1)}, u32[]{:S(2)}, u32[]{:S(2)}) collective-permute-start(bf16[272,128]{1,0:T(8,128)(2,1)S(1)} %get-tuple-element.74), channel_id=1, source_target_pairs={{0,16},{1,17},{2,18},{3,19},{4,20},{5,21},{6,22},{7,23},{8,24},{9,... | collective-permute-start | bytes 208904 | tf_op jit(solution)/shard_map/ppermute | solution.py:490
  76.1 1.3 %collective-permute-start.10 = (bf16[272,128]{1,0:T(8,128)(2,1)S(1)}, bf16[272,128]{1,0:T(8,128)(2,1)S(1)}, u32[]{:S(2)}, u32[]{:S(2)}) collective-permute-start(bf16[272,128]{1,0:T(8,128)(2,1)S(1)} %get-tuple-element.74), channel_id=1, source_target_pairs={{0,24},{1,25},{2,26},{3,27},{4,28},{5,29},{6,30},{7,31},{8,16},{9,... | collective-permute-start | bytes 208904 | tf_op jit(solution)/shard_map/ppermute | solution.py:490
  77.4 1.0 collective-permute-start.17
  78.5 0.4 collective-permute-start.18
  78.9 1.3 %collective-permute-start.19 = (bf16[288,128]{1,0:T(8,128)(2,1)S(1)}, bf16[288,128]{1,0:T(8,128)(2,1)S(1)}, u32[]{:S(2)}, u32[]{:S(2)}) collective-permute-start(bf16[288,128]{1,0:T(8,128)(2,1)S(1)} %add_convert_fusion.6), channel_id=1, source_target_pairs={{0,24},{1,25},{2,26},{3,27},{4,28},{5,29},{6,30},{7,31},{8,16},{9,... | collective-permute-start | bytes 221192 | tf_op jit(solution)/shard_map/ppermute | solution.py:490
  80.2 4.5 %collective-permute-done.10 = bf16[272,128]{1,0:T(8,128)(2,1)S(1)} collective-permute-done((bf16[272,128]{1,0:T(8,128)(2,1)S(1)}, bf16[272,128]{1,0:T(8,128)(2,1)S(1)}, u32[]{:S(2)}, u32[]{:S(2)}) %collective-permute-start.10) | collective-permute-done | bytes 69664 | tf_op jit(solution)/shard_map/ppermute | solution.py:490
  84.7 0.3 collective-permute-start.11
  85.1 0.1 collective-permute-start.12
  85.2 2.2 %collective-permute-start.13 = (bf16[1088,128]{1,0:T(8,128)(2,1)S(1)}, bf16[1088,128]{1,0:T(8,128)(2,1)S(1)}, u32[]{:S(2)}, u32[]{:S(2)}) collective-permute-start(bf16[1088,128]{1,0:T(8,128)(2,1)S(1)} %bitcast.36), channel_id=1, source_target_pairs={{0,6},{1,7},{2,4},{3,5},{4,2},{5,3},{6,0},{7,1},{8,14},{9,15},{10,... | collective-permute-start | bytes 835592 | tf_op jit(solution)/shard_map/ppermute | solution.py:490
  87.4 2.6 %collective-permute-done.19 = bf16[288,128]{1,0:T(8,128)(2,1)S(1)} collective-permute-done((bf16[288,128]{1,0:T(8,128)(2,1)S(1)}, bf16[288,128]{1,0:T(8,128)(2,1)S(1)}, u32[]{:S(2)}, u32[]{:S(2)}) %collective-permute-start.19) | collective-permute-done | bytes 73760 | tf_op jit(solution)/shard_map/ppermute | solution.py:490
  90.1 2.4 %collective-permute-start.20 = (bf16[288,128]{1,0:T(8,128)(2,1)S(1)}, bf16[288,128]{1,0:T(8,128)(2,1)S(1)}, u32[]{:S(2)}, u32[]{:S(2)}) collective-permute-start(bf16[288,128]{1,0:T(8,128)(2,1)S(1)} %add_convert_fusion.5), channel_id=1, source_target_pairs={{0,1},{1,0},{2,3},{3,2},{4,5},{5,4},{6,7},{7,6},{8,9},{9,8},{10,11... | collective-permute-start | bytes 221192 | tf_op jit(solution)/shard_map/ppermute | solution.py:490
  92.6 0.8 collective-permute-done.20
  93.5 0.8 collective-permute-done.13.refs_3_
  94.2 5.9 %collective-permute-start.22 = (bf16[1088,128]{1,0:T(8,128)(2,1)S(1)}, bf16[1088,128]{1,0:T(8,128)(2,1)S(1)}, u32[]{:S(2)}, u32[]{:S(2)}) collective-permute-start(bf16[1088,128]{1,0:T(8,128)(2,1)S(1)} %collective-permute-done.11.refs_1_), channel_id=1, source_target_pairs={{0,1},{1,0},{2,3},{3,2},{4,5},{5,4},{6,7},{7,6},{8,9},{9,8},{10,11... | collective-permute-start | bytes 835592 | tf_op jit(solution)/shard_map/ppermute | solution.py:490
  100.1 0.5 collective-permute-start.24
  100.6 1.2 %collective-permute-start.25 = (bf16[576,128]{1,0:T(8,128)(2,1)S(1)}, bf16[576,128]{1,0:T(8,128)(2,1)S(1)}, u32[]{:S(2)}, u32[]{:S(2)}) collective-permute-start(bf16[576,128]{1,0:T(8,128)(2,1)S(1)} %pad_maximum_fusion.refs_0_), channel_id=1, source_target_pairs={{0,2},{1,3},{2,0},{3,1},{4,6},{5,7},{6,4},{7,5},{8,10},{9,11},{10,... | collective-permute-start | bytes 442376 | tf_op jit(solution)/shard_map/ppermute | solution.py:490
  101.8 0.3 collective-permute-start.26
  102.2 1.1 collective-permute-start.27
  103.3 3.0 %early_out.1 = (f32[512,1536]{1,0:T(8,128)}, f32[512,512]{1,0:T(8,128)}, f32[512,128]{1,0:T(8,128)}) custom-call(s32[2]{0:T(128)S(1)} %pad_add_fusion.core_ref.place_ref, bf16[1088,128]{1,0:T(8,128)(2,1)S(1)} %bitcast.38, bf16[1088,128]{1,0:T(8,128)(2,1)S(1)} %collective-permute-done.11.refs_1_, bf16[1088,128]{1,0:T(8,128)(2,1)S(1)} %collective-permute-done.12.refs_2_, ...), custom_call_target="tpu_custom_call" | custom-call | flops 1000000000 | bytes 5000000 | tf_op jit(solution)/shard_map/early_out/pallas_call | solution.py:458
  106.3 1.0 collective-permute-done.26.refs_2_
  107.2 2.7 %collective-permute-done.27.refs_3_ = bf16[576,128]{1,0:T(8,128)(2,1)S(1)} collective-permute-done((bf16[576,128]{1,0:T(8,128)(2,1)S(1)}, bf16[576,128]{1,0:T(8,128)(2,1)S(1)}, u32[]{:S(2)}, u32[]{:S(2)}) %collective-permute-start.27) | collective-permute-done | bytes 147488 | tf_op jit(solution)/shard_map/ppermute | solution.py:490
  109.9 1.7 %late_out.1 = (f32[512,512]{1,0:T(8,128)}, f32[64,256]{1,0:T(8,128)}, f32[1,512]{1,0:T(1,128)}) custom-call(s32[2]{0:T(128)S(1)} %pad_add_fusion.core_ref.place_ref, bf16[576,128]{1,0:T(8,128)(2,1)S(1)} %pad_maximum_fusion.refs_0_, bf16[576,128]{1,0:T(8,128)(2,1)S(1)} %collective-permute-done.25.refs_1_, ...), custom_call_target="tpu_custom_call" | custom-call | flops 1000000000 | bytes 5000000 | tf_op jit(solution)/shard_map/late_out/pallas_call | solution.py:458
  (51 shorter events, 0.5 us)
Async XLA Ops:
  0.6 14.2 %copy-start.9 = (bf16[512]{0:T(512)(128)(2,1)S(1)}, bf16[512]{0:T(512)(128)(2,1)}, u32[]{:S(2)}) copy-start(bf16[512]{0:T(512)(128)(2,1)} %param.16) | copy-start | bytes 3076
  0.6 21.5 %copy-start.6 = (bf16[512,512]{1,0:T(8,128)(2,1)S(1)}, bf16[512,512]{1,0:T(8,128)(2,1)}, u32[]{:S(2)}) copy-start(bf16[512,512]{1,0:T(8,128)(2,1)} %wo_ref.1) | copy-start | bytes 1572868
  0.7 21.5 %copy-start.7 = (bf16[512,128]{1,0:T(8,128)(2,1)S(1)}, bf16[512,128]{1,0:T(8,128)(2,1)}, u32[]{:S(2)}) copy-start(bf16[512,128]{1,0:T(8,128)(2,1)} %wh_ref.1) | copy-start | bytes 393220
  0.7 21.5 %copy-start.8 = (s32[16]{0:T(128)S(1)}, s32[16]{0:T(128)}, u32[]{:S(2)}) copy-start(s32[16]{0:T(128)} %param.13) | copy-start | bytes 196
  9.1 13.0 %all-to-all-start = ((bf16[8,32,640]{2,1,0:T(8,128)(2,1)}), bf16[8,32,640]{2,1,0:T(8,128)(2,1)S(1)}, u32[]{:S(2)}, u32[]{:S(2)}) async-start(bf16[8,32,640]{2,1,0:T(8,128)(2,1)} %bitcast.46), calls=%async_computation | async-start | bytes 655360 | tf_op jit(solution)/shard_map/all_to_all | solution.py:569
  22.2 1.4 %copy-start.5 = (bf16[512,1536]{1,0:T(8,128)(2,1)S(1)}, bf16[512,1536]{1,0:T(8,128)(2,1)}, u32[]{:S(2)}) copy-start(bf16[512,1536]{1,0:T(8,128)(2,1)} %wp_ref.1) | copy-start | bytes 4718596
  33.9 7.3 %collective-permute-start = (bf16[4352,128]{1,0:T(8,128)(2,1)S(1)}, bf16[4352,128]{1,0:T(8,128)(2,1)}, u32[]{:S(2)}, u32[]{:S(2)}) collective-permute-start(bf16[4352,128]{1,0:T(8,128)(2,1)S(1)} %get-tuple-element.43), channel_id=1, source_target_pairs={{0,1},{1,0},{2,3},{3,2},{4,5},{5,4},{6,7},{7,6},{8,9},{9,8},{10,11... | collective-permute-start | bytes 3342344 | tf_op jit(solution)/shard_map/ppermute | solution.py:490
  37.1 10.9 %all-to-all-start.1 = ((bf16[8,32,512]{2,1,0:T(8,128)(2,1)}), bf16[8,32,512]{2,1,0:T(8,128)(2,1)S(1)}, u32[]{:S(2)}, u32[]{:S(2)}) async-start(bf16[8,32,512]{2,1,0:T(8,128)(2,1)} %bitcast.8), calls=%async_computation.1 | async-start | bytes 524288 | tf_op jit(solution)/shard_map/all_to_all | solution.py:569
  41.2 6.8 %copy-start.1 = (bf16[512,512]{1,0:T(8,128)(2,1)S(1)}, bf16[512,512]{1,0:T(8,128)(2,1)}, u32[]{:S(2)}) copy-start(bf16[512,512]{1,0:T(8,128)(2,1)} %w_ref.3) | copy-start | bytes 1572868
  41.2 6.8 %copy-start.2 = (bf16[8,32,128]{2,1,0:T(8,128)(2,1)S(1)}, bf16[8,32,128]{2,1,0:T(8,128)(2,1)}, u32[]{:S(2)}) copy-start(bf16[8,32,128]{2,1,0:T(8,128)(2,1)} %get-tuple-element.46.codes_ref) | copy-start | bytes 196612
  41.2 6.8 %copy-start.3 = (bf16[256,64]{0,1:T(8,128)(2,1)S(1)}, bf16[256,64]{0,1:T(8,128)(2,1)}, u32[]{:S(2)}) copy-start(bf16[256,64]{0,1:T(8,128)(2,1)} %param.14) | copy-start | bytes 98308
  41.2 6.8 %copy-start.4 = (s32[128]{0:T(128)S(1)}, s32[128]{0:T(128)}, u32[]{:S(2)}) copy-start(s32[128]{0:T(128)} %param.11) | copy-start | bytes 1540
  42.8 22.1 %collective-permute-start.1 = (bf16[1088,128]{1,0:T(8,128)(2,1)S(1)}, bf16[1088,128]{1,0:T(8,128)(2,1)S(1)}, u32[]{:S(2)}, u32[]{:S(2)}) collective-permute-start(bf16[1088,128]{1,0:T(8,128)(2,1)S(1)} %get-tuple-element.78), channel_id=1, source_target_pairs={{0,2},{1,3},{2,0},{3,1},{4,6},{5,7},{6,4},{7,5},{8,10},{9,11},{10,... | collective-permute-start | bytes 835592 | tf_op jit(solution)/shard_map/ppermute | solution.py:490
  43.1 21.8 %collective-permute-start.2 = (bf16[1088,128]{1,0:T(8,128)(2,1)S(1)}, bf16[1088,128]{1,0:T(8,128)(2,1)S(1)}, u32[]{:S(2)}, u32[]{:S(2)}) collective-permute-start(bf16[1088,128]{1,0:T(8,128)(2,1)S(1)} %get-tuple-element.77), channel_id=1, source_target_pairs={{0,4},{1,5},{2,6},{3,7},{4,0},{5,1},{6,2},{7,3},{8,12},{9,13},{10,... | collective-permute-start | bytes 835592 | tf_op jit(solution)/shard_map/ppermute | solution.py:490
  44.3 20.6 %collective-permute-start.3 = (bf16[1088,128]{1,0:T(8,128)(2,1)S(1)}, bf16[1088,128]{1,0:T(8,128)(2,1)S(1)}, u32[]{:S(2)}, u32[]{:S(2)}) collective-permute-start(bf16[1088,128]{1,0:T(8,128)(2,1)S(1)} %get-tuple-element.76), channel_id=1, source_target_pairs={{0,6},{1,7},{2,4},{3,5},{4,2},{5,3},{6,0},{7,1},{8,14},{9,15},{10,... | collective-permute-start | bytes 835592 | tf_op jit(solution)/shard_map/ppermute | solution.py:490
  48.0 2.2 %copy-start = (bf16[512,4096]{1,0:T(8,128)(2,1)S(1)}, bf16[512,4096]{1,0:T(8,128)(2,1)}, u32[]{:S(2)}) copy-start(bf16[512,4096]{1,0:T(8,128)(2,1)} %get-tuple-element.47.slope_ref) | copy-start | bytes 12582916
  62.3 5.5 %collective-permute-start.7 = (bf16[1152,128]{1,0:T(8,128)(2,1)S(1)}, bf16[1152,128]{1,0:T(8,128)(2,1)S(1)}, u32[]{:S(2)}, u32[]{:S(2)}) collective-permute-start(bf16[1152,128]{1,0:T(8,128)(2,1)S(1)} %get-tuple-element.53), channel_id=1, source_target_pairs={{0,1},{1,0},{2,3},{3,2},{4,5},{5,4},{6,7},{7,6},{8,9},{9,8},{10,11... | collective-permute-start | bytes 884744 | tf_op jit(solution)/shard_map/ppermute | solution.py:490
  65.1 3.8 %collective-permute-start.4 = (bf16[272,128]{1,0:T(8,128)(2,1)S(1)}, bf16[272,128]{1,0:T(8,128)(2,1)S(1)}, u32[]{:S(2)}, u32[]{:S(2)}) collective-permute-start(bf16[272,128]{1,0:T(8,128)(2,1)S(1)} %get-tuple-element.85), channel_id=1, source_target_pairs={{0,8},{1,9},{2,10},{3,11},{4,12},{5,13},{6,14},{7,15},{8,0},{9,1},... | collective-permute-start | bytes 208904 | tf_op jit(solution)/shard_map/ppermute | solution.py:490
  65.9 4.8 %collective-permute-start.5 = (bf16[272,128]{1,0:T(8,128)(2,1)S(1)}, bf16[272,128]{1,0:T(8,128)(2,1)S(1)}, u32[]{:S(2)}, u32[]{:S(2)}) collective-permute-start(bf16[272,128]{1,0:T(8,128)(2,1)S(1)} %get-tuple-element.84), channel_id=1, source_target_pairs={{0,16},{1,17},{2,18},{3,19},{4,20},{5,21},{6,22},{7,23},{8,24},{9,... | collective-permute-start | bytes 208904 | tf_op jit(solution)/shard_map/ppermute | solution.py:490
  66.2 8.3 %collective-permute-start.6 = (bf16[272,128]{1,0:T(8,128)(2,1)S(1)}, bf16[272,128]{1,0:T(8,128)(2,1)S(1)}, u32[]{:S(2)}, u32[]{:S(2)}) collective-permute-start(bf16[272,128]{1,0:T(8,128)(2,1)S(1)} %get-tuple-element.83), channel_id=1, source_target_pairs={{0,24},{1,25},{2,26},{3,27},{4,28},{5,29},{6,30},{7,31},{8,16},{9,... | collective-permute-start | bytes 208904 | tf_op jit(solution)/shard_map/ppermute | solution.py:490
  67.9 8.2 %collective-permute-start.14 = (bf16[288,128]{1,0:T(8,128)(2,1)S(1)}, bf16[288,128]{1,0:T(8,128)(2,1)S(1)}, u32[]{:S(2)}, u32[]{:S(2)}) collective-permute-start(bf16[288,128]{1,0:T(8,128)(2,1)S(1)} %get-tuple-element.81), channel_id=1, source_target_pairs={{0,2},{1,3},{2,0},{3,1},{4,6},{5,7},{6,4},{7,5},{8,10},{9,11},{10,... | collective-permute-start | bytes 221192 | tf_op jit(solution)/shard_map/ppermute | solution.py:490
  68.2 9.2 %collective-permute-start.15 = (bf16[288,128]{1,0:T(8,128)(2,1)S(1)}, bf16[288,128]{1,0:T(8,128)(2,1)S(1)}, u32[]{:S(2)}, u32[]{:S(2)}) collective-permute-start(bf16[288,128]{1,0:T(8,128)(2,1)S(1)} %get-tuple-element.80), channel_id=1, source_target_pairs={{0,4},{1,5},{2,6},{3,7},{4,0},{5,1},{6,2},{7,3},{8,12},{9,13},{10,... | collective-permute-start | bytes 221192 | tf_op jit(solution)/shard_map/ppermute | solution.py:490
  69.0 8.4 %collective-permute-start.16 = (bf16[288,128]{1,0:T(8,128)(2,1)S(1)}, bf16[288,128]{1,0:T(8,128)(2,1)S(1)}, u32[]{:S(2)}, u32[]{:S(2)}) collective-permute-start(bf16[288,128]{1,0:T(8,128)(2,1)S(1)} %get-tuple-element.79), channel_id=1, source_target_pairs={{0,6},{1,7},{2,4},{3,5},{4,2},{5,3},{6,0},{7,1},{8,14},{9,15},{10,... | collective-permute-start | bytes 221192 | tf_op jit(solution)/shard_map/ppermute | solution.py:490
  74.7 4.2 %collective-permute-start.8 = (bf16[272,128]{1,0:T(8,128)(2,1)S(1)}, bf16[272,128]{1,0:T(8,128)(2,1)S(1)}, u32[]{:S(2)}, u32[]{:S(2)}) collective-permute-start(bf16[272,128]{1,0:T(8,128)(2,1)S(1)} %get-tuple-element.74), channel_id=1, source_target_pairs={{0,8},{1,9},{2,10},{3,11},{4,12},{5,13},{6,14},{7,15},{8,0},{9,1},... | collective-permute-start | bytes 208904 | tf_op jit(solution)/shard_map/ppermute | solution.py:490
  74.8 5.4 %collective-permute-start.9 = (bf16[272,128]{1,0:T(8,128)(2,1)S(1)}, bf16[272,128]{1,0:T(8,128)(2,1)S(1)}, u32[]{:S(2)}, u32[]{:S(2)}) collective-permute-start(bf16[272,128]{1,0:T(8,128)(2,1)S(1)} %get-tuple-element.74), channel_id=1, source_target_pairs={{0,16},{1,17},{2,18},{3,19},{4,20},{5,21},{6,22},{7,23},{8,24},{9,... | collective-permute-start | bytes 208904 | tf_op jit(solution)/shard_map/ppermute | solution.py:490
  76.1 8.6 %collective-permute-start.10 = (bf16[272,128]{1,0:T(8,128)(2,1)S(1)}, bf16[272,128]{1,0:T(8,128)(2,1)S(1)}, u32[]{:S(2)}, u32[]{:S(2)}) collective-permute-start(bf16[272,128]{1,0:T(8,128)(2,1)S(1)} %get-tuple-element.74), channel_id=1, source_target_pairs={{0,24},{1,25},{2,26},{3,27},{4,28},{5,29},{6,30},{7,31},{8,16},{9,... | collective-permute-start | bytes 208904 | tf_op jit(solution)/shard_map/ppermute | solution.py:490
  77.4 7.7 %collective-permute-start.17 = (bf16[288,128]{1,0:T(8,128)(2,1)S(1)}, bf16[288,128]{1,0:T(8,128)(2,1)S(1)}, u32[]{:S(2)}, u32[]{:S(2)}) collective-permute-start(bf16[288,128]{1,0:T(8,128)(2,1)S(1)} %add_convert_fusion.6), channel_id=1, source_target_pairs={{0,8},{1,9},{2,10},{3,11},{4,12},{5,13},{6,14},{7,15},{8,0},{9,1},... | collective-permute-start | bytes 221192 | tf_op jit(solution)/shard_map/ppermute | solution.py:490
  78.5 9.0 %collective-permute-start.18 = (bf16[288,128]{1,0:T(8,128)(2,1)S(1)}, bf16[288,128]{1,0:T(8,128)(2,1)S(1)}, u32[]{:S(2)}, u32[]{:S(2)}) collective-permute-start(bf16[288,128]{1,0:T(8,128)(2,1)S(1)} %add_convert_fusion.6), channel_id=1, source_target_pairs={{0,16},{1,17},{2,18},{3,19},{4,20},{5,21},{6,22},{7,23},{8,24},{9,... | collective-permute-start | bytes 221192 | tf_op jit(solution)/shard_map/ppermute | solution.py:490
  78.9 11.2 %collective-permute-start.19 = (bf16[288,128]{1,0:T(8,128)(2,1)S(1)}, bf16[288,128]{1,0:T(8,128)(2,1)S(1)}, u32[]{:S(2)}, u32[]{:S(2)}) collective-permute-start(bf16[288,128]{1,0:T(8,128)(2,1)S(1)} %add_convert_fusion.6), channel_id=1, source_target_pairs={{0,24},{1,25},{2,26},{3,27},{4,28},{5,29},{6,30},{7,31},{8,16},{9,... | collective-permute-start | bytes 221192 | tf_op jit(solution)/shard_map/ppermute | solution.py:490
  84.7 8.7 %collective-permute-start.11 = (bf16[1088,128]{1,0:T(8,128)(2,1)S(1)}, bf16[1088,128]{1,0:T(8,128)(2,1)S(1)}, u32[]{:S(2)}, u32[]{:S(2)}) collective-permute-start(bf16[1088,128]{1,0:T(8,128)(2,1)S(1)} %bitcast.34), channel_id=1, source_target_pairs={{0,2},{1,3},{2,0},{3,1},{4,6},{5,7},{6,4},{7,5},{8,10},{9,11},{10,... | collective-permute-start | bytes 835592 | tf_op jit(solution)/shard_map/ppermute | solution.py:490
  85.1 8.4 %collective-permute-start.12 = (bf16[1088,128]{1,0:T(8,128)(2,1)S(1)}, bf16[1088,128]{1,0:T(8,128)(2,1)S(1)}, u32[]{:S(2)}, u32[]{:S(2)}) collective-permute-start(bf16[1088,128]{1,0:T(8,128)(2,1)S(1)} %bitcast.35), channel_id=1, source_target_pairs={{0,4},{1,5},{2,6},{3,7},{4,0},{5,1},{6,2},{7,3},{8,12},{9,13},{10,... | collective-permute-start | bytes 835592 | tf_op jit(solution)/shard_map/ppermute | solution.py:490
  85.2 9.0 %collective-permute-start.13 = (bf16[1088,128]{1,0:T(8,128)(2,1)S(1)}, bf16[1088,128]{1,0:T(8,128)(2,1)S(1)}, u32[]{:S(2)}, u32[]{:S(2)}) collective-permute-start(bf16[1088,128]{1,0:T(8,128)(2,1)S(1)} %bitcast.36), channel_id=1, source_target_pairs={{0,6},{1,7},{2,4},{3,5},{4,2},{5,3},{6,0},{7,1},{8,14},{9,15},{10,... | collective-permute-start | bytes 835592 | tf_op jit(solution)/shard_map/ppermute | solution.py:490
  90.1 3.3 %collective-permute-start.20 = (bf16[288,128]{1,0:T(8,128)(2,1)S(1)}, bf16[288,128]{1,0:T(8,128)(2,1)S(1)}, u32[]{:S(2)}, u32[]{:S(2)}) collective-permute-start(bf16[288,128]{1,0:T(8,128)(2,1)S(1)} %add_convert_fusion.5), channel_id=1, source_target_pairs={{0,1},{1,0},{2,3},{3,2},{4,5},{5,4},{6,7},{7,6},{8,9},{9,8},{10,11... | collective-permute-start | bytes 221192 | tf_op jit(solution)/shard_map/ppermute | solution.py:490
  92.5 9.3 %collective-permute-start.21 = (bf16[1088,128]{1,0:T(8,128)(2,1)S(1)}, bf16[1088,128]{1,0:T(8,128)(2,1)S(1)}, u32[]{:S(2)}, u32[]{:S(2)}) collective-permute-start(bf16[1088,128]{1,0:T(8,128)(2,1)S(1)} %bitcast.37), channel_id=1, source_target_pairs={{0,1},{1,0},{2,3},{3,2},{4,5},{5,4},{6,7},{7,6},{8,9},{9,8},{10,11... | collective-permute-start | bytes 835592 | tf_op jit(solution)/shard_map/ppermute | solution.py:490
  94.2 7.9 %collective-permute-start.22 = (bf16[1088,128]{1,0:T(8,128)(2,1)S(1)}, bf16[1088,128]{1,0:T(8,128)(2,1)S(1)}, u32[]{:S(2)}, u32[]{:S(2)}) collective-permute-start(bf16[1088,128]{1,0:T(8,128)(2,1)S(1)} %collective-permute-done.11.refs_1_), channel_id=1, source_target_pairs={{0,1},{1,0},{2,3},{3,2},{4,5},{5,4},{6,7},{7,6},{8,9},{9,8},{10,11... | collective-permute-start | bytes 835592 | tf_op jit(solution)/shard_map/ppermute | solution.py:490
  100.1 3.2 %collective-permute-start.23 = (bf16[1088,128]{1,0:T(8,128)(2,1)S(1)}, bf16[1088,128]{1,0:T(8,128)(2,1)S(1)}, u32[]{:S(2)}, u32[]{:S(2)}) collective-permute-start(bf16[1088,128]{1,0:T(8,128)(2,1)S(1)} %collective-permute-done.12.refs_2_), channel_id=1, source_target_pairs={{0,1},{1,0},{2,3},{3,2},{4,5},{5,4},{6,7},{7,6},{8,9},{9,8},{10,11... | collective-permute-start | bytes 835592 | tf_op jit(solution)/shard_map/ppermute | solution.py:490
  100.1 3.2 %collective-permute-start.24 = (bf16[1088,128]{1,0:T(8,128)(2,1)S(1)}, bf16[1088,128]{1,0:T(8,128)(2,1)S(1)}, u32[]{:S(2)}, u32[]{:S(2)}) collective-permute-start(bf16[1088,128]{1,0:T(8,128)(2,1)S(1)} %collective-permute-done.13.refs_3_), channel_id=1, source_target_pairs={{0,1},{1,0},{2,3},{3,2},{4,5},{5,4},{6,7},{7,6},{8,9},{9,8},{10,11... | collective-permute-start | bytes 835592 | tf_op jit(solution)/shard_map/ppermute | solution.py:490
  100.6 5.6 %collective-permute-start.25 = (bf16[576,128]{1,0:T(8,128)(2,1)S(1)}, bf16[576,128]{1,0:T(8,128)(2,1)S(1)}, u32[]{:S(2)}, u32[]{:S(2)}) collective-permute-start(bf16[576,128]{1,0:T(8,128)(2,1)S(1)} %pad_maximum_fusion.refs_0_), channel_id=1, source_target_pairs={{0,2},{1,3},{2,0},{3,1},{4,6},{5,7},{6,4},{7,5},{8,10},{9,11},{10,... | collective-permute-start | bytes 442376 | tf_op jit(solution)/shard_map/ppermute | solution.py:490
  101.8 5.4 %collective-permute-start.26 = (bf16[576,128]{1,0:T(8,128)(2,1)S(1)}, bf16[576,128]{1,0:T(8,128)(2,1)S(1)}, u32[]{:S(2)}, u32[]{:S(2)}) collective-permute-start(bf16[576,128]{1,0:T(8,128)(2,1)S(1)} %pad_maximum_fusion.refs_0_), channel_id=1, source_target_pairs={{0,4},{1,5},{2,6},{3,7},{4,0},{5,1},{6,2},{7,3},{8,12},{9,13},{10,... | collective-permute-start | bytes 442376 | tf_op jit(solution)/shard_map/ppermute | solution.py:490
  102.2 7.8 %collective-permute-start.27 = (bf16[576,128]{1,0:T(8,128)(2,1)S(1)}, bf16[576,128]{1,0:T(8,128)(2,1)S(1)}, u32[]{:S(2)}, u32[]{:S(2)}) collective-permute-start(bf16[576,128]{1,0:T(8,128)(2,1)S(1)} %pad_maximum_fusion.refs_0_), channel_id=1, source_target_pairs={{0,6},{1,7},{2,4},{3,5},{4,2},{5,3},{6,0},{7,1},{8,14},{9,15},{10,... | collective-permute-start | bytes 442376 | tf_op jit(solution)/shard_map/ppermute | solution.py:490
